TPU v7x, 32 devices: a whole 2x2x4 slice. The times are simulated.
32 devices in a mesh: grp: 2 (over x), tile: 16 (over z, y, core).
Axes of the slice: x: 2, y: 2, z: 4, core: 2. Of those that a mesh axis runs over, the one named last changes fastest.
Arguments:
- projections: bfloat16 [512, 61, 128], P('grp', None, 'tile'), parts along dimension 0, may hold values from -1.1953125 to 1.1953125
- tilt_angle: float32 [122], P('grp'), parts along dimension 0, may hold values from -1.05 to 1.05
- row_range: int32 [122, 2], P('grp'), parts along dimension 0, may hold values from 0 to 256, as said below
- template_bank: bfloat16 [64, 16, 256], replicated, may hold values from -0.09375 to 0.09375
- rot_index: int32 [8], replicated, may hold values from 0 to 63
Outputs:
- score: float32 [16, 64, 1024], P('tile', 'grp'), parts along dimension 1
There are 2 independent parts, one for each index of `grp`. A program takes and returns all parts, laid end to end along the dimension named above; an argument that names none is the same for every part. Nothing has to cross between parts.
Inputs may be any that keep to these rules, and one draw needn't show every extreme that they name: `row_range`: each tilt's valid rows run from its first value up to but not including its second, which is larger; the tilt of index 30 covers all 256 rows.
All inputs are finite; a program needn't handle non-finite values.
Results may differ from a plain program's by a relative error of at most 0.0095.
Values may be sent and summed in bfloat16 or wider, within the bound.
No kernel may reach another device: no remote copies, remote signals or barrier semaphores. Data moves between devices by JAX's collectives and lax.ppermute only.
A program may use at most 64 MiB of HBM per device.

v0:
```python
import math

import jax
import jax.numpy as jnp
from jax import lax
from jax.sharding import PartitionSpec as P

EDGE = 32
XT = 2
ZT = 1
K = 16
NTILT = 61
NTPL = 8


voxel_scale = 1.4


def passed_along(x, axis, by):
    length = lax.axis_size(axis)
    pairs = [(i, i + by) for i in range(length) if 0 <= i + by < length]
    return lax.ppermute(x, axis, pairs)


def phase_tables(length, out_count, in_count):
    row_index = jnp.arange(out_count, dtype=jnp.int32)[:, None]
    col_index = jnp.arange(in_count, dtype=jnp.int32)[None, :]
    phases = (row_index * col_index % length).astype(jnp.float32) * (2.0 * math.pi / length)
    return (jnp.cos(phases).astype(jnp.bfloat16), jnp.sin(phases).astype(jnp.bfloat16))


def contract(pattern, table, values):
    return jnp.einsum(pattern, values, table, preferred_element_type=jnp.float32)


def complex_pass(pattern, cos_t, sin_t, real_part, imag_part, sign):
    real_next = contract(pattern, cos_t, real_part) - sign * contract(pattern, sin_t, imag_part)
    imag_next = contract(pattern, cos_t, imag_part) + sign * contract(pattern, sin_t, real_part)
    return (real_next.astype(jnp.bfloat16), imag_next.astype(jnp.bfloat16))


def forward_spectrum(voxels, length):
    cos_z, sin_z = phase_tables(length, length, voxels.shape[-1])
    real_part = contract("...z,kz->...k", cos_z, voxels).astype(jnp.bfloat16)
    imag_part = (-contract("...z,kz->...k", sin_z, voxels)).astype(jnp.bfloat16)
    cos_x, sin_x = phase_tables(length, length, voxels.shape[-2])
    real_part, imag_part = complex_pass("...xz,kx->...kz", cos_x, sin_x, real_part, imag_part, -1.0)
    cos_y, sin_y = phase_tables(length, length, voxels.shape[-3])
    real_part, imag_part = complex_pass(
        "...yxz,ky->...kxz", cos_y, sin_y, real_part, imag_part, -1.0
    )
    return (real_part, imag_part)


def inverse_real(real_part, imag_part, length, edge_count):
    cos_t, sin_t = phase_tables(length, edge_count, length)
    real_part, imag_part = complex_pass(
        "...yxz,ky->...kxz", cos_t, sin_t, real_part, imag_part, 1.0
    )
    real_part, imag_part = complex_pass("...xz,kx->...kz", cos_t, sin_t, real_part, imag_part, 1.0)
    pattern = "...z,kz->...k"
    summed = contract(pattern, cos_t, real_part) - contract(pattern, sin_t, imag_part)
    return summed / float(length**3)


def best_scores(tmpl_real, tmpl_imag, tile_real, tile_imag, length, edge_count):
    tr32 = tmpl_real.astype(jnp.float32)
    ti32 = tmpl_imag.astype(jnp.float32)
    er32 = tile_real.astype(jnp.float32)
    ei32 = tile_imag.astype(jnp.float32)
    prod_real = (tr32 * er32 + ti32 * ei32).astype(jnp.bfloat16)
    prod_imag = (tr32 * ei32 - ti32 * er32).astype(jnp.bfloat16)
    return jnp.max(inverse_real(prod_real, prod_imag, length, edge_count), axis=0)


def interp_weights(angles, det_count, x_count, z_count):
    x_offset = jnp.arange(x_count, dtype=jnp.float32) - (x_count - 1) / 2.0
    z_offset = jnp.arange(z_count, dtype=jnp.float32) - (z_count - 1) / 2.0
    detector_pos = (
        voxel_scale
        * (
            x_offset[None, :, None] * jnp.cos(angles)[:, None, None]
            + z_offset[None, None, :] * jnp.sin(angles)[:, None, None]
        )
        + (det_count - 1) / 2.0
    )
    detector = jnp.arange(det_count, dtype=jnp.float32)
    weights = jnp.maximum(
        0.0, 1.0 - jnp.abs(detector[None, :, None, None] - detector_pos[:, None, :, :])
    )
    return weights.astype(jnp.bfloat16).reshape(angles.shape[0] * det_count, x_count * z_count)


def local(projections, tilt_angle, row_range, template_bank, rot_index):
    strips = lax.all_to_all(projections, "tile", split_axis=0, concat_axis=2, tiled=True)
    slab_rows = strips.shape[0]
    det_count = strips.shape[2]
    x_count = XT * EDGE
    z_count = ZT * EDGE
    halo_width = K // 2
    length = EDGE + K
    position = lax.axis_index("tile")
    first_row = position * slab_rows
    y_index = first_row + jnp.arange(slab_rows, dtype=jnp.int32)
    row_mask = (y_index[:, None] >= row_range[None, :, 0]) & (
        y_index[:, None] < row_range[None, :, 1]
    )
    masked = strips * row_mask[:, :, None].astype(jnp.bfloat16)
    padded_count = (NTILT + 7) // 8 * 8
    masked = jnp.pad(masked, ((0, 0), (0, padded_count - NTILT), (0, 0)))
    angles = jnp.pad(tilt_angle, (0, padded_count - NTILT))

    def add_block(block_index, summed, source, source_angles):
        strip_rows = lax.dynamic_slice_in_dim(source, block_index * 8, 8, 1).reshape(
            slab_rows, 8 * det_count
        )
        weights = interp_weights(
            lax.dynamic_slice_in_dim(source_angles, block_index * 8, 8, 0),
            det_count,
            x_count,
            z_count,
        )
        return summed + jnp.dot(strip_rows, weights, preferred_element_type=jnp.float32)

    zero_sum = jnp.zeros((slab_rows, x_count * z_count), jnp.float32)
    summed = lax.fori_loop(
        0, padded_count // 8, lambda b, s: add_block(b, s, masked, angles), zero_sum
    )
    volume = summed.astype(jnp.bfloat16).reshape(slab_rows, x_count, z_count)
    column_block = position % XT
    wide = jnp.pad(volume, ((0, 0), (halo_width, halo_width), (0, 0)))
    windows = jnp.stack([wide[:, j * EDGE : j * EDGE + length, :] for j in range(XT)])
    arranged = jnp.zeros((XT + 2, slab_rows, length, z_count), jnp.bfloat16)
    slot_ids = jnp.arange(XT + 2, dtype=jnp.int32)
    for offset in range(-XT, XT + 1):
        outgoing = lax.dynamic_index_in_dim(windows, (position + offset) % XT, 0, keepdims=False)
        if offset == 0:
            arrived = outgoing
        else:
            arrived = passed_along(outgoing, "tile", offset)
        target_slot = column_block - offset + 1
        arranged = jnp.where(
            (slot_ids == target_slot)[:, None, None, None], arrived[None], arranged
        )
    region = arranged.reshape((XT + 2) * slab_rows, length, z_count)[
        slab_rows - halo_width : slab_rows - halo_width + length
    ]
    deep = jnp.pad(region, ((0, 0), (0, 0), (halo_width, halo_width)))
    tile_spectra = [forward_spectrum(deep, length)]
    per_block = min(8, NTPL)
    chosen = jnp.take(template_bank, rot_index, axis=0).reshape(
        NTPL // per_block, per_block, K, K, K
    )

    def score_block(best, templates):
        tmpl_real, tmpl_imag = forward_spectrum(templates, length)
        tile_real, tile_imag = tile_spectra[0]
        found = best_scores(tmpl_real, tmpl_imag, tile_real, tile_imag, length, EDGE)
        updated = [jnp.maximum(best[:, :, 0], found)]
        return (jnp.stack(updated, axis=2), None)

    initial = jnp.full((EDGE, EDGE, ZT, EDGE), -jnp.inf, jnp.float32)
    best, _ = lax.scan(score_block, initial, chosen)
    return best.reshape(1, EDGE, EDGE * z_count)


def solution(mesh):
    return jax.shard_map(
        local,
        mesh=mesh,
        in_specs=(P("grp", None, "tile"), P("grp"), P("grp", None), P(), P()),
        out_specs=P("tile", "grp", None),
        check_vma=False,
    )
```

profile of v0, /device:TPU:1, one launch (start us, length us, event | category | flops | bytes accessed | tf_op | source)
XLA Modules:
  0.0 158.5 jit_solution(6777749314067413382)
XLA Ops:
  3.4 7.3 %all-to-all-start = ((bf16[16,2,3904]{2,1,0:T(2,128)(2,1)}), bf16[16,2,3904]{2,1,0:T(2,128)(2,1)S(1)}, u32[]{:S(2)}, u32[]{:S(2)}) async-start(bf16[16,2,3904]{2,1,0:T(2,128)(2,1)} %reshape.262), calls=%async_computation | async-start | bytes 507904 | tf_op jit(solution)/shard_map/all_to_all | solution.py:95
  17.9 5.1 %fusion.43 = f32[48,8,48,48]{3,0,2,1:T(8,128)} fusion(bf16[8,16,48,48]{3,2,1,0:T(8,128)(2,1)S(1)} %fusion.38), kind=kOutput, calls=%fused_computation.59 | convolution fusion | flops 28319232 | bytes 4128768 | tf_op jit(solution)/shard_map/while/body/eval_jaxpr/...yxz,ky->...kxz/dot_general | solution.py:33
  23.1 3.7 %subtract_convert_fusion = bf16[48,8,48,48]{3,0,2,1:T(8,128)(2,1)} fusion(f32[48,8,48,48]{3,0,2,1:T(8,128)S(1)} %fusion.47, bf16[8,16,48,48]{3,2,1,0:T(8,128)(2,1)S(1)} %fusion.38), kind=kOutput, calls=%fused_computation.25 | convolution fusion | flops 30973440 | bytes 5898240 | tf_op jit(solution)/shard_map/while/body/eval_jaxpr/...yxz,ky->...kxz/dot_general | solution.py:33
  26.9 7.3 %add_convert_fusion = bf16[48,8,48,48]{3,0,2,1:T(8,128)(2,1)} fusion(f32[48,8,48,48]{3,0,2,1:T(8,128)} %fusion.43, bf16[8,16,48,48]{3,2,1,0:T(8,128)(2,1)S(1)} %fusion.37), kind=kOutput, calls=%fused_computation.24 | convolution fusion | flops 30973440 | bytes 5898240 | tf_op jit(solution)/shard_map/while/body/eval_jaxpr/...yxz,ky->...kxz/dot_general | solution.py:33
  36.2 61.7 %while.20 = (s32[]{:T(128)}, f32[16,2048]{1,0:T(8,128)S(1)}, bf16[16,64,128]{2,1,0:T(8,128)(2,1)S(1)}, f32[64]{0:T(128)S(1)}, s32[]{:T(128)}, /*index=5*/s32[]{:T(128)}, s32[]{:T(128)}, s32[]{:T(128)}) while((s32[]{:T(128)}, f32[16,2048]{1,0:T(8,128)S(1)}, bf16[16,64,128]{2,1,0:T(8,128)(2,1)S(1)}, f32[64]{0:T(128)S(1)}, s32[]{:T(128)}, ...), condition=%wide.region_1.2_spmd.clone, body=%wide.region_0.1_spmd.clone.sunk | while | flops 77710184 | bytes 8887349 | solution.py:126
  36.7 3.8 %maximum_convert_fusion.2 = bf16[8,128,64,32]{1,0,3,2:T(8,128)(2,1)} fusion(f32[8,64,32]{0,2,1:T(8,128)S(1)} %multiply_add_fusion.2), kind=kLoop, calls=%fused_computation.1.clone.1 | loop fusion | flops 10485760 | bytes 4259840 | tf_op jit(solution)/shard_map/while/body/eval_jaxpr/convert_element_type | solution.py:91
  40.5 3.4 %fusion.247 = f32[16,2048]{1,0:T(8,128)S(1)} fusion(bf16[256,8,8,128]{3,2,1,0:T(8,128)(2,1)} %bitcast.135, f32[16,2048]{1,0:T(8,128)S(1)} %get-tuple-element.208, pred[]{:T(512)S(6)} %compare.12, bf16[2,8,8,128]{3,2,1,0:T(8,128)(2,1)S(1)} %bitcast.140), kind=kOutput, calls=%fused_computation.5.clone.1 | convolution fusion | flops 67174400 | bytes 4489217 | tf_op jit(solution)/shard_map/while/body/eval_jaxpr/dot_general | solution.py:123
  44.4 3.8 %maximum_convert_fusion.2 = bf16[8,128,64,32]{1,0,3,2:T(8,128)(2,1)} fusion(f32[8,64,32]{0,2,1:T(8,128)S(1)} %multiply_add_fusion.2), kind=kLoop, calls=%fused_computation.1.clone.1 | loop fusion | flops 10485760 | bytes 4259840 | tf_op jit(solution)/shard_map/while/body/eval_jaxpr/convert_element_type | solution.py:91
  48.2 3.4 %fusion.247 = f32[16,2048]{1,0:T(8,128)S(1)} fusion(bf16[256,8,8,128]{3,2,1,0:T(8,128)(2,1)} %bitcast.135, f32[16,2048]{1,0:T(8,128)S(1)} %get-tuple-element.208, pred[]{:T(512)S(6)} %compare.12, bf16[2,8,8,128]{3,2,1,0:T(8,128)(2,1)S(1)} %bitcast.140), kind=kOutput, calls=%fused_computation.5.clone.1 | convolution fusion | flops 67174400 | bytes 4489217 | tf_op jit(solution)/shard_map/while/body/eval_jaxpr/dot_general | solution.py:123
  52.1 3.8 %maximum_convert_fusion.2 = bf16[8,128,64,32]{1,0,3,2:T(8,128)(2,1)} fusion(f32[8,64,32]{0,2,1:T(8,128)S(1)} %multiply_add_fusion.2), kind=kLoop, calls=%fused_computation.1.clone.1 | loop fusion | flops 10485760 | bytes 4259840 | tf_op jit(solution)/shard_map/while/body/eval_jaxpr/convert_element_type | solution.py:91
  56.0 3.4 %fusion.247 = f32[16,2048]{1,0:T(8,128)S(1)} fusion(bf16[256,8,8,128]{3,2,1,0:T(8,128)(2,1)} %bitcast.135, f32[16,2048]{1,0:T(8,128)S(1)} %get-tuple-element.208, pred[]{:T(512)S(6)} %compare.12, bf16[2,8,8,128]{3,2,1,0:T(8,128)(2,1)S(1)} %bitcast.140), kind=kOutput, calls=%fused_computation.5.clone.1 | convolution fusion | flops 67174400 | bytes 4489217 | tf_op jit(solution)/shard_map/while/body/eval_jaxpr/dot_general | solution.py:123
  59.8 3.8 %maximum_convert_fusion.2 = bf16[8,128,64,32]{1,0,3,2:T(8,128)(2,1)} fusion(f32[8,64,32]{0,2,1:T(8,128)S(1)} %multiply_add_fusion.2), kind=kLoop, calls=%fused_computation.1.clone.1 | loop fusion | flops 10485760 | bytes 4259840 | tf_op jit(solution)/shard_map/while/body/eval_jaxpr/convert_element_type | solution.py:91
  63.7 3.4 %fusion.247 = f32[16,2048]{1,0:T(8,128)S(1)} fusion(bf16[256,8,8,128]{3,2,1,0:T(8,128)(2,1)} %bitcast.135, f32[16,2048]{1,0:T(8,128)S(1)} %get-tuple-element.208, pred[]{:T(512)S(6)} %compare.12, bf16[2,8,8,128]{3,2,1,0:T(8,128)(2,1)S(1)} %bitcast.140), kind=kOutput, calls=%fused_computation.5.clone.1 | convolution fusion | flops 67174400 | bytes 4489217 | tf_op jit(solution)/shard_map/while/body/eval_jaxpr/dot_general | solution.py:123
  67.5 3.8 %maximum_convert_fusion.2 = bf16[8,128,64,32]{1,0,3,2:T(8,128)(2,1)} fusion(f32[8,64,32]{0,2,1:T(8,128)S(1)} %multiply_add_fusion.2), kind=kLoop, calls=%fused_computation.1.clone.1 | loop fusion | flops 10485760 | bytes 4259840 | tf_op jit(solution)/shard_map/while/body/eval_jaxpr/convert_element_type | solution.py:91
  71.4 3.4 %fusion.247 = f32[16,2048]{1,0:T(8,128)S(1)} fusion(bf16[256,8,8,128]{3,2,1,0:T(8,128)(2,1)} %bitcast.135, f32[16,2048]{1,0:T(8,128)S(1)} %get-tuple-element.208, pred[]{:T(512)S(6)} %compare.12, bf16[2,8,8,128]{3,2,1,0:T(8,128)(2,1)S(1)} %bitcast.140), kind=kOutput, calls=%fused_computation.5.clone.1 | convolution fusion | flops 67174400 | bytes 4489217 | tf_op jit(solution)/shard_map/while/body/eval_jaxpr/dot_general | solution.py:123
  75.2 3.8 %maximum_convert_fusion.2 = bf16[8,128,64,32]{1,0,3,2:T(8,128)(2,1)} fusion(f32[8,64,32]{0,2,1:T(8,128)S(1)} %multiply_add_fusion.2), kind=kLoop, calls=%fused_computation.1.clone.1 | loop fusion | flops 10485760 | bytes 4259840 | tf_op jit(solution)/shard_map/while/body/eval_jaxpr/convert_element_type | solution.py:91
  82.9 3.8 %maximum_convert_fusion.2 = bf16[8,128,64,32]{1,0,3,2:T(8,128)(2,1)} fusion(f32[8,64,32]{0,2,1:T(8,128)S(1)} %multiply_add_fusion.2), kind=kLoop, calls=%fused_computation.1.clone.1 | loop fusion | flops 10485760 | bytes 4259840 | tf_op jit(solution)/shard_map/while/body/eval_jaxpr/convert_element_type | solution.py:91
  90.6 3.8 %maximum_convert_fusion.2 = bf16[8,128,64,32]{1,0,3,2:T(8,128)(2,1)} fusion(f32[8,64,32]{0,2,1:T(8,128)S(1)} %multiply_add_fusion.2), kind=kLoop, calls=%fused_computation.1.clone.1 | loop fusion | flops 10485760 | bytes 4259840 | tf_op jit(solution)/shard_map/while/body/eval_jaxpr/convert_element_type | solution.py:91
  102.1 3.6 %collective-permute-start.1 = (bf16[16,48,32]{2,1,0:T(8,128)(2,1)S(1)}, bf16[16,48,32]{2,1,0:T(8,128)(2,1)S(1)}, u32[]{:S(2)}, u32[]{:S(2)}) collective-permute-start(bf16[16,48,32]{2,1,0:T(8,128)(2,1)S(1)} %get-tuple-element.163), channel_id=1, source_target_pairs={{0,1},{1,2},{2,3},{3,4},{4,5},{5,6},{6,7},{7,8},{8,9},{9,10},{10,1... | collective-permute-start | bytes 147464 | tf_op jit(solution)/shard_map/ppermute | solution.py:22
  124.1 4.5 %fusion.116 = f32[32,8,48,48]{3,0,2,1:T(8,128)} fusion(bf16[48,8,48,48]{3,0,2,1:T(8,128)(2,1)S(1)} %bitcast.139, bf16[48,8,48,48]{3,0,2,1:T(8,128)(2,1)S(1)} %bitcast.137, f32[48,48,48]{2,0,1:T(8,128)S(1)} %fusion.55, f32[48,48,48]{2,0,1:T(8,128)S(1)} %fusion.53), kind=kOutput, calls=%fused_computation.149 | convolution fusion | flops 61946880 | bytes 6782976 | tf_op jit(solution)/shard_map/while/body/eval_jaxpr/...yxz,ky->...kxz/dot_general | solution.py:33
  128.7 5.2 %fusion.15 = bf16[8,32,48,48]{3,1,2,0:T(8,128)(2,1)S(1)} fusion(f32[32,8,48,48]{3,0,2,1:T(8,128)} %fusion.116, bf16[48,8,48,48]{3,0,2,1:T(8,128)(2,1)S(1)} %bitcast.139, bf16[48,8,48,48]{3,0,2,1:T(8,128)(2,1)S(1)} %bitcast.137, f32[48,48,48]{2,0,1:T(8,128)S(1)} %fusion.55, f32[48,48,48]{2,0,1:T(8,128)S(1)} %fusion.53), kind=kOutput, calls=%fused_computation.34 | convolution fusion | flops 63126528 | bytes 7962624 | tf_op jit(solution)/shard_map/while/body/eval_jaxpr/...yxz,ky->...kxz/dot_general | solution.py:33
  140.0 4.0 %fusion.14 = bf16[8,32,48,48]{3,1,2,0:T(8,128)(2,1)} fusion(f32[32,8,48,48]{3,0,2,1:T(8,128)S(1)} %fusion.119, bf16[48,8,48,48]{3,0,2,1:T(8,128)(2,1)S(1)} %bitcast.139, bf16[48,8,48,48]{3,0,2,1:T(8,128)(2,1)S(1)} %bitcast.137, f32[48,48,48]{2,0,1:T(8,128)S(1)} %fusion.55, f32[48,48,48]{2,0,1:T(8,128)S(1)} %fusion.53), kind=kOutput, calls=%fused_computation.33 | convolution fusion | flops 63126528 | bytes 7962624 | tf_op jit(solution)/shard_map/while/body/eval_jaxpr/...yxz,ky->...kxz/dot_general | solution.py:33
  144.1 6.9 %fusion.25 = f32[8,32,32,32]{3,2,1,0:T(8,128)} fusion(f32[32,8,32,48]{3,0,2,1:T(8,128)} %fusion.18, bf16[8,32,48,48]{3,1,2,0:T(8,128)(2,1)} %fusion.14), kind=kOutput, calls=%fused_computation.46 | convolution fusion | flops 63731712 | bytes 3801088 | tf_op jit(solution)/shard_map/while/body/eval_jaxpr/...z,kz->...k/dot_general | solution.py:33
  150.9 6.6 %multiply_reduce_fusion = f32[32,32,32]{2,1,0:T(8,128)S(1)} fusion(f32[8,32,32,32]{3,2,1,0:T(8,128)} %fusion.25, f32[32,8,32,48]{3,0,2,1:T(8,128)} %fusion.16, bf16[8,32,48,48]{3,1,2,0:T(8,128)(2,1)} %fusion.14), kind=kOutput, calls=%fused_computation.30 | convolution fusion | flops 64485376 | bytes 3932160 | tf_op jit(solution)/shard_map/while/body/eval_jaxpr/...z,kz->...k/dot_general | solution.py:33
  (152 shorter events, 55.7 us)
Async XLA Ops:
  0.0 12.1 %copy-start = (bf16[64,16,256]{2,1,0:T(8,128)(2,1)S(1)}, bf16[64,16,256]{2,1,0:T(8,128)(2,1)}, u32[]{:S(2)}) copy-start(bf16[64,16,256]{2,1,0:T(8,128)(2,1)} %param.10) | copy-start | bytes 1572868
  0.0 13.7 %copy-start.2 = (s32[61,2]{0,1:T(2,128)S(1)}, s32[61,2]{0,1:T(2,128)}, u32[]{:S(2)}) copy-start(s32[61,2]{0,1:T(2,128)} %param.9) | copy-start | bytes 1468
  3.4 30.8 %all-to-all-start = ((bf16[16,2,3904]{2,1,0:T(2,128)(2,1)}), bf16[16,2,3904]{2,1,0:T(2,128)(2,1)S(1)}, u32[]{:S(2)}, u32[]{:S(2)}) async-start(bf16[16,2,3904]{2,1,0:T(2,128)(2,1)} %reshape.262), calls=%async_computation | async-start | bytes 507904 | tf_op jit(solution)/shard_map/all_to_all | solution.py:95
  23.1 3.7 %copy-start.3 = (f32[61]{0:T(128)S(1)}, f32[61]{0:T(128)}, u32[]{:S(2)}) copy-start(f32[61]{0:T(128)} %param.8) | copy-start | bytes 736
  98.8 11.4 %collective-permute-start = (bf16[16,48,32]{2,1,0:T(8,128)(2,1)S(1)}, bf16[16,48,32]{2,1,0:T(8,128)(2,1)S(1)}, u32[]{:S(2)}, u32[]{:S(2)}) collective-permute-start(bf16[16,48,32]{2,1,0:T(8,128)(2,1)S(1)} %get-tuple-element.162), channel_id=1, source_target_pairs={{0,2},{1,3},{2,4},{3,5},{4,6},{5,7},{6,8},{7,9},{8,10},{9,11},{10,... | collective-permute-start | bytes 147464 | tf_op jit(solution)/shard_map/ppermute | solution.py:22
  102.1 8.1 %collective-permute-start.1 = (bf16[16,48,32]{2,1,0:T(8,128)(2,1)S(1)}, bf16[16,48,32]{2,1,0:T(8,128)(2,1)S(1)}, u32[]{:S(2)}, u32[]{:S(2)}) collective-permute-start(bf16[16,48,32]{2,1,0:T(8,128)(2,1)S(1)} %get-tuple-element.163), channel_id=1, source_target_pairs={{0,1},{1,2},{2,3},{3,4},{4,5},{5,6},{6,7},{7,8},{8,9},{9,10},{10,1... | collective-permute-start | bytes 147464 | tf_op jit(solution)/shard_map/ppermute | solution.py:22
  105.7 7.8 %collective-permute-start.2 = (bf16[16,48,32]{2,1,0:T(8,128)(2,1)S(1)}, bf16[16,48,32]{2,1,0:T(8,128)(2,1)S(1)}, u32[]{:S(2)}, u32[]{:S(2)}) collective-permute-start(bf16[16,48,32]{2,1,0:T(8,128)(2,1)S(1)} %get-tuple-element.165), channel_id=1, source_target_pairs={{1,0},{2,1},{3,2},{4,3},{5,4},{6,5},{7,6},{8,7},{9,8},{10,9},{11,1... | collective-permute-start | bytes 147464 | tf_op jit(solution)/shard_map/ppermute | solution.py:22
  107.6 8.9 %collective-permute-start.3 = (bf16[16,48,32]{2,1,0:T(8,128)(2,1)S(1)}, bf16[16,48,32]{2,1,0:T(8,128)(2,1)S(1)}, u32[]{:S(2)}, u32[]{:S(2)}) collective-permute-start(bf16[16,48,32]{2,1,0:T(8,128)(2,1)S(1)} %get-tuple-element.161), channel_id=1, source_target_pairs={{2,0},{3,1},{4,2},{5,3},{6,4},{7,5},{8,6},{9,7},{10,8},{11,9},{12,... | collective-permute-start | bytes 147464 | tf_op jit(solution)/shard_map/ppermute | solution.py:22
  117.0 4.9 %slice-start.2 = ((s8[4718592]{0:T(1024)(128)(4,1)}), s8[4194304]{0:T(1024)(128)(4,1)S(1)}, s32[]{:S(2)}) async-start(s8[4718592]{0:T(1024)(128)(4,1)} %bitcast.138), calls=%async_computation.3 | async-start | bytes 8388608
  119.3 2.6 %slice-start.3 = ((s8[4718592]{0:T(1024)(128)(4,1)}), s8[524288]{0:T(1024)(128)(4,1)S(1)}, s32[]{:S(2)}) async-start(s8[4718592]{0:T(1024)(128)(4,1)} %bitcast.138), calls=%async_computation.4 | async-start | bytes 1048576
  119.8 2.2 %slice-start = ((s8[4718592]{0:T(1024)(128)(4,1)}), s8[4194304]{0:T(1024)(128)(4,1)S(1)}, s32[]{:S(2)}) async-start(s8[4718592]{0:T(1024)(128)(4,1)} %bitcast.136), calls=%async_computation.1 | async-start | bytes 8388608
  120.6 1.6 %slice-start.1 = ((s8[4718592]{0:T(1024)(128)(4,1)}), s8[524288]{0:T(1024)(128)(4,1)S(1)}, s32[]{:S(2)}) async-start(s8[4718592]{0:T(1024)(128)(4,1)} %bitcast.136), calls=%async_computation.2 | async-start | bytes 1048576
  144.1 14.4 %copy-start.1 = (bf16[64,16,256]{2,1,0:T(8,128)(2,1)S(1)}, bf16[64,16,256]{2,1,0:T(8,128)(2,1)}, u32[]{:S(2)}) copy-start(bf16[64,16,256]{2,1,0:T(8,128)(2,1)} %param.10) | copy-start | bytes 1572868
where the time goes:
time: 160 us; the launch traced here: 158 us
  matrix products  87.5 us (55%)
  other arithmetic  35.9 us (22%)
  starting transfers between devices  17.5 us (11%)
  local copies, waits for them, and re-layouts  10.5 us (7%)
  waiting for transfers between devices  6.34 us (4%)
    dot_general x28, matrix products, contract(): jnp.einsum(pattern, values, table, preferred_element_type=jnp.float32)  60.5 us
    convert_element_type x8, other arithmetic, interp_weights(): weights.astype(jnp.bfloat16)  30.8 us
    dot_general x8, matrix products, add_block(): jnp.dot(strip_rows, weights, preferred_element_type=jnp.float32)  27 us
    ppermute x4, starting transfers between devices, passed_along(): return lax.ppermute(x, axis, pairs)  10.1 us
    all_to_all x1, starting transfers between devices, local(): lax.all_to_all(projections, 'tile', split_axis=0, concat_axis=2, tiled=True)  7.35 us
    ppermute x4, waiting for transfers between devices, passed_along(): return lax.ppermute(x, axis, pairs)  6.34 us
    unnamed x20, local copies, waits for them, and re-layouts  5.64 us
  transfers between devices with their start and end apart: 5, of which 2 were waited for; matrix products, arithmetic and copies ran while one was open for 15% of the time, Pallas kernels for 0%

commit v1 on v0

v1 whole, which is shorter than its diff:
```python
import math

import jax
import jax.numpy as jnp
import numpy as np
from jax import lax
from jax.experimental import pallas as pl
from jax.experimental.pallas import tpu as pltpu
from jax.sharding import PartitionSpec as P

EDGE = 32
XT = 2
K = 16
NTILT = 61
NTPL = 8
NDET = 128
HALO = K // 2
LEN = EDGE + K
X = XT * EDGE
Z = EDGE
XR = EDGE + HALO
LZ = Z + HALO
KZ = LZ // 2 + 1
NF = LEN * KZ
FP = 1024
XB = 8
NQ = XR // XB
LB = XB * Z
MAX_ANGLE = 1.05
VOXEL = 1.4
SCALE = 1.0 / (LEN * LEN * LZ)
BF = jnp.bfloat16
F32 = jnp.float32


def reach(q):
    x = np.arange(q * XB, (q + 1) * XB) - (X - 1) / 2.0
    z = np.arange(Z) - (Z - 1) / 2.0
    top = 0.0
    low = 0.0
    angle = np.linspace(-MAX_ANGLE, MAX_ANGLE, 4001)
    first = True
    for xv in (x[0], x[-1]):
        for zv in (z[0], z[-1]):
            pos = VOXEL * (xv * np.cos(angle) + zv * np.sin(angle)) + (NDET - 1) / 2.0
            low = pos.min() if first else min(low, pos.min())
            top = pos.max() if first else max(top, pos.max())
            first = False
    return math.ceil(low - 1.0 - 0.01), math.floor(top + 1.0 + 0.01)


def pair_list(n_det):
    pairs = []
    for q in range(NQ):
        low, top = reach(q)
        pairs.append(list(range(max(low, 0) // n_det, min(top, NDET - 1) // n_det + 1)))
    return pairs


def rounded(table):
    return np.asarray(table, np.float32).astype(jnp.bfloat16)


def plane_tables():
    kx = np.repeat(np.arange(LEN), KZ)
    kz = np.tile(np.arange(KZ), LEN)

    def phase(xs, zs):
        x = np.repeat(xs, len(zs))[:, None]
        z = np.tile(zs, len(xs))[:, None]
        return 2.0 * np.pi * ((kx * x % LEN) / LEN + (kz * z % LZ) / LZ)

    def padded(a):
        return np.pad(a, ((0, 0), (0, FP - NF)))

    def forward(xs, zs):
        p = phase(xs, zs)
        return rounded(np.concatenate([padded(np.cos(p)), padded(-np.sin(p))], 1))

    p = phase(np.arange(EDGE), np.arange(EDGE) - HALO)
    weight = np.where((kz == 0) | (kz == LZ // 2), 1.0, 2.0)
    inverse = rounded(
        np.concatenate([padded(weight * np.cos(p)), padded(-weight * np.sin(p))], 1).T
    )
    shift = 2.0 * np.pi * (kx * HALO % LEN) / LEN
    turn = np.zeros((4, FP), np.float32)
    turn[0, :NF], turn[1, :NF] = np.cos(shift), -np.sin(shift)
    turn[2, :NF] = 1.0
    return (
        forward(np.arange(XR), np.arange(Z)),
        forward(np.arange(K), np.arange(K)),
        inverse,
        turn,
    )


def line_tables():
    def table(outs, ins, sign):
        p = 2.0 * np.pi * (np.outer(np.arange(outs), np.arange(ins)) % LEN) / LEN
        c, s = np.cos(p), np.sin(p) * sign
        return c, s

    c, s = table(LEN, LEN, 1.0)
    region = rounded(np.block([[c, s], [-s, c]]))
    c, s = table(LEN, K, 1.0)
    template = rounded(np.block([[c, s], [-s, c]]))
    c, s = table(EDGE, LEN, 1.0)
    back = rounded(np.block([[c, -s], [s, c]]))
    return region, template, back


def pack_kernel(n_block, proj_ref, range_ref, out_ref):
    rows, y_count = proj_ref.shape
    depth = out_ref.shape[2]
    x = proj_ref[...].astype(F32)
    y = lax.broadcasted_iota(jnp.int32, (rows, y_count), 1)
    keep = (y >= range_ref[:, 0:1]) & (y < range_ref[:, 1:2])
    x = jnp.where(keep, x, 0.0)
    if depth > rows:
        x = jnp.concatenate([x, jnp.zeros((depth - rows, y_count), F32)], 0)
    xt = x.T
    for b in range(n_block):
        low, top = b * EDGE - HALO, b * EDGE - HALO + LEN
        part = xt[max(low, 0) : min(top, y_count)]
        if low < 0:
            part = jnp.concatenate([jnp.zeros((-low, depth), F32), part], 0)
        if top > y_count:
            part = jnp.concatenate([part, jnp.zeros((top - y_count, depth), F32)], 0)
        out_ref[b] = part.astype(BF)


def weight_kernel(n_det, n_tile, pairs, col_ref, turns_ref, w_ref, p_ref):
    col = col_ref[0]
    depth = turns_ref.shape[0]
    lane = lax.broadcasted_iota(jnp.int32, (1, LB), 1)
    z = (lane % Z).astype(F32) - (Z - 1) / 2.0
    step = (lane // Z).astype(F32)
    row = lax.broadcasted_iota(jnp.int32, (depth, 1), 0)
    own = (row % n_det).astype(F32)
    base = 0
    for q, sources in enumerate(pairs):
        block = jnp.where(col == 0, q, NQ - 1 - q) * XB + col * (X - XR)
        x = step + (block.astype(F32) - (X - 1) / 2.0)
        pos = VOXEL * (x * turns_ref[:, 0:1] + z * turns_ref[:, 1:2])
        p_ref[...] = pos + ((NDET - 1) / 2.0 - own)

        def build(j, carry, base=base, first=sources[0]):
            src = first + j
            src = jnp.where(col == 0, src, n_tile - 1 - src)
            shift = (src * n_det).astype(F32)
            w_ref[base + j] = jnp.maximum(0.0, 1.0 - jnp.abs(p_ref[...] - shift)).astype(BF)
            return carry

        lax.fori_loop(0, len(sources), build, 0)
        base += len(sources)


def template_kernel(col_ref, rot_ref, bank_ref, plane_ref, line_ref, turn_ref, out_ref):
    col = col_ref[0]
    chosen = jnp.concatenate([bank_ref[rot_ref[r]] for r in range(NTPL)], 0)
    flat = jnp.dot(chosen, plane_ref[...], preferred_element_type=F32).astype(BF)
    cos = jnp.where(col == 0, turn_ref[0:1], turn_ref[2:3])
    sin = jnp.where(col == 0, turn_ref[1:2], turn_ref[3:4])
    for r in range(NTPL):
        part = flat[r * K : (r + 1) * K]
        stacked = jnp.concatenate([part[:, :FP], part[:, FP:]], 0)
        full = jnp.dot(line_ref[...], stacked, preferred_element_type=F32)
        real, imag = full[:LEN], -full[LEN:]
        out_ref[r, :LEN] = (real * cos - imag * sin).astype(BF)
        out_ref[r, LEN:] = (real * sin + imag * cos).astype(BF)


def score_kernel(
    n_block,
    pairs,
    col_ref,
    own_ref,
    other_ref,
    w_ref,
    tmpl_ref,
    plane_ref,
    line_ref,
    back_ref,
    inverse_ref,
    out_ref,
    vol_ref,
    mid_ref,
):
    col = col_ref[0]
    base = 0
    for q, sources in enumerate(pairs):
        total = jnp.zeros((LEN, LB), F32)
        for j, src in enumerate(sources):
            chip = jnp.where(col == 0, src // 2, n_block - 1 - src // 2)
            part = own_ref[chip] if src % 2 == 0 else other_ref[chip]
            total += jnp.dot(part, w_ref[base + j], preferred_element_type=F32)
        block = jnp.where(col == 0, q, NQ - 1 - q)
        vol_ref[:, pl.ds(pl.multiple_of(block * LB, LB), LB)] = total.astype(BF)
        base += len(sources)
    flat = jnp.dot(vol_ref[...], plane_ref[...], preferred_element_type=F32).astype(BF)
    stacked = jnp.concatenate([flat[:, :FP], flat[:, FP:]], 0)
    full = jnp.dot(line_ref[...], stacked, preferred_element_type=F32)
    real, imag = full[:LEN], full[LEN:]
    for r in range(NTPL):
        t_real = tmpl_ref[r, :LEN].astype(F32)
        t_imag = tmpl_ref[r, LEN:].astype(F32)
        prod = jnp.concatenate(
            [
                (t_real * real - t_imag * imag).astype(BF),
                (t_real * imag + t_imag * real).astype(BF),
            ],
            0,
        )
        line = jnp.dot(back_ref[...], prod, preferred_element_type=F32).astype(BF)
        mid_ref[r * EDGE : (r + 1) * EDGE, :FP] = line[:EDGE]
        mid_ref[r * EDGE : (r + 1) * EDGE, FP:] = line[EDGE:]
    corr = jnp.dot(mid_ref[...], inverse_ref[...], preferred_element_type=F32)
    best = corr[:EDGE]
    for r in range(1, NTPL):
        best = jnp.maximum(best, corr[r * EDGE : (r + 1) * EDGE])
    out_ref[0] = best * SCALE


VMEM = pl.BlockSpec(memory_space=pltpu.VMEM)
SMEM = pl.BlockSpec(memory_space=pltpu.SMEM)
LIMIT = pltpu.CompilerParams(vmem_limit_bytes=48 << 20)


def solution(mesh):
    n_tile = mesh.shape["tile"]
    n_block = n_tile // XT
    n_det = NDET // n_tile
    rows = NTILT * n_det
    depth = (rows + 127) // 128 * 128
    pairs = pair_list(n_det)
    n_pair = sum(len(p) for p in pairs)
    plane, plane_t, inverse, turn = plane_tables()
    line, line_t, back = line_tables()

    def local(projections, tilt_angle, row_range, template_bank, rot_index):
        y_count = projections.shape[0]
        position = lax.axis_index("tile")
        col = (position % XT).astype(jnp.int32).reshape(1)
        by_y = jnp.transpose(projections, (1, 2, 0)).reshape(rows, y_count)
        ranges = jnp.repeat(row_range, n_det, axis=0)
        send = pl.pallas_call(
            lambda *refs: pack_kernel(n_block, *refs),
            out_shape=jax.ShapeDtypeStruct((n_block, LEN, depth), BF),
            in_specs=[VMEM, VMEM],
            out_specs=VMEM,
            compiler_params=LIMIT,
        )(by_y, ranges)
        same = [[c + XT * k for k in range(n_block)] for c in range(XT)]
        own = lax.all_to_all(send, "tile", 0, 0, tiled=True, axis_index_groups=same)
        other = lax.ppermute(own, "tile", [(i, i ^ 1) for i in range(n_tile)])
        turns = jnp.stack([jnp.cos(tilt_angle), jnp.sin(tilt_angle)], 1)
        turns = jnp.pad(jnp.repeat(turns, n_det, axis=0), ((0, depth - rows), (0, 0)))
        weights = pl.pallas_call(
            lambda *refs: weight_kernel(n_det, n_tile, pairs, *refs),
            out_shape=jax.ShapeDtypeStruct((n_pair, depth, LB), BF),
            in_specs=[SMEM, VMEM],
            out_specs=VMEM,
            scratch_shapes=[pltpu.VMEM((depth, LB), F32)],
            compiler_params=LIMIT,
        )(col, turns)
        spectra = pl.pallas_call(
            template_kernel,
            out_shape=jax.ShapeDtypeStruct((NTPL, 2 * LEN, FP), BF),
            in_specs=[SMEM, SMEM, VMEM, VMEM, VMEM, VMEM],
            out_specs=VMEM,
            compiler_params=LIMIT,
        )(col, rot_index, template_bank, jnp.asarray(plane_t), jnp.asarray(line_t), jnp.asarray(turn))
        return pl.pallas_call(
            lambda *refs: score_kernel(n_block, pairs, *refs),
            out_shape=jax.ShapeDtypeStruct((1, EDGE, EDGE * Z), F32),
            in_specs=[SMEM] + [VMEM] * 8,
            out_specs=VMEM,
            scratch_shapes=[
                pltpu.VMEM((LEN, XR * Z), BF),
                pltpu.VMEM((NTPL * EDGE, 2 * FP), BF),
            ],
            compiler_params=LIMIT,
        )(
            col,
            own,
            other,
            weights,
            spectra,
            jnp.asarray(plane),
            jnp.asarray(line),
            jnp.asarray(back),
            jnp.asarray(inverse),
        )

    return jax.shard_map(
        local,
        mesh=mesh,
        in_specs=(P("grp", None, "tile"), P("grp"), P("grp", None), P(), P()),
        out_specs=P("tile", "grp", None),
        check_vma=False,
    )
```

time: 160 us -> 43.1 us (0.27)
  matrix products: 87.5 us -> 0 us
  other arithmetic: 35.9 us -> 0.01 us
  Pallas kernels: 0 us -> 20.7 us
  blocking collectives: 0 us -> 16.7 us
  starting transfers between devices: 17.5 us -> 2.7 us
  local copies, waits for them, and re-layouts: 10.5 us -> 2.62 us
  waiting for transfers between devices: 6.34 us -> 0.01 us
    dot_general x36 -> x0, matrix products: 87.5 us -> none  [the longest x28 60.5 us: contract(): jnp.einsum(pattern, values, table, preferred_element_type=jnp.float32)]
    convert_element_type x10 -> x0, other arithmetic: 30.8 us -> none  [the longest x8 30.8 us: interp_weights(): weights.astype(jnp.bfloat16)]
    pallas_call x0 -> x4, Pallas kernels: none -> 20.7 us  [the longest x1 11.7 us: local(): pl.pallas_call(lambda *refs: score_kernel(n_block, pairs, *refs), out_sha...]
    all_to_all x0 -> x1, blocking collectives: none -> 16.7 us  [local(): own = lax.all_to_all(send, 'tile', 0, 0, tiled=True, axis_index_groups=same)]
    ppermute x4 -> x1, starting transfers between devices: 10.1 us -> 2.7 us  [local(): other = lax.ppermute(own, 'tile', [(i, i ^ 1) for i in range(n_tile)])]
    all_to_all x1 -> x0, starting transfers between devices: 7.35 us -> none  [local(): lax.all_to_all(projections, 'tile', split_axis=0, concat_axis=2, tiled=True)]
    ppermute x4 -> x1, waiting for transfers between devices: 6.34 us -> 0.01 us  [local(): other = lax.ppermute(own, 'tile', [(i, i ^ 1) for i in range(n_tile)])]
    unnamed x20 -> x17, local copies, waits for them, and re-layouts: 5.64 us -> 1.77 us
  transfers between devices with their start and end apart: 5 -> 1, of which waited for: 2 -> 0; matrix products, arithmetic and copies ran while one was open for 15% -> 2% of each run, Pallas kernels for 0% -> 20%
where the time goes in v1:
time: 43.1 us; the launch traced here: 42.9 us
  Pallas kernels  20.7 us (48%)
  blocking collectives  16.7 us (39%)
  starting transfers between devices  2.7 us (6%)
  local copies, waits for them, and re-layouts  2.62 us (6%)
    all_to_all x1, blocking collectives, local(): own = lax.all_to_all(send, 'tile', 0, 0, tiled=True, axis_index_groups=same)  16.7 us
    pallas_call x1, Pallas kernels, local(): pl.pallas_call(lambda *refs: score_kernel(n_block, pairs, *refs), out_sha...  11.7 us
    pallas_call x1, Pallas kernels, local(): pl.pallas_call(lambda *refs: weight_kernel(n_det, n_tile, pairs, *refs),...  7.32 us
    ppermute x1, starting transfers between devices, local(): other = lax.ppermute(own, 'tile', [(i, i ^ 1) for i in range(n_tile)])  2.7 us
    unnamed x17, local copies, waits for them, and re-layouts  1.77 us
    pallas_call x1, Pallas kernels, local(): pl.pallas_call(template_kernel, out_shape=jax.ShapeDtypeStruct((NTPL, 2 *...  1.37 us
  transfers between devices with their start and end apart: 1, of which 0 were waited for; matrix products, arithmetic and copies ran while one was open for 2% of the time, Pallas kernels for 20%

profile of v1, /device:TPU:1, one launch (start us, length us, event | category | flops | bytes accessed | tf_op | source)
XLA Modules:
  0.0 42.9 jit_solution(3174232641863453721)
XLA Ops:
  0.0 0.8 %copy.13 = s32[61,2]{1,0:T(8,128)S(1)} copy(s32[61,2]{0,1:T(2,128)} %param.14) | data formatting | bytes 976 | tf_op args[2]
  0.8 0.0 copy-start.2
  0.8 0.9 %copy-done.2 = bf16[256,61,8]{0,2,1:T(8,128)(2,1)S(1)} copy-done((bf16[256,61,8]{0,2,1:T(8,128)(2,1)S(1)}, bf16[256,61,8]{0,2,1:T(8,128)(2,1)}, u32[]{:S(2)}) %copy-start.2) | copy-done | bytes 249880
  1.8 0.3 shard_map.118
  2.1 0.0 copy-start
  2.1 0.0 copy-start.1
  2.1 0.0 copy-start.3
  2.1 0.0 copy-start.5
  2.1 0.0 copy-start.7
  2.1 16.7 %all_to_all.5.refs_1_ = bf16[8,48,512]{2,1,0:T(8,128)(2,1)S(1)} all-to-all(bf16[8,48,512]{2,1,0:T(8,128)(2,1)S(1)} %shard_map.118), channel_id=1, replica_groups={{0,2,4,6,8,10,12,14},{1,3,5,7,9,11,13,15},{16,18,20,22,24,26,28,30},{17..., dimensions={0} | all-to-all | bytes 786432 | tf_op jit(solution)/shard_map/all_to_all | solution.py:254
  18.8 2.7 %collective-permute-start = (bf16[8,48,512]{2,1,0:T(8,128)(2,1)S(1)}, bf16[8,48,512]{2,1,0:T(8,128)(2,1)S(1)}, u32[]{:S(2)}, u32[]{:S(2)}) collective-permute-start(bf16[8,48,512]{2,1,0:T(8,128)(2,1)S(1)} %all_to_all.5.refs_1_), channel_id=1, source_target_pairs={{0,1},{1,0},{2,3},{3,2},{4,5},{5,4},{6,7},{7,6},{8,9},{9,8},{10,11... | collective-permute-start | bytes 1179656 | tf_op jit(solution)/shard_map/ppermute | solution.py:255
  21.5 0.7 %cosine_bitcast_fusion = (f32[61,1]{0,1:T(1,128)S(1)}, f32[61,1]{0,1:T(1,128)S(1)}) fusion(f32[61]{0:T(128)} %param.13), kind=kLoop, calls=%fused_computation.4 | loop fusion | bytes 732 | tf_op jit(solution)/shard_map/stack | solution.py:256
  22.2 0.1 copy.14
  22.4 0.0 copy-start.4
  22.4 0.0 copy-start.6
  22.4 7.3 %shard_map.119.refs_3_ = bf16[34,512,256]{2,1,0:T(8,128)(2,1)} custom-call(s32[1]{0:T(128)} %bitcast.refs_0_.col_ref, f32[512,2]{1,0:T(8,128)S(1)} %pad.4.refs_1_), custom_call_target="tpu_custom_call" | custom-call | tf_op jit(solution)/shard_map/pallas_call | solution.py:258
  29.7 0.0 copy-done
  29.7 0.0 copy-done.1
  29.7 0.0 copy-done.3
  29.7 0.0 copy-done.5
  29.7 0.0 copy-done.7
  29.7 1.4 %shard_map.120.refs_4_ = bf16[8,96,1024]{2,1,0:T(8,128)(2,1)S(1)} custom-call(s32[1]{0:T(128)} %bitcast.refs_0_.col_ref, s32[8]{0:T(128)S(1)} %copy-done.7, bf16[64,16,256]{2,1,0:T(8,128)(2,1)S(1)} %copy-done.1, bf16[256,2048]{1,0:T(8,128)(2,1)S(1)} %copy-done, bf16[96,32]{1,0:T(8,128)(2,1)S(1)} %copy-done.3, f32[4,1024]{1,0:T(4,128)S(1)} %copy-done.5), custom_call_target="tpu_custom_call" | custom-call | tf_op jit(solution)/shard_map/pallas_call | solution.py:266
  31.1 0.0 collective-permute-done.refs_2_
  31.2 11.7 %shard_map.121 = f32[1,32,1024]{2,1,0:T(8,128)} custom-call(s32[1]{0:T(128)} %bitcast.refs_0_.col_ref, bf16[8,48,512]{2,1,0:T(8,128)(2,1)S(1)} %all_to_all.5.refs_1_, bf16[8,48,512]{2,1,0:T(8,128)(2,1)S(1)} %collective-permute-done.refs_2_, bf16[34,512,256]{2,1,0:T(8,128)(2,1)} %shard_map.119.refs_3_, bf16[8,96,1024]{2,1,0:T(8,128)(2,1)S(1)} %shard_map.120.refs_4_, ...), custom_call_target="tpu_custom_call" | custom-call | tf_op jit(solution)/shard_map/pallas_call | solution.py:273
  (6 shorter events, 0.1 us)
Async XLA Ops:
  0.8 0.9 %copy-start.2 = (bf16[256,61,8]{0,2,1:T(8,128)(2,1)S(1)}, bf16[256,61,8]{0,2,1:T(8,128)(2,1)}, u32[]{:S(2)}) copy-start(bf16[256,61,8]{0,2,1:T(8,128)(2,1)} %param.12) | copy-start | bytes 749572
  2.1 27.6 %copy-start = (bf16[256,2048]{1,0:T(8,128)(2,1)S(1)}, bf16[256,2048]{1,0:T(8,128)(2,1)}, u32[]{:S(2)}) copy-start(bf16[256,2048]{1,0:T(8,128)(2,1)} %constant.34.clone.plane_ref) | copy-start | bytes 3145732
  2.1 27.6 %copy-start.1 = (bf16[64,16,256]{2,1,0:T(8,128)(2,1)S(1)}, bf16[64,16,256]{2,1,0:T(8,128)(2,1)}, u32[]{:S(2)}) copy-start(bf16[64,16,256]{2,1,0:T(8,128)(2,1)} %bank_ref.1) | copy-start | bytes 1572868
  2.1 27.6 %copy-start.3 = (bf16[96,32]{1,0:T(8,128)(2,1)S(1)}, bf16[96,32]{1,0:T(8,128)(2,1)}, u32[]{:S(2)}) copy-start(bf16[96,32]{1,0:T(8,128)(2,1)} %constant.35.clone.line_ref) | copy-start | bytes 18436
  2.1 27.6 %copy-start.5 = (f32[4,1024]{1,0:T(4,128)S(1)}, f32[4,1024]{1,0:T(4,128)}, u32[]{:S(2)}) copy-start(f32[4,1024]{1,0:T(4,128)} %constant.36.clone.turn_ref) | copy-start | bytes 49156
  2.1 27.6 %copy-start.7 = (s32[8]{0:T(128)S(1)}, s32[8]{0:T(128)}, u32[]{:S(2)}) copy-start(s32[8]{0:T(128)} %rot_ref.1) | copy-start | bytes 100
  18.8 12.3 %collective-permute-start = (bf16[8,48,512]{2,1,0:T(8,128)(2,1)S(1)}, bf16[8,48,512]{2,1,0:T(8,128)(2,1)S(1)}, u32[]{:S(2)}, u32[]{:S(2)}) collective-permute-start(bf16[8,48,512]{2,1,0:T(8,128)(2,1)S(1)} %all_to_all.5.refs_1_), channel_id=1, source_target_pairs={{0,1},{1,0},{2,3},{3,2},{4,5},{5,4},{6,7},{7,6},{8,9},{9,8},{10,11... | collective-permute-start | bytes 1179656 | tf_op jit(solution)/shard_map/ppermute | solution.py:255
  22.4 8.8 %copy-start.4 = (bf16[96,96]{1,0:T(8,128)(2,1)S(1)}, bf16[96,96]{1,0:T(8,128)(2,1)}, u32[]{:S(2)}) copy-start(bf16[96,96]{1,0:T(8,128)(2,1)} %constant.38.clone.refs_6_) | copy-start | bytes 55300
  22.4 8.8 %copy-start.6 = (bf16[64,96]{1,0:T(8,128)(2,1)S(1)}, bf16[64,96]{1,0:T(8,128)(2,1)}, u32[]{:S(2)}) copy-start(bf16[64,96]{1,0:T(8,128)(2,1)} %constant.39.clone.refs_7_) | copy-start | bytes 36868

commit v2 on v1

v2 whole, which is shorter than its diff:
```python
import math

import jax
import jax.numpy as jnp
import numpy as np
from jax import lax
from jax.experimental import pallas as pl
from jax.experimental.pallas import tpu as pltpu
from jax.sharding import Mesh
from jax.sharding import PartitionSpec as P

EDGE = 32
XT = 2
K = 16
NTILT = 61
NTPL = 8
NDET = 128
HALO = K // 2
LEN = EDGE + K
X = XT * EDGE
Z = EDGE
XR = EDGE + HALO
LZ = Z + HALO
KZ = LZ // 2 + 1
NF = LEN * KZ
FP = 1024
XB = 8
NQ = XR // XB
LB = XB * Z
MAX_ANGLE = 1.05
VOXEL = 1.4
SCALE = 1.0 / (LEN * LEN * LZ)
BF = jnp.bfloat16
F32 = jnp.float32


def reach(q):
    x = np.arange(q * XB, (q + 1) * XB) - (X - 1) / 2.0
    z = np.arange(Z) - (Z - 1) / 2.0
    top = 0.0
    low = 0.0
    angle = np.linspace(-MAX_ANGLE, MAX_ANGLE, 4001)
    first = True
    for xv in (x[0], x[-1]):
        for zv in (z[0], z[-1]):
            pos = VOXEL * (xv * np.cos(angle) + zv * np.sin(angle)) + (NDET - 1) / 2.0
            low = pos.min() if first else min(low, pos.min())
            top = pos.max() if first else max(top, pos.max())
            first = False
    return math.ceil(low - 1.0 - 0.01), math.floor(top + 1.0 + 0.01)


def pair_list(n_det):
    pairs = []
    for q in range(NQ):
        low, top = reach(q)
        pairs.append(list(range(max(low, 0) // n_det, min(top, NDET - 1) // n_det + 1)))
    return pairs


def rounded(table):
    return np.asarray(table, np.float32).astype(jnp.bfloat16)


def plane_tables():
    kz = np.repeat(np.arange(KZ), LEN)
    kx = np.tile(np.arange(LEN), KZ)

    def waves(k, at, length):
        p = 2.0 * np.pi * (np.outer(at, k) % length) / length
        out = np.zeros((2, len(at), FP), np.float32)
        out[0, :, : len(k)], out[1, :, : len(k)] = np.cos(p), np.sin(p)
        return out

    vx = np.repeat(np.arange(EDGE), EDGE)
    vz = np.tile(np.arange(EDGE) - HALO, EDGE)
    weight = np.full((KZ, 1), 2.0)
    weight[0] = weight[-1] = 1.0
    return (
        waves(kx, np.arange(XR), LEN),
        waves(kz, np.arange(Z), LZ),
        waves(vx, np.arange(LEN), LEN),
        waves(vz, np.arange(KZ), LZ) * weight,
        waves(kx, np.array([HALO, 0]), LEN) * np.array([1.0, -1.0])[:, None, None],
    )


def line_tables():
    def table(outs, ins, sign):
        p = 2.0 * np.pi * (np.outer(np.arange(outs), np.arange(ins)) % LEN) / LEN
        c, s = np.cos(p), np.sin(p) * sign
        return c, s

    c, s = table(LEN, LEN, 1.0)
    region = rounded(np.block([[c, s], [-s, c]]))
    c, s = table(LEN, K, 1.0)
    template = rounded(np.block([[c, s], [-s, c]]))
    c, s = table(EDGE, LEN, 1.0)
    back = rounded(np.block([[c, -s], [s, c]]))
    return region, template, back


def pack_kernel(n_block, range_ref, proj_ref, out_ref):
    n_tilt, n_det, y_count = proj_ref.shape
    depth = out_ref.shape[2]
    y = lax.broadcasted_iota(jnp.int32, (n_det, y_count), 1)
    parts = []
    for t in range(n_tilt):
        keep = (y >= range_ref[0, t]) & (y < range_ref[1, t])
        parts.append(jnp.where(keep, proj_ref[t].astype(F32), 0.0))
    if depth > n_tilt * n_det:
        parts.append(jnp.zeros((depth - n_tilt * n_det, y_count), F32))
    xt = jnp.concatenate(parts, 0).T
    for b in range(n_block):
        low, top = b * EDGE - HALO, b * EDGE - HALO + LEN
        part = xt[max(low, 0) : min(top, y_count)]
        if low < 0:
            part = jnp.concatenate([jnp.zeros((-low, depth), F32), part], 0)
        if top > y_count:
            part = jnp.concatenate([part, jnp.zeros((top - y_count, depth), F32)], 0)
        out_ref[b] = part.astype(BF)


def build_weights(n_det, n_tile, pairs, col, turns_ref, w_ref, p_ref):
    depth = turns_ref.shape[0]
    lane = lax.broadcasted_iota(jnp.int32, (1, LB), 1)
    z = (lane % Z).astype(F32) - (Z - 1) / 2.0
    step = (lane // Z).astype(F32)
    row = lax.broadcasted_iota(jnp.int32, (depth, 1), 0)
    own = (row % n_det).astype(F32)
    base = 0
    for q, sources in enumerate(pairs):
        block = jnp.where(col == 0, q, NQ - 1 - q) * XB + col * (X - XR)
        x = step + (block.astype(F32) - (X - 1) / 2.0)
        pos = VOXEL * (x * turns_ref[:, 0:1] + z * turns_ref[:, 1:2])
        p_ref[...] = pos + ((NDET - 1) / 2.0 - own)

        def build(j, carry, base=base, first=sources[0]):
            src = first + j
            src = jnp.where(col == 0, src, n_tile - 1 - src)
            shift = (src * n_det).astype(F32)
            w_ref[base + j] = jnp.maximum(0.0, 1.0 - jnp.abs(p_ref[...] - shift)).astype(BF)
            return carry

        lax.fori_loop(0, len(sources), build, 0)
        base += len(sources)


def build_planes(fx_ref, fz_ref, ix_ref, iz_ref, plane_ref, inverse_ref):
    def forward(x, carry):
        cos_x, sin_x = fx_ref[0, pl.ds(x, 1)], fx_ref[1, pl.ds(x, 1)]
        cos_z, sin_z = fz_ref[0], fz_ref[1]
        at = pl.ds(pl.multiple_of(x * Z, Z), Z)
        plane_ref[at, :FP] = (cos_x * cos_z - sin_x * sin_z).astype(BF)
        plane_ref[at, FP:] = (-sin_x * cos_z - cos_x * sin_z).astype(BF)
        return carry

    lax.fori_loop(0, XR, forward, 0)

    def inverse(k, carry):
        cos_z, sin_z = iz_ref[0, pl.ds(k, 1)], iz_ref[1, pl.ds(k, 1)]
        cos_x, sin_x = ix_ref[0], ix_ref[1]
        low = pl.multiple_of(k * LEN, 16)
        inverse_ref[pl.ds(low, LEN)] = (cos_x * cos_z - sin_x * sin_z).astype(BF)
        inverse_ref[pl.ds(FP + low, LEN)] = (-sin_x * cos_z - cos_x * sin_z).astype(BF)
        return carry

    lax.fori_loop(0, KZ, inverse, 0)
    inverse_ref[NF:FP] = jnp.zeros((FP - NF, EDGE * EDGE), BF)
    inverse_ref[FP + NF :] = jnp.zeros((FP - NF, EDGE * EDGE), BF)


def build_templates(col, rot_ref, bank_ref, plane_ref, line_ref, turn_ref, out_ref):
    chosen = jnp.concatenate([bank_ref[rot_ref[r]] for r in range(NTPL)], 0)
    plane = jnp.concatenate([plane_ref[b * Z : b * Z + K] for b in range(K)], 0)
    flat = jnp.dot(chosen, plane, preferred_element_type=F32).astype(BF)
    cos = jnp.where(col == 0, turn_ref[0, 0:1], turn_ref[0, 1:2])
    sin = jnp.where(col == 0, turn_ref[1, 0:1], turn_ref[1, 1:2])
    for r in range(NTPL):
        part = flat[r * K : (r + 1) * K]
        stacked = jnp.concatenate([part[:, :FP], part[:, FP:]], 0)
        full = jnp.dot(line_ref[...], stacked, preferred_element_type=F32)
        real, imag = full[:LEN], -full[LEN:]
        out_ref[r, :LEN] = (real * cos - imag * sin).astype(BF)
        out_ref[r, LEN:] = (real * sin + imag * cos).astype(BF)


def prepare_kernel(
    n_det,
    n_tile,
    pairs,
    col_ref,
    rot_ref,
    turns_ref,
    bank_ref,
    fx_ref,
    fz_ref,
    ix_ref,
    iz_ref,
    line_ref,
    turn_ref,
    w_ref,
    plane_ref,
    inverse_ref,
    tmpl_ref,
    done_ref,
    p_ref,
):
    col = col_ref[0]
    build_planes(fx_ref, fz_ref, ix_ref, iz_ref, plane_ref, inverse_ref)
    build_weights(n_det, n_tile, pairs, col, turns_ref, w_ref, p_ref)
    build_templates(col, rot_ref, bank_ref, plane_ref, line_ref, turn_ref, tmpl_ref)
    done_ref[...] = jnp.zeros_like(done_ref)


def partial_sums(n_block, pairs, parity, col, data_ref, w_ref):
    base = 0
    for sources in pairs:
        total = jnp.zeros((LEN, LB), F32)
        for j, src in enumerate(sources):
            if src % 2 == parity:
                chip = jnp.where(col == 0, src // 2, n_block - 1 - src // 2)
                total += jnp.dot(data_ref[chip], w_ref[base + j], preferred_element_type=F32)
        base += len(sources)
        yield total


def half_kernel(n_block, pairs, col_ref, done_ref, own_ref, w_ref, out_ref):
    del done_ref
    for q, total in enumerate(partial_sums(n_block, pairs, 0, col_ref[0], own_ref, w_ref)):
        out_ref[q] = total


def score_kernel(
    n_block,
    pairs,
    col_ref,
    half_ref,
    other_ref,
    w_ref,
    tmpl_ref,
    plane_ref,
    line_ref,
    back_ref,
    inverse_ref,
    out_ref,
    vol_ref,
    mid_ref,
):
    col = col_ref[0]
    for q, total in enumerate(partial_sums(n_block, pairs, 1, col, other_ref, w_ref)):
        block = jnp.where(col == 0, q, NQ - 1 - q)
        at = pl.ds(pl.multiple_of(block * LB, LB), LB)
        vol_ref[:, at] = (total + half_ref[q]).astype(BF)
    flat = jnp.dot(vol_ref[...], plane_ref[...], preferred_element_type=F32).astype(BF)
    stacked = jnp.concatenate([flat[:, :FP], flat[:, FP:]], 0)
    full = jnp.dot(line_ref[...], stacked, preferred_element_type=F32)
    real, imag = full[:LEN], full[LEN:]
    for r in range(NTPL):
        t_real = tmpl_ref[r, :LEN].astype(F32)
        t_imag = tmpl_ref[r, LEN:].astype(F32)
        prod = jnp.concatenate(
            [
                (t_real * real - t_imag * imag).astype(BF),
                (t_real * imag + t_imag * real).astype(BF),
            ],
            0,
        )
        line = jnp.dot(back_ref[...], prod, preferred_element_type=F32).astype(BF)
        mid_ref[r * EDGE : (r + 1) * EDGE, :FP] = line[:EDGE]
        mid_ref[r * EDGE : (r + 1) * EDGE, FP:] = line[EDGE:]
    corr = jnp.dot(mid_ref[...], inverse_ref[...], preferred_element_type=F32)
    best = corr[:EDGE]
    for r in range(1, NTPL):
        best = jnp.maximum(best, corr[r * EDGE : (r + 1) * EDGE])
    out_ref[0] = best * SCALE


VMEM = pl.BlockSpec(memory_space=pltpu.VMEM)
SMEM = pl.BlockSpec(memory_space=pltpu.SMEM)


def limit(mib):
    return pltpu.CompilerParams(vmem_limit_bytes=mib << 20)


def cost(flops, nbytes):
    return pl.CostEstimate(flops=flops, bytes_accessed=nbytes, transcendentals=0)


def solution(mesh):
    n_tile = mesh.shape["tile"]
    n_block = n_tile // XT
    n_det = NDET // n_tile
    rows = NTILT * n_det
    depth = (rows + 127) // 128 * 128
    pairs = pair_list(n_det)
    n_pair = sum(len(p) for p in pairs)
    tables = plane_tables()
    line, line_t, back = line_tables()

    def local(projections, tilt_angle, row_range, template_bank, rot_index):
        col = lax.axis_index("core").astype(jnp.int32).reshape(1)
        by_y = jnp.transpose(projections, (1, 2, 0))
        send = pl.pallas_call(
            lambda *refs: pack_kernel(n_block, *refs),
            out_shape=jax.ShapeDtypeStruct((n_block, LEN, depth), BF),
            in_specs=[SMEM, VMEM],
            out_specs=VMEM,
            compiler_params=limit(4),
        )(row_range.T, by_y)
        own = lax.all_to_all(send, "chip", 0, 0, tiled=True)
        turns = jnp.stack([jnp.cos(tilt_angle), jnp.sin(tilt_angle)], 1)
        turns = jnp.pad(jnp.repeat(turns, n_det, axis=0), ((0, depth - rows), (0, 0)))
        weights, plane, inverse, spectra, done = pl.pallas_call(
            lambda *refs: prepare_kernel(n_det, n_tile, pairs, *refs),
            out_shape=(
                jax.ShapeDtypeStruct((n_pair, depth, LB), BF),
                jax.ShapeDtypeStruct((XR * Z, 2 * FP), BF),
                jax.ShapeDtypeStruct((2 * FP, EDGE * EDGE), BF),
                jax.ShapeDtypeStruct((NTPL, 2 * LEN, FP), BF),
                jax.ShapeDtypeStruct((8, 128), F32),
            ),
            in_specs=[SMEM, SMEM] + [VMEM] * 8,
            out_specs=(VMEM,) * 5,
            scratch_shapes=[pltpu.VMEM((depth, LB), F32)],
            compiler_params=limit(28),
            cost_estimate=cost(1 << 32, 24 << 20),
        )(
            col,
            rot_index,
            turns,
            template_bank,
            *[jnp.asarray(t) for t in tables[:4]],
            jnp.asarray(line_t),
            jnp.asarray(tables[4]),
        )
        own, done = lax.optimization_barrier((own, done))
        other = lax.ppermute(own, "core", [(0, 1), (1, 0)])
        half = pl.pallas_call(
            lambda *refs: half_kernel(n_block, pairs, *refs),
            out_shape=jax.ShapeDtypeStruct((NQ, LEN, LB), F32),
            in_specs=[SMEM, VMEM, VMEM, VMEM],
            out_specs=VMEM,
            compiler_params=limit(16),
            cost_estimate=cost(n_pair * LEN * depth * LB, n_pair * depth * LB),
        )(col, done, own, weights)
        return pl.pallas_call(
            lambda *refs: score_kernel(n_block, pairs, *refs),
            out_shape=jax.ShapeDtypeStruct((1, EDGE, EDGE * Z), F32),
            in_specs=[SMEM] + [VMEM] * 8,
            out_specs=VMEM,
            scratch_shapes=[
                pltpu.VMEM((LEN, XR * Z), BF),
                pltpu.VMEM((NTPL * EDGE, 2 * FP), BF),
            ],
            compiler_params=limit(28),
            cost_estimate=cost(4 << 30, 20 << 20),
        )(
            col,
            half,
            other,
            weights,
            spectra,
            plane,
            jnp.asarray(line),
            jnp.asarray(back),
            inverse,
        )

    tile = ("chip", "core")
    split = Mesh(mesh.devices.reshape(-1, n_block, XT), ("grp",) + tile)
    return jax.shard_map(
        local,
        mesh=split,
        in_specs=(P("grp", None, tile), P("grp"), P("grp", None), P(), P()),
        out_specs=P(tile, "grp", None),
        check_vma=False,
    )
```

time: 43.1 us -> 51.5 us (1.19)
  local copies, waits for them, and re-layouts: 2.62 us -> 28.1 us
  blocking collectives: 16.7 us -> 0 us
  Pallas kernels: 20.7 us -> 15.2 us
  starting transfers between devices: 2.7 us -> 7.34 us
    unnamed x17 -> x38, local copies, waits for them, and re-layouts: 1.77 us -> 27.2 us
    all_to_all x1 -> x0, blocking collectives: 16.7 us -> none  [local(): own = lax.all_to_all(send, 'tile', 0, 0, tiled=True, axis_index_groups=same)]
    pallas_call x1, Pallas kernels: 11.7 us -> 4.62 us  [local(): pl.pallas_call(lambda *refs: score_kernel(n_block, pairs, *refs), out_sha...]
    all_to_all x0 -> x1, starting transfers between devices: none -> 6.38 us  [local(): own = lax.all_to_all(send, 'chip', 0, 0, tiled=True)]
    ppermute x1, starting transfers between devices: 2.7 us -> 0.96 us  [local(): other = lax.ppermute(own, 'core', [(0, 1), (1, 0)])]
    pallas_call x1, Pallas kernels: 0.32 us -> 1.49 us  [local(): pl.pallas_call(lambda *refs: pack_kernel(n_block, *refs), out_shape=jax.S...]
  transfers between devices with their start and end apart: 1 -> 2, of which waited for: 0 -> 0; matrix products, arithmetic and copies ran while one was open for 2% -> 2% of each run, Pallas kernels for 20% -> 18%
where the time goes in v2:
time: 51.5 us; the launch traced here: 50.8 us
  local copies, waits for them, and re-layouts  28.1 us (55%)
  Pallas kernels  15.2 us (30%)
  starting transfers between devices  7.34 us (14%)
    unnamed x38, local copies, waits for them, and re-layouts  27.2 us
    pallas_call x1, Pallas kernels, local(): pl.pallas_call(lambda *refs: prepare_kernel(n_det, n_tile, pairs, *refs),...  8.26 us
    all_to_all x1, starting transfers between devices, local(): own = lax.all_to_all(send, 'chip', 0, 0, tiled=True)  6.38 us
    pallas_call x1, Pallas kernels, local(): pl.pallas_call(lambda *refs: score_kernel(n_block, pairs, *refs), out_sha...  4.62 us
    pallas_call x1, Pallas kernels, local(): pl.pallas_call(lambda *refs: pack_kernel(n_block, *refs), out_shape=jax.S...  1.49 us
  transfers between devices with their start and end apart: 2, of which 0 were waited for; matrix products, arithmetic and copies ran while one was open for 2% of the time, Pallas kernels for 18%

profile of v2, /device:TPU:1, one launch (start us, length us, event | category | flops | bytes accessed | tf_op | source)
XLA Modules:
  0.0 50.8 jit_solution(5857619437342394208)
XLA Ops:
  0.0 0.9 %copy-done.7 = bf16[256,61,8]{0,2,1:T(8,128)(2,1)S(1)} copy-done((bf16[256,61,8]{0,2,1:T(8,128)(2,1)S(1)}, bf16[256,61,8]{0,2,1:T(8,128)(2,1)}, u32[]{:S(2)}) %copy-start.7) | copy-done | bytes 249880
  0.9 0.7 %copy-done.10 = s32[61,2]{0,1:T(2,128)S(1)} copy-done((s32[61,2]{0,1:T(2,128)S(1)}, s32[61,2]{0,1:T(2,128)}, u32[]{:S(2)}) %copy-start.10) | copy-done | bytes 512
  1.6 1.5 %shard_map.127 = bf16[8,48,512]{2,1,0:T(8,128)(2,1)} custom-call(s32[2,61]{1,0:T(2,128)S(1)} %bitcast.10, bf16[61,8,256]{2,1,0:T(8,128)(2,1)S(1)} %bitcast.9), custom_call_target="tpu_custom_call" | custom-call | tf_op jit(solution)/shard_map/pallas_call | solution.py:305
  3.1 6.4 %all-to-all-start = ((bf16[8,48,512]{2,1,0:T(8,128)(2,1)}), bf16[8,48,512]{2,1,0:T(8,128)(2,1)S(1)}, u32[]{:S(2)}, u32[]{:S(2)}) async-start(bf16[8,48,512]{2,1,0:T(8,128)(2,1)} %shard_map.127), calls=%async_computation | async-start | bytes 786432 | tf_op jit(solution)/shard_map/all_to_all | solution.py:312
  9.5 0.7 %cosine_bitcast_fusion = (f32[61,1]{0,1:T(1,128)S(1)}, f32[61,1]{0,1:T(1,128)S(1)}) fusion(f32[61]{0:T(128)} %param.14), kind=kLoop, calls=%fused_computation.3 | loop fusion | bytes 732 | tf_op jit(solution)/shard_map/stack | solution.py:313
  10.4 1.0 %copy-done.11 = bf16[64,16,256]{2,1,0:T(8,128)(2,1)S(1)} copy-done((bf16[64,16,256]{2,1,0:T(8,128)(2,1)S(1)}, bf16[64,16,256]{2,1,0:T(8,128)(2,1)}, u32[]{:S(2)}) %copy-start.11) | copy-done | bytes 524312
  11.4 0.7 %copy-done.12 = s32[8]{0:T(128)S(1)} copy-done((s32[8]{0:T(128)S(1)}, s32[8]{0:T(128)}, u32[]{:S(2)}) %copy-start.12) | copy-done | bytes 56
  12.1 1.0 %copy-done.13 = f32[2,48,1024]{2,1,0:T(8,128)S(1)} copy-done((f32[2,48,1024]{2,1,0:T(8,128)S(1)}, f32[2,48,1024]{2,1,0:T(8,128)}, u32[]{:S(2)}) %copy-start.13) | copy-done | bytes 393240
  13.1 1.0 %copy-done.14 = f32[2,40,1024]{2,1,0:T(8,128)S(1)} copy-done((f32[2,40,1024]{2,1,0:T(8,128)S(1)}, f32[2,40,1024]{2,1,0:T(8,128)}, u32[]{:S(2)}) %copy-start.14) | copy-done | bytes 327704
  14.0 0.9 %copy-done.15 = f32[2,32,1024]{2,1,0:T(8,128)S(1)} copy-done((f32[2,32,1024]{2,1,0:T(8,128)S(1)}, f32[2,32,1024]{2,1,0:T(8,128)}, u32[]{:S(2)}) %copy-start.15) | copy-done | bytes 262168
  15.0 0.9 %copy-done.16 = f32[2,21,1024]{2,1,0:T(8,128)S(1)} copy-done((f32[2,21,1024]{2,1,0:T(8,128)S(1)}, f32[2,21,1024]{2,1,0:T(8,128)}, u32[]{:S(2)}) %copy-start.16) | copy-done | bytes 172056
  15.9 0.7 %copy-done.17 = bf16[96,32]{1,0:T(8,128)(2,1)S(1)} copy-done((bf16[96,32]{1,0:T(8,128)(2,1)S(1)}, bf16[96,32]{1,0:T(8,128)(2,1)}, u32[]{:S(2)}) %copy-start.17) | copy-done | bytes 6168
  16.7 0.7 %copy-done.18 = f32[2,2,1024]{2,1,0:T(2,128)S(1)} copy-done((f32[2,2,1024]{2,1,0:T(2,128)S(1)}, f32[2,2,1024]{2,1,0:T(2,128)}, u32[]{:S(2)}) %copy-start.18) | copy-done | bytes 16408
  17.4 8.3 %shard_map.128 = (bf16[34,512,256]{2,1,0:T(8,128)(2,1)S(1)}, bf16[1280,2048]{1,0:T(8,128)(2,1)S(1)}, bf16[2048,1024]{1,0:T(8,128)(2,1)S(1)}, bf16[8,96,1024]{2,1,0:T(8,128)(2,1)S(1)}, f32[8,128]{1,0:T(8,128)S(1)}) custom-call(s32[1]{0:T(128)} %bitcast.refs_0_, s32[8]{0:T(128)S(1)} %copy-done.12, f32[512,2]{1,0:T(8,128)S(1)} %pad.4.refs_2_, ...), custom_call_target="tpu_custom_call" | custom-call | flops 4294967296 | bytes 25165824 | tf_op jit(solution)/shard_map/pallas_call | solution.py:315
  25.7 3.5 %copy-done = bf16[34,512,256]{2,1,0:T(8,128)(2,1)} copy-done((bf16[34,512,256]{2,1,0:T(8,128)(2,1)}, bf16[34,512,256]{2,1,0:T(8,128)(2,1)S(1)}, u32[]{:S(2)}) %copy-start) | copy-done | bytes 8912920
  29.1 2.4 %copy-done.3 = bf16[1280,2048]{1,0:T(8,128)(2,1)} copy-done((bf16[1280,2048]{1,0:T(8,128)(2,1)}, bf16[1280,2048]{1,0:T(8,128)(2,1)S(1)}, u32[]{:S(2)}) %copy-start.3) | copy-done | bytes 5242904
  31.5 2.0 %copy-done.5 = bf16[2048,1024]{1,0:T(8,128)(2,1)} copy-done((bf16[2048,1024]{1,0:T(8,128)(2,1)}, bf16[2048,1024]{1,0:T(8,128)(2,1)S(1)}, u32[]{:S(2)}) %copy-start.5) | copy-done | bytes 4194328
  33.5 1.0 %collective-permute-start = (bf16[8,48,512]{2,1,0:T(8,128)(2,1)S(1)}, bf16[8,48,512]{2,1,0:T(8,128)(2,1)S(1)}, u32[]{:S(2)}, u32[]{:S(2)}) collective-permute-start(bf16[8,48,512]{2,1,0:T(8,128)(2,1)S(1)} %all-to-all-done.refs_2_), channel_id=1, source_target_pairs={{0,1},{1,0},{2,3},{3,2},{4,5},{5,4},{6,7},{7,6},{8,9},{9,8},{10,11... | collective-permute-start | bytes 1179656 | tf_op jit(solution)/shard_map/ppermute | solution.py:339
  34.4 3.5 %copy-done.1 = bf16[34,512,256]{2,1,0:T(8,128)(2,1)S(1)} copy-done((bf16[34,512,256]{2,1,0:T(8,128)(2,1)S(1)}, bf16[34,512,256]{2,1,0:T(8,128)(2,1)}, u32[]{:S(2)}) %copy-start.1) | copy-done | bytes 8912920
  38.0 0.9 %shard_map.129.refs_1_ = f32[5,48,256]{2,1,0:T(8,128)S(1)} custom-call(s32[1]{0:T(128)} %bitcast.refs_0_, f32[8,128]{1,0:T(8,128)S(1)} %get-tuple-element.13.refs_1_, bf16[8,48,512]{2,1,0:T(8,128)(2,1)S(1)} %all-to-all-done.refs_2_, bf16[34,512,256]{2,1,0:T(8,128)(2,1)S(1)} %copy-done.1), custom_call_target="tpu_custom_call" | custom-call | flops 213909504 | bytes 4456448 | tf_op jit(solution)/shard_map/pallas_call | solution.py:340
  38.9 2.6 %copy-done.2 = bf16[34,512,256]{2,1,0:T(8,128)(2,1)S(1)} copy-done((bf16[34,512,256]{2,1,0:T(8,128)(2,1)S(1)}, bf16[34,512,256]{2,1,0:T(8,128)(2,1)}, u32[]{:S(2)}) %copy-start.2) | copy-done | bytes 8912920
  41.5 2.5 %copy-done.4 = bf16[1280,2048]{1,0:T(8,128)(2,1)S(1)} copy-done((bf16[1280,2048]{1,0:T(8,128)(2,1)S(1)}, bf16[1280,2048]{1,0:T(8,128)(2,1)}, u32[]{:S(2)}) %copy-start.4) | copy-done | bytes 5242904
  44.0 2.2 %copy-done.6 = bf16[2048,1024]{1,0:T(8,128)(2,1)S(1)} copy-done((bf16[2048,1024]{1,0:T(8,128)(2,1)S(1)}, bf16[2048,1024]{1,0:T(8,128)(2,1)}, u32[]{:S(2)}) %copy-start.6) | copy-done | bytes 4194328
  46.2 4.6 %shard_map.130 = f32[1,32,1024]{2,1,0:T(8,128)} custom-call(s32[1]{0:T(128)} %bitcast.refs_0_, f32[5,48,256]{2,1,0:T(8,128)S(1)} %shard_map.129.refs_1_, bf16[8,48,512]{2,1,0:T(8,128)(2,1)S(1)} %collective-permute-done.refs_2_, bf16[34,512,256]{2,1,0:T(8,128)(2,1)S(1)} %copy-done.2, bf16[8,96,1024]{2,1,0:T(8,128)(2,1)S(1)} %get-tuple-element.16.refs_4_, ...), custom_call_target="tpu_custom_call" | custom-call | flops 4294967296 | bytes 20971520 | tf_op jit(solution)/shard_map/pallas_call | solution.py:348
  (27 shorter events, 0.2 us)
Async XLA Ops:
  0.0 0.9 %copy-start.7 = (bf16[256,61,8]{0,2,1:T(8,128)(2,1)S(1)}, bf16[256,61,8]{0,2,1:T(8,128)(2,1)}, u32[]{:S(2)}) copy-start(bf16[256,61,8]{0,2,1:T(8,128)(2,1)} %param.13) | copy-start | bytes 749572
  0.9 0.7 %copy-start.10 = (s32[61,2]{0,1:T(2,128)S(1)}, s32[61,2]{0,1:T(2,128)}, u32[]{:S(2)}) copy-start(s32[61,2]{0,1:T(2,128)} %param.15) | copy-start | bytes 1468
  3.1 30.3 %all-to-all-start = ((bf16[8,48,512]{2,1,0:T(8,128)(2,1)}), bf16[8,48,512]{2,1,0:T(8,128)(2,1)S(1)}, u32[]{:S(2)}, u32[]{:S(2)}) async-start(bf16[8,48,512]{2,1,0:T(8,128)(2,1)} %shard_map.127), calls=%async_computation | async-start | bytes 786432 | tf_op jit(solution)/shard_map/all_to_all | solution.py:312
  10.4 1.0 %copy-start.11 = (bf16[64,16,256]{2,1,0:T(8,128)(2,1)S(1)}, bf16[64,16,256]{2,1,0:T(8,128)(2,1)}, u32[]{:S(2)}) copy-start(bf16[64,16,256]{2,1,0:T(8,128)(2,1)} %refs_3_.1) | copy-start | bytes 1572868
  11.4 0.7 %copy-start.12 = (s32[8]{0:T(128)S(1)}, s32[8]{0:T(128)}, u32[]{:S(2)}) copy-start(s32[8]{0:T(128)} %refs_1_.1) | copy-start | bytes 100
  12.1 1.0 %copy-start.13 = (f32[2,48,1024]{2,1,0:T(8,128)S(1)}, f32[2,48,1024]{2,1,0:T(8,128)}, u32[]{:S(2)}) copy-start(f32[2,48,1024]{2,1,0:T(8,128)} %constant.25.clone.refs_6_) | copy-start | bytes 1179652
  13.1 1.0 %copy-start.14 = (f32[2,40,1024]{2,1,0:T(8,128)S(1)}, f32[2,40,1024]{2,1,0:T(8,128)}, u32[]{:S(2)}) copy-start(f32[2,40,1024]{2,1,0:T(8,128)} %constant.23.clone.refs_4_) | copy-start | bytes 983044
  14.0 0.9 %copy-start.15 = (f32[2,32,1024]{2,1,0:T(8,128)S(1)}, f32[2,32,1024]{2,1,0:T(8,128)}, u32[]{:S(2)}) copy-start(f32[2,32,1024]{2,1,0:T(8,128)} %constant.24.clone.refs_5_) | copy-start | bytes 786436
  15.0 0.9 %copy-start.16 = (f32[2,21,1024]{2,1,0:T(8,128)S(1)}, f32[2,21,1024]{2,1,0:T(8,128)}, u32[]{:S(2)}) copy-start(f32[2,21,1024]{2,1,0:T(8,128)} %constant.26.clone.refs_7_) | copy-start | bytes 516100
  15.9 0.7 %copy-start.17 = (bf16[96,32]{1,0:T(8,128)(2,1)S(1)}, bf16[96,32]{1,0:T(8,128)(2,1)}, u32[]{:S(2)}) copy-start(bf16[96,32]{1,0:T(8,128)(2,1)} %constant.27.clone.refs_8_) | copy-start | bytes 18436
  16.7 0.7 %copy-start.18 = (f32[2,2,1024]{2,1,0:T(2,128)S(1)}, f32[2,2,1024]{2,1,0:T(2,128)}, u32[]{:S(2)}) copy-start(f32[2,2,1024]{2,1,0:T(2,128)} %constant.28.clone.refs_9_) | copy-start | bytes 49156
  17.4 21.5 %copy-start.8 = (bf16[96,96]{1,0:T(8,128)(2,1)S(1)}, bf16[96,96]{1,0:T(8,128)(2,1)}, u32[]{:S(2)}) copy-start(bf16[96,96]{1,0:T(8,128)(2,1)} %constant.29.clone.refs_6_) | copy-start | bytes 55300
  17.4 21.5 %copy-start.9 = (bf16[64,96]{1,0:T(8,128)(2,1)S(1)}, bf16[64,96]{1,0:T(8,128)(2,1)}, u32[]{:S(2)}) copy-start(bf16[64,96]{1,0:T(8,128)(2,1)} %constant.30.clone.refs_7_) | copy-start | bytes 36868
  25.6 3.5 %copy-start = (bf16[34,512,256]{2,1,0:T(8,128)(2,1)}, bf16[34,512,256]{2,1,0:T(8,128)(2,1)S(1)}, u32[]{:S(2)}) copy-start(bf16[34,512,256]{2,1,0:T(8,128)(2,1)S(1)} %get-tuple-element.15.refs_3_) | copy-start | bytes 26738692
  29.1 2.4 %copy-start.3 = (bf16[1280,2048]{1,0:T(8,128)(2,1)}, bf16[1280,2048]{1,0:T(8,128)(2,1)S(1)}, u32[]{:S(2)}) copy-start(bf16[1280,2048]{1,0:T(8,128)(2,1)S(1)} %get-tuple-element.17.refs_5_) | copy-start | bytes 15728644
  31.5 2.0 %copy-start.5 = (bf16[2048,1024]{1,0:T(8,128)(2,1)}, bf16[2048,1024]{1,0:T(8,128)(2,1)S(1)}, u32[]{:S(2)}) copy-start(bf16[2048,1024]{1,0:T(8,128)(2,1)S(1)} %get-tuple-element.18.refs_8_) | copy-start | bytes 12582916
  33.5 5.4 %collective-permute-start = (bf16[8,48,512]{2,1,0:T(8,128)(2,1)S(1)}, bf16[8,48,512]{2,1,0:T(8,128)(2,1)S(1)}, u32[]{:S(2)}, u32[]{:S(2)}) collective-permute-start(bf16[8,48,512]{2,1,0:T(8,128)(2,1)S(1)} %all-to-all-done.refs_2_), channel_id=1, source_target_pairs={{0,1},{1,0},{2,3},{3,2},{4,5},{5,4},{6,7},{7,6},{8,9},{9,8},{10,11... | collective-permute-start | bytes 1179656 | tf_op jit(solution)/shard_map/ppermute | solution.py:339
  34.4 3.5 %copy-start.1 = (bf16[34,512,256]{2,1,0:T(8,128)(2,1)S(1)}, bf16[34,512,256]{2,1,0:T(8,128)(2,1)}, u32[]{:S(2)}) copy-start(bf16[34,512,256]{2,1,0:T(8,128)(2,1)} %copy-done) | copy-start | bytes 26738692
  37.9 3.5 %copy-start.2 = (bf16[34,512,256]{2,1,0:T(8,128)(2,1)S(1)}, bf16[34,512,256]{2,1,0:T(8,128)(2,1)}, u32[]{:S(2)}) copy-start(bf16[34,512,256]{2,1,0:T(8,128)(2,1)} %copy-done) | copy-start | bytes 26738692
  41.5 2.5 %copy-start.4 = (bf16[1280,2048]{1,0:T(8,128)(2,1)S(1)}, bf16[1280,2048]{1,0:T(8,128)(2,1)}, u32[]{:S(2)}) copy-start(bf16[1280,2048]{1,0:T(8,128)(2,1)} %copy-done.3) | copy-start | bytes 15728644
  44.0 2.2 %copy-start.6 = (bf16[2048,1024]{1,0:T(8,128)(2,1)S(1)}, bf16[2048,1024]{1,0:T(8,128)(2,1)}, u32[]{:S(2)}) copy-start(bf16[2048,1024]{1,0:T(8,128)(2,1)} %copy-done.5) | copy-start | bytes 12582916

commit v3 on v2

--- a/solution.py
+++ b/solution.py
@@ -6,7 +6,6 @@
 from jax import lax
 from jax.experimental import pallas as pl
 from jax.experimental.pallas import tpu as pltpu
-from jax.sharding import Mesh
 from jax.sharding import PartitionSpec as P
 
 EDGE = 32
@@ -100,9 +99,31 @@
     return region, template, back
 
 
-def pack_kernel(n_block, range_ref, proj_ref, out_ref):
+def pack_kernel(
+    near_bit,
+    masks,
+    at_ref,
+    range_hbm,
+    proj_hbm,
+    home_ref,
+    near_ref,
+    give_ref,
+    mine_ref,
+    proj_ref,
+    range_ref,
+    rows_ref,
+    sem,
+):
+    fetch = [
+        pltpu.make_async_copy(range_hbm, range_ref, sem.at[0]),
+        pltpu.make_async_copy(proj_hbm, proj_ref, sem.at[1]),
+    ]
+    for copy in fetch:
+        copy.start()
+    for copy in fetch:
+        copy.wait()
     n_tilt, n_det, y_count = proj_ref.shape
-    depth = out_ref.shape[2]
+    depth = home_ref.shape[1]
     y = lax.broadcasted_iota(jnp.int32, (n_det, y_count), 1)
     parts = []
     for t in range(n_tilt):
@@ -110,30 +131,42 @@
         parts.append(jnp.where(keep, proj_ref[t].astype(F32), 0.0))
     if depth > n_tilt * n_det:
         parts.append(jnp.zeros((depth - n_tilt * n_det, y_count), F32))
-    xt = jnp.concatenate(parts, 0).T
-    for b in range(n_block):
-        low, top = b * EDGE - HALO, b * EDGE - HALO + LEN
-        part = xt[max(low, 0) : min(top, y_count)]
-        if low < 0:
-            part = jnp.concatenate([jnp.zeros((-low, depth), F32), part], 0)
-        if top > y_count:
-            part = jnp.concatenate([part, jnp.zeros((top - y_count, depth), F32)], 0)
-        out_ref[b] = part.astype(BF)
+    edge = jnp.zeros((HALO, depth), F32)
+    rows_ref[...] = jnp.concatenate([edge, jnp.concatenate(parts, 0).T, edge], 0).astype(BF)
+    chip, core = at_ref[0], at_ref[1]
+
+    def rows(target):
+        return rows_ref[pl.ds(pl.multiple_of(target * EDGE, EDGE), LEN)]
+
+    home_ref[...] = rows(chip)
+    near_ref[...] = rows(chip ^ near_bit)
+    give_ref[0] = home_ref[...]
+    for j, mask in enumerate(masks):
+        mine_ref[j] = rows(chip ^ mask ^ (near_bit * core))
+        give_ref[1 + j] = rows(chip ^ mask ^ (near_bit * (1 - core)))
+
+
+def merge_kernel(mine_ref, got_ref, *out_refs):
+    for j, out_ref in enumerate(out_refs):
+        out_ref[0] = mine_ref[j]
+        out_ref[1] = got_ref[1 + j]
 
 
 def build_weights(n_det, n_tile, pairs, col, turns_ref, w_ref, p_ref):
-    depth = turns_ref.shape[0]
+    depth = p_ref.shape[0]
     lane = lax.broadcasted_iota(jnp.int32, (1, LB), 1)
     z = (lane % Z).astype(F32) - (Z - 1) / 2.0
     step = (lane // Z).astype(F32)
-    row = lax.broadcasted_iota(jnp.int32, (depth, 1), 0)
-    own = (row % n_det).astype(F32)
+    own = lax.broadcasted_iota(jnp.int32, (n_det, LB), 0).astype(F32)
+    if depth > NTILT * n_det:
+        p_ref[NTILT * n_det :] = jnp.zeros((depth - NTILT * n_det, LB), F32)
     base = 0
     for q, sources in enumerate(pairs):
         block = jnp.where(col == 0, q, NQ - 1 - q) * XB + col * (X - XR)
         x = step + (block.astype(F32) - (X - 1) / 2.0)
-        pos = VOXEL * (x * turns_ref[:, 0:1] + z * turns_ref[:, 1:2])
-        p_ref[...] = pos + ((NDET - 1) / 2.0 - own)
+        for t in range(NTILT):
+            pos = VOXEL * (x * turns_ref[0, t] + z * turns_ref[1, t])
+            p_ref[t * n_det : (t + 1) * n_det] = pos + ((NDET - 1) / 2.0 - own)
 
         def build(j, carry, base=base, first=sources[0]):
             src = first + j
@@ -189,69 +222,73 @@
     n_det,
     n_tile,
     pairs,
-    col_ref,
-    rot_ref,
-    turns_ref,
-    bank_ref,
-    fx_ref,
-    fz_ref,
-    ix_ref,
-    iz_ref,
-    line_ref,
-    turn_ref,
+    at_ref,
+    rot_hbm,
+    turns_hbm,
+    bank_hbm,
+    fx_hbm,
+    fz_hbm,
+    ix_hbm,
+    iz_hbm,
+    line_hbm,
+    turn_hbm,
     w_ref,
     plane_ref,
     inverse_ref,
     tmpl_ref,
     done_ref,
     p_ref,
+    rot_ref,
+    turns_ref,
+    *rest,
 ):
-    col = col_ref[0]
+    *buffers, sem = rest
+    sources = (turns_hbm, rot_hbm, bank_hbm, fx_hbm, fz_hbm, ix_hbm, iz_hbm, line_hbm, turn_hbm)
+    targets = (turns_ref, rot_ref, *buffers)
+    fetch = [
+        pltpu.make_async_copy(a, b, sem.at[i]) for i, (a, b) in enumerate(zip(sources, targets))
+    ]
+    for copy in fetch:
+        copy.start()
+    fetch[0].wait()
+    col = at_ref[1]
+    build_weights(n_det, n_tile, pairs, col, turns_ref, w_ref, p_ref)
+    for copy in fetch[1:]:
+        copy.wait()
+    bank_ref, fx_ref, fz_ref, ix_ref, iz_ref, line_ref, turn_ref = buffers
     build_planes(fx_ref, fz_ref, ix_ref, iz_ref, plane_ref, inverse_ref)
-    build_weights(n_det, n_tile, pairs, col, turns_ref, w_ref, p_ref)
     build_templates(col, rot_ref, bank_ref, plane_ref, line_ref, turn_ref, tmpl_ref)
     done_ref[...] = jnp.zeros_like(done_ref)
 
 
-def partial_sums(n_block, pairs, parity, col, data_ref, w_ref):
+def score_kernel(near_bit, masks, pairs, n_tile, *refs):
+    n_op = len(masks)
+    at_ref, home_ref, got_ref, near_ref, near_swap_ref = refs[:5]
+    recv_refs, swap_refs = refs[5 : 5 + n_op], refs[5 + n_op : 5 + 2 * n_op]
+    w_ref, tmpl_ref, plane_ref, line_ref, back_ref, inverse_ref = refs[5 + 2 * n_op : 11 + 2 * n_op]
+    _, out_ref, data_ref, vol_ref, mid_ref = refs[11 + 2 * n_op :]
+    chip, core = at_ref[0], at_ref[1]
+    mate = 1 - core
+    data_ref[chip * XT + core] = home_ref[...]
+    data_ref[chip * XT + mate] = got_ref[0]
+    data_ref[(chip ^ near_bit) * XT + core] = near_ref[...]
+    data_ref[(chip ^ near_bit) * XT + mate] = near_swap_ref[...]
+    for j, mask in enumerate(masks):
+        here = (chip ^ mask ^ (near_bit * core)) * XT
+        there = (chip ^ mask ^ (near_bit * mate)) * XT
+        data_ref[here + core] = recv_refs[j][0]
+        data_ref[here + mate] = recv_refs[j][1]
+        data_ref[there + mate] = swap_refs[j][0]
+        data_ref[there + core] = swap_refs[j][1]
     base = 0
-    for sources in pairs:
+    for q, sources in enumerate(pairs):
         total = jnp.zeros((LEN, LB), F32)
         for j, src in enumerate(sources):
-            if src % 2 == parity:
-                chip = jnp.where(col == 0, src // 2, n_block - 1 - src // 2)
-                total += jnp.dot(data_ref[chip], w_ref[base + j], preferred_element_type=F32)
+            part = data_ref[jnp.where(core == 0, src, n_tile - 1 - src)]
+            total += jnp.dot(part, w_ref[base + j], preferred_element_type=F32)
         base += len(sources)
-        yield total
-
-
-def half_kernel(n_block, pairs, col_ref, done_ref, own_ref, w_ref, out_ref):
-    del done_ref
-    for q, total in enumerate(partial_sums(n_block, pairs, 0, col_ref[0], own_ref, w_ref)):
-        out_ref[q] = total
-
-
-def score_kernel(
-    n_block,
-    pairs,
-    col_ref,
-    half_ref,
-    other_ref,
-    w_ref,
-    tmpl_ref,
-    plane_ref,
-    line_ref,
-    back_ref,
-    inverse_ref,
-    out_ref,
-    vol_ref,
-    mid_ref,
-):
-    col = col_ref[0]
-    for q, total in enumerate(partial_sums(n_block, pairs, 1, col, other_ref, w_ref)):
-        block = jnp.where(col == 0, q, NQ - 1 - q)
-        at = pl.ds(pl.multiple_of(block * LB, LB), LB)
-        vol_ref[:, at] = (total + half_ref[q]).astype(BF)
+        block = jnp.where(core == 0, q, NQ - 1 - q)
+        vol_ref[:, pl.ds(pl.multiple_of(block * LB, LB), LB)] = total.astype(BF)
     flat = jnp.dot(vol_ref[...], plane_ref[...], preferred_element_type=F32).astype(BF)
     stacked = jnp.concatenate([flat[:, :FP], flat[:, FP:]], 0)
     full = jnp.dot(line_ref[...], stacked, preferred_element_type=F32)
@@ -278,6 +315,7 @@
 
 VMEM = pl.BlockSpec(memory_space=pltpu.VMEM)
 SMEM = pl.BlockSpec(memory_space=pltpu.SMEM)
+HBM = pl.BlockSpec(memory_space=pltpu.HBM)
 
 
 def limit(mib):
@@ -286,94 +324,132 @@
 
 def cost(flops, nbytes):
     return pl.CostEstimate(flops=flops, bytes_accessed=nbytes, transcendentals=0)
+
+
+def shape(*dims, dtype=BF):
+    return jax.ShapeDtypeStruct(dims, dtype)
 
 
 def solution(mesh):
     n_tile = mesh.shape["tile"]
     n_block = n_tile // XT
     n_det = NDET // n_tile
-    rows = NTILT * n_det
-    depth = (rows + 127) // 128 * 128
+    depth = (NTILT * n_det + 127) // 128 * 128
+    near_bit = 2
+    masks = [k for k in range(1, n_block) if not k & near_bit]
+    n_op = len(masks)
     pairs = pair_list(n_det)
     n_pair = sum(len(p) for p in pairs)
     tables = plane_tables()
     line, line_t, back = line_tables()
+    mate = [(i, i ^ 1) for i in range(n_tile)]
+    near_pairs = [(i, i ^ (near_bit * XT)) for i in range(n_tile)]
+
+    def route(mask):
+        return [(i, i ^ (mask * XT) ^ (near_bit * XT * (i % XT))) for i in range(n_tile)]
 
     def local(projections, tilt_angle, row_range, template_bank, rot_index):
-        col = lax.axis_index("core").astype(jnp.int32).reshape(1)
+        y_count = projections.shape[0]
+        position = lax.axis_index("tile").astype(jnp.int32)
+        at = jnp.stack([position // XT, position % XT])
         by_y = jnp.transpose(projections, (1, 2, 0))
-        send = pl.pallas_call(
-            lambda *refs: pack_kernel(n_block, *refs),
-            out_shape=jax.ShapeDtypeStruct((n_block, LEN, depth), BF),
-            in_specs=[SMEM, VMEM],
-            out_specs=VMEM,
-            compiler_params=limit(4),
-        )(row_range.T, by_y)
-        own = lax.all_to_all(send, "chip", 0, 0, tiled=True)
-        turns = jnp.stack([jnp.cos(tilt_angle), jnp.sin(tilt_angle)], 1)
-        turns = jnp.pad(jnp.repeat(turns, n_det, axis=0), ((0, depth - rows), (0, 0)))
+        home, near, give, mine = pl.pallas_call(
+            lambda *refs: pack_kernel(near_bit, masks, *refs),
+            out_shape=(
+                shape(LEN, depth),
+                shape(LEN, depth),
+                shape(1 + n_op, LEN, depth),
+                shape(n_op, LEN, depth),
+            ),
+            in_specs=[SMEM, HBM, HBM],
+            out_specs=(VMEM,) * 4,
+            scratch_shapes=[
+                pltpu.VMEM(by_y.shape, BF),
+                pltpu.SMEM((2, NTILT), jnp.int32),
+                pltpu.VMEM((y_count + 2 * HALO, depth), BF),
+                pltpu.SemaphoreType.DMA((2,)),
+            ],
+            compiler_params=limit(8),
+        )(at, row_range.T, by_y)
+        got = lax.ppermute(give, "tile", mate)
+        near_in = lax.ppermute(near, "tile", near_pairs)
+        payload = pl.pallas_call(
+            merge_kernel,
+            out_shape=(shape(2, LEN, depth),) * n_op,
+            in_specs=[VMEM, VMEM],
+            out_specs=(VMEM,) * n_op,
+            compiler_params=limit(8),
+        )(mine, got)
+        arrived = [lax.ppermute(p, "tile", route(m)) for p, m in zip(payload, masks)]
+        turns = jnp.stack([jnp.cos(tilt_angle), jnp.sin(tilt_angle)])
         weights, plane, inverse, spectra, done = pl.pallas_call(
             lambda *refs: prepare_kernel(n_det, n_tile, pairs, *refs),
             out_shape=(
-                jax.ShapeDtypeStruct((n_pair, depth, LB), BF),
-                jax.ShapeDtypeStruct((XR * Z, 2 * FP), BF),
-                jax.ShapeDtypeStruct((2 * FP, EDGE * EDGE), BF),
-                jax.ShapeDtypeStruct((NTPL, 2 * LEN, FP), BF),
-                jax.ShapeDtypeStruct((8, 128), F32),
+                shape(n_pair, depth, LB),
+                shape(XR * Z, 2 * FP),
+                shape(2 * FP, EDGE * EDGE),
+                shape(NTPL, 2 * LEN, FP),
+                shape(8, 128, dtype=F32),
             ),
-            in_specs=[SMEM, SMEM] + [VMEM] * 8,
+            in_specs=[SMEM] + [HBM] * 9,
             out_specs=(VMEM,) * 5,
-            scratch_shapes=[pltpu.VMEM((depth, LB), F32)],
+            scratch_shapes=[
+                pltpu.VMEM((depth, LB), F32),
+                pltpu.SMEM((NTPL,), jnp.int32),
+                pltpu.SMEM((2, NTILT), F32),
+                pltpu.VMEM(template_bank.shape, BF),
+                *[pltpu.VMEM(t.shape, F32) for t in tables[:4]],
+                pltpu.VMEM(line_t.shape, BF),
+                pltpu.VMEM(tables[4].shape, F32),
+                pltpu.SemaphoreType.DMA((9,)),
+            ],
             compiler_params=limit(28),
             cost_estimate=cost(1 << 32, 24 << 20),
         )(
-            col,
+            at,
             rot_index,
             turns,
             template_bank,
-            *[jnp.asarray(t) for t in tables[:4]],
+            *[jnp.asarray(t, F32) for t in tables[:4]],
             jnp.asarray(line_t),
-            jnp.asarray(tables[4]),
+            jnp.asarray(tables[4], F32),
         )
-        own, done = lax.optimization_barrier((own, done))
-        other = lax.ppermute(own, "core", [(0, 1), (1, 0)])
-        half = pl.pallas_call(
-            lambda *refs: half_kernel(n_block, pairs, *refs),
-            out_shape=jax.ShapeDtypeStruct((NQ, LEN, LB), F32),
-            in_specs=[SMEM, VMEM, VMEM, VMEM],
-            out_specs=VMEM,
-            compiler_params=limit(16),
-            cost_estimate=cost(n_pair * LEN * depth * LB, n_pair * depth * LB),
-        )(col, done, own, weights)
+        near_in, done, *arrived = lax.optimization_barrier((near_in, done, *arrived))
+        near_swap = lax.ppermute(near_in, "tile", mate)
+        swapped = [lax.ppermute(a, "tile", mate) for a in arrived]
         return pl.pallas_call(
-            lambda *refs: score_kernel(n_block, pairs, *refs),
-            out_shape=jax.ShapeDtypeStruct((1, EDGE, EDGE * Z), F32),
-            in_specs=[SMEM] + [VMEM] * 8,
+            lambda *refs: score_kernel(near_bit, masks, pairs, n_tile, *refs),
+            out_shape=shape(1, EDGE, EDGE * Z, dtype=F32),
+            in_specs=[SMEM] + [VMEM] * (11 + 2 * n_op),
             out_specs=VMEM,
             scratch_shapes=[
+                pltpu.VMEM((n_tile, LEN, depth), BF),
                 pltpu.VMEM((LEN, XR * Z), BF),
                 pltpu.VMEM((NTPL * EDGE, 2 * FP), BF),
             ],
             compiler_params=limit(28),
             cost_estimate=cost(4 << 30, 20 << 20),
         )(
-            col,
-            half,
-            other,
+            at,
+            home,
+            got,
+            near_in,
+            near_swap,
+            *arrived,
+            *swapped,
             weights,
             spectra,
             plane,
             jnp.asarray(line),
             jnp.asarray(back),
             inverse,
+            done,
         )
 
-    tile = ("chip", "core")
-    split = Mesh(mesh.devices.reshape(-1, n_block, XT), ("grp",) + tile)
     return jax.shard_map(
         local,
-        mesh=split,
-        in_specs=(P("grp", None, tile), P("grp"), P("grp", None), P(), P()),
-        out_specs=P(tile, "grp", None),
+        mesh=mesh,
+        in_specs=(P("grp", None, "tile"), P("grp"), P("grp", None), P(), P()),
+        out_specs=P("tile", "grp", None),
         check_vma=False,
     )

time: 51.5 us -> 36.1 us (0.70)
  local copies, waits for them, and re-layouts: 28.1 us -> 9.33 us
  starting transfers between devices: 7.34 us -> 8.75 us
  waiting for transfers between devices: 0.01 us -> 1.38 us
  Pallas kernels: 15.2 us -> 15.8 us
    unnamed x38 -> x24, local copies, waits for them, and re-layouts: 27.2 us -> 8.64 us
    ppermute x1 -> x9, starting transfers between devices: 0.96 us -> 8.75 us  [the longest x3 4.52 us: local(): lax.ppermute(p, 'tile', route(m))]
    all_to_all x1 -> x0, starting transfers between devices: 6.38 us -> none  [local(): own = lax.all_to_all(send, 'chip', 0, 0, tiled=True)]
    ppermute x1 -> x9, waiting for transfers between devices: 0.01 us -> 1.38 us  [the longest x1 1 us: local(): near_swap = lax.ppermute(near_in, 'tile', mate)]
  transfers between devices with their start and end apart: 2 -> 9, of which waited for: 0 -> 2; matrix products, arithmetic and copies ran while one was open for 2% -> 2% of each run, Pallas kernels for 18% -> 24%
where the time goes in v3:
time: 36.1 us; the launch traced here: 35.5 us
  Pallas kernels  15.8 us (44%)
  local copies, waits for them, and re-layouts  9.33 us (26%)
  starting transfers between devices  8.75 us (24%)
  waiting for transfers between devices  1.38 us (4%)
    unnamed x24, local copies, waits for them, and re-layouts  8.64 us
    pallas_call x1, Pallas kernels, local(): pl.pallas_call(lambda *refs: prepare_kernel(n_det, n_tile, pairs, *refs),...  8.47 us
    pallas_call x1, Pallas kernels, local(): pl.pallas_call(lambda *refs: score_kernel(near_bit, masks, pairs, n_tile,...  6.03 us
    ppermute x3, starting transfers between devices, local(): lax.ppermute(p, 'tile', route(m))  4.52 us
    ppermute x1, starting transfers between devices, local(): near_in = lax.ppermute(near, 'tile', near_pairs)  2.19 us
    pallas_call x1, Pallas kernels, local(): pl.pallas_call(lambda *refs: pack_kernel(near_bit, masks, *refs), out_sha...  1.31 us
    ppermute x1, waiting for transfers between devices, local(): near_swap = lax.ppermute(near_in, 'tile', mate)  1 us
    ppermute x1, starting transfers between devices, local(): got = lax.ppermute(give, 'tile', mate)  0.96 us
  transfers between devices with their start and end apart: 9, of which 2 were waited for; matrix products, arithmetic and copies ran while one was open for 2% of the time, Pallas kernels for 24%

profile of v3, /device:TPU:1, one launch (start us, length us, event | category | flops | bytes accessed | tf_op | source)
XLA Modules:
  0.0 35.5 jit_solution(16677363371183435670)
XLA Ops:
  0.1 0.9 %copy-done = bf16[256,61,8]{0,2,1:T(8,128)(2,1)S(1)} copy-done((bf16[256,61,8]{0,2,1:T(8,128)(2,1)S(1)}, bf16[256,61,8]{0,2,1:T(8,128)(2,1)}, u32[]{:S(2)}) %copy-start) | copy-done | bytes 249880
  1.0 0.7 %copy-done.3 = s32[61,2]{0,1:T(2,128)S(1)} copy-done((s32[61,2]{0,1:T(2,128)S(1)}, s32[61,2]{0,1:T(2,128)}, u32[]{:S(2)}) %copy-start.3) | copy-done | bytes 512
  1.7 1.3 %shard_map.127 = (bf16[48,512]{1,0:T(8,128)(2,1)S(1)}, bf16[48,512]{1,0:T(8,128)(2,1)S(1)}, bf16[4,48,512]{2,1,0:T(8,128)(2,1)S(1)}, bf16[3,48,512]{2,1,0:T(8,128)(2,1)S(1)}) custom-call(s32[2]{0:T(128)S(1)} %pad_add_fusion.refs_0_, s32[2,61]{1,0:T(2,128)S(1)} %bitcast.9, bf16[61,8,256]{2,1,0:T(8,128)(2,1)S(1)} %bitcast.8), custom_call_target="tpu_custom_call" | custom-call | tf_op jit(solution)/shard_map/pallas_call | solution.py:356
  3.0 2.2 %collective-permute-start.1 = (bf16[48,512]{1,0:T(8,128)(2,1)S(1)}, bf16[48,512]{1,0:T(8,128)(2,1)S(1)}, u32[]{:S(2)}, u32[]{:S(2)}) collective-permute-start(bf16[48,512]{1,0:T(8,128)(2,1)S(1)} %get-tuple-element.24), channel_id=1, source_target_pairs={{0,4},{1,5},{2,6},{3,7},{4,0},{5,1},{6,2},{7,3},{8,12},{9,13},{10,... | collective-permute-start | bytes 147464 | tf_op jit(solution)/shard_map/ppermute | solution.py:375
  5.2 1.0 %collective-permute-start = (bf16[4,48,512]{2,1,0:T(8,128)(2,1)S(1)}, bf16[4,48,512]{2,1,0:T(8,128)(2,1)S(1)}, u32[]{:S(2)}, u32[]{:S(2)}) collective-permute-start(bf16[4,48,512]{2,1,0:T(8,128)(2,1)S(1)} %get-tuple-element.23), channel_id=1, source_target_pairs={{0,1},{1,0},{2,3},{3,2},{4,5},{5,4},{6,7},{7,6},{8,9},{9,8},{10,11... | collective-permute-start | bytes 589832 | tf_op jit(solution)/shard_map/ppermute | solution.py:374
  6.2 0.7 %cosine_bitcast_fusion = (f32[1,61]{1,0:T(1,128)S(1)}, f32[1,61]{1,0:T(1,128)S(1)}) fusion(f32[61]{0:T(128)} %param.14), kind=kLoop, calls=%fused_computation.3 | loop fusion | bytes 732 | tf_op jit(solution)/shard_map/stack | solution.py:384
  6.9 0.4 %collective-permute-done.got_ref.refs_2_ = bf16[4,48,512]{2,1,0:T(8,128)(2,1)S(1)} collective-permute-done((bf16[4,48,512]{2,1,0:T(8,128)(2,1)S(1)}, bf16[4,48,512]{2,1,0:T(8,128)(2,1)S(1)}, u32[]{:S(2)}, u32[]{:S(2)}) %collective-permute-start) | collective-permute-done | bytes 196640 | tf_op jit(solution)/shard_map/ppermute | solution.py:374
  7.3 1.2 %collective-permute-start.2 = (bf16[2,48,512]{2,1,0:T(8,128)(2,1)S(1)}, bf16[2,48,512]{2,1,0:T(8,128)(2,1)S(1)}, u32[]{:S(2)}, u32[]{:S(2)}) collective-permute-start(bf16[2,48,512]{2,1,0:T(8,128)(2,1)S(1)} %get-tuple-element.27), channel_id=1, source_target_pairs={{0,2},{1,7},{2,0},{3,5},{4,6},{5,3},{6,4},{7,1},{8,10},{9,15},{10,... | collective-permute-start | bytes 294920 | tf_op jit(solution)/shard_map/ppermute | solution.py:383
  8.5 3.3 %collective-permute-start.3 = (bf16[2,48,512]{2,1,0:T(8,128)(2,1)S(1)}, bf16[2,48,512]{2,1,0:T(8,128)(2,1)S(1)}, u32[]{:S(2)}, u32[]{:S(2)}) collective-permute-start(bf16[2,48,512]{2,1,0:T(8,128)(2,1)S(1)} %get-tuple-element.28), channel_id=1, source_target_pairs={{0,8},{1,13},{2,10},{3,15},{4,12},{5,9},{6,14},{7,11},{8,0},{9,5},... | collective-permute-start | bytes 294920 | tf_op jit(solution)/shard_map/ppermute | solution.py:383
  11.8 1.1 %copy-done.4 = bf16[64,16,256]{2,1,0:T(8,128)(2,1)S(1)} copy-done((bf16[64,16,256]{2,1,0:T(8,128)(2,1)S(1)}, bf16[64,16,256]{2,1,0:T(8,128)(2,1)}, u32[]{:S(2)}) %copy-start.4) | copy-done | bytes 524312
  12.9 0.7 %copy-done.5 = s32[8]{0:T(128)S(1)} copy-done((s32[8]{0:T(128)S(1)}, s32[8]{0:T(128)}, u32[]{:S(2)}) %copy-start.5) | copy-done | bytes 56
  13.5 1.0 %copy-done.6 = f32[2,48,1024]{2,1,0:T(8,128)S(1)} copy-done((f32[2,48,1024]{2,1,0:T(8,128)S(1)}, f32[2,48,1024]{2,1,0:T(8,128)}, u32[]{:S(2)}) %copy-start.6) | copy-done | bytes 393240
  14.5 1.0 %copy-done.7 = f32[2,40,1024]{2,1,0:T(8,128)S(1)} copy-done((f32[2,40,1024]{2,1,0:T(8,128)S(1)}, f32[2,40,1024]{2,1,0:T(8,128)}, u32[]{:S(2)}) %copy-start.7) | copy-done | bytes 327704
  15.5 0.9 %copy-done.8 = f32[2,32,1024]{2,1,0:T(8,128)S(1)} copy-done((f32[2,32,1024]{2,1,0:T(8,128)S(1)}, f32[2,32,1024]{2,1,0:T(8,128)}, u32[]{:S(2)}) %copy-start.8) | copy-done | bytes 262168
  16.4 0.9 %copy-done.9 = f32[2,21,1024]{2,1,0:T(8,128)S(1)} copy-done((f32[2,21,1024]{2,1,0:T(8,128)S(1)}, f32[2,21,1024]{2,1,0:T(8,128)}, u32[]{:S(2)}) %copy-start.9) | copy-done | bytes 172056
  17.4 0.7 %copy-done.10 = bf16[96,32]{1,0:T(8,128)(2,1)S(1)} copy-done((bf16[96,32]{1,0:T(8,128)(2,1)S(1)}, bf16[96,32]{1,0:T(8,128)(2,1)}, u32[]{:S(2)}) %copy-start.10) | copy-done | bytes 6168
  18.1 0.7 %copy-done.11 = f32[2,2,1024]{2,1,0:T(2,128)S(1)} copy-done((f32[2,2,1024]{2,1,0:T(2,128)S(1)}, f32[2,2,1024]{2,1,0:T(2,128)}, u32[]{:S(2)}) %copy-start.11) | copy-done | bytes 16408
  18.8 8.5 %shard_map.128 = (bf16[34,512,256]{2,1,0:T(8,128)(2,1)S(1)}, bf16[1280,2048]{1,0:T(8,128)(2,1)S(1)}, bf16[2048,1024]{1,0:T(8,128)(2,1)S(1)}, bf16[8,96,1024]{2,1,0:T(8,128)(2,1)S(1)}, f32[8,128]{1,0:T(8,128)S(1)}) custom-call(s32[2]{0:T(128)S(1)} %pad_add_fusion.refs_0_, s32[8]{0:T(128)S(1)} %copy-done.5, f32[2,61]{1,0:T(2,128)S(1)} %pad_maximum_fusion.refs_2_, ...), custom_call_target="tpu_custom_call" | custom-call | flops 4294967296 | bytes 25165824 | tf_op jit(solution)/shard_map/pallas_call | solution.py:385
  27.3 0.3 collective-permute-start.6
  27.7 0.2 collective-permute-start.7
  27.9 0.3 collective-permute-start.8
  28.2 0.2 collective-permute-start.5
  28.4 1.0 %collective-permute-done.5.refs_4_ = bf16[48,512]{1,0:T(8,128)(2,1)S(1)} collective-permute-done((bf16[48,512]{1,0:T(8,128)(2,1)S(1)}, bf16[48,512]{1,0:T(8,128)(2,1)S(1)}, u32[]{:S(2)}, u32[]{:S(2)}) %collective-permute-start.5) | collective-permute-done | bytes 49184 | tf_op jit(solution)/shard_map/ppermute | solution.py:418
  29.5 6.0 %shard_map.130 = f32[1,32,1024]{2,1,0:T(8,128)} custom-call(s32[2]{0:T(128)S(1)} %pad_add_fusion.refs_0_, bf16[48,512]{1,0:T(8,128)(2,1)S(1)} %get-tuple-element.22.refs_1_, bf16[4,48,512]{2,1,0:T(8,128)(2,1)S(1)} %collective-permute-done.got_ref.refs_2_, bf16[48,512]{1,0:T(8,128)(2,1)S(1)} %collective-permute-done.1.refs_3_, ...), custom_call_target="tpu_custom_call" | custom-call | flops 4294967296 | bytes 20971520 | tf_op jit(solution)/shard_map/pallas_call | solution.py:420
  (25 shorter events, 0.2 us)
Async XLA Ops:
  0.1 0.9 %copy-start = (bf16[256,61,8]{0,2,1:T(8,128)(2,1)S(1)}, bf16[256,61,8]{0,2,1:T(8,128)(2,1)}, u32[]{:S(2)}) copy-start(bf16[256,61,8]{0,2,1:T(8,128)(2,1)} %param.13) | copy-start | bytes 749572
  1.0 0.7 %copy-start.3 = (s32[61,2]{0,1:T(2,128)S(1)}, s32[61,2]{0,1:T(2,128)}, u32[]{:S(2)}) copy-start(s32[61,2]{0,1:T(2,128)} %param.15) | copy-start | bytes 1468
  3.0 24.3 %collective-permute-start.1 = (bf16[48,512]{1,0:T(8,128)(2,1)S(1)}, bf16[48,512]{1,0:T(8,128)(2,1)S(1)}, u32[]{:S(2)}, u32[]{:S(2)}) collective-permute-start(bf16[48,512]{1,0:T(8,128)(2,1)S(1)} %get-tuple-element.24), channel_id=1, source_target_pairs={{0,4},{1,5},{2,6},{3,7},{4,0},{5,1},{6,2},{7,3},{8,12},{9,13},{10,... | collective-permute-start | bytes 147464 | tf_op jit(solution)/shard_map/ppermute | solution.py:375
  5.2 2.0 %collective-permute-start = (bf16[4,48,512]{2,1,0:T(8,128)(2,1)S(1)}, bf16[4,48,512]{2,1,0:T(8,128)(2,1)S(1)}, u32[]{:S(2)}, u32[]{:S(2)}) collective-permute-start(bf16[4,48,512]{2,1,0:T(8,128)(2,1)S(1)} %get-tuple-element.23), channel_id=1, source_target_pairs={{0,1},{1,0},{2,3},{3,2},{4,5},{5,4},{6,7},{7,6},{8,9},{9,8},{10,11... | collective-permute-start | bytes 589832 | tf_op jit(solution)/shard_map/ppermute | solution.py:374
  7.3 20.0 %collective-permute-start.2 = (bf16[2,48,512]{2,1,0:T(8,128)(2,1)S(1)}, bf16[2,48,512]{2,1,0:T(8,128)(2,1)S(1)}, u32[]{:S(2)}, u32[]{:S(2)}) collective-permute-start(bf16[2,48,512]{2,1,0:T(8,128)(2,1)S(1)} %get-tuple-element.27), channel_id=1, source_target_pairs={{0,2},{1,7},{2,0},{3,5},{4,6},{5,3},{6,4},{7,1},{8,10},{9,15},{10,... | collective-permute-start | bytes 294920 | tf_op jit(solution)/shard_map/ppermute | solution.py:383
  8.5 18.9 %collective-permute-start.3 = (bf16[2,48,512]{2,1,0:T(8,128)(2,1)S(1)}, bf16[2,48,512]{2,1,0:T(8,128)(2,1)S(1)}, u32[]{:S(2)}, u32[]{:S(2)}) collective-permute-start(bf16[2,48,512]{2,1,0:T(8,128)(2,1)S(1)} %get-tuple-element.28), channel_id=1, source_target_pairs={{0,8},{1,13},{2,10},{3,15},{4,12},{5,9},{6,14},{7,11},{8,0},{9,5},... | collective-permute-start | bytes 294920 | tf_op jit(solution)/shard_map/ppermute | solution.py:383
  11.8 17.7 %copy-start.1 = (bf16[96,96]{1,0:T(8,128)(2,1)S(1)}, bf16[96,96]{1,0:T(8,128)(2,1)}, u32[]{:S(2)}) copy-start(bf16[96,96]{1,0:T(8,128)(2,1)} %constant.50.clone.refs_14_) | copy-start | bytes 55300
  11.8 17.7 %copy-start.2 = (bf16[64,96]{1,0:T(8,128)(2,1)S(1)}, bf16[64,96]{1,0:T(8,128)(2,1)}, u32[]{:S(2)}) copy-start(bf16[64,96]{1,0:T(8,128)(2,1)} %constant.51.clone.refs_15_) | copy-start | bytes 36868
  11.8 15.5 %collective-permute-start.4 = (bf16[2,48,512]{2,1,0:T(8,128)(2,1)S(1)}, bf16[2,48,512]{2,1,0:T(8,128)(2,1)S(1)}, u32[]{:S(2)}, u32[]{:S(2)}) collective-permute-start(bf16[2,48,512]{2,1,0:T(8,128)(2,1)S(1)} %get-tuple-element.29), channel_id=1, source_target_pairs={{0,10},{1,15},{2,8},{3,13},{4,14},{5,11},{6,12},{7,9},{8,2},{9,7},... | collective-permute-start | bytes 294920 | tf_op jit(solution)/shard_map/ppermute | solution.py:383
  11.8 1.1 %copy-start.4 = (bf16[64,16,256]{2,1,0:T(8,128)(2,1)S(1)}, bf16[64,16,256]{2,1,0:T(8,128)(2,1)}, u32[]{:S(2)}) copy-start(bf16[64,16,256]{2,1,0:T(8,128)(2,1)} %refs_3_.1) | copy-start | bytes 1572868
  12.9 0.7 %copy-start.5 = (s32[8]{0:T(128)S(1)}, s32[8]{0:T(128)}, u32[]{:S(2)}) copy-start(s32[8]{0:T(128)} %refs_1_.1) | copy-start | bytes 100
  13.5 1.0 %copy-start.6 = (f32[2,48,1024]{2,1,0:T(8,128)S(1)}, f32[2,48,1024]{2,1,0:T(8,128)}, u32[]{:S(2)}) copy-start(f32[2,48,1024]{2,1,0:T(8,128)} %constant.46.clone.refs_6_) | copy-start | bytes 1179652
  14.5 1.0 %copy-start.7 = (f32[2,40,1024]{2,1,0:T(8,128)S(1)}, f32[2,40,1024]{2,1,0:T(8,128)}, u32[]{:S(2)}) copy-start(f32[2,40,1024]{2,1,0:T(8,128)} %constant.44.clone.refs_4_) | copy-start | bytes 983044
  15.5 0.9 %copy-start.8 = (f32[2,32,1024]{2,1,0:T(8,128)S(1)}, f32[2,32,1024]{2,1,0:T(8,128)}, u32[]{:S(2)}) copy-start(f32[2,32,1024]{2,1,0:T(8,128)} %constant.45.clone.refs_5_) | copy-start | bytes 786436
  16.4 0.9 %copy-start.9 = (f32[2,21,1024]{2,1,0:T(8,128)S(1)}, f32[2,21,1024]{2,1,0:T(8,128)}, u32[]{:S(2)}) copy-start(f32[2,21,1024]{2,1,0:T(8,128)} %constant.47.clone.refs_7_) | copy-start | bytes 516100
  17.4 0.7 %copy-start.10 = (bf16[96,32]{1,0:T(8,128)(2,1)S(1)}, bf16[96,32]{1,0:T(8,128)(2,1)}, u32[]{:S(2)}) copy-start(bf16[96,32]{1,0:T(8,128)(2,1)} %constant.48.clone.refs_8_) | copy-start | bytes 18436
  18.1 0.7 %copy-start.11 = (f32[2,2,1024]{2,1,0:T(2,128)S(1)}, f32[2,2,1024]{2,1,0:T(2,128)}, u32[]{:S(2)}) copy-start(f32[2,2,1024]{2,1,0:T(2,128)} %constant.49.clone.refs_9_) | copy-start | bytes 49156
  27.3 2.1 %collective-permute-start.6 = (bf16[2,48,512]{2,1,0:T(8,128)(2,1)S(1)}, bf16[2,48,512]{2,1,0:T(8,128)(2,1)S(1)}, u32[]{:S(2)}, u32[]{:S(2)}) collective-permute-start(bf16[2,48,512]{2,1,0:T(8,128)(2,1)S(1)} %collective-permute-done.2.refs_5_), channel_id=1, source_target_pairs={{0,1},{1,0},{2,3},{3,2},{4,5},{5,4},{6,7},{7,6},{8,9},{9,8},{10,11... | collective-permute-start | bytes 294920 | tf_op jit(solution)/shard_map/ppermute | solution.py:419
  27.7 1.7 %collective-permute-start.7 = (bf16[2,48,512]{2,1,0:T(8,128)(2,1)S(1)}, bf16[2,48,512]{2,1,0:T(8,128)(2,1)S(1)}, u32[]{:S(2)}, u32[]{:S(2)}) collective-permute-start(bf16[2,48,512]{2,1,0:T(8,128)(2,1)S(1)} %collective-permute-done.3.refs_6_), channel_id=1, source_target_pairs={{0,1},{1,0},{2,3},{3,2},{4,5},{5,4},{6,7},{7,6},{8,9},{9,8},{10,11... | collective-permute-start | bytes 294920 | tf_op jit(solution)/shard_map/ppermute | solution.py:419
  27.9 1.5 %collective-permute-start.8 = (bf16[2,48,512]{2,1,0:T(8,128)(2,1)S(1)}, bf16[2,48,512]{2,1,0:T(8,128)(2,1)S(1)}, u32[]{:S(2)}, u32[]{:S(2)}) collective-permute-start(bf16[2,48,512]{2,1,0:T(8,128)(2,1)S(1)} %collective-permute-done.4.refs_7_), channel_id=1, source_target_pairs={{0,1},{1,0},{2,3},{3,2},{4,5},{5,4},{6,7},{7,6},{8,9},{9,8},{10,11... | collective-permute-start | bytes 294920 | tf_op jit(solution)/shard_map/ppermute | solution.py:419
  28.2 1.2 %collective-permute-start.5 = (bf16[48,512]{1,0:T(8,128)(2,1)S(1)}, bf16[48,512]{1,0:T(8,128)(2,1)S(1)}, u32[]{:S(2)}, u32[]{:S(2)}) collective-permute-start(bf16[48,512]{1,0:T(8,128)(2,1)S(1)} %collective-permute-done.1.refs_3_), channel_id=1, source_target_pairs={{0,1},{1,0},{2,3},{3,2},{4,5},{5,4},{6,7},{7,6},{8,9},{9,8},{10,11... | collective-permute-start | bytes 147464 | tf_op jit(solution)/shard_map/ppermute | solution.py:418

commit v4 on v3

--- a/solution.py
+++ b/solution.py
@@ -152,27 +152,41 @@
         out_ref[1] = got_ref[1 + j]
 
 
-def build_weights(n_det, n_tile, pairs, col, turns_ref, w_ref, p_ref):
-    depth = p_ref.shape[0]
+def build_weights(n_det, n_tile, pairs, col, turns_ref, w_ref, whole_ref, part_ref):
+    depth = whole_ref.shape[0]
     lane = lax.broadcasted_iota(jnp.int32, (1, LB), 1)
     z = (lane % Z).astype(F32) - (Z - 1) / 2.0
     step = (lane // Z).astype(F32)
+    pack = 16 // n_det
     own = lax.broadcasted_iota(jnp.int32, (n_det, LB), 0).astype(F32)
-    if depth > NTILT * n_det:
-        p_ref[NTILT * n_det :] = jnp.zeros((depth - NTILT * n_det, LB), F32)
+    top = NTILT // pack * pack
+    tail = depth - top * n_det
     base = 0
     for q, sources in enumerate(pairs):
         block = jnp.where(col == 0, q, NQ - 1 - q) * XB + col * (X - XR)
         x = step + (block.astype(F32) - (X - 1) / 2.0)
-        for t in range(NTILT):
-            pos = VOXEL * (x * turns_ref[0, t] + z * turns_ref[1, t])
-            p_ref[t * n_det : (t + 1) * n_det] = pos + ((NDET - 1) / 2.0 - own)
+
+        def tilt(t, z=z, x=x):
+            pos = VOXEL * (x * turns_ref[0, t] + z * turns_ref[1, t]) + (NDET - 1) / 2.0
+            whole = jnp.floor(pos)
+            return own - whole, jnp.broadcast_to(pos - whole, own.shape)
+
+        for first in range(0, NTILT, pack):
+            got = [tilt(t) for t in range(first, min(first + pack, NTILT))]
+            rows = pack * n_det if first < top else tail
+            gap = rows - len(got) * n_det
+            for ref, values in ((whole_ref, [g[0] for g in got]), (part_ref, [g[1] for g in got])):
+                if gap:
+                    values.append(jnp.zeros((gap, LB), F32))
+                ref[first * n_det : first * n_det + rows] = jnp.concatenate(values, 0).astype(BF)
 
         def build(j, carry, base=base, first=sources[0]):
             src = first + j
             src = jnp.where(col == 0, src, n_tile - 1 - src)
-            shift = (src * n_det).astype(F32)
-            w_ref[base + j] = jnp.maximum(0.0, 1.0 - jnp.abs(p_ref[...] - shift)).astype(BF)
+            shift = (src * n_det).astype(F32).astype(BF)
+            off = (whole_ref[...] + shift) - part_ref[...]
+            one = jnp.ones((), BF)
+            w_ref[base + j] = jnp.maximum(one - jnp.abs(off), jnp.zeros((), BF))
             return carry
 
         lax.fori_loop(0, len(sources), build, 0)
@@ -180,22 +194,35 @@
 
 
 def build_planes(fx_ref, fz_ref, ix_ref, iz_ref, plane_ref, inverse_ref):
-    def forward(x, carry):
+    mid = LEN // 2
+    flip = fx_ref[0, mid : mid + 1]
+
+    def forward(x, carry, both):
         cos_x, sin_x = fx_ref[0, pl.ds(x, 1)], fx_ref[1, pl.ds(x, 1)]
         cos_z, sin_z = fz_ref[0], fz_ref[1]
+        real = cos_x * cos_z - sin_x * sin_z
+        imag = -sin_x * cos_z - cos_x * sin_z
         at = pl.ds(pl.multiple_of(x * Z, Z), Z)
-        plane_ref[at, :FP] = (cos_x * cos_z - sin_x * sin_z).astype(BF)
-        plane_ref[at, FP:] = (-sin_x * cos_z - cos_x * sin_z).astype(BF)
+        plane_ref[at, :FP] = real.astype(BF)
+        plane_ref[at, FP:] = imag.astype(BF)
+        if both:
+            at = pl.ds(pl.multiple_of((x + mid) * Z, Z), Z)
+            plane_ref[at, :FP] = (real * flip).astype(BF)
+            plane_ref[at, FP:] = (imag * flip).astype(BF)
         return carry
 
-    lax.fori_loop(0, XR, forward, 0)
+    lax.fori_loop(0, XR - mid, lambda x, c: forward(x, c, True), 0)
+    lax.fori_loop(XR - mid, mid, lambda x, c: forward(x, c, False), 0)
+    turn = ix_ref[0, mid : mid + 1]
 
     def inverse(k, carry):
         cos_z, sin_z = iz_ref[0, pl.ds(k, 1)], iz_ref[1, pl.ds(k, 1)]
-        cos_x, sin_x = ix_ref[0], ix_ref[1]
+        cos_x, sin_x = ix_ref[0, :mid], ix_ref[1, :mid]
+        real = cos_x * cos_z - sin_x * sin_z
+        imag = -sin_x * cos_z - cos_x * sin_z
         low = pl.multiple_of(k * LEN, 16)
-        inverse_ref[pl.ds(low, LEN)] = (cos_x * cos_z - sin_x * sin_z).astype(BF)
-        inverse_ref[pl.ds(FP + low, LEN)] = (-sin_x * cos_z - cos_x * sin_z).astype(BF)
+        inverse_ref[pl.ds(low, LEN)] = jnp.concatenate([real, real * turn], 0).astype(BF)
+        inverse_ref[pl.ds(FP + low, LEN)] = jnp.concatenate([imag, imag * turn], 0).astype(BF)
         return carry
 
     lax.fori_loop(0, KZ, inverse, 0)
@@ -223,8 +250,8 @@
     n_tile,
     pairs,
     at_ref,
+    turns_hbm,
     rot_hbm,
-    turns_hbm,
     bank_hbm,
     fx_hbm,
     fz_hbm,
@@ -237,7 +264,8 @@
     inverse_ref,
     tmpl_ref,
     done_ref,
-    p_ref,
+    whole_ref,
+    part_ref,
     rot_ref,
     turns_ref,
     *rest,
@@ -252,7 +280,7 @@
         copy.start()
     fetch[0].wait()
     col = at_ref[1]
-    build_weights(n_det, n_tile, pairs, col, turns_ref, w_ref, p_ref)
+    build_weights(n_det, n_tile, pairs, col, turns_ref, w_ref, whole_ref, part_ref)
     for copy in fetch[1:]:
         copy.wait()
     bank_ref, fx_ref, fz_ref, ix_ref, iz_ref, line_ref, turn_ref = buffers
@@ -326,6 +354,10 @@
     return pl.CostEstimate(flops=flops, bytes_accessed=nbytes, transcendentals=0)
 
 
+def pinned(array):
+    return pltpu.with_memory_space_constraint(array, pltpu.HBM)
+
+
 def shape(*dims, dtype=BF):
     return jax.ShapeDtypeStruct(dims, dtype)
 
@@ -335,7 +367,7 @@
     n_block = n_tile // XT
     n_det = NDET // n_tile
     depth = (NTILT * n_det + 127) // 128 * 128
-    near_bit = 2
+    near_bit = n_block // 2
     masks = [k for k in range(1, n_block) if not k & near_bit]
     n_op = len(masks)
     pairs = pair_list(n_det)
@@ -370,7 +402,7 @@
                 pltpu.SemaphoreType.DMA((2,)),
             ],
             compiler_params=limit(8),
-        )(at, row_range.T, by_y)
+        )(at, pinned(row_range.T), pinned(by_y))
         got = lax.ppermute(give, "tile", mate)
         near_in = lax.ppermute(near, "tile", near_pairs)
         payload = pl.pallas_call(
@@ -394,7 +426,8 @@
             in_specs=[SMEM] + [HBM] * 9,
             out_specs=(VMEM,) * 5,
             scratch_shapes=[
-                pltpu.VMEM((depth, LB), F32),
+                pltpu.VMEM((depth, LB), BF),
+                pltpu.VMEM((depth, LB), BF),
                 pltpu.SMEM((NTPL,), jnp.int32),
                 pltpu.SMEM((2, NTILT), F32),
                 pltpu.VMEM(template_bank.shape, BF),
@@ -407,12 +440,17 @@
             cost_estimate=cost(1 << 32, 24 << 20),
         )(
             at,
-            rot_index,
-            turns,
-            template_bank,
-            *[jnp.asarray(t, F32) for t in tables[:4]],
-            jnp.asarray(line_t),
-            jnp.asarray(tables[4], F32),
+            *[
+                pinned(a)
+                for a in (
+                    turns,
+                    rot_index,
+                    template_bank,
+                    *[jnp.asarray(t, F32) for t in tables[:4]],
+                    jnp.asarray(line_t),
+                    jnp.asarray(tables[4], F32),
+                )
+            ],
         )
         near_in, done, *arrived = lax.optimization_barrier((near_in, done, *arrived))
         near_swap = lax.ppermute(near_in, "tile", mate)

time: 36.1 us -> 27.4 us (0.76)
  local copies, waits for them, and re-layouts: 9.33 us -> 0.7 us
  starting transfers between devices: 8.75 us -> 9.64 us
  Pallas kernels: 15.8 us -> 15 us
  other arithmetic: 0.09 us -> 0.65 us
  waiting for transfers between devices: 1.38 us -> 0.9 us
    unnamed x24 -> x4, local copies, waits for them, and re-layouts: 8.64 us -> 0.01 us
    pallas_call x1, Pallas kernels: 8.47 us -> 7.21 us  [local(): pl.pallas_call(lambda *refs: prepare_kernel(n_det, n_tile, pairs, *refs),...]
    ppermute x1, starting transfers between devices: 2.19 us -> 3.21 us  [local(): near_in = lax.ppermute(near, 'tile', near_pairs)]
    another operation x1, other arithmetic: 0.01 us -> 0.58 us  [local(): turns = jnp.stack([jnp.cos(tilt_angle), jnp.sin(tilt_angle)])]
    pallas_call x1, Pallas kernels: 1.31 us -> 1.71 us  [local(): pl.pallas_call(lambda *refs: pack_kernel(near_bit, masks, *refs), out_sha...]
  transfers between devices with their start and end apart: 9 -> 9, of which waited for: 2 -> 1; matrix products, arithmetic and copies ran while one was open for 2% -> 5% of each run, Pallas kernels for 24% -> 27%
where the time goes in v4:
time: 27.4 us; the launch traced here: 27 us
  Pallas kernels  15 us (55%)
  starting transfers between devices  9.64 us (35%)
  waiting for transfers between devices  0.9 us (3%)
  local copies, waits for them, and re-layouts  0.7 us (3%)
  other arithmetic  0.65 us (2%)
    pallas_call x1, Pallas kernels, local(): pl.pallas_call(lambda *refs: prepare_kernel(n_det, n_tile, pairs, *refs),...  7.21 us
    pallas_call x1, Pallas kernels, local(): pl.pallas_call(lambda *refs: score_kernel(near_bit, masks, pairs, n_tile,...  6.03 us
    ppermute x3, starting transfers between devices, local(): lax.ppermute(p, 'tile', route(m))  4.4 us
    ppermute x1, starting transfers between devices, local(): near_in = lax.ppermute(near, 'tile', near_pairs)  3.21 us
    pallas_call x1, Pallas kernels, local(): pl.pallas_call(lambda *refs: pack_kernel(near_bit, masks, *refs), out_sha...  1.71 us
    ppermute x1, starting transfers between devices, local(): got = lax.ppermute(give, 'tile', mate)  0.96 us
    ppermute x1, waiting for transfers between devices, local(): near_swap = lax.ppermute(near_in, 'tile', mate)  0.88 us
    another operation x1, local copies, waits for them, and re-layouts, local(): turns = jnp.stack([jnp.cos(tilt_angle), jnp.sin(tilt_angle)])  0.69 us
  transfers between devices with their start and end apart: 9, of which 1 were waited for; matrix products, arithmetic and copies ran while one was open for 5% of the time, Pallas kernels for 27%

profile of v4, /device:TPU:1, one launch (start us, length us, event | category | flops | bytes accessed | tf_op | source)
XLA Modules:
  0.0 27.0 jit_solution(12550430597256185898)
XLA Ops:
  0.0 0.1 pad_add_fusion.refs_0_
  0.1 1.7 %shard_map.127 = (bf16[48,512]{1,0:T(8,128)(2,1)S(1)}, bf16[48,512]{1,0:T(8,128)(2,1)S(1)}, bf16[4,48,512]{2,1,0:T(8,128)(2,1)S(1)}, bf16[3,48,512]{2,1,0:T(8,128)(2,1)S(1)}) custom-call(s32[2]{0:T(128)S(1)} %pad_add_fusion.refs_0_, s32[2,61]{1,0:T(2,128)} %bitcast.9, bf16[61,8,256]{2,1,0:T(8,128)(2,1)} %bitcast.8), custom_call_target="tpu_custom_call" | custom-call | tf_op jit(solution)/shard_map/pallas_call | solution.py:388
  1.8 3.2 %collective-permute-start.1 = (bf16[48,512]{1,0:T(8,128)(2,1)S(1)}, bf16[48,512]{1,0:T(8,128)(2,1)S(1)}, u32[]{:S(2)}, u32[]{:S(2)}) collective-permute-start(bf16[48,512]{1,0:T(8,128)(2,1)S(1)} %get-tuple-element.24), channel_id=1, source_target_pairs={{0,8},{1,9},{2,10},{3,11},{4,12},{5,13},{6,14},{7,15},{8,0},{9,1},... | collective-permute-start | bytes 147464 | tf_op jit(solution)/shard_map/ppermute | solution.py:407
  5.0 1.0 %collective-permute-start = (bf16[4,48,512]{2,1,0:T(8,128)(2,1)S(1)}, bf16[4,48,512]{2,1,0:T(8,128)(2,1)S(1)}, u32[]{:S(2)}, u32[]{:S(2)}) collective-permute-start(bf16[4,48,512]{2,1,0:T(8,128)(2,1)S(1)} %get-tuple-element.23), channel_id=1, source_target_pairs={{0,1},{1,0},{2,3},{3,2},{4,5},{5,4},{6,7},{7,6},{8,9},{9,8},{10,11... | collective-permute-start | bytes 589832 | tf_op jit(solution)/shard_map/ppermute | solution.py:406
  6.0 0.7 %cosine_bitcast_fusion = (f32[1,61]{1,0:T(1,128)S(1)}, f32[1,61]{1,0:T(1,128)S(1)}) fusion(f32[61]{0:T(128)} %param.14), kind=kLoop, calls=%fused_computation.3 | loop fusion | bytes 732 | tf_op jit(solution)/shard_map/stack | solution.py:416
  6.7 0.6 %pad_maximum_fusion.refs_1_ = f32[2,61]{1,0:T(2,128)} fusion(f32[1,61]{1,0:T(1,128)S(1)} %get-tuple-element.40, f32[1,61]{1,0:T(1,128)S(1)} %get-tuple-element.39), kind=kLoop, calls=%fused_computation | loop fusion | flops 122 | bytes 976 | tf_op jit(solution)/shard_map/stack | solution.py:416
  7.2 0.0 collective-permute-done.got_ref.refs_2_
  7.3 1.1 %collective-permute-start.2 = (bf16[2,48,512]{2,1,0:T(8,128)(2,1)S(1)}, bf16[2,48,512]{2,1,0:T(8,128)(2,1)S(1)}, u32[]{:S(2)}, u32[]{:S(2)}) collective-permute-start(bf16[2,48,512]{2,1,0:T(8,128)(2,1)S(1)} %get-tuple-element.27), channel_id=1, source_target_pairs={{0,2},{1,11},{2,0},{3,9},{4,6},{5,15},{6,4},{7,13},{8,10},{9,3},{1... | collective-permute-start | bytes 294920 | tf_op jit(solution)/shard_map/ppermute | solution.py:415
  8.3 3.3 %collective-permute-start.3 = (bf16[2,48,512]{2,1,0:T(8,128)(2,1)S(1)}, bf16[2,48,512]{2,1,0:T(8,128)(2,1)S(1)}, u32[]{:S(2)}, u32[]{:S(2)}) collective-permute-start(bf16[2,48,512]{2,1,0:T(8,128)(2,1)S(1)} %get-tuple-element.28), channel_id=1, source_target_pairs={{0,4},{1,13},{2,6},{3,15},{4,0},{5,9},{6,2},{7,11},{8,12},{9,5},{1... | collective-permute-start | bytes 294920 | tf_op jit(solution)/shard_map/ppermute | solution.py:415
  11.7 0.0 collective-permute-start.4
  11.7 7.2 %shard_map.128 = (bf16[34,512,256]{2,1,0:T(8,128)(2,1)S(1)}, bf16[1280,2048]{1,0:T(8,128)(2,1)S(1)}, bf16[2048,1024]{1,0:T(8,128)(2,1)S(1)}, bf16[8,96,1024]{2,1,0:T(8,128)(2,1)S(1)}, f32[8,128]{1,0:T(8,128)S(1)}) custom-call(s32[2]{0:T(128)S(1)} %pad_add_fusion.refs_0_, f32[2,61]{1,0:T(2,128)} %pad_maximum_fusion.refs_1_, s32[8]{0:T(128)} %refs_2_.1, ...), custom_call_target="tpu_custom_call" | custom-call | flops 4294967296 | bytes 25165824 | tf_op jit(solution)/shard_map/pallas_call | solution.py:417
  18.9 0.0 collective-permute-done.1.refs_3_
  18.9 0.0 collective-permute-done.2.refs_5_
  18.9 0.0 collective-permute-done.3.refs_6_
  18.9 0.0 collective-permute-done.4.refs_7_
  18.9 0.1 collective-permute-start.6
  19.0 0.5 %collective-permute-start.7 = (bf16[2,48,512]{2,1,0:T(8,128)(2,1)S(1)}, bf16[2,48,512]{2,1,0:T(8,128)(2,1)S(1)}, u32[]{:S(2)}, u32[]{:S(2)}) collective-permute-start(bf16[2,48,512]{2,1,0:T(8,128)(2,1)S(1)} %collective-permute-done.3.refs_6_), channel_id=1, source_target_pairs={{0,1},{1,0},{2,3},{3,2},{4,5},{5,4},{6,7},{7,6},{8,9},{9,8},{10,11... | collective-permute-start | bytes 294920 | tf_op jit(solution)/shard_map/ppermute | solution.py:457
  19.5 0.1 collective-permute-start.8
  19.6 0.4 %collective-permute-start.5 = (bf16[48,512]{1,0:T(8,128)(2,1)S(1)}, bf16[48,512]{1,0:T(8,128)(2,1)S(1)}, u32[]{:S(2)}, u32[]{:S(2)}) collective-permute-start(bf16[48,512]{1,0:T(8,128)(2,1)S(1)} %collective-permute-done.1.refs_3_), channel_id=1, source_target_pairs={{0,1},{1,0},{2,3},{3,2},{4,5},{5,4},{6,7},{7,6},{8,9},{9,8},{10,11... | collective-permute-start | bytes 147464 | tf_op jit(solution)/shard_map/ppermute | solution.py:456
  20.0 0.9 %collective-permute-done.5.refs_4_ = bf16[48,512]{1,0:T(8,128)(2,1)S(1)} collective-permute-done((bf16[48,512]{1,0:T(8,128)(2,1)S(1)}, bf16[48,512]{1,0:T(8,128)(2,1)S(1)}, u32[]{:S(2)}, u32[]{:S(2)}) %collective-permute-start.5) | collective-permute-done | bytes 49184 | tf_op jit(solution)/shard_map/ppermute | solution.py:456
  20.9 0.0 collective-permute-done.6.refs_8_
  20.9 0.0 collective-permute-done.7.refs_9_
  20.9 0.0 collective-permute-done.8.refs_10_
  20.9 6.0 %shard_map.130 = f32[1,32,1024]{2,1,0:T(8,128)} custom-call(s32[2]{0:T(128)S(1)} %pad_add_fusion.refs_0_, bf16[48,512]{1,0:T(8,128)(2,1)S(1)} %get-tuple-element.22.refs_1_, bf16[4,48,512]{2,1,0:T(8,128)(2,1)S(1)} %collective-permute-done.got_ref.refs_2_, bf16[48,512]{1,0:T(8,128)(2,1)S(1)} %collective-permute-done.1.refs_3_, ...), custom_call_target="tpu_custom_call" | custom-call | flops 4294967296 | bytes 20971520 | tf_op jit(solution)/shard_map/pallas_call | solution.py:458
  (5 shorter events, 0.0 us)
Async XLA Ops:
  1.8 17.1 %collective-permute-start.1 = (bf16[48,512]{1,0:T(8,128)(2,1)S(1)}, bf16[48,512]{1,0:T(8,128)(2,1)S(1)}, u32[]{:S(2)}, u32[]{:S(2)}) collective-permute-start(bf16[48,512]{1,0:T(8,128)(2,1)S(1)} %get-tuple-element.24), channel_id=1, source_target_pairs={{0,8},{1,9},{2,10},{3,11},{4,12},{5,13},{6,14},{7,15},{8,0},{9,1},... | collective-permute-start | bytes 147464 | tf_op jit(solution)/shard_map/ppermute | solution.py:407
  5.0 2.2 %collective-permute-start = (bf16[4,48,512]{2,1,0:T(8,128)(2,1)S(1)}, bf16[4,48,512]{2,1,0:T(8,128)(2,1)S(1)}, u32[]{:S(2)}, u32[]{:S(2)}) collective-permute-start(bf16[4,48,512]{2,1,0:T(8,128)(2,1)S(1)} %get-tuple-element.23), channel_id=1, source_target_pairs={{0,1},{1,0},{2,3},{3,2},{4,5},{5,4},{6,7},{7,6},{8,9},{9,8},{10,11... | collective-permute-start | bytes 589832 | tf_op jit(solution)/shard_map/ppermute | solution.py:406
  7.3 11.6 %collective-permute-start.2 = (bf16[2,48,512]{2,1,0:T(8,128)(2,1)S(1)}, bf16[2,48,512]{2,1,0:T(8,128)(2,1)S(1)}, u32[]{:S(2)}, u32[]{:S(2)}) collective-permute-start(bf16[2,48,512]{2,1,0:T(8,128)(2,1)S(1)} %get-tuple-element.27), channel_id=1, source_target_pairs={{0,2},{1,11},{2,0},{3,9},{4,6},{5,15},{6,4},{7,13},{8,10},{9,3},{1... | collective-permute-start | bytes 294920 | tf_op jit(solution)/shard_map/ppermute | solution.py:415
  8.3 10.6 %collective-permute-start.3 = (bf16[2,48,512]{2,1,0:T(8,128)(2,1)S(1)}, bf16[2,48,512]{2,1,0:T(8,128)(2,1)S(1)}, u32[]{:S(2)}, u32[]{:S(2)}) collective-permute-start(bf16[2,48,512]{2,1,0:T(8,128)(2,1)S(1)} %get-tuple-element.28), channel_id=1, source_target_pairs={{0,4},{1,13},{2,6},{3,15},{4,0},{5,9},{6,2},{7,11},{8,12},{9,5},{1... | collective-permute-start | bytes 294920 | tf_op jit(solution)/shard_map/ppermute | solution.py:415
  11.7 9.3 %copy-start = (bf16[96,96]{1,0:T(8,128)(2,1)S(1)}, bf16[96,96]{1,0:T(8,128)(2,1)}, u32[]{:S(2)}) copy-start(bf16[96,96]{1,0:T(8,128)(2,1)} %constant.50.clone.refs_14_) | copy-start | bytes 55300
  11.7 9.3 %copy-start.1 = (bf16[64,96]{1,0:T(8,128)(2,1)S(1)}, bf16[64,96]{1,0:T(8,128)(2,1)}, u32[]{:S(2)}) copy-start(bf16[64,96]{1,0:T(8,128)(2,1)} %constant.51.clone.refs_15_) | copy-start | bytes 36868
  11.7 7.3 %collective-permute-start.4 = (bf16[2,48,512]{2,1,0:T(8,128)(2,1)S(1)}, bf16[2,48,512]{2,1,0:T(8,128)(2,1)S(1)}, u32[]{:S(2)}, u32[]{:S(2)}) collective-permute-start(bf16[2,48,512]{2,1,0:T(8,128)(2,1)S(1)} %get-tuple-element.29), channel_id=1, source_target_pairs={{0,6},{1,15},{2,4},{3,13},{4,2},{5,11},{6,0},{7,9},{8,14},{9,7},{1... | collective-permute-start | bytes 294920 | tf_op jit(solution)/shard_map/ppermute | solution.py:415
  18.9 2.0 %collective-permute-start.6 = (bf16[2,48,512]{2,1,0:T(8,128)(2,1)S(1)}, bf16[2,48,512]{2,1,0:T(8,128)(2,1)S(1)}, u32[]{:S(2)}, u32[]{:S(2)}) collective-permute-start(bf16[2,48,512]{2,1,0:T(8,128)(2,1)S(1)} %collective-permute-done.2.refs_5_), channel_id=1, source_target_pairs={{0,1},{1,0},{2,3},{3,2},{4,5},{5,4},{6,7},{7,6},{8,9},{9,8},{10,11... | collective-permute-start | bytes 294920 | tf_op jit(solution)/shard_map/ppermute | solution.py:457
  19.0 1.9 %collective-permute-start.7 = (bf16[2,48,512]{2,1,0:T(8,128)(2,1)S(1)}, bf16[2,48,512]{2,1,0:T(8,128)(2,1)S(1)}, u32[]{:S(2)}, u32[]{:S(2)}) collective-permute-start(bf16[2,48,512]{2,1,0:T(8,128)(2,1)S(1)} %collective-permute-done.3.refs_6_), channel_id=1, source_target_pairs={{0,1},{1,0},{2,3},{3,2},{4,5},{5,4},{6,7},{7,6},{8,9},{9,8},{10,11... | collective-permute-start | bytes 294920 | tf_op jit(solution)/shard_map/ppermute | solution.py:457
  19.5 1.4 %collective-permute-start.8 = (bf16[2,48,512]{2,1,0:T(8,128)(2,1)S(1)}, bf16[2,48,512]{2,1,0:T(8,128)(2,1)S(1)}, u32[]{:S(2)}, u32[]{:S(2)}) collective-permute-start(bf16[2,48,512]{2,1,0:T(8,128)(2,1)S(1)} %collective-permute-done.4.refs_7_), channel_id=1, source_target_pairs={{0,1},{1,0},{2,3},{3,2},{4,5},{5,4},{6,7},{7,6},{8,9},{9,8},{10,11... | collective-permute-start | bytes 294920 | tf_op jit(solution)/shard_map/ppermute | solution.py:457
  19.6 1.3 %collective-permute-start.5 = (bf16[48,512]{1,0:T(8,128)(2,1)S(1)}, bf16[48,512]{1,0:T(8,128)(2,1)S(1)}, u32[]{:S(2)}, u32[]{:S(2)}) collective-permute-start(bf16[48,512]{1,0:T(8,128)(2,1)S(1)} %collective-permute-done.1.refs_3_), channel_id=1, source_target_pairs={{0,1},{1,0},{2,3},{3,2},{4,5},{5,4},{6,7},{7,6},{8,9},{9,8},{10,11... | collective-permute-start | bytes 147464 | tf_op jit(solution)/shard_map/ppermute | solution.py:456

commit v5 on v4

--- a/solution.py
+++ b/solution.py
@@ -23,6 +23,8 @@
 KZ = LZ // 2 + 1
 NF = LEN * KZ
 FP = 1024
+VH = XR * Z // 2
+OH = EDGE * EDGE // 2
 XB = 8
 NQ = XR // XB
 LB = XB * Z
@@ -64,23 +66,29 @@
 def plane_tables():
     kz = np.repeat(np.arange(KZ), LEN)
     kx = np.tile(np.arange(LEN), KZ)
-
-    def waves(k, at, length):
+    mid = (EDGE - 1) / 2.0
+
+    def waves(k, at, length, width):
         p = 2.0 * np.pi * (np.outer(at, k) % length) / length
-        out = np.zeros((2, len(at), FP), np.float32)
+        out = np.zeros((2, len(at), width), np.float32)
         out[0, :, : len(k)], out[1, :, : len(k)] = np.cos(p), np.sin(p)
         return out
 
-    vx = np.repeat(np.arange(EDGE), EDGE)
-    vz = np.tile(np.arange(EDGE) - HALO, EDGE)
+    vx = np.repeat(np.arange(EDGE // 2) - mid, EDGE)
+    vz = np.tile(np.arange(EDGE) - mid, EDGE // 2)
     weight = np.full((KZ, 1), 2.0)
     weight[0] = weight[-1] = 1.0
+    turn = np.zeros((2, XT, FP))
+    for col in range(XT):
+        back = HALO if col == 0 else 0
+        p = 2.0 * np.pi * (kx * (mid - back) / LEN + kz * (mid - HALO) / LZ)
+        turn[0, col, :NF], turn[1, col, :NF] = np.cos(p), np.sin(p)
     return (
-        waves(kx, np.arange(XR), LEN),
-        waves(kz, np.arange(Z), LZ),
-        waves(vx, np.arange(LEN), LEN),
-        waves(vz, np.arange(KZ), LZ) * weight,
-        waves(kx, np.array([HALO, 0]), LEN) * np.array([1.0, -1.0])[:, None, None],
+        waves(kx, np.arange(XR // 2) - (XR - 1) / 2.0, LEN, FP),
+        waves(kz, np.arange(Z) - (Z - 1) / 2.0, LZ, FP),
+        waves(vx, np.arange(LEN // 2), LEN, OH),
+        waves(vz, np.arange(KZ), LZ, OH) * weight,
+        turn,
     )
 
 
@@ -104,24 +112,31 @@
     masks,
     at_ref,
     range_hbm,
+    angle_hbm,
     proj_hbm,
+    turns_ref,
     home_ref,
     near_ref,
     give_ref,
     mine_ref,
     proj_ref,
+    angle_ref,
     range_ref,
     rows_ref,
     sem,
 ):
     fetch = [
         pltpu.make_async_copy(range_hbm, range_ref, sem.at[0]),
-        pltpu.make_async_copy(proj_hbm, proj_ref, sem.at[1]),
+        pltpu.make_async_copy(angle_hbm, angle_ref, sem.at[1]),
+        pltpu.make_async_copy(proj_hbm, proj_ref, sem.at[2]),
     ]
     for copy in fetch:
         copy.start()
-    for copy in fetch:
-        copy.wait()
+    fetch[1].wait()
+    turns_ref[0:1] = jnp.cos(angle_ref[...])
+    turns_ref[1:2] = jnp.sin(angle_ref[...])
+    fetch[0].wait()
+    fetch[2].wait()
     n_tilt, n_det, y_count = proj_ref.shape
     depth = home_ref.shape[1]
     y = lax.broadcasted_iota(jnp.int32, (n_det, y_count), 1)
@@ -146,7 +161,8 @@
         give_ref[1 + j] = rows(chip ^ mask ^ (near_bit * (1 - core)))
 
 
-def merge_kernel(mine_ref, got_ref, *out_refs):
+def merge_kernel(mine_ref, got_ref, done_ref, *out_refs):
+    done_ref[...] = jnp.zeros_like(done_ref)
     for j, out_ref in enumerate(out_refs):
         out_ref[0] = mine_ref[j]
         out_ref[1] = got_ref[1 + j]
@@ -154,22 +170,26 @@
 
 def build_weights(n_det, n_tile, pairs, col, turns_ref, w_ref, whole_ref, part_ref):
     depth = whole_ref.shape[0]
-    lane = lax.broadcasted_iota(jnp.int32, (1, LB), 1)
-    z = (lane % Z).astype(F32) - (Z - 1) / 2.0
-    step = (lane // Z).astype(F32)
+    lane = lax.broadcasted_iota(jnp.int32, (n_det, LB), 1)
+    step = lane // Z
     pack = 16 // n_det
     own = lax.broadcasted_iota(jnp.int32, (n_det, LB), 0).astype(F32)
     top = NTILT // pack * pack
     tail = depth - top * n_det
     base = 0
     for q, sources in enumerate(pairs):
-        block = jnp.where(col == 0, q, NQ - 1 - q) * XB + col * (X - XR)
-        x = step + (block.astype(F32) - (X - 1) / 2.0)
+        block = jnp.where(col == 0, q, NQ - 1 - q)
+        flip = (block * LB + lane) >= VH
+        x = jnp.where(flip, XB - 1 - step + jnp.where(block == NQ // 2, XB // 2, 0), step)
+        x = x + (block * XB + col * (X - XR))
+        x = VOXEL * (x.astype(F32) - (X - 1) / 2.0)
+        z = jnp.where(flip, Z - 1 - lane % Z, lane % Z)
+        z = VOXEL * (z.astype(F32) - (Z - 1) / 2.0)
 
         def tilt(t, z=z, x=x):
-            pos = VOXEL * (x * turns_ref[0, t] + z * turns_ref[1, t]) + (NDET - 1) / 2.0
+            pos = x * turns_ref[0, t] + z * turns_ref[1, t] + (NDET - 1) / 2.0
             whole = jnp.floor(pos)
-            return own - whole, jnp.broadcast_to(pos - whole, own.shape)
+            return own - whole, pos - whole
 
         for first in range(0, NTILT, pack):
             got = [tilt(t) for t in range(first, min(first + pack, NTILT))]
@@ -194,40 +214,31 @@
 
 
 def build_planes(fx_ref, fz_ref, ix_ref, iz_ref, plane_ref, inverse_ref):
-    mid = LEN // 2
-    flip = fx_ref[0, mid : mid + 1]
-
-    def forward(x, carry, both):
+    def forward(x, carry):
         cos_x, sin_x = fx_ref[0, pl.ds(x, 1)], fx_ref[1, pl.ds(x, 1)]
         cos_z, sin_z = fz_ref[0], fz_ref[1]
-        real = cos_x * cos_z - sin_x * sin_z
-        imag = -sin_x * cos_z - cos_x * sin_z
         at = pl.ds(pl.multiple_of(x * Z, Z), Z)
-        plane_ref[at, :FP] = real.astype(BF)
-        plane_ref[at, FP:] = imag.astype(BF)
-        if both:
-            at = pl.ds(pl.multiple_of((x + mid) * Z, Z), Z)
-            plane_ref[at, :FP] = (real * flip).astype(BF)
-            plane_ref[at, FP:] = (imag * flip).astype(BF)
+        plane_ref[at, :FP] = (cos_x * cos_z - sin_x * sin_z).astype(BF)
+        plane_ref[at, FP:] = (-sin_x * cos_z - cos_x * sin_z).astype(BF)
         return carry
 
-    lax.fori_loop(0, XR - mid, lambda x, c: forward(x, c, True), 0)
-    lax.fori_loop(XR - mid, mid, lambda x, c: forward(x, c, False), 0)
-    turn = ix_ref[0, mid : mid + 1]
+    lax.fori_loop(0, XR // 2, forward, 0)
+    odd = lax.broadcasted_iota(jnp.int32, (1, OH), 1) // EDGE % 2
+    turn = 1.0 - 2.0 * odd.astype(F32)
 
     def inverse(k, carry):
         cos_z, sin_z = iz_ref[0, pl.ds(k, 1)], iz_ref[1, pl.ds(k, 1)]
-        cos_x, sin_x = ix_ref[0, :mid], ix_ref[1, :mid]
+        cos_x, sin_x = ix_ref[0], ix_ref[1]
         real = cos_x * cos_z - sin_x * sin_z
         imag = -sin_x * cos_z - cos_x * sin_z
         low = pl.multiple_of(k * LEN, 16)
-        inverse_ref[pl.ds(low, LEN)] = jnp.concatenate([real, real * turn], 0).astype(BF)
-        inverse_ref[pl.ds(FP + low, LEN)] = jnp.concatenate([imag, imag * turn], 0).astype(BF)
+        inverse_ref[pl.ds(low, LEN)] = jnp.concatenate([real, imag * turn], 0).astype(BF)
+        inverse_ref[pl.ds(FP + low, LEN)] = jnp.concatenate([imag, -real * turn], 0).astype(BF)
         return carry
 
     lax.fori_loop(0, KZ, inverse, 0)
-    inverse_ref[NF:FP] = jnp.zeros((FP - NF, EDGE * EDGE), BF)
-    inverse_ref[FP + NF :] = jnp.zeros((FP - NF, EDGE * EDGE), BF)
+    inverse_ref[NF:FP] = jnp.zeros((FP - NF, OH), BF)
+    inverse_ref[FP + NF :] = jnp.zeros((FP - NF, OH), BF)
 
 
 def build_templates(col, rot_ref, bank_ref, plane_ref, line_ref, turn_ref, out_ref):
@@ -245,47 +256,24 @@
         out_ref[r, LEN:] = (real * sin + imag * cos).astype(BF)
 
 
-def prepare_kernel(
-    n_det,
-    n_tile,
-    pairs,
-    at_ref,
-    turns_hbm,
-    rot_hbm,
-    bank_hbm,
-    fx_hbm,
-    fz_hbm,
-    ix_hbm,
-    iz_hbm,
-    line_hbm,
-    turn_hbm,
-    w_ref,
-    plane_ref,
-    inverse_ref,
-    tmpl_ref,
-    done_ref,
-    whole_ref,
-    part_ref,
-    rot_ref,
-    turns_ref,
-    *rest,
-):
-    *buffers, sem = rest
-    sources = (turns_hbm, rot_hbm, bank_hbm, fx_hbm, fz_hbm, ix_hbm, iz_hbm, line_hbm, turn_hbm)
-    targets = (turns_ref, rot_ref, *buffers)
+def weight_kernel(n_det, n_tile, pairs, at_ref, turns_ref, _, w_ref, done_ref, whole_ref, part_ref):
+    build_weights(n_det, n_tile, pairs, at_ref[1], turns_ref, w_ref, whole_ref, part_ref)
+    done_ref[...] = jnp.zeros_like(done_ref)
+
+
+def table_kernel(at_ref, _, *refs):
+    sources, outs, targets, sem = refs[:8], refs[8:12], refs[12:20], refs[20]
     fetch = [
         pltpu.make_async_copy(a, b, sem.at[i]) for i, (a, b) in enumerate(zip(sources, targets))
     ]
     for copy in fetch:
         copy.start()
-    fetch[0].wait()
-    col = at_ref[1]
-    build_weights(n_det, n_tile, pairs, col, turns_ref, w_ref, whole_ref, part_ref)
-    for copy in fetch[1:]:
+    for copy in fetch:
         copy.wait()
-    bank_ref, fx_ref, fz_ref, ix_ref, iz_ref, line_ref, turn_ref = buffers
+    rot_ref, bank_ref, fx_ref, fz_ref, ix_ref, iz_ref, line_ref, turn_ref = targets
+    plane_ref, inverse_ref, tmpl_ref, done_ref = outs
     build_planes(fx_ref, fz_ref, ix_ref, iz_ref, plane_ref, inverse_ref)
-    build_templates(col, rot_ref, bank_ref, plane_ref, line_ref, turn_ref, tmpl_ref)
+    build_templates(at_ref[1], rot_ref, bank_ref, plane_ref, line_ref, turn_ref, tmpl_ref)
     done_ref[...] = jnp.zeros_like(done_ref)
 
 
@@ -294,7 +282,7 @@
     at_ref, home_ref, got_ref, near_ref, near_swap_ref = refs[:5]
     recv_refs, swap_refs = refs[5 : 5 + n_op], refs[5 + n_op : 5 + 2 * n_op]
     w_ref, tmpl_ref, plane_ref, line_ref, back_ref, inverse_ref = refs[5 + 2 * n_op : 11 + 2 * n_op]
-    _, out_ref, data_ref, vol_ref, mid_ref = refs[11 + 2 * n_op :]
+    _, _, out_ref, data_ref, vol_ref, mid_ref = refs[11 + 2 * n_op :]
     chip, core = at_ref[0], at_ref[1]
     mate = 1 - core
     data_ref[chip * XT + core] = home_ref[...]
@@ -316,9 +304,19 @@
             total += jnp.dot(part, w_ref[base + j], preferred_element_type=F32)
         base += len(sources)
         block = jnp.where(core == 0, q, NQ - 1 - q)
-        vol_ref[:, pl.ds(pl.multiple_of(block * LB, LB), LB)] = total.astype(BF)
-    flat = jnp.dot(vol_ref[...], plane_ref[...], preferred_element_type=F32).astype(BF)
-    stacked = jnp.concatenate([flat[:, :FP], flat[:, FP:]], 0)
+        vol_ref[:, pl.ds(pl.multiple_of(block * LB, LB), LB)] = total
+    near_half = vol_ref[:, :VH]
+    far_half = jnp.concatenate(
+        [vol_ref[:, 4 * LB :], vol_ref[:, 3 * LB : 4 * LB], vol_ref[:, VH : 3 * LB]], 1
+    )
+    even, odd = (near_half + far_half).astype(BF), (near_half - far_half).astype(BF)
+    stacked = jnp.concatenate(
+        [
+            jnp.dot(even, plane_ref[:, :FP], preferred_element_type=F32).astype(BF),
+            jnp.dot(odd, plane_ref[:, FP:], preferred_element_type=F32).astype(BF),
+        ],
+        0,
+    )
     full = jnp.dot(line_ref[...], stacked, preferred_element_type=F32)
     real, imag = full[:LEN], full[LEN:]
     for r in range(NTPL):
@@ -334,11 +332,20 @@
         line = jnp.dot(back_ref[...], prod, preferred_element_type=F32).astype(BF)
         mid_ref[r * EDGE : (r + 1) * EDGE, :FP] = line[:EDGE]
         mid_ref[r * EDGE : (r + 1) * EDGE, FP:] = line[EDGE:]
-    corr = jnp.dot(mid_ref[...], inverse_ref[...], preferred_element_type=F32)
-    best = corr[:EDGE]
+    even = jnp.dot(mid_ref[:, :FP], inverse_ref[:FP], preferred_element_type=F32)
+    odd = jnp.dot(mid_ref[:, FP:], inverse_ref[FP:], preferred_element_type=F32)
+    best = even[:EDGE] + odd[:EDGE]
+    mirrored = even[:EDGE] - odd[:EDGE]
     for r in range(1, NTPL):
-        best = jnp.maximum(best, corr[r * EDGE : (r + 1) * EDGE])
-    out_ref[0] = best * SCALE
+        at = slice(r * EDGE, (r + 1) * EDGE)
+        best = jnp.maximum(best, even[at] + odd[at])
+        mirrored = jnp.maximum(mirrored, even[at] - odd[at])
+    out_ref[0, :, :OH] = best * SCALE
+    mirrored = mirrored * SCALE
+    order = 127 - lax.broadcasted_iota(jnp.int32, (EDGE, 128), 1)
+    for low in range(0, OH, 128):
+        part = jnp.take_along_axis(mirrored[:, low : low + 128], order, axis=1)
+        out_ref[0, :, 2 * OH - 128 - low : 2 * OH - low] = part
 
 
 VMEM = pl.BlockSpec(memory_space=pltpu.VMEM)
@@ -385,84 +392,84 @@
         position = lax.axis_index("tile").astype(jnp.int32)
         at = jnp.stack([position // XT, position % XT])
         by_y = jnp.transpose(projections, (1, 2, 0))
-        home, near, give, mine = pl.pallas_call(
+        turns, home, near, give, mine = pl.pallas_call(
             lambda *refs: pack_kernel(near_bit, masks, *refs),
             out_shape=(
+                shape(2, NTILT, dtype=F32),
                 shape(LEN, depth),
                 shape(LEN, depth),
                 shape(1 + n_op, LEN, depth),
                 shape(n_op, LEN, depth),
             ),
-            in_specs=[SMEM, HBM, HBM],
-            out_specs=(VMEM,) * 4,
+            in_specs=[SMEM, HBM, HBM, HBM],
+            out_specs=(VMEM,) * 5,
             scratch_shapes=[
                 pltpu.VMEM(by_y.shape, BF),
+                pltpu.VMEM((1, NTILT), F32),
                 pltpu.SMEM((2, NTILT), jnp.int32),
                 pltpu.VMEM((y_count + 2 * HALO, depth), BF),
-                pltpu.SemaphoreType.DMA((2,)),
+                pltpu.SemaphoreType.DMA((3,)),
             ],
             compiler_params=limit(8),
-        )(at, pinned(row_range.T), pinned(by_y))
+        )(at, pinned(row_range.T), pinned(tilt_angle.reshape(1, NTILT)), pinned(by_y))
         got = lax.ppermute(give, "tile", mate)
         near_in = lax.ppermute(near, "tile", near_pairs)
-        payload = pl.pallas_call(
+        merged, *payload = pl.pallas_call(
             merge_kernel,
-            out_shape=(shape(2, LEN, depth),) * n_op,
+            out_shape=(shape(8, 128, dtype=F32),) + (shape(2, LEN, depth),) * n_op,
             in_specs=[VMEM, VMEM],
-            out_specs=(VMEM,) * n_op,
+            out_specs=(VMEM,) * (1 + n_op),
             compiler_params=limit(8),
         )(mine, got)
         arrived = [lax.ppermute(p, "tile", route(m)) for p, m in zip(payload, masks)]
-        turns = jnp.stack([jnp.cos(tilt_angle), jnp.sin(tilt_angle)])
-        weights, plane, inverse, spectra, done = pl.pallas_call(
-            lambda *refs: prepare_kernel(n_det, n_tile, pairs, *refs),
+        weights, done_w = pl.pallas_call(
+            lambda *refs: weight_kernel(n_det, n_tile, pairs, *refs),
+            out_shape=(shape(n_pair, depth, LB), shape(8, 128, dtype=F32)),
+            in_specs=[SMEM, SMEM, VMEM],
+            out_specs=(VMEM,) * 2,
+            scratch_shapes=[pltpu.VMEM((depth, LB), BF)] * 2,
+            compiler_params=limit(16),
+            cost_estimate=cost(1 << 32, 9 << 20),
+        )(at, turns, merged)
+        last = arrived[-1]
+        near_in, done_w, *arrived = lax.optimization_barrier((near_in, done_w, *arrived[:-1]))
+        constants = (
+            rot_index,
+            template_bank,
+            *[jnp.asarray(t, F32) for t in tables[:4]],
+            jnp.asarray(line_t),
+            jnp.asarray(tables[4], F32),
+        )
+        plane, inverse, spectra, done_t = pl.pallas_call(
+            table_kernel,
             out_shape=(
-                shape(n_pair, depth, LB),
-                shape(XR * Z, 2 * FP),
-                shape(2 * FP, EDGE * EDGE),
+                shape(VH, 2 * FP),
+                shape(2 * FP, OH),
                 shape(NTPL, 2 * LEN, FP),
                 shape(8, 128, dtype=F32),
             ),
-            in_specs=[SMEM] + [HBM] * 9,
-            out_specs=(VMEM,) * 5,
+            in_specs=[SMEM, VMEM] + [HBM] * 8,
+            out_specs=(VMEM,) * 4,
             scratch_shapes=[
-                pltpu.VMEM((depth, LB), BF),
-                pltpu.VMEM((depth, LB), BF),
                 pltpu.SMEM((NTPL,), jnp.int32),
-                pltpu.SMEM((2, NTILT), F32),
-                pltpu.VMEM(template_bank.shape, BF),
-                *[pltpu.VMEM(t.shape, F32) for t in tables[:4]],
-                pltpu.VMEM(line_t.shape, BF),
-                pltpu.VMEM(tables[4].shape, F32),
-                pltpu.SemaphoreType.DMA((9,)),
+                *[pltpu.VMEM(c.shape, c.dtype) for c in constants[1:]],
+                pltpu.SemaphoreType.DMA((8,)),
             ],
-            compiler_params=limit(28),
-            cost_estimate=cost(1 << 32, 24 << 20),
-        )(
-            at,
-            *[
-                pinned(a)
-                for a in (
-                    turns,
-                    rot_index,
-                    template_bank,
-                    *[jnp.asarray(t, F32) for t in tables[:4]],
-                    jnp.asarray(line_t),
-                    jnp.asarray(tables[4], F32),
-                )
-            ],
-        )
-        near_in, done, *arrived = lax.optimization_barrier((near_in, done, *arrived))
+            compiler_params=limit(20),
+            cost_estimate=cost(1 << 32, 8 << 20),
+        )(at, done_w, *[pinned(c) for c in constants])
+        last, done_t = lax.optimization_barrier((last, done_t))
+        arrived.append(last)
         near_swap = lax.ppermute(near_in, "tile", mate)
         swapped = [lax.ppermute(a, "tile", mate) for a in arrived]
         return pl.pallas_call(
             lambda *refs: score_kernel(near_bit, masks, pairs, n_tile, *refs),
             out_shape=shape(1, EDGE, EDGE * Z, dtype=F32),
-            in_specs=[SMEM] + [VMEM] * (11 + 2 * n_op),
+            in_specs=[SMEM] + [VMEM] * (12 + 2 * n_op),
             out_specs=VMEM,
             scratch_shapes=[
                 pltpu.VMEM((n_tile, LEN, depth), BF),
-                pltpu.VMEM((LEN, XR * Z), BF),
+                pltpu.VMEM((LEN, XR * Z), F32),
                 pltpu.VMEM((NTPL * EDGE, 2 * FP), BF),
             ],
             compiler_params=limit(28),
@@ -481,7 +488,8 @@
             jnp.asarray(line),
             jnp.asarray(back),
             inverse,
-            done,
+            done_w,
+            done_t,
         )
 
     return jax.shard_map(

time: 27.4 us -> 26.7 us (0.974)
  Pallas kernels: 15 us -> 14.1 us
  waiting for transfers between devices: 0.9 us -> 1.71 us
  local copies, waits for them, and re-layouts: 0.7 us -> 0.01 us
  starting transfers between devices: 9.64 us -> 10.3 us
  other arithmetic: 0.65 us -> 0.07 us
    pallas_call x1, Pallas kernels: 6.03 us -> 5.09 us  [local(): pl.pallas_call(lambda *refs: score_kernel(near_bit, masks, pairs, n_tile,...]
    ppermute x3, starting transfers between devices: 4.4 us -> 5.28 us  [local(): lax.ppermute(p, 'tile', route(m))]
    ppermute x1, starting transfers between devices: 0.96 us -> 0.12 us  [local(): got = lax.ppermute(give, 'tile', mate)]
    ppermute x3, waiting for transfers between devices: 0.01 us -> 0.81 us  [local(): lax.ppermute(p, 'tile', route(m))]
    another operation x1 -> x0, local copies, waits for them, and re-layouts: 0.69 us -> none  [local(): turns = jnp.stack([jnp.cos(tilt_angle), jnp.sin(tilt_angle)])]
    another operation x1 -> x0, other arithmetic: 0.58 us -> none  [local(): turns = jnp.stack([jnp.cos(tilt_angle), jnp.sin(tilt_angle)])]
    ppermute x1, starting transfers between devices: 3.21 us -> 3.77 us  [local(): near_in = lax.ppermute(near, 'tile', near_pairs)]
    pallas_call x2 -> x3, Pallas kernels: 7.23 us -> 7.3 us  [the longest x1 4.09 us: local(): pl.pallas_call(table_kernel, out_shape=(shape(VH, 2 * FP), shape(2 * FP,...]
  transfers between devices with their start and end apart: 9 -> 9, of which waited for: 1 -> 2; matrix products, arithmetic and copies ran while one was open for 5% -> 0% of each run, Pallas kernels for 27% -> 28%
where the time goes in v5:
time: 26.7 us; the launch traced here: 26.3 us
  Pallas kernels  14.1 us (53%)
  starting transfers between devices  10.3 us (39%)
  waiting for transfers between devices  1.71 us (6%)
    ppermute x3, starting transfers between devices, local(): lax.ppermute(p, 'tile', route(m))  5.28 us
    pallas_call x1, Pallas kernels, local(): pl.pallas_call(lambda *refs: score_kernel(near_bit, masks, pairs, n_tile,...  5.09 us
    pallas_call x1, Pallas kernels, local(): pl.pallas_call(table_kernel, out_shape=(shape(VH, 2 * FP), shape(2 * FP,...  4.09 us
    ppermute x1, starting transfers between devices, local(): near_in = lax.ppermute(near, 'tile', near_pairs)  3.77 us
    pallas_call x1, Pallas kernels, local(): pl.pallas_call(lambda *refs: weight_kernel(n_det, n_tile, pairs, *refs),...  3.19 us
    pallas_call x1, Pallas kernels, local(): pl.pallas_call(lambda *refs: pack_kernel(near_bit, masks, *refs), out_sha...  1.74 us
    ppermute x1, waiting for transfers between devices, local(): near_swap = lax.ppermute(near_in, 'tile', mate)  0.88 us
    ppermute x3, waiting for transfers between devices, local(): lax.ppermute(p, 'tile', route(m))  0.81 us
  transfers between devices with their start and end apart: 9, of which 2 were waited for; matrix products, arithmetic and copies ran while one was open for 0% of the time, Pallas kernels for 28%

profile of v5, /device:TPU:1, one launch (start us, length us, event | category | flops | bytes accessed | tf_op | source)
XLA Modules:
  0.0 26.3 jit_solution(3544796944921406763)
XLA Ops:
  0.0 0.1 pad_add_fusion.refs_0_.at_ref
  0.1 1.7 %shard_map.127 = (f32[2,61]{1,0:T(2,128)S(1)}, bf16[48,512]{1,0:T(8,128)(2,1)S(1)}, bf16[48,512]{1,0:T(8,128)(2,1)S(1)}, bf16[4,48,512]{2,1,0:T(8,128)(2,1)S(1)}, bf16[3,48,512]{2,1,0:T(8,128)(2,1)S(1)}) custom-call(s32[2]{0:T(128)S(1)} %pad_add_fusion.refs_0_.at_ref, s32[2,61]{1,0:T(2,128)} %bitcast.6, f32[1,61]{1,0:T(1,128)} %bitcast.7, ...), custom_call_target="tpu_custom_call" | custom-call | tf_op jit(solution)/shard_map/pallas_call | solution.py:395
  1.8 0.1 collective-permute-start
  1.9 3.8 %collective-permute-start.1 = (bf16[48,512]{1,0:T(8,128)(2,1)S(1)}, bf16[48,512]{1,0:T(8,128)(2,1)S(1)}, u32[]{:S(2)}, u32[]{:S(2)}) collective-permute-start(bf16[48,512]{1,0:T(8,128)(2,1)S(1)} %get-tuple-element.28), channel_id=1, source_target_pairs={{0,8},{1,9},{2,10},{3,11},{4,12},{5,13},{6,14},{7,15},{8,0},{9,1},... | collective-permute-start | bytes 147464 | tf_op jit(solution)/shard_map/ppermute | solution.py:416
  5.7 0.0 collective-permute-done.got_ref.refs_2_
  5.7 2.1 %collective-permute-start.2 = (bf16[2,48,512]{2,1,0:T(8,128)(2,1)S(1)}, bf16[2,48,512]{2,1,0:T(8,128)(2,1)S(1)}, u32[]{:S(2)}, u32[]{:S(2)}) collective-permute-start(bf16[2,48,512]{2,1,0:T(8,128)(2,1)S(1)} %get-tuple-element.33), channel_id=1, source_target_pairs={{0,2},{1,11},{2,0},{3,9},{4,6},{5,15},{6,4},{7,13},{8,10},{9,3},{1... | collective-permute-start | bytes 294920 | tf_op jit(solution)/shard_map/ppermute | solution.py:424
  7.8 2.3 %collective-permute-start.3 = (bf16[2,48,512]{2,1,0:T(8,128)(2,1)S(1)}, bf16[2,48,512]{2,1,0:T(8,128)(2,1)S(1)}, u32[]{:S(2)}, u32[]{:S(2)}) collective-permute-start(bf16[2,48,512]{2,1,0:T(8,128)(2,1)S(1)} %get-tuple-element.34), channel_id=1, source_target_pairs={{0,4},{1,13},{2,6},{3,15},{4,0},{5,9},{6,2},{7,11},{8,12},{9,5},{1... | collective-permute-start | bytes 294920 | tf_op jit(solution)/shard_map/ppermute | solution.py:424
  10.1 0.9 %collective-permute-start.5 = (bf16[2,48,512]{2,1,0:T(8,128)(2,1)S(1)}, bf16[2,48,512]{2,1,0:T(8,128)(2,1)S(1)}, u32[]{:S(2)}, u32[]{:S(2)}) collective-permute-start(bf16[2,48,512]{2,1,0:T(8,128)(2,1)S(1)} %get-tuple-element.38), channel_id=1, source_target_pairs={{0,6},{1,15},{2,4},{3,13},{4,2},{5,11},{6,0},{7,9},{8,14},{9,7},{1... | collective-permute-start | bytes 294920 | tf_op jit(solution)/shard_map/ppermute | solution.py:424
  11.0 3.2 %shard_map.129 = (bf16[34,512,256]{2,1,0:T(8,128)(2,1)S(1)}, f32[8,128]{1,0:T(8,128)S(1)}) custom-call(s32[2]{0:T(128)S(1)} %pad_add_fusion.refs_0_.at_ref, f32[2,61]{1,0:T(2,128)S(1)} %get-tuple-element.29.refs_1_, f32[8,128]{1,0:T(8,128)S(1)} %get-tuple-element.31.refs_2_), custom_call_target="tpu_custom_call" | custom-call | flops 4294967296 | bytes 9437184 | tf_op jit(solution)/shard_map/pallas_call | solution.py:425
  14.2 0.0 collective-permute-done.1.refs_3_
  14.2 0.0 collective-permute-done.2.refs_5_
  14.2 0.8 %collective-permute-done.3.refs_6_ = bf16[2,48,512]{2,1,0:T(8,128)(2,1)S(1)} collective-permute-done((bf16[2,48,512]{2,1,0:T(8,128)(2,1)S(1)}, bf16[2,48,512]{2,1,0:T(8,128)(2,1)S(1)}, u32[]{:S(2)}, u32[]{:S(2)}) %collective-permute-start.3) | collective-permute-done | bytes 98336 | tf_op jit(solution)/shard_map/ppermute | solution.py:424
  15.1 0.0 collective-permute-start.6
  15.1 0.5 %collective-permute-start.7 = (bf16[2,48,512]{2,1,0:T(8,128)(2,1)S(1)}, bf16[2,48,512]{2,1,0:T(8,128)(2,1)S(1)}, u32[]{:S(2)}, u32[]{:S(2)}) collective-permute-start(bf16[2,48,512]{2,1,0:T(8,128)(2,1)S(1)} %collective-permute-done.3.refs_6_), channel_id=1, source_target_pairs={{0,1},{1,0},{2,3},{3,2},{4,5},{5,4},{6,7},{7,6},{8,9},{9,8},{10,11... | collective-permute-start | bytes 294920 | tf_op jit(solution)/shard_map/ppermute | solution.py:464
  15.6 4.1 %shard_map.130 = (bf16[640,2048]{1,0:T(8,128)(2,1)S(1)}, bf16[2048,512]{1,0:T(8,128)(2,1)S(1)}, bf16[8,96,1024]{2,1,0:T(8,128)(2,1)S(1)}, f32[8,128]{1,0:T(8,128)S(1)}) custom-call(s32[2]{0:T(128)S(1)} %pad_add_fusion.refs_0_.at_ref, f32[8,128]{1,0:T(8,128)S(1)} %get-tuple-element.39._.refs_17_, s32[8]{0:T(128)} %refs_0_.1, bf16[64,16,256]{2,1,0:T(8,128)(2,1)} %refs_1_.1, ...), custom_call_target="tpu_custom_call" | custom-call | flops 4294967296 | bytes 8388608 | tf_op jit(solution)/shard_map/pallas_call | solution.py:443
  19.7 0.0 collective-permute-done.5.refs_7_
  19.7 0.1 collective-permute-start.8
  19.8 0.5 %collective-permute-start.4 = (bf16[48,512]{1,0:T(8,128)(2,1)S(1)}, bf16[48,512]{1,0:T(8,128)(2,1)S(1)}, u32[]{:S(2)}, u32[]{:S(2)}) collective-permute-start(bf16[48,512]{1,0:T(8,128)(2,1)S(1)} %collective-permute-done.1.refs_3_), channel_id=1, source_target_pairs={{0,1},{1,0},{2,3},{3,2},{4,5},{5,4},{6,7},{7,6},{8,9},{9,8},{10,11... | collective-permute-start | bytes 147464 | tf_op jit(solution)/shard_map/ppermute | solution.py:463
  20.3 0.9 %collective-permute-done.4.refs_4_ = bf16[48,512]{1,0:T(8,128)(2,1)S(1)} collective-permute-done((bf16[48,512]{1,0:T(8,128)(2,1)S(1)}, bf16[48,512]{1,0:T(8,128)(2,1)S(1)}, u32[]{:S(2)}, u32[]{:S(2)}) %collective-permute-start.4) | collective-permute-done | bytes 49184 | tf_op jit(solution)/shard_map/ppermute | solution.py:463
  21.1 0.0 collective-permute-done.6.refs_8_
  21.1 0.0 collective-permute-done.7.refs_9_
  21.1 0.0 collective-permute-done.8.refs_10_
  21.1 0.0 copy-done
  21.2 5.1 %shard_map.131 = f32[1,32,1024]{2,1,0:T(8,128)} custom-call(s32[2]{0:T(128)S(1)} %pad_add_fusion.refs_0_.at_ref, bf16[48,512]{1,0:T(8,128)(2,1)S(1)} %get-tuple-element.26.refs_1_, bf16[4,48,512]{2,1,0:T(8,128)(2,1)S(1)} %collective-permute-done.got_ref.refs_2_, bf16[48,512]{1,0:T(8,128)(2,1)S(1)} %collective-permute-done.1.refs_3_, ...), custom_call_target="tpu_custom_call" | custom-call | flops 4294967296 | bytes 20971520 | tf_op jit(solution)/shard_map/pallas_call | solution.py:465
  (4 shorter events, 0.0 us)
Async XLA Ops:
  1.8 3.9 %collective-permute-start = (bf16[4,48,512]{2,1,0:T(8,128)(2,1)S(1)}, bf16[4,48,512]{2,1,0:T(8,128)(2,1)S(1)}, u32[]{:S(2)}, u32[]{:S(2)}) collective-permute-start(bf16[4,48,512]{2,1,0:T(8,128)(2,1)S(1)} %get-tuple-element.27), channel_id=1, source_target_pairs={{0,1},{1,0},{2,3},{3,2},{4,5},{5,4},{6,7},{7,6},{8,9},{9,8},{10,11... | collective-permute-start | bytes 589832 | tf_op jit(solution)/shard_map/ppermute | solution.py:415
  1.9 12.3 %collective-permute-start.1 = (bf16[48,512]{1,0:T(8,128)(2,1)S(1)}, bf16[48,512]{1,0:T(8,128)(2,1)S(1)}, u32[]{:S(2)}, u32[]{:S(2)}) collective-permute-start(bf16[48,512]{1,0:T(8,128)(2,1)S(1)} %get-tuple-element.28), channel_id=1, source_target_pairs={{0,8},{1,9},{2,10},{3,11},{4,12},{5,13},{6,14},{7,15},{8,0},{9,1},... | collective-permute-start | bytes 147464 | tf_op jit(solution)/shard_map/ppermute | solution.py:416
  5.7 8.5 %collective-permute-start.2 = (bf16[2,48,512]{2,1,0:T(8,128)(2,1)S(1)}, bf16[2,48,512]{2,1,0:T(8,128)(2,1)S(1)}, u32[]{:S(2)}, u32[]{:S(2)}) collective-permute-start(bf16[2,48,512]{2,1,0:T(8,128)(2,1)S(1)} %get-tuple-element.33), channel_id=1, source_target_pairs={{0,2},{1,11},{2,0},{3,9},{4,6},{5,15},{6,4},{7,13},{8,10},{9,3},{1... | collective-permute-start | bytes 294920 | tf_op jit(solution)/shard_map/ppermute | solution.py:424
  7.8 7.2 %collective-permute-start.3 = (bf16[2,48,512]{2,1,0:T(8,128)(2,1)S(1)}, bf16[2,48,512]{2,1,0:T(8,128)(2,1)S(1)}, u32[]{:S(2)}, u32[]{:S(2)}) collective-permute-start(bf16[2,48,512]{2,1,0:T(8,128)(2,1)S(1)} %get-tuple-element.34), channel_id=1, source_target_pairs={{0,4},{1,13},{2,6},{3,15},{4,0},{5,9},{6,2},{7,11},{8,12},{9,5},{1... | collective-permute-start | bytes 294920 | tf_op jit(solution)/shard_map/ppermute | solution.py:424
  10.1 9.5 %collective-permute-start.5 = (bf16[2,48,512]{2,1,0:T(8,128)(2,1)S(1)}, bf16[2,48,512]{2,1,0:T(8,128)(2,1)S(1)}, u32[]{:S(2)}, u32[]{:S(2)}) collective-permute-start(bf16[2,48,512]{2,1,0:T(8,128)(2,1)S(1)} %get-tuple-element.38), channel_id=1, source_target_pairs={{0,6},{1,15},{2,4},{3,13},{4,2},{5,11},{6,0},{7,9},{8,14},{9,7},{1... | collective-permute-start | bytes 294920 | tf_op jit(solution)/shard_map/ppermute | solution.py:424
  15.1 6.1 %copy-start = (bf16[96,96]{1,0:T(8,128)(2,1)S(1)}, bf16[96,96]{1,0:T(8,128)(2,1)}, u32[]{:S(2)}) copy-start(bf16[96,96]{1,0:T(8,128)(2,1)} %constant.50.clone.refs_14_) | copy-start | bytes 55300
  15.1 6.1 %copy-start.1 = (bf16[64,96]{1,0:T(8,128)(2,1)S(1)}, bf16[64,96]{1,0:T(8,128)(2,1)}, u32[]{:S(2)}) copy-start(bf16[64,96]{1,0:T(8,128)(2,1)} %constant.51.clone.refs_15_) | copy-start | bytes 36868
  15.1 6.1 %collective-permute-start.6 = (bf16[2,48,512]{2,1,0:T(8,128)(2,1)S(1)}, bf16[2,48,512]{2,1,0:T(8,128)(2,1)S(1)}, u32[]{:S(2)}, u32[]{:S(2)}) collective-permute-start(bf16[2,48,512]{2,1,0:T(8,128)(2,1)S(1)} %collective-permute-done.2.refs_5_), channel_id=1, source_target_pairs={{0,1},{1,0},{2,3},{3,2},{4,5},{5,4},{6,7},{7,6},{8,9},{9,8},{10,11... | collective-permute-start | bytes 294920 | tf_op jit(solution)/shard_map/ppermute | solution.py:464
  15.1 6.1 %collective-permute-start.7 = (bf16[2,48,512]{2,1,0:T(8,128)(2,1)S(1)}, bf16[2,48,512]{2,1,0:T(8,128)(2,1)S(1)}, u32[]{:S(2)}, u32[]{:S(2)}) collective-permute-start(bf16[2,48,512]{2,1,0:T(8,128)(2,1)S(1)} %collective-permute-done.3.refs_6_), channel_id=1, source_target_pairs={{0,1},{1,0},{2,3},{3,2},{4,5},{5,4},{6,7},{7,6},{8,9},{9,8},{10,11... | collective-permute-start | bytes 294920 | tf_op jit(solution)/shard_map/ppermute | solution.py:464
  19.7 1.5 %collective-permute-start.8 = (bf16[2,48,512]{2,1,0:T(8,128)(2,1)S(1)}, bf16[2,48,512]{2,1,0:T(8,128)(2,1)S(1)}, u32[]{:S(2)}, u32[]{:S(2)}) collective-permute-start(bf16[2,48,512]{2,1,0:T(8,128)(2,1)S(1)} %collective-permute-done.5.refs_7_), channel_id=1, source_target_pairs={{0,1},{1,0},{2,3},{3,2},{4,5},{5,4},{6,7},{7,6},{8,9},{9,8},{10,11... | collective-permute-start | bytes 294920 | tf_op jit(solution)/shard_map/ppermute | solution.py:464
  19.8 1.3 %collective-permute-start.4 = (bf16[48,512]{1,0:T(8,128)(2,1)S(1)}, bf16[48,512]{1,0:T(8,128)(2,1)S(1)}, u32[]{:S(2)}, u32[]{:S(2)}) collective-permute-start(bf16[48,512]{1,0:T(8,128)(2,1)S(1)} %collective-permute-done.1.refs_3_), channel_id=1, source_target_pairs={{0,1},{1,0},{2,3},{3,2},{4,5},{5,4},{6,7},{7,6},{8,9},{9,8},{10,11... | collective-permute-start | bytes 147464 | tf_op jit(solution)/shard_map/ppermute | solution.py:463

commit v6 on v5

--- a/solution.py
+++ b/solution.py
@@ -256,24 +256,21 @@
         out_ref[r, LEN:] = (real * sin + imag * cos).astype(BF)
 
 
-def weight_kernel(n_det, n_tile, pairs, at_ref, turns_ref, _, w_ref, done_ref, whole_ref, part_ref):
-    build_weights(n_det, n_tile, pairs, at_ref[1], turns_ref, w_ref, whole_ref, part_ref)
-    done_ref[...] = jnp.zeros_like(done_ref)
-
-
-def table_kernel(at_ref, _, *refs):
-    sources, outs, targets, sem = refs[:8], refs[8:12], refs[12:20], refs[20]
+def prepare_kernel(n_det, n_tile, pairs, at_ref, turns_ref, _, *refs):
+    sources, outs, targets, (sem, whole_ref, part_ref) = refs[:8], refs[8:13], refs[13:21], refs[21:]
     fetch = [
         pltpu.make_async_copy(a, b, sem.at[i]) for i, (a, b) in enumerate(zip(sources, targets))
     ]
     for copy in fetch:
         copy.start()
+    w_ref, plane_ref, inverse_ref, tmpl_ref, done_ref = outs
+    col = at_ref[1]
+    build_weights(n_det, n_tile, pairs, col, turns_ref, w_ref, whole_ref, part_ref)
     for copy in fetch:
         copy.wait()
     rot_ref, bank_ref, fx_ref, fz_ref, ix_ref, iz_ref, line_ref, turn_ref = targets
-    plane_ref, inverse_ref, tmpl_ref, done_ref = outs
     build_planes(fx_ref, fz_ref, ix_ref, iz_ref, plane_ref, inverse_ref)
-    build_templates(at_ref[1], rot_ref, bank_ref, plane_ref, line_ref, turn_ref, tmpl_ref)
+    build_templates(col, rot_ref, bank_ref, plane_ref, line_ref, turn_ref, tmpl_ref)
     done_ref[...] = jnp.zeros_like(done_ref)
 
 
@@ -282,7 +279,7 @@
     at_ref, home_ref, got_ref, near_ref, near_swap_ref = refs[:5]
     recv_refs, swap_refs = refs[5 : 5 + n_op], refs[5 + n_op : 5 + 2 * n_op]
     w_ref, tmpl_ref, plane_ref, line_ref, back_ref, inverse_ref = refs[5 + 2 * n_op : 11 + 2 * n_op]
-    _, _, out_ref, data_ref, vol_ref, mid_ref = refs[11 + 2 * n_op :]
+    _, out_ref, data_ref, vol_ref, mid_ref = refs[11 + 2 * n_op :]
     chip, core = at_ref[0], at_ref[1]
     mate = 1 - core
     data_ref[chip * XT + core] = home_ref[...]
@@ -422,17 +419,6 @@
             compiler_params=limit(8),
         )(mine, got)
         arrived = [lax.ppermute(p, "tile", route(m)) for p, m in zip(payload, masks)]
-        weights, done_w = pl.pallas_call(
-            lambda *refs: weight_kernel(n_det, n_tile, pairs, *refs),
-            out_shape=(shape(n_pair, depth, LB), shape(8, 128, dtype=F32)),
-            in_specs=[SMEM, SMEM, VMEM],
-            out_specs=(VMEM,) * 2,
-            scratch_shapes=[pltpu.VMEM((depth, LB), BF)] * 2,
-            compiler_params=limit(16),
-            cost_estimate=cost(1 << 32, 9 << 20),
-        )(at, turns, merged)
-        last = arrived[-1]
-        near_in, done_w, *arrived = lax.optimization_barrier((near_in, done_w, *arrived[:-1]))
         constants = (
             rot_index,
             template_bank,
@@ -440,32 +426,34 @@
             jnp.asarray(line_t),
             jnp.asarray(tables[4], F32),
         )
-        plane, inverse, spectra, done_t = pl.pallas_call(
-            table_kernel,
+        weights, plane, inverse, spectra, done = pl.pallas_call(
+            lambda *refs: prepare_kernel(n_det, n_tile, pairs, *refs),
             out_shape=(
+                shape(n_pair, depth, LB),
                 shape(VH, 2 * FP),
                 shape(2 * FP, OH),
                 shape(NTPL, 2 * LEN, FP),
                 shape(8, 128, dtype=F32),
             ),
-            in_specs=[SMEM, VMEM] + [HBM] * 8,
-            out_specs=(VMEM,) * 4,
+            in_specs=[SMEM, SMEM, VMEM] + [HBM] * 8,
+            out_specs=(VMEM,) * 5,
             scratch_shapes=[
                 pltpu.SMEM((NTPL,), jnp.int32),
                 *[pltpu.VMEM(c.shape, c.dtype) for c in constants[1:]],
                 pltpu.SemaphoreType.DMA((8,)),
+                pltpu.VMEM((depth, LB), BF),
+                pltpu.VMEM((depth, LB), BF),
             ],
-            compiler_params=limit(20),
-            cost_estimate=cost(1 << 32, 8 << 20),
-        )(at, done_w, *[pinned(c) for c in constants])
-        last, done_t = lax.optimization_barrier((last, done_t))
-        arrived.append(last)
+            compiler_params=limit(24),
+            cost_estimate=cost(1 << 32, 16 << 20),
+        )(at, turns, merged, *[pinned(c) for c in constants])
+        near_in, done, *arrived = lax.optimization_barrier((near_in, done, *arrived))
         near_swap = lax.ppermute(near_in, "tile", mate)
         swapped = [lax.ppermute(a, "tile", mate) for a in arrived]
         return pl.pallas_call(
             lambda *refs: score_kernel(near_bit, masks, pairs, n_tile, *refs),
             out_shape=shape(1, EDGE, EDGE * Z, dtype=F32),
-            in_specs=[SMEM] + [VMEM] * (12 + 2 * n_op),
+            in_specs=[SMEM] + [VMEM] * (11 + 2 * n_op),
             out_specs=VMEM,
             scratch_shapes=[
                 pltpu.VMEM((n_tile, LEN, depth), BF),
@@ -488,8 +476,7 @@
             jnp.asarray(line),
             jnp.asarray(back),
             inverse,
-            done_w,
-            done_t,
+            done,
         )
 
     return jax.shard_map(

time: 26.7 us -> 24.1 us (0.903)
  Pallas kernels: 14.1 us -> 12.3 us
  waiting for transfers between devices: 1.71 us -> 0.9 us
    pallas_call x2 -> x1, Pallas kernels: 7.28 us -> 5.54 us  [local(): pl.pallas_call(lambda *refs: prepare_kernel(n_det, n_tile, pairs, *refs),...]
    ppermute x3, waiting for transfers between devices: 0.81 us -> 0.01 us  [local(): lax.ppermute(p, 'tile', route(m))]
  transfers between devices with their start and end apart: 9 -> 9, of which waited for: 2 -> 1; matrix products, arithmetic and copies ran while one was open for 0% -> 0% of each run, Pallas kernels for 28% -> 23%
where the time goes in v6:
time: 24.1 us; the launch traced here: 23.7 us
  Pallas kernels  12.3 us (51%)
  starting transfers between devices  10.3 us (43%)
  waiting for transfers between devices  0.9 us (4%)
    pallas_call x1, Pallas kernels, local(): pl.pallas_call(lambda *refs: prepare_kernel(n_det, n_tile, pairs, *refs),...  5.54 us
    ppermute x3, starting transfers between devices, local(): lax.ppermute(p, 'tile', route(m))  5.28 us
    pallas_call x1, Pallas kernels, local(): pl.pallas_call(lambda *refs: score_kernel(near_bit, masks, pairs, n_tile,...  5.03 us
    ppermute x1, starting transfers between devices, local(): near_in = lax.ppermute(near, 'tile', near_pairs)  3.77 us
    pallas_call x1, Pallas kernels, local(): pl.pallas_call(lambda *refs: pack_kernel(near_bit, masks, *refs), out_sha...  1.74 us
    ppermute x1, waiting for transfers between devices, local(): near_swap = lax.ppermute(near_in, 'tile', mate)  0.88 us
    ppermute x3, starting transfers between devices, local(): swapped = [lax.ppermute(a, 'tile', mate) for a in arrived]  0.65 us
  transfers between devices with their start and end apart: 9, of which 1 were waited for; matrix products, arithmetic and copies ran while one was open for 0% of the time, Pallas kernels for 23%

profile of v6, /device:TPU:1, one launch (start us, length us, event | category | flops | bytes accessed | tf_op | source)
XLA Modules:
  0.0 23.7 jit_solution(11784942625022174943)
XLA Ops:
  0.0 0.1 pad_add_fusion.refs_0_
  0.1 1.7 %shard_map.127 = (f32[2,61]{1,0:T(2,128)S(1)}, bf16[48,512]{1,0:T(8,128)(2,1)S(1)}, bf16[48,512]{1,0:T(8,128)(2,1)S(1)}, bf16[4,48,512]{2,1,0:T(8,128)(2,1)S(1)}, bf16[3,48,512]{2,1,0:T(8,128)(2,1)S(1)}) custom-call(s32[2]{0:T(128)S(1)} %pad_add_fusion.refs_0_, s32[2,61]{1,0:T(2,128)} %bitcast.6, f32[1,61]{1,0:T(1,128)} %bitcast.7, bf16[61,8,256]{2,1,0:T(8,128)(2,1)} %bitcast.5), custom_call_target="tpu_custom_call" | custom-call | tf_op jit(solution)/shard_map/pallas_call | solution.py:392
  1.8 0.1 collective-permute-start
  1.9 3.8 %collective-permute-start.1 = (bf16[48,512]{1,0:T(8,128)(2,1)S(1)}, bf16[48,512]{1,0:T(8,128)(2,1)S(1)}, u32[]{:S(2)}, u32[]{:S(2)}) collective-permute-start(bf16[48,512]{1,0:T(8,128)(2,1)S(1)} %get-tuple-element.26), channel_id=1, source_target_pairs={{0,8},{1,9},{2,10},{3,11},{4,12},{5,13},{6,14},{7,15},{8,0},{9,1},... | collective-permute-start | bytes 147464 | tf_op jit(solution)/shard_map/ppermute | solution.py:413
  5.7 0.0 collective-permute-done.got_ref.refs_2_
  5.7 2.1 %collective-permute-start.2 = (bf16[2,48,512]{2,1,0:T(8,128)(2,1)S(1)}, bf16[2,48,512]{2,1,0:T(8,128)(2,1)S(1)}, u32[]{:S(2)}, u32[]{:S(2)}) collective-permute-start(bf16[2,48,512]{2,1,0:T(8,128)(2,1)S(1)} %get-tuple-element.31), channel_id=1, source_target_pairs={{0,2},{1,11},{2,0},{3,9},{4,6},{5,15},{6,4},{7,13},{8,10},{9,3},{1... | collective-permute-start | bytes 294920 | tf_op jit(solution)/shard_map/ppermute | solution.py:421
  7.8 2.3 %collective-permute-start.3 = (bf16[2,48,512]{2,1,0:T(8,128)(2,1)S(1)}, bf16[2,48,512]{2,1,0:T(8,128)(2,1)S(1)}, u32[]{:S(2)}, u32[]{:S(2)}) collective-permute-start(bf16[2,48,512]{2,1,0:T(8,128)(2,1)S(1)} %get-tuple-element.32), channel_id=1, source_target_pairs={{0,4},{1,13},{2,6},{3,15},{4,0},{5,9},{6,2},{7,11},{8,12},{9,5},{1... | collective-permute-start | bytes 294920 | tf_op jit(solution)/shard_map/ppermute | solution.py:421
  10.1 0.9 %collective-permute-start.4 = (bf16[2,48,512]{2,1,0:T(8,128)(2,1)S(1)}, bf16[2,48,512]{2,1,0:T(8,128)(2,1)S(1)}, u32[]{:S(2)}, u32[]{:S(2)}) collective-permute-start(bf16[2,48,512]{2,1,0:T(8,128)(2,1)S(1)} %get-tuple-element.33), channel_id=1, source_target_pairs={{0,6},{1,15},{2,4},{3,13},{4,2},{5,11},{6,0},{7,9},{8,14},{9,7},{1... | collective-permute-start | bytes 294920 | tf_op jit(solution)/shard_map/ppermute | solution.py:421
  11.0 5.5 %shard_map.129 = (bf16[34,512,256]{2,1,0:T(8,128)(2,1)S(1)}, bf16[640,2048]{1,0:T(8,128)(2,1)S(1)}, bf16[2048,512]{1,0:T(8,128)(2,1)S(1)}, bf16[8,96,1024]{2,1,0:T(8,128)(2,1)S(1)}, f32[8,128]{1,0:T(8,128)S(1)}) custom-call(s32[2]{0:T(128)S(1)} %pad_add_fusion.refs_0_, f32[2,61]{1,0:T(2,128)S(1)} %get-tuple-element.27.refs_1_, ...), custom_call_target="tpu_custom_call" | custom-call | flops 4294967296 | bytes 16777216 | tf_op jit(solution)/shard_map/pallas_call | solution.py:429
  16.6 0.0 collective-permute-done.1.refs_3_
  16.6 0.0 collective-permute-done.2.refs_5_
  16.6 0.0 collective-permute-done.3.refs_6_
  16.6 0.0 collective-permute-done.4.refs_7_
  16.6 0.1 collective-permute-start.6
  16.7 0.5 %collective-permute-start.7 = (bf16[2,48,512]{2,1,0:T(8,128)(2,1)S(1)}, bf16[2,48,512]{2,1,0:T(8,128)(2,1)S(1)}, u32[]{:S(2)}, u32[]{:S(2)}) collective-permute-start(bf16[2,48,512]{2,1,0:T(8,128)(2,1)S(1)} %collective-permute-done.3.refs_6_), channel_id=1, source_target_pairs={{0,1},{1,0},{2,3},{3,2},{4,5},{5,4},{6,7},{7,6},{8,9},{9,8},{10,11... | collective-permute-start | bytes 294920 | tf_op jit(solution)/shard_map/ppermute | solution.py:452
  17.2 0.1 collective-permute-start.8
  17.3 0.4 %collective-permute-start.5 = (bf16[48,512]{1,0:T(8,128)(2,1)S(1)}, bf16[48,512]{1,0:T(8,128)(2,1)S(1)}, u32[]{:S(2)}, u32[]{:S(2)}) collective-permute-start(bf16[48,512]{1,0:T(8,128)(2,1)S(1)} %collective-permute-done.1.refs_3_), channel_id=1, source_target_pairs={{0,1},{1,0},{2,3},{3,2},{4,5},{5,4},{6,7},{7,6},{8,9},{9,8},{10,11... | collective-permute-start | bytes 147464 | tf_op jit(solution)/shard_map/ppermute | solution.py:451
  17.7 0.9 %collective-permute-done.5.refs_4_ = bf16[48,512]{1,0:T(8,128)(2,1)S(1)} collective-permute-done((bf16[48,512]{1,0:T(8,128)(2,1)S(1)}, bf16[48,512]{1,0:T(8,128)(2,1)S(1)}, u32[]{:S(2)}, u32[]{:S(2)}) %collective-permute-start.5) | collective-permute-done | bytes 49184 | tf_op jit(solution)/shard_map/ppermute | solution.py:451
  18.6 0.0 collective-permute-done.6.refs_8_
  18.6 0.0 collective-permute-done.7.refs_9_
  18.6 0.0 collective-permute-done.8.refs_10_
  18.6 0.0 copy-done
  18.6 0.0 copy-done.1
  18.6 5.0 %shard_map.130 = f32[1,32,1024]{2,1,0:T(8,128)} custom-call(s32[2]{0:T(128)S(1)} %pad_add_fusion.refs_0_, bf16[48,512]{1,0:T(8,128)(2,1)S(1)} %get-tuple-element.24.refs_1_, bf16[4,48,512]{2,1,0:T(8,128)(2,1)S(1)} %collective-permute-done.got_ref.refs_2_, bf16[48,512]{1,0:T(8,128)(2,1)S(1)} %collective-permute-done.1.refs_3_, ...), custom_call_target="tpu_custom_call" | custom-call | flops 4294967296 | bytes 20971520 | tf_op jit(solution)/shard_map/pallas_call | solution.py:453
  (3 shorter events, 0.0 us)
Async XLA Ops:
  1.8 3.9 %collective-permute-start = (bf16[4,48,512]{2,1,0:T(8,128)(2,1)S(1)}, bf16[4,48,512]{2,1,0:T(8,128)(2,1)S(1)}, u32[]{:S(2)}, u32[]{:S(2)}) collective-permute-start(bf16[4,48,512]{2,1,0:T(8,128)(2,1)S(1)} %get-tuple-element.25), channel_id=1, source_target_pairs={{0,1},{1,0},{2,3},{3,2},{4,5},{5,4},{6,7},{7,6},{8,9},{9,8},{10,11... | collective-permute-start | bytes 589832 | tf_op jit(solution)/shard_map/ppermute | solution.py:412
  1.9 14.6 %collective-permute-start.1 = (bf16[48,512]{1,0:T(8,128)(2,1)S(1)}, bf16[48,512]{1,0:T(8,128)(2,1)S(1)}, u32[]{:S(2)}, u32[]{:S(2)}) collective-permute-start(bf16[48,512]{1,0:T(8,128)(2,1)S(1)} %get-tuple-element.26), channel_id=1, source_target_pairs={{0,8},{1,9},{2,10},{3,11},{4,12},{5,13},{6,14},{7,15},{8,0},{9,1},... | collective-permute-start | bytes 147464 | tf_op jit(solution)/shard_map/ppermute | solution.py:413
  5.7 10.8 %collective-permute-start.2 = (bf16[2,48,512]{2,1,0:T(8,128)(2,1)S(1)}, bf16[2,48,512]{2,1,0:T(8,128)(2,1)S(1)}, u32[]{:S(2)}, u32[]{:S(2)}) collective-permute-start(bf16[2,48,512]{2,1,0:T(8,128)(2,1)S(1)} %get-tuple-element.31), channel_id=1, source_target_pairs={{0,2},{1,11},{2,0},{3,9},{4,6},{5,15},{6,4},{7,13},{8,10},{9,3},{1... | collective-permute-start | bytes 294920 | tf_op jit(solution)/shard_map/ppermute | solution.py:421
  7.8 8.8 %collective-permute-start.3 = (bf16[2,48,512]{2,1,0:T(8,128)(2,1)S(1)}, bf16[2,48,512]{2,1,0:T(8,128)(2,1)S(1)}, u32[]{:S(2)}, u32[]{:S(2)}) collective-permute-start(bf16[2,48,512]{2,1,0:T(8,128)(2,1)S(1)} %get-tuple-element.32), channel_id=1, source_target_pairs={{0,4},{1,13},{2,6},{3,15},{4,0},{5,9},{6,2},{7,11},{8,12},{9,5},{1... | collective-permute-start | bytes 294920 | tf_op jit(solution)/shard_map/ppermute | solution.py:421
  10.1 6.5 %collective-permute-start.4 = (bf16[2,48,512]{2,1,0:T(8,128)(2,1)S(1)}, bf16[2,48,512]{2,1,0:T(8,128)(2,1)S(1)}, u32[]{:S(2)}, u32[]{:S(2)}) collective-permute-start(bf16[2,48,512]{2,1,0:T(8,128)(2,1)S(1)} %get-tuple-element.33), channel_id=1, source_target_pairs={{0,6},{1,15},{2,4},{3,13},{4,2},{5,11},{6,0},{7,9},{8,14},{9,7},{1... | collective-permute-start | bytes 294920 | tf_op jit(solution)/shard_map/ppermute | solution.py:421
  11.0 7.6 %copy-start = (bf16[96,96]{1,0:T(8,128)(2,1)S(1)}, bf16[96,96]{1,0:T(8,128)(2,1)}, u32[]{:S(2)}) copy-start(bf16[96,96]{1,0:T(8,128)(2,1)} %constant.50.clone.refs_14_) | copy-start | bytes 55300
  11.0 7.6 %copy-start.1 = (bf16[64,96]{1,0:T(8,128)(2,1)S(1)}, bf16[64,96]{1,0:T(8,128)(2,1)}, u32[]{:S(2)}) copy-start(bf16[64,96]{1,0:T(8,128)(2,1)} %constant.51.clone.refs_15_) | copy-start | bytes 36868
  16.6 2.0 %collective-permute-start.6 = (bf16[2,48,512]{2,1,0:T(8,128)(2,1)S(1)}, bf16[2,48,512]{2,1,0:T(8,128)(2,1)S(1)}, u32[]{:S(2)}, u32[]{:S(2)}) collective-permute-start(bf16[2,48,512]{2,1,0:T(8,128)(2,1)S(1)} %collective-permute-done.2.refs_5_), channel_id=1, source_target_pairs={{0,1},{1,0},{2,3},{3,2},{4,5},{5,4},{6,7},{7,6},{8,9},{9,8},{10,11... | collective-permute-start | bytes 294920 | tf_op jit(solution)/shard_map/ppermute | solution.py:452
  16.7 1.9 %collective-permute-start.7 = (bf16[2,48,512]{2,1,0:T(8,128)(2,1)S(1)}, bf16[2,48,512]{2,1,0:T(8,128)(2,1)S(1)}, u32[]{:S(2)}, u32[]{:S(2)}) collective-permute-start(bf16[2,48,512]{2,1,0:T(8,128)(2,1)S(1)} %collective-permute-done.3.refs_6_), channel_id=1, source_target_pairs={{0,1},{1,0},{2,3},{3,2},{4,5},{5,4},{6,7},{7,6},{8,9},{9,8},{10,11... | collective-permute-start | bytes 294920 | tf_op jit(solution)/shard_map/ppermute | solution.py:452
  17.2 1.4 %collective-permute-start.8 = (bf16[2,48,512]{2,1,0:T(8,128)(2,1)S(1)}, bf16[2,48,512]{2,1,0:T(8,128)(2,1)S(1)}, u32[]{:S(2)}, u32[]{:S(2)}) collective-permute-start(bf16[2,48,512]{2,1,0:T(8,128)(2,1)S(1)} %collective-permute-done.4.refs_7_), channel_id=1, source_target_pairs={{0,1},{1,0},{2,3},{3,2},{4,5},{5,4},{6,7},{7,6},{8,9},{9,8},{10,11... | collective-permute-start | bytes 294920 | tf_op jit(solution)/shard_map/ppermute | solution.py:452
  17.3 1.3 %collective-permute-start.5 = (bf16[48,512]{1,0:T(8,128)(2,1)S(1)}, bf16[48,512]{1,0:T(8,128)(2,1)S(1)}, u32[]{:S(2)}, u32[]{:S(2)}) collective-permute-start(bf16[48,512]{1,0:T(8,128)(2,1)S(1)} %collective-permute-done.1.refs_3_), channel_id=1, source_target_pairs={{0,1},{1,0},{2,3},{3,2},{4,5},{5,4},{6,7},{7,6},{8,9},{9,8},{10,11... | collective-permute-start | bytes 147464 | tf_op jit(solution)/shard_map/ppermute | solution.py:451

commit v7 on v6

--- a/solution.py
+++ b/solution.py
@@ -23,6 +23,8 @@
 KZ = LZ // 2 + 1
 NF = LEN * KZ
 FP = 1024
+TB = 4
+PB = 2
 VH = XR * Z // 2
 OH = EDGE * EDGE // 2
 XB = 8
@@ -101,9 +103,9 @@
     c, s = table(LEN, LEN, 1.0)
     region = rounded(np.block([[c, s], [-s, c]]))
     c, s = table(LEN, K, 1.0)
-    template = rounded(np.block([[c, s], [-s, c]]))
+    template = rounded(np.kron(np.eye(TB), np.block([[c, s], [-s, c]])))
     c, s = table(EDGE, LEN, 1.0)
-    back = rounded(np.block([[c, -s], [s, c]]))
+    back = rounded(np.kron(np.eye(PB), np.block([[c, -s], [s, c]])))
     return region, template, back
 
 
@@ -125,29 +127,35 @@
     rows_ref,
     sem,
 ):
+    n_tilt, n_det, y_count = proj_ref.shape
+    depth = home_ref.shape[1]
+    group = 128 // n_det
+    spans = [(low, min(low + group, n_tilt)) for low in range(0, n_tilt, group)]
     fetch = [
-        pltpu.make_async_copy(range_hbm, range_ref, sem.at[0]),
-        pltpu.make_async_copy(angle_hbm, angle_ref, sem.at[1]),
-        pltpu.make_async_copy(proj_hbm, proj_ref, sem.at[2]),
+        pltpu.make_async_copy(angle_hbm, angle_ref, sem.at[0]),
+        pltpu.make_async_copy(range_hbm, range_ref, sem.at[1]),
     ]
-    for copy in fetch:
+    for i, (low, top) in enumerate(spans):
+        at = pl.ds(low, top - low)
+        fetch.append(pltpu.make_async_copy(proj_hbm.at[at], proj_ref.at[at], sem.at[2 + i]))
+    for copy in fetch[1:] + fetch[:1]:
         copy.start()
-    fetch[1].wait()
+    fetch[0].wait()
     turns_ref[0:1] = jnp.cos(angle_ref[...])
     turns_ref[1:2] = jnp.sin(angle_ref[...])
-    fetch[0].wait()
-    fetch[2].wait()
-    n_tilt, n_det, y_count = proj_ref.shape
-    depth = home_ref.shape[1]
+    fetch[1].wait()
     y = lax.broadcasted_iota(jnp.int32, (n_det, y_count), 1)
-    parts = []
-    for t in range(n_tilt):
-        keep = (y >= range_ref[0, t]) & (y < range_ref[1, t])
-        parts.append(jnp.where(keep, proj_ref[t].astype(F32), 0.0))
-    if depth > n_tilt * n_det:
-        parts.append(jnp.zeros((depth - n_tilt * n_det, y_count), F32))
-    edge = jnp.zeros((HALO, depth), F32)
-    rows_ref[...] = jnp.concatenate([edge, jnp.concatenate(parts, 0).T, edge], 0).astype(BF)
+    edge = jnp.zeros((HALO, 128), F32)
+    for i, (low, top) in enumerate(spans):
+        fetch[2 + i].wait()
+        parts = []
+        for t in range(low, top):
+            keep = (y >= range_ref[0, t]) & (y < range_ref[1, t])
+            parts.append(jnp.where(keep, proj_ref[t].astype(F32), 0.0))
+        if (top - low) * n_det < 128:
+            parts.append(jnp.zeros((128 - (top - low) * n_det, y_count), F32))
+        block = jnp.concatenate([edge, jnp.concatenate(parts, 0).T, edge], 0)
+        rows_ref[:, i * 128 : (i + 1) * 128] = block.astype(BF)
     chip, core = at_ref[0], at_ref[1]
 
     def rows(target):
@@ -247,13 +255,18 @@
     flat = jnp.dot(chosen, plane, preferred_element_type=F32).astype(BF)
     cos = jnp.where(col == 0, turn_ref[0, 0:1], turn_ref[0, 1:2])
     sin = jnp.where(col == 0, turn_ref[1, 0:1], turn_ref[1, 1:2])
-    for r in range(NTPL):
-        part = flat[r * K : (r + 1) * K]
-        stacked = jnp.concatenate([part[:, :FP], part[:, FP:]], 0)
+    for first in range(0, NTPL, TB):
+        stacked = []
+        for r in range(first, first + TB):
+            part = flat[r * K : (r + 1) * K]
+            stacked += [part[:, :FP], part[:, FP:]]
+        stacked = jnp.concatenate(stacked, 0)
         full = jnp.dot(line_ref[...], stacked, preferred_element_type=F32)
-        real, imag = full[:LEN], -full[LEN:]
-        out_ref[r, :LEN] = (real * cos - imag * sin).astype(BF)
-        out_ref[r, LEN:] = (real * sin + imag * cos).astype(BF)
+        for i in range(TB):
+            low = i * 2 * LEN
+            real, imag = full[low : low + LEN], -full[low + LEN : low + 2 * LEN]
+            out_ref[first + i, :LEN] = (real * cos - imag * sin).astype(BF)
+            out_ref[first + i, LEN:] = (real * sin + imag * cos).astype(BF)
 
 
 def prepare_kernel(n_det, n_tile, pairs, at_ref, turns_ref, _, *refs):
@@ -316,19 +329,19 @@
     )
     full = jnp.dot(line_ref[...], stacked, preferred_element_type=F32)
     real, imag = full[:LEN], full[LEN:]
-    for r in range(NTPL):
-        t_real = tmpl_ref[r, :LEN].astype(F32)
-        t_imag = tmpl_ref[r, LEN:].astype(F32)
-        prod = jnp.concatenate(
-            [
-                (t_real * real - t_imag * imag).astype(BF),
-                (t_real * imag + t_imag * real).astype(BF),
-            ],
-            0,
-        )
+    for first in range(0, NTPL, PB):
+        prod = []
+        for r in range(first, first + PB):
+            t_real = tmpl_ref[r, :LEN].astype(F32)
+            t_imag = tmpl_ref[r, LEN:].astype(F32)
+            prod.append((t_real * real - t_imag * imag).astype(BF))
+            prod.append((t_real * imag + t_imag * real).astype(BF))
+        prod = jnp.concatenate(prod, 0)
         line = jnp.dot(back_ref[...], prod, preferred_element_type=F32).astype(BF)
-        mid_ref[r * EDGE : (r + 1) * EDGE, :FP] = line[:EDGE]
-        mid_ref[r * EDGE : (r + 1) * EDGE, FP:] = line[EDGE:]
+        for i in range(PB):
+            at = slice((first + i) * EDGE, (first + i + 1) * EDGE)
+            mid_ref[at, :FP] = line[2 * i * EDGE : (2 * i + 1) * EDGE]
+            mid_ref[at, FP:] = line[(2 * i + 1) * EDGE : (2 * i + 2) * EDGE]
     even = jnp.dot(mid_ref[:, :FP], inverse_ref[:FP], preferred_element_type=F32)
     odd = jnp.dot(mid_ref[:, FP:], inverse_ref[FP:], preferred_element_type=F32)
     best = even[:EDGE] + odd[:EDGE]
@@ -405,7 +418,7 @@
                 pltpu.VMEM((1, NTILT), F32),
                 pltpu.SMEM((2, NTILT), jnp.int32),
                 pltpu.VMEM((y_count + 2 * HALO, depth), BF),
-                pltpu.SemaphoreType.DMA((3,)),
+                pltpu.SemaphoreType.DMA((2 + depth // 128,)),
             ],
             compiler_params=limit(8),
         )(at, pinned(row_range.T), pinned(tilt_angle.reshape(1, NTILT)), pinned(by_y))

time: 24.1 us -> 24.3 us (level)
  no operation moved by 1% of the time
where the time goes in v7:
time: 24.3 us; the launch traced here: 23.9 us
  Pallas kernels  12.5 us (51%)
  starting transfers between devices  10.3 us (42%)
  waiting for transfers between devices  0.9 us (4%)
    pallas_call x1, Pallas kernels, local(): pl.pallas_call(lambda *refs: prepare_kernel(n_det, n_tile, pairs, *refs),...  5.54 us
    ppermute x3, starting transfers between devices, local(): lax.ppermute(p, 'tile', route(m))  5.28 us
    pallas_call x1, Pallas kernels, local(): pl.pallas_call(lambda *refs: score_kernel(near_bit, masks, pairs, n_tile,...  5.06 us
    ppermute x1, starting transfers between devices, local(): near_in = lax.ppermute(near, 'tile', near_pairs)  3.77 us
    pallas_call x1, Pallas kernels, local(): pl.pallas_call(lambda *refs: pack_kernel(near_bit, masks, *refs), out_sha...  1.9 us
    ppermute x1, waiting for transfers between devices, local(): near_swap = lax.ppermute(near_in, 'tile', mate)  0.88 us
    ppermute x3, starting transfers between devices, local(): swapped = [lax.ppermute(a, 'tile', mate) for a in arrived]  0.65 us
  transfers between devices with their start and end apart: 9, of which 1 were waited for; matrix products, arithmetic and copies ran while one was open for 0% of the time, Pallas kernels for 23%

profile of v7, /device:TPU:1, one launch (start us, length us, event | category | flops | bytes accessed | tf_op | source)
XLA Modules:
  0.0 23.9 jit_solution(12883161167004369152)
XLA Ops:
  0.0 0.1 pad_add_fusion.refs_0_
  0.1 1.9 %shard_map.127 = (f32[2,61]{1,0:T(2,128)S(1)}, bf16[48,512]{1,0:T(8,128)(2,1)S(1)}, bf16[48,512]{1,0:T(8,128)(2,1)S(1)}, bf16[4,48,512]{2,1,0:T(8,128)(2,1)S(1)}, bf16[3,48,512]{2,1,0:T(8,128)(2,1)S(1)}) custom-call(s32[2]{0:T(128)S(1)} %pad_add_fusion.refs_0_, s32[2,61]{1,0:T(2,128)} %bitcast.6, f32[1,61]{1,0:T(1,128)} %bitcast.7, bf16[61,8,256]{2,1,0:T(8,128)(2,1)} %bitcast.5), custom_call_target="tpu_custom_call" | custom-call | tf_op jit(solution)/shard_map/pallas_call | solution.py:405
  2.0 0.1 collective-permute-start
  2.1 3.8 %collective-permute-start.1 = (bf16[48,512]{1,0:T(8,128)(2,1)S(1)}, bf16[48,512]{1,0:T(8,128)(2,1)S(1)}, u32[]{:S(2)}, u32[]{:S(2)}) collective-permute-start(bf16[48,512]{1,0:T(8,128)(2,1)S(1)} %get-tuple-element.26), channel_id=1, source_target_pairs={{0,8},{1,9},{2,10},{3,11},{4,12},{5,13},{6,14},{7,15},{8,0},{9,1},... | collective-permute-start | bytes 147464 | tf_op jit(solution)/shard_map/ppermute | solution.py:426
  5.9 0.0 collective-permute-done.got_ref.refs_2_
  5.9 2.1 %collective-permute-start.2 = (bf16[2,48,512]{2,1,0:T(8,128)(2,1)S(1)}, bf16[2,48,512]{2,1,0:T(8,128)(2,1)S(1)}, u32[]{:S(2)}, u32[]{:S(2)}) collective-permute-start(bf16[2,48,512]{2,1,0:T(8,128)(2,1)S(1)} %get-tuple-element.31), channel_id=1, source_target_pairs={{0,2},{1,11},{2,0},{3,9},{4,6},{5,15},{6,4},{7,13},{8,10},{9,3},{1... | collective-permute-start | bytes 294920 | tf_op jit(solution)/shard_map/ppermute | solution.py:434
  8.0 2.3 %collective-permute-start.3 = (bf16[2,48,512]{2,1,0:T(8,128)(2,1)S(1)}, bf16[2,48,512]{2,1,0:T(8,128)(2,1)S(1)}, u32[]{:S(2)}, u32[]{:S(2)}) collective-permute-start(bf16[2,48,512]{2,1,0:T(8,128)(2,1)S(1)} %get-tuple-element.32), channel_id=1, source_target_pairs={{0,4},{1,13},{2,6},{3,15},{4,0},{5,9},{6,2},{7,11},{8,12},{9,5},{1... | collective-permute-start | bytes 294920 | tf_op jit(solution)/shard_map/ppermute | solution.py:434
  10.3 0.9 %collective-permute-start.4 = (bf16[2,48,512]{2,1,0:T(8,128)(2,1)S(1)}, bf16[2,48,512]{2,1,0:T(8,128)(2,1)S(1)}, u32[]{:S(2)}, u32[]{:S(2)}) collective-permute-start(bf16[2,48,512]{2,1,0:T(8,128)(2,1)S(1)} %get-tuple-element.33), channel_id=1, source_target_pairs={{0,6},{1,15},{2,4},{3,13},{4,2},{5,11},{6,0},{7,9},{8,14},{9,7},{1... | collective-permute-start | bytes 294920 | tf_op jit(solution)/shard_map/ppermute | solution.py:434
  11.2 5.5 %shard_map.129 = (bf16[34,512,256]{2,1,0:T(8,128)(2,1)S(1)}, bf16[640,2048]{1,0:T(8,128)(2,1)S(1)}, bf16[2048,512]{1,0:T(8,128)(2,1)S(1)}, bf16[8,96,1024]{2,1,0:T(8,128)(2,1)S(1)}, f32[8,128]{1,0:T(8,128)S(1)}) custom-call(s32[2]{0:T(128)S(1)} %pad_add_fusion.refs_0_, f32[2,61]{1,0:T(2,128)S(1)} %get-tuple-element.27.refs_1_, ...), custom_call_target="tpu_custom_call" | custom-call | flops 4294967296 | bytes 16777216 | tf_op jit(solution)/shard_map/pallas_call | solution.py:442
  16.7 0.0 collective-permute-done.1.refs_3_
  16.8 0.0 collective-permute-done.2.refs_5_
  16.8 0.0 collective-permute-done.3.refs_6_
  16.8 0.0 collective-permute-done.4.refs_7_
  16.8 0.1 collective-permute-start.6
  16.9 0.5 %collective-permute-start.7 = (bf16[2,48,512]{2,1,0:T(8,128)(2,1)S(1)}, bf16[2,48,512]{2,1,0:T(8,128)(2,1)S(1)}, u32[]{:S(2)}, u32[]{:S(2)}) collective-permute-start(bf16[2,48,512]{2,1,0:T(8,128)(2,1)S(1)} %collective-permute-done.3.refs_6_), channel_id=1, source_target_pairs={{0,1},{1,0},{2,3},{3,2},{4,5},{5,4},{6,7},{7,6},{8,9},{9,8},{10,11... | collective-permute-start | bytes 294920 | tf_op jit(solution)/shard_map/ppermute | solution.py:465
  17.4 0.1 collective-permute-start.8
  17.4 0.4 %collective-permute-start.5 = (bf16[48,512]{1,0:T(8,128)(2,1)S(1)}, bf16[48,512]{1,0:T(8,128)(2,1)S(1)}, u32[]{:S(2)}, u32[]{:S(2)}) collective-permute-start(bf16[48,512]{1,0:T(8,128)(2,1)S(1)} %collective-permute-done.1.refs_3_), channel_id=1, source_target_pairs={{0,1},{1,0},{2,3},{3,2},{4,5},{5,4},{6,7},{7,6},{8,9},{9,8},{10,11... | collective-permute-start | bytes 147464 | tf_op jit(solution)/shard_map/ppermute | solution.py:464
  17.9 0.9 %collective-permute-done.5.refs_4_ = bf16[48,512]{1,0:T(8,128)(2,1)S(1)} collective-permute-done((bf16[48,512]{1,0:T(8,128)(2,1)S(1)}, bf16[48,512]{1,0:T(8,128)(2,1)S(1)}, u32[]{:S(2)}, u32[]{:S(2)}) %collective-permute-start.5) | collective-permute-done | bytes 49184 | tf_op jit(solution)/shard_map/ppermute | solution.py:464
  18.8 0.0 collective-permute-done.6.refs_8_
  18.8 0.0 collective-permute-done.7.refs_9_
  18.8 0.0 collective-permute-done.8.refs_10_
  18.8 0.0 copy-done
  18.8 0.0 copy-done.1
  18.8 5.1 %shard_map.130 = f32[1,32,1024]{2,1,0:T(8,128)} custom-call(s32[2]{0:T(128)S(1)} %pad_add_fusion.refs_0_, bf16[48,512]{1,0:T(8,128)(2,1)S(1)} %get-tuple-element.24.refs_1_, bf16[4,48,512]{2,1,0:T(8,128)(2,1)S(1)} %collective-permute-done.got_ref.refs_2_, bf16[48,512]{1,0:T(8,128)(2,1)S(1)} %collective-permute-done.1.refs_3_, ...), custom_call_target="tpu_custom_call" | custom-call | flops 4294967296 | bytes 20971520 | tf_op jit(solution)/shard_map/pallas_call | solution.py:466
  (3 shorter events, 0.0 us)
Async XLA Ops:
  2.0 3.9 %collective-permute-start = (bf16[4,48,512]{2,1,0:T(8,128)(2,1)S(1)}, bf16[4,48,512]{2,1,0:T(8,128)(2,1)S(1)}, u32[]{:S(2)}, u32[]{:S(2)}) collective-permute-start(bf16[4,48,512]{2,1,0:T(8,128)(2,1)S(1)} %get-tuple-element.25), channel_id=1, source_target_pairs={{0,1},{1,0},{2,3},{3,2},{4,5},{5,4},{6,7},{7,6},{8,9},{9,8},{10,11... | collective-permute-start | bytes 589832 | tf_op jit(solution)/shard_map/ppermute | solution.py:425
  2.1 14.6 %collective-permute-start.1 = (bf16[48,512]{1,0:T(8,128)(2,1)S(1)}, bf16[48,512]{1,0:T(8,128)(2,1)S(1)}, u32[]{:S(2)}, u32[]{:S(2)}) collective-permute-start(bf16[48,512]{1,0:T(8,128)(2,1)S(1)} %get-tuple-element.26), channel_id=1, source_target_pairs={{0,8},{1,9},{2,10},{3,11},{4,12},{5,13},{6,14},{7,15},{8,0},{9,1},... | collective-permute-start | bytes 147464 | tf_op jit(solution)/shard_map/ppermute | solution.py:426
  5.9 10.8 %collective-permute-start.2 = (bf16[2,48,512]{2,1,0:T(8,128)(2,1)S(1)}, bf16[2,48,512]{2,1,0:T(8,128)(2,1)S(1)}, u32[]{:S(2)}, u32[]{:S(2)}) collective-permute-start(bf16[2,48,512]{2,1,0:T(8,128)(2,1)S(1)} %get-tuple-element.31), channel_id=1, source_target_pairs={{0,2},{1,11},{2,0},{3,9},{4,6},{5,15},{6,4},{7,13},{8,10},{9,3},{1... | collective-permute-start | bytes 294920 | tf_op jit(solution)/shard_map/ppermute | solution.py:434
  8.0 8.8 %collective-permute-start.3 = (bf16[2,48,512]{2,1,0:T(8,128)(2,1)S(1)}, bf16[2,48,512]{2,1,0:T(8,128)(2,1)S(1)}, u32[]{:S(2)}, u32[]{:S(2)}) collective-permute-start(bf16[2,48,512]{2,1,0:T(8,128)(2,1)S(1)} %get-tuple-element.32), channel_id=1, source_target_pairs={{0,4},{1,13},{2,6},{3,15},{4,0},{5,9},{6,2},{7,11},{8,12},{9,5},{1... | collective-permute-start | bytes 294920 | tf_op jit(solution)/shard_map/ppermute | solution.py:434
  10.3 6.5 %collective-permute-start.4 = (bf16[2,48,512]{2,1,0:T(8,128)(2,1)S(1)}, bf16[2,48,512]{2,1,0:T(8,128)(2,1)S(1)}, u32[]{:S(2)}, u32[]{:S(2)}) collective-permute-start(bf16[2,48,512]{2,1,0:T(8,128)(2,1)S(1)} %get-tuple-element.33), channel_id=1, source_target_pairs={{0,6},{1,15},{2,4},{3,13},{4,2},{5,11},{6,0},{7,9},{8,14},{9,7},{1... | collective-permute-start | bytes 294920 | tf_op jit(solution)/shard_map/ppermute | solution.py:434
  11.2 7.6 %copy-start = (bf16[128,192]{1,0:T(8,128)(2,1)S(1)}, bf16[128,192]{1,0:T(8,128)(2,1)}, u32[]{:S(2)}) copy-start(bf16[128,192]{1,0:T(8,128)(2,1)} %constant.51.clone.refs_15_) | copy-start | bytes 147460
  11.2 7.6 %copy-start.1 = (bf16[96,96]{1,0:T(8,128)(2,1)S(1)}, bf16[96,96]{1,0:T(8,128)(2,1)}, u32[]{:S(2)}) copy-start(bf16[96,96]{1,0:T(8,128)(2,1)} %constant.50.clone.refs_14_) | copy-start | bytes 55300
  16.8 2.0 %collective-permute-start.6 = (bf16[2,48,512]{2,1,0:T(8,128)(2,1)S(1)}, bf16[2,48,512]{2,1,0:T(8,128)(2,1)S(1)}, u32[]{:S(2)}, u32[]{:S(2)}) collective-permute-start(bf16[2,48,512]{2,1,0:T(8,128)(2,1)S(1)} %collective-permute-done.2.refs_5_), channel_id=1, source_target_pairs={{0,1},{1,0},{2,3},{3,2},{4,5},{5,4},{6,7},{7,6},{8,9},{9,8},{10,11... | collective-permute-start | bytes 294920 | tf_op jit(solution)/shard_map/ppermute | solution.py:465
  16.9 1.9 %collective-permute-start.7 = (bf16[2,48,512]{2,1,0:T(8,128)(2,1)S(1)}, bf16[2,48,512]{2,1,0:T(8,128)(2,1)S(1)}, u32[]{:S(2)}, u32[]{:S(2)}) collective-permute-start(bf16[2,48,512]{2,1,0:T(8,128)(2,1)S(1)} %collective-permute-done.3.refs_6_), channel_id=1, source_target_pairs={{0,1},{1,0},{2,3},{3,2},{4,5},{5,4},{6,7},{7,6},{8,9},{9,8},{10,11... | collective-permute-start | bytes 294920 | tf_op jit(solution)/shard_map/ppermute | solution.py:465
  17.4 1.4 %collective-permute-start.8 = (bf16[2,48,512]{2,1,0:T(8,128)(2,1)S(1)}, bf16[2,48,512]{2,1,0:T(8,128)(2,1)S(1)}, u32[]{:S(2)}, u32[]{:S(2)}) collective-permute-start(bf16[2,48,512]{2,1,0:T(8,128)(2,1)S(1)} %collective-permute-done.4.refs_7_), channel_id=1, source_target_pairs={{0,1},{1,0},{2,3},{3,2},{4,5},{5,4},{6,7},{7,6},{8,9},{9,8},{10,11... | collective-permute-start | bytes 294920 | tf_op jit(solution)/shard_map/ppermute | solution.py:465
  17.4 1.3 %collective-permute-start.5 = (bf16[48,512]{1,0:T(8,128)(2,1)S(1)}, bf16[48,512]{1,0:T(8,128)(2,1)S(1)}, u32[]{:S(2)}, u32[]{:S(2)}) collective-permute-start(bf16[48,512]{1,0:T(8,128)(2,1)S(1)} %collective-permute-done.1.refs_3_), channel_id=1, source_target_pairs={{0,1},{1,0},{2,3},{3,2},{4,5},{5,4},{6,7},{7,6},{8,9},{9,8},{10,11... | collective-permute-start | bytes 147464 | tf_op jit(solution)/shard_map/ppermute | solution.py:464

commit v8 on v6

--- a/solution.py
+++ b/solution.py
@@ -107,10 +107,14 @@
     return region, template, back
 
 
+def place():
+    position = lax.axis_index("tile").astype(jnp.int32)
+    return position // XT, position % XT
+
+
 def pack_kernel(
     near_bit,
     masks,
-    at_ref,
     range_hbm,
     angle_hbm,
     proj_hbm,
@@ -133,8 +137,10 @@
     for copy in fetch:
         copy.start()
     fetch[1].wait()
-    turns_ref[0:1] = jnp.cos(angle_ref[...])
-    turns_ref[1:2] = jnp.sin(angle_ref[...])
+    for i, wave in enumerate((jnp.cos, jnp.sin)):
+        spread = jnp.broadcast_to(wave(angle_ref[...]), (128, angle_ref.shape[1])).T
+        turns_ref[i, :, :128] = spread
+        turns_ref[i, :, 128:] = spread
     fetch[0].wait()
     fetch[2].wait()
     n_tilt, n_det, y_count = proj_ref.shape
@@ -148,7 +154,7 @@
         parts.append(jnp.zeros((depth - n_tilt * n_det, y_count), F32))
     edge = jnp.zeros((HALO, depth), F32)
     rows_ref[...] = jnp.concatenate([edge, jnp.concatenate(parts, 0).T, edge], 0).astype(BF)
-    chip, core = at_ref[0], at_ref[1]
+    chip, core = place()
 
     def rows(target):
         return rows_ref[pl.ds(pl.multiple_of(target * EDGE, EDGE), LEN)]
@@ -187,7 +193,7 @@
         z = VOXEL * (z.astype(F32) - (Z - 1) / 2.0)
 
         def tilt(t, z=z, x=x):
-            pos = x * turns_ref[0, t] + z * turns_ref[1, t] + (NDET - 1) / 2.0
+            pos = x * turns_ref[0, t : t + 1] + z * turns_ref[1, t : t + 1] + (NDET - 1) / 2.0
             whole = jnp.floor(pos)
             return own - whole, pos - whole
 
@@ -256,7 +262,7 @@
         out_ref[r, LEN:] = (real * sin + imag * cos).astype(BF)
 
 
-def prepare_kernel(n_det, n_tile, pairs, at_ref, turns_ref, _, *refs):
+def prepare_kernel(n_det, n_tile, pairs, turns_ref, _, *refs):
     sources, outs, targets, (sem, whole_ref, part_ref) = refs[:8], refs[8:13], refs[13:21], refs[21:]
     fetch = [
         pltpu.make_async_copy(a, b, sem.at[i]) for i, (a, b) in enumerate(zip(sources, targets))
@@ -264,7 +270,7 @@
     for copy in fetch:
         copy.start()
     w_ref, plane_ref, inverse_ref, tmpl_ref, done_ref = outs
-    col = at_ref[1]
+    _, col = place()
     build_weights(n_det, n_tile, pairs, col, turns_ref, w_ref, whole_ref, part_ref)
     for copy in fetch:
         copy.wait()
@@ -276,11 +282,11 @@
 
 def score_kernel(near_bit, masks, pairs, n_tile, *refs):
     n_op = len(masks)
-    at_ref, home_ref, got_ref, near_ref, near_swap_ref = refs[:5]
-    recv_refs, swap_refs = refs[5 : 5 + n_op], refs[5 + n_op : 5 + 2 * n_op]
-    w_ref, tmpl_ref, plane_ref, line_ref, back_ref, inverse_ref = refs[5 + 2 * n_op : 11 + 2 * n_op]
-    _, out_ref, data_ref, vol_ref, mid_ref = refs[11 + 2 * n_op :]
-    chip, core = at_ref[0], at_ref[1]
+    home_ref, got_ref, near_ref, near_swap_ref = refs[:4]
+    recv_refs, swap_refs = refs[4 : 4 + n_op], refs[4 + n_op : 4 + 2 * n_op]
+    w_ref, tmpl_ref, plane_ref, line_ref, back_ref, inverse_ref = refs[4 + 2 * n_op : 10 + 2 * n_op]
+    _, out_ref, data_ref, vol_ref, mid_ref = refs[10 + 2 * n_op :]
+    chip, core = place()
     mate = 1 - core
     data_ref[chip * XT + core] = home_ref[...]
     data_ref[chip * XT + mate] = got_ref[0]
@@ -386,19 +392,17 @@
 
     def local(projections, tilt_angle, row_range, template_bank, rot_index):
         y_count = projections.shape[0]
-        position = lax.axis_index("tile").astype(jnp.int32)
-        at = jnp.stack([position // XT, position % XT])
         by_y = jnp.transpose(projections, (1, 2, 0))
         turns, home, near, give, mine = pl.pallas_call(
             lambda *refs: pack_kernel(near_bit, masks, *refs),
             out_shape=(
-                shape(2, NTILT, dtype=F32),
+                shape(2, NTILT, LB, dtype=F32),
                 shape(LEN, depth),
                 shape(LEN, depth),
                 shape(1 + n_op, LEN, depth),
                 shape(n_op, LEN, depth),
             ),
-            in_specs=[SMEM, HBM, HBM, HBM],
+            in_specs=[HBM, HBM, HBM],
             out_specs=(VMEM,) * 5,
             scratch_shapes=[
                 pltpu.VMEM(by_y.shape, BF),
@@ -408,7 +412,7 @@
                 pltpu.SemaphoreType.DMA((3,)),
             ],
             compiler_params=limit(8),
-        )(at, pinned(row_range.T), pinned(tilt_angle.reshape(1, NTILT)), pinned(by_y))
+        )(pinned(row_range.T), pinned(tilt_angle.reshape(1, NTILT)), pinned(by_y))
         got = lax.ppermute(give, "tile", mate)
         near_in = lax.ppermute(near, "tile", near_pairs)
         merged, *payload = pl.pallas_call(
@@ -435,7 +439,7 @@
                 shape(NTPL, 2 * LEN, FP),
                 shape(8, 128, dtype=F32),
             ),
-            in_specs=[SMEM, SMEM, VMEM] + [HBM] * 8,
+            in_specs=[VMEM, VMEM] + [HBM] * 8,
             out_specs=(VMEM,) * 5,
             scratch_shapes=[
                 pltpu.SMEM((NTPL,), jnp.int32),
@@ -446,14 +450,14 @@
             ],
             compiler_params=limit(24),
             cost_estimate=cost(1 << 32, 16 << 20),
-        )(at, turns, merged, *[pinned(c) for c in constants])
+        )(turns, merged, *[pinned(c) for c in constants])
         near_in, done, *arrived = lax.optimization_barrier((near_in, done, *arrived))
         near_swap = lax.ppermute(near_in, "tile", mate)
         swapped = [lax.ppermute(a, "tile", mate) for a in arrived]
         return pl.pallas_call(
             lambda *refs: score_kernel(near_bit, masks, pairs, n_tile, *refs),
             out_shape=shape(1, EDGE, EDGE * Z, dtype=F32),
-            in_specs=[SMEM] + [VMEM] * (11 + 2 * n_op),
+            in_specs=[VMEM] * (11 + 2 * n_op),
             out_specs=VMEM,
             scratch_shapes=[
                 pltpu.VMEM((n_tile, LEN, depth), BF),
@@ -463,7 +467,6 @@
             compiler_params=limit(28),
             cost_estimate=cost(4 << 30, 20 << 20),
         )(
-            at,
             home,
             got,
             near_in,

time: 24.1 us -> 22.7 us (0.942)
  Pallas kernels: 12.3 us -> 10.7 us
  waiting for transfers between devices: 0.9 us -> 1.26 us
    pallas_call x1, Pallas kernels: 5.54 us -> 4.91 us  [local(): pl.pallas_call(lambda *refs: prepare_kernel(n_det, n_tile, pairs, *refs),...]
    pallas_call x1, Pallas kernels: 1.74 us -> 1.21 us  [local(): pl.pallas_call(lambda *refs: pack_kernel(near_bit, masks, *refs), out_sha...]
    pallas_call x1, Pallas kernels: 5.03 us -> 4.55 us  [local(): pl.pallas_call(lambda *refs: score_kernel(near_bit, masks, pairs, n_tile,...]
    ppermute x3, waiting for transfers between devices: 0.01 us -> 0.37 us  [local(): lax.ppermute(p, 'tile', route(m))]
  transfers between devices with their start and end apart: 9 -> 9, of which waited for: 1 -> 2; matrix products, arithmetic and copies ran while one was open for 0% -> 0% of each run, Pallas kernels for 23% -> 22%
where the time goes in v8:
time: 22.7 us; the launch traced here: 22.2 us
  Pallas kernels  10.7 us (47%)
  starting transfers between devices  10.2 us (45%)
  waiting for transfers between devices  1.26 us (6%)
    ppermute x3, starting transfers between devices, local(): lax.ppermute(p, 'tile', route(m))  5.28 us
    pallas_call x1, Pallas kernels, local(): pl.pallas_call(lambda *refs: prepare_kernel(n_det, n_tile, pairs, *refs),...  4.91 us
    pallas_call x1, Pallas kernels, local(): pl.pallas_call(lambda *refs: score_kernel(near_bit, masks, pairs, n_tile,...  4.55 us
    ppermute x1, starting transfers between devices, local(): near_in = lax.ppermute(near, 'tile', near_pairs)  3.77 us
    pallas_call x1, Pallas kernels, local(): pl.pallas_call(lambda *refs: pack_kernel(near_bit, masks, *refs), out_sha...  1.21 us
    ppermute x1, waiting for transfers between devices, local(): near_swap = lax.ppermute(near_in, 'tile', mate)  0.88 us
    ppermute x3, starting transfers between devices, local(): swapped = [lax.ppermute(a, 'tile', mate) for a in arrived]  0.51 us
    ppermute x1, starting transfers between devices, local(): near_swap = lax.ppermute(near_in, 'tile', mate)  0.51 us
  transfers between devices with their start and end apart: 9, of which 2 were waited for; matrix products, arithmetic and copies ran while one was open for 0% of the time, Pallas kernels for 22%

profile of v8, /device:TPU:1, one launch (start us, length us, event | category | flops | bytes accessed | tf_op | source)
XLA Modules:
  0.0 22.2 jit_solution(15180893556851878809)
XLA Ops:
  0.0 1.2 %shard_map.127 = (f32[2,61,256]{2,1,0:T(8,128)S(1)}, bf16[48,512]{1,0:T(8,128)(2,1)S(1)}, bf16[48,512]{1,0:T(8,128)(2,1)S(1)}, bf16[4,48,512]{2,1,0:T(8,128)(2,1)S(1)}, bf16[3,48,512]{2,1,0:T(8,128)(2,1)S(1)}) custom-call(s32[2,61]{1,0:T(2,128)} %bitcast.4, f32[1,61]{1,0:T(1,128)} %bitcast.5, bf16[61,8,256]{2,1,0:T(8,128)(2,1)} %bitcast.3), custom_call_target="tpu_custom_call" | custom-call | tf_op jit(solution)/shard_map/pallas_call | solution.py:396
  1.2 0.1 collective-permute-start
  1.3 3.8 %collective-permute-start.1 = (bf16[48,512]{1,0:T(8,128)(2,1)S(1)}, bf16[48,512]{1,0:T(8,128)(2,1)S(1)}, u32[]{:S(2)}, u32[]{:S(2)}) collective-permute-start(bf16[48,512]{1,0:T(8,128)(2,1)S(1)} %get-tuple-element.26), channel_id=1, source_target_pairs={{0,8},{1,9},{2,10},{3,11},{4,12},{5,13},{6,14},{7,15},{8,0},{9,1},... | collective-permute-start | bytes 147464 | tf_op jit(solution)/shard_map/ppermute | solution.py:417
  5.1 0.0 collective-permute-done.got_ref.refs_1_
  5.1 2.1 %collective-permute-start.2 = (bf16[2,48,512]{2,1,0:T(8,128)(2,1)S(1)}, bf16[2,48,512]{2,1,0:T(8,128)(2,1)S(1)}, u32[]{:S(2)}, u32[]{:S(2)}) collective-permute-start(bf16[2,48,512]{2,1,0:T(8,128)(2,1)S(1)} %get-tuple-element.31), channel_id=1, source_target_pairs={{0,2},{1,11},{2,0},{3,9},{4,6},{5,15},{6,4},{7,13},{8,10},{9,3},{1... | collective-permute-start | bytes 294920 | tf_op jit(solution)/shard_map/ppermute | solution.py:425
  7.2 2.3 %collective-permute-start.3 = (bf16[2,48,512]{2,1,0:T(8,128)(2,1)S(1)}, bf16[2,48,512]{2,1,0:T(8,128)(2,1)S(1)}, u32[]{:S(2)}, u32[]{:S(2)}) collective-permute-start(bf16[2,48,512]{2,1,0:T(8,128)(2,1)S(1)} %get-tuple-element.32), channel_id=1, source_target_pairs={{0,4},{1,13},{2,6},{3,15},{4,0},{5,9},{6,2},{7,11},{8,12},{9,5},{1... | collective-permute-start | bytes 294920 | tf_op jit(solution)/shard_map/ppermute | solution.py:425
  9.5 0.9 %collective-permute-start.4 = (bf16[2,48,512]{2,1,0:T(8,128)(2,1)S(1)}, bf16[2,48,512]{2,1,0:T(8,128)(2,1)S(1)}, u32[]{:S(2)}, u32[]{:S(2)}) collective-permute-start(bf16[2,48,512]{2,1,0:T(8,128)(2,1)S(1)} %get-tuple-element.33), channel_id=1, source_target_pairs={{0,6},{1,15},{2,4},{3,13},{4,2},{5,11},{6,0},{7,9},{8,14},{9,7},{1... | collective-permute-start | bytes 294920 | tf_op jit(solution)/shard_map/ppermute | solution.py:425
  10.4 0.0 copy-start
  10.4 4.9 %shard_map.129 = (bf16[34,512,256]{2,1,0:T(8,128)(2,1)S(1)}, bf16[640,2048]{1,0:T(8,128)(2,1)S(1)}, bf16[2048,512]{1,0:T(8,128)(2,1)S(1)}, bf16[8,96,1024]{2,1,0:T(8,128)(2,1)S(1)}, f32[8,128]{1,0:T(8,128)S(1)}) custom-call(f32[2,61,256]{2,1,0:T(8,128)S(1)} %get-tuple-element.27.refs_0_, f32[8,128]{1,0:T(8,128)S(1)} %get-tuple-element.29.refs_1_, s32[8]{0:T(128)} %refs_2_.1, ...), custom_call_target="tpu_custom_call" | custom-call | flops 4294967296 | bytes 16777216 | tf_op jit(solution)/shard_map/pallas_call | solution.py:433
  15.3 0.0 collective-permute-done.1.refs_2_
  15.4 0.0 collective-permute-done.2.refs_4_
  15.4 0.0 collective-permute-done.3.refs_5_
  15.4 0.4 %collective-permute-done.4.refs_6_ = bf16[2,48,512]{2,1,0:T(8,128)(2,1)S(1)} collective-permute-done((bf16[2,48,512]{2,1,0:T(8,128)(2,1)S(1)}, bf16[2,48,512]{2,1,0:T(8,128)(2,1)S(1)}, u32[]{:S(2)}, u32[]{:S(2)}) %collective-permute-start.4) | collective-permute-done | bytes 98336 | tf_op jit(solution)/shard_map/ppermute | solution.py:425
  15.7 0.0 collective-permute-start.6
  15.7 0.5 %collective-permute-start.7 = (bf16[2,48,512]{2,1,0:T(8,128)(2,1)S(1)}, bf16[2,48,512]{2,1,0:T(8,128)(2,1)S(1)}, u32[]{:S(2)}, u32[]{:S(2)}) collective-permute-start(bf16[2,48,512]{2,1,0:T(8,128)(2,1)S(1)} %collective-permute-done.3.refs_5_), channel_id=1, source_target_pairs={{0,1},{1,0},{2,3},{3,2},{4,5},{5,4},{6,7},{7,6},{8,9},{9,8},{10,11... | collective-permute-start | bytes 294920 | tf_op jit(solution)/shard_map/ppermute | solution.py:456
  16.3 0.0 collective-permute-start.8
  16.3 0.5 %collective-permute-start.5 = (bf16[48,512]{1,0:T(8,128)(2,1)S(1)}, bf16[48,512]{1,0:T(8,128)(2,1)S(1)}, u32[]{:S(2)}, u32[]{:S(2)}) collective-permute-start(bf16[48,512]{1,0:T(8,128)(2,1)S(1)} %collective-permute-done.1.refs_2_), channel_id=1, source_target_pairs={{0,1},{1,0},{2,3},{3,2},{4,5},{5,4},{6,7},{7,6},{8,9},{9,8},{10,11... | collective-permute-start | bytes 147464 | tf_op jit(solution)/shard_map/ppermute | solution.py:455
  16.8 0.9 %collective-permute-done.5.refs_3_ = bf16[48,512]{1,0:T(8,128)(2,1)S(1)} collective-permute-done((bf16[48,512]{1,0:T(8,128)(2,1)S(1)}, bf16[48,512]{1,0:T(8,128)(2,1)S(1)}, u32[]{:S(2)}, u32[]{:S(2)}) %collective-permute-start.5) | collective-permute-done | bytes 49184 | tf_op jit(solution)/shard_map/ppermute | solution.py:455
  17.6 0.0 collective-permute-done.6.refs_7_
  17.6 0.0 collective-permute-done.7.refs_8_
  17.7 0.0 collective-permute-done.8.refs_9_
  17.7 0.0 copy-done
  17.7 0.0 copy-done.1
  17.7 4.5 %shard_map.130 = f32[1,32,1024]{2,1,0:T(8,128)} custom-call(bf16[48,512]{1,0:T(8,128)(2,1)S(1)} %get-tuple-element.24.refs_0_, bf16[4,48,512]{2,1,0:T(8,128)(2,1)S(1)} %collective-permute-done.got_ref.refs_1_, bf16[48,512]{1,0:T(8,128)(2,1)S(1)} %collective-permute-done.1.refs_2_, bf16[48,512]{1,0:T(8,128)(2,1)S(1)} %collective-permute-done.5.refs_3_, ...), custom_call_target="tpu_custom_call" | custom-call | flops 4294967296 | bytes 20971520 | tf_op jit(solution)/shard_map/pallas_call | solution.py:457
  (2 shorter events, 0.0 us)
Async XLA Ops:
  1.2 3.9 %collective-permute-start = (bf16[4,48,512]{2,1,0:T(8,128)(2,1)S(1)}, bf16[4,48,512]{2,1,0:T(8,128)(2,1)S(1)}, u32[]{:S(2)}, u32[]{:S(2)}) collective-permute-start(bf16[4,48,512]{2,1,0:T(8,128)(2,1)S(1)} %get-tuple-element.25), channel_id=1, source_target_pairs={{0,1},{1,0},{2,3},{3,2},{4,5},{5,4},{6,7},{7,6},{8,9},{9,8},{10,11... | collective-permute-start | bytes 589832 | tf_op jit(solution)/shard_map/ppermute | solution.py:416
  1.3 14.0 %collective-permute-start.1 = (bf16[48,512]{1,0:T(8,128)(2,1)S(1)}, bf16[48,512]{1,0:T(8,128)(2,1)S(1)}, u32[]{:S(2)}, u32[]{:S(2)}) collective-permute-start(bf16[48,512]{1,0:T(8,128)(2,1)S(1)} %get-tuple-element.26), channel_id=1, source_target_pairs={{0,8},{1,9},{2,10},{3,11},{4,12},{5,13},{6,14},{7,15},{8,0},{9,1},... | collective-permute-start | bytes 147464 | tf_op jit(solution)/shard_map/ppermute | solution.py:417
  5.1 10.2 %collective-permute-start.2 = (bf16[2,48,512]{2,1,0:T(8,128)(2,1)S(1)}, bf16[2,48,512]{2,1,0:T(8,128)(2,1)S(1)}, u32[]{:S(2)}, u32[]{:S(2)}) collective-permute-start(bf16[2,48,512]{2,1,0:T(8,128)(2,1)S(1)} %get-tuple-element.31), channel_id=1, source_target_pairs={{0,2},{1,11},{2,0},{3,9},{4,6},{5,15},{6,4},{7,13},{8,10},{9,3},{1... | collective-permute-start | bytes 294920 | tf_op jit(solution)/shard_map/ppermute | solution.py:425
  7.2 8.2 %collective-permute-start.3 = (bf16[2,48,512]{2,1,0:T(8,128)(2,1)S(1)}, bf16[2,48,512]{2,1,0:T(8,128)(2,1)S(1)}, u32[]{:S(2)}, u32[]{:S(2)}) collective-permute-start(bf16[2,48,512]{2,1,0:T(8,128)(2,1)S(1)} %get-tuple-element.32), channel_id=1, source_target_pairs={{0,4},{1,13},{2,6},{3,15},{4,0},{5,9},{6,2},{7,11},{8,12},{9,5},{1... | collective-permute-start | bytes 294920 | tf_op jit(solution)/shard_map/ppermute | solution.py:425
  9.5 6.2 %collective-permute-start.4 = (bf16[2,48,512]{2,1,0:T(8,128)(2,1)S(1)}, bf16[2,48,512]{2,1,0:T(8,128)(2,1)S(1)}, u32[]{:S(2)}, u32[]{:S(2)}) collective-permute-start(bf16[2,48,512]{2,1,0:T(8,128)(2,1)S(1)} %get-tuple-element.33), channel_id=1, source_target_pairs={{0,6},{1,15},{2,4},{3,13},{4,2},{5,11},{6,0},{7,9},{8,14},{9,7},{1... | collective-permute-start | bytes 294920 | tf_op jit(solution)/shard_map/ppermute | solution.py:425
  10.4 7.2 %copy-start = (bf16[96,96]{1,0:T(8,128)(2,1)S(1)}, bf16[96,96]{1,0:T(8,128)(2,1)}, u32[]{:S(2)}) copy-start(bf16[96,96]{1,0:T(8,128)(2,1)} %constant.22.clone.refs_13_) | copy-start | bytes 55300
  10.4 7.2 %copy-start.1 = (bf16[64,96]{1,0:T(8,128)(2,1)S(1)}, bf16[64,96]{1,0:T(8,128)(2,1)}, u32[]{:S(2)}) copy-start(bf16[64,96]{1,0:T(8,128)(2,1)} %constant.23.clone.refs_14_) | copy-start | bytes 36868
  15.7 1.9 %collective-permute-start.6 = (bf16[2,48,512]{2,1,0:T(8,128)(2,1)S(1)}, bf16[2,48,512]{2,1,0:T(8,128)(2,1)S(1)}, u32[]{:S(2)}, u32[]{:S(2)}) collective-permute-start(bf16[2,48,512]{2,1,0:T(8,128)(2,1)S(1)} %collective-permute-done.2.refs_4_), channel_id=1, source_target_pairs={{0,1},{1,0},{2,3},{3,2},{4,5},{5,4},{6,7},{7,6},{8,9},{9,8},{10,11... | collective-permute-start | bytes 294920 | tf_op jit(solution)/shard_map/ppermute | solution.py:456
  15.7 1.9 %collective-permute-start.7 = (bf16[2,48,512]{2,1,0:T(8,128)(2,1)S(1)}, bf16[2,48,512]{2,1,0:T(8,128)(2,1)S(1)}, u32[]{:S(2)}, u32[]{:S(2)}) collective-permute-start(bf16[2,48,512]{2,1,0:T(8,128)(2,1)S(1)} %collective-permute-done.3.refs_5_), channel_id=1, source_target_pairs={{0,1},{1,0},{2,3},{3,2},{4,5},{5,4},{6,7},{7,6},{8,9},{9,8},{10,11... | collective-permute-start | bytes 294920 | tf_op jit(solution)/shard_map/ppermute | solution.py:456
  16.3 1.4 %collective-permute-start.8 = (bf16[2,48,512]{2,1,0:T(8,128)(2,1)S(1)}, bf16[2,48,512]{2,1,0:T(8,128)(2,1)S(1)}, u32[]{:S(2)}, u32[]{:S(2)}) collective-permute-start(bf16[2,48,512]{2,1,0:T(8,128)(2,1)S(1)} %collective-permute-done.4.refs_6_), channel_id=1, source_target_pairs={{0,1},{1,0},{2,3},{3,2},{4,5},{5,4},{6,7},{7,6},{8,9},{9,8},{10,11... | collective-permute-start | bytes 294920 | tf_op jit(solution)/shard_map/ppermute | solution.py:456
  16.3 1.4 %collective-permute-start.5 = (bf16[48,512]{1,0:T(8,128)(2,1)S(1)}, bf16[48,512]{1,0:T(8,128)(2,1)S(1)}, u32[]{:S(2)}, u32[]{:S(2)}) collective-permute-start(bf16[48,512]{1,0:T(8,128)(2,1)S(1)} %collective-permute-done.1.refs_2_), channel_id=1, source_target_pairs={{0,1},{1,0},{2,3},{3,2},{4,5},{5,4},{6,7},{7,6},{8,9},{9,8},{10,11... | collective-permute-start | bytes 147464 | tf_op jit(solution)/shard_map/ppermute | solution.py:455

commit v9 on v8

--- a/solution.py
+++ b/solution.py
@@ -280,34 +280,77 @@
     done_ref[...] = jnp.zeros_like(done_ref)
 
 
-def score_kernel(near_bit, masks, pairs, n_tile, *refs):
-    n_op = len(masks)
-    home_ref, got_ref, near_ref, near_swap_ref = refs[:4]
-    recv_refs, swap_refs = refs[4 : 4 + n_op], refs[4 + n_op : 4 + 2 * n_op]
-    w_ref, tmpl_ref, plane_ref, line_ref, back_ref, inverse_ref = refs[4 + 2 * n_op : 10 + 2 * n_op]
-    _, out_ref, data_ref, vol_ref, mid_ref = refs[10 + 2 * n_op :]
+def gather_pieces(near_bit, masks, from_mate, data_ref, home_ref, got_ref, near_ref, refs):
     chip, core = place()
     mate = 1 - core
     data_ref[chip * XT + core] = home_ref[...]
     data_ref[chip * XT + mate] = got_ref[0]
     data_ref[(chip ^ near_bit) * XT + core] = near_ref[...]
-    data_ref[(chip ^ near_bit) * XT + mate] = near_swap_ref[...]
-    for j, mask in enumerate(masks):
-        here = (chip ^ mask ^ (near_bit * core)) * XT
-        there = (chip ^ mask ^ (near_bit * mate)) * XT
-        data_ref[here + core] = recv_refs[j][0]
-        data_ref[here + mate] = recv_refs[j][1]
-        data_ref[there + mate] = swap_refs[j][0]
-        data_ref[there + core] = swap_refs[j][1]
+    taker, other = (mate, core) if from_mate else (core, mate)
+    for ref, mask in zip(refs, masks):
+        source = (chip ^ mask ^ (near_bit * taker)) * XT
+        data_ref[source + taker] = ref[0]
+        data_ref[source + other] = ref[1]
+    return (chip ^ near_bit) * XT + mate
+
+
+def partial_sums(n_tile, pairs, upper, core, data_ref, w_ref):
+    base = 0
+    for sources in pairs:
+        total = jnp.zeros((LEN, LB), F32)
+        for j, src in enumerate(sources):
+            if (src >= n_tile // 2) == upper:
+                part = data_ref[jnp.where(core == 0, src, n_tile - 1 - src)]
+                total += jnp.dot(part, w_ref[base + j], preferred_element_type=F32)
+        base += len(sources)
+        yield total
+
+
+def half_kernel(near_bit, masks, pairs, n_tile, *refs):
+    w_ref, _, half_ref, data_ref = refs[3 + len(masks) :]
+    held = refs[3 : 3 + len(masks)]
+    absent = gather_pieces(near_bit, masks, False, data_ref, *refs[:3], held)
+    data_ref[absent] = jnp.zeros(data_ref.shape[1:], BF)
+    chip, core = place()
+    for upper in (False, True):
+
+        @pl.when((chip >= near_bit) == upper)
+        def _():
+            for q, total in enumerate(partial_sums(n_tile, pairs, upper, core, data_ref, w_ref)):
+                half_ref[q] = total
+
+
+def score_kernel(near_bit, masks, pairs, n_tile, *refs):
+    held, near_swap_ref = refs[3 : 3 + len(masks)], refs[3 + len(masks)]
+    half_ref, w_ref, tmpl_ref, plane_ref, line_ref, back_ref, inverse_ref = refs[
+        4 + len(masks) : 11 + len(masks)
+    ]
+    out_ref, data_ref, vol_ref, mid_ref = refs[11 + len(masks) :]
+    absent = gather_pieces(near_bit, masks, True, data_ref, *refs[:3], held)
+    data_ref[absent] = near_swap_ref[...]
+    chip, core = place()
+
+    def volume(q):
+        block = jnp.where(core == 0, q, NQ - 1 - q)
+        return pl.ds(pl.multiple_of(block * LB, LB), LB)
+
+    for upper in (False, True):
+
+        @pl.when((chip < near_bit) == upper)
+        def _():
+            for q, total in enumerate(partial_sums(n_tile, pairs, upper, core, data_ref, w_ref)):
+                vol_ref[:, volume(q)] = total + half_ref[q]
+
+    late = n_tile - 1 - absent
     base = 0
     for q, sources in enumerate(pairs):
-        total = jnp.zeros((LEN, LB), F32)
-        for j, src in enumerate(sources):
-            part = data_ref[jnp.where(core == 0, src, n_tile - 1 - src)]
-            total += jnp.dot(part, w_ref[base + j], preferred_element_type=F32)
+
+        @pl.when((core == 1) & (late >= sources[0]) & (late <= sources[-1]))
+        def _():
+            weight = w_ref[base + late - sources[0]]
+            vol_ref[:, volume(q)] += jnp.dot(data_ref[absent], weight, preferred_element_type=F32)
+
         base += len(sources)
-        block = jnp.where(core == 0, q, NQ - 1 - q)
-        vol_ref[:, pl.ds(pl.multiple_of(block * LB, LB), LB)] = total
     near_half = vol_ref[:, :VH]
     far_half = jnp.concatenate(
         [vol_ref[:, 4 * LB :], vol_ref[:, 3 * LB : 4 * LB], vol_ref[:, VH : 3 * LB]], 1
@@ -452,34 +495,42 @@
             cost_estimate=cost(1 << 32, 16 << 20),
         )(turns, merged, *[pinned(c) for c in constants])
         near_in, done, *arrived = lax.optimization_barrier((near_in, done, *arrived))
+        swapped = [lax.ppermute(a, "tile", mate) for a in arrived]
         near_swap = lax.ppermute(near_in, "tile", mate)
-        swapped = [lax.ppermute(a, "tile", mate) for a in arrived]
+        held = (home, got, near_in)
+        pieces = pltpu.VMEM((n_tile, LEN, depth), BF)
+        half = pl.pallas_call(
+            lambda *refs: half_kernel(near_bit, masks, pairs, n_tile, *refs),
+            out_shape=shape(NQ, LEN, LB, dtype=F32),
+            in_specs=[VMEM] * (5 + n_op),
+            out_specs=VMEM,
+            scratch_shapes=[pieces],
+            compiler_params=limit(12),
+            cost_estimate=cost(n_pair * LEN * depth * LB, n_pair * depth * LB),
+        )(*held, *arrived, weights, done)
         return pl.pallas_call(
             lambda *refs: score_kernel(near_bit, masks, pairs, n_tile, *refs),
             out_shape=shape(1, EDGE, EDGE * Z, dtype=F32),
-            in_specs=[VMEM] * (11 + 2 * n_op),
+            in_specs=[VMEM] * (11 + n_op),
             out_specs=VMEM,
             scratch_shapes=[
-                pltpu.VMEM((n_tile, LEN, depth), BF),
+                pieces,
                 pltpu.VMEM((LEN, XR * Z), F32),
                 pltpu.VMEM((NTPL * EDGE, 2 * FP), BF),
             ],
             compiler_params=limit(28),
             cost_estimate=cost(4 << 30, 20 << 20),
         )(
-            home,
-            got,
-            near_in,
+            *held,
+            *swapped,
             near_swap,
-            *arrived,
-            *swapped,
+            half,
             weights,
             spectra,
             plane,
             jnp.asarray(line),
             jnp.asarray(back),
             inverse,
-            done,
         )
 
     return jax.shard_map(

time: 22.7 us -> 22.5 us (level); the launches traced: 22.2 us -> 22.4 us
  Pallas kernels: 10.7 us -> 11.7 us
  waiting for transfers between devices: 1.26 us -> 0.38 us
    pallas_call x0 -> x1, Pallas kernels: none -> 1.16 us  [local(): pl.pallas_call(lambda *refs: half_kernel(near_bit, masks, pairs, n_tile,...]
    ppermute x1, waiting for transfers between devices: 0.88 us -> 0.01 us  [local(): near_swap = lax.ppermute(near_in, 'tile', mate)]
  transfers between devices with their start and end apart: 9 -> 9, of which waited for: 2 -> 1; matrix products, arithmetic and copies ran while one was open for 0% -> 0% of each run, Pallas kernels for 22% -> 27%
where the time goes in v9:
time: 22.5 us; the launch traced here: 22.4 us
  Pallas kernels  11.7 us (52%)
  starting transfers between devices  10.2 us (45%)
  waiting for transfers between devices  0.38 us (2%)
    ppermute x3, starting transfers between devices, local(): lax.ppermute(p, 'tile', route(m))  5.28 us
    pallas_call x1, Pallas kernels, local(): pl.pallas_call(lambda *refs: prepare_kernel(n_det, n_tile, pairs, *refs),...  4.92 us
    pallas_call x1, Pallas kernels, local(): pl.pallas_call(lambda *refs: score_kernel(near_bit, masks, pairs, n_tile,...  4.36 us
    ppermute x1, starting transfers between devices, local(): near_in = lax.ppermute(near, 'tile', near_pairs)  3.77 us
    pallas_call x1, Pallas kernels, local(): pl.pallas_call(lambda *refs: pack_kernel(near_bit, masks, *refs), out_sha...  1.21 us
    pallas_call x1, Pallas kernels, local(): pl.pallas_call(lambda *refs: half_kernel(near_bit, masks, pairs, n_tile,...  1.16 us
    ppermute x3, starting transfers between devices, local(): swapped = [lax.ppermute(a, 'tile', mate) for a in arrived]  0.51 us
    ppermute x1, starting transfers between devices, local(): near_swap = lax.ppermute(near_in, 'tile', mate)  0.51 us
  transfers between devices with their start and end apart: 9, of which 1 were waited for; matrix products, arithmetic and copies ran while one was open for 0% of the time, Pallas kernels for 27%

profile of v9, /device:TPU:1, one launch (start us, length us, event | category | flops | bytes accessed | tf_op | source)
XLA Modules:
  0.0 22.4 jit_solution(7087723769609063461)
XLA Ops:
  0.0 1.2 %shard_map.127 = (f32[2,61,256]{2,1,0:T(8,128)S(1)}, bf16[48,512]{1,0:T(8,128)(2,1)S(1)}, bf16[48,512]{1,0:T(8,128)(2,1)S(1)}, bf16[4,48,512]{2,1,0:T(8,128)(2,1)S(1)}, bf16[3,48,512]{2,1,0:T(8,128)(2,1)S(1)}) custom-call(s32[2,61]{1,0:T(2,128)} %bitcast.4, f32[1,61]{1,0:T(1,128)} %bitcast.5, bf16[61,8,256]{2,1,0:T(8,128)(2,1)} %bitcast.3), custom_call_target="tpu_custom_call" | custom-call | tf_op jit(solution)/shard_map/pallas_call | solution.py:439
  1.2 0.1 collective-permute-start
  1.3 3.8 %collective-permute-start.1 = (bf16[48,512]{1,0:T(8,128)(2,1)S(1)}, bf16[48,512]{1,0:T(8,128)(2,1)S(1)}, u32[]{:S(2)}, u32[]{:S(2)}) collective-permute-start(bf16[48,512]{1,0:T(8,128)(2,1)S(1)} %get-tuple-element.26), channel_id=1, source_target_pairs={{0,8},{1,9},{2,10},{3,11},{4,12},{5,13},{6,14},{7,15},{8,0},{9,1},... | collective-permute-start | bytes 147464 | tf_op jit(solution)/shard_map/ppermute | solution.py:460
  5.1 0.0 collective-permute-done.got_ref.refs_1_
  5.1 2.1 %collective-permute-start.2 = (bf16[2,48,512]{2,1,0:T(8,128)(2,1)S(1)}, bf16[2,48,512]{2,1,0:T(8,128)(2,1)S(1)}, u32[]{:S(2)}, u32[]{:S(2)}) collective-permute-start(bf16[2,48,512]{2,1,0:T(8,128)(2,1)S(1)} %get-tuple-element.31), channel_id=1, source_target_pairs={{0,2},{1,11},{2,0},{3,9},{4,6},{5,15},{6,4},{7,13},{8,10},{9,3},{1... | collective-permute-start | bytes 294920 | tf_op jit(solution)/shard_map/ppermute | solution.py:468
  7.2 2.3 %collective-permute-start.3 = (bf16[2,48,512]{2,1,0:T(8,128)(2,1)S(1)}, bf16[2,48,512]{2,1,0:T(8,128)(2,1)S(1)}, u32[]{:S(2)}, u32[]{:S(2)}) collective-permute-start(bf16[2,48,512]{2,1,0:T(8,128)(2,1)S(1)} %get-tuple-element.32), channel_id=1, source_target_pairs={{0,4},{1,13},{2,6},{3,15},{4,0},{5,9},{6,2},{7,11},{8,12},{9,5},{1... | collective-permute-start | bytes 294920 | tf_op jit(solution)/shard_map/ppermute | solution.py:468
  9.5 0.9 %collective-permute-start.4 = (bf16[2,48,512]{2,1,0:T(8,128)(2,1)S(1)}, bf16[2,48,512]{2,1,0:T(8,128)(2,1)S(1)}, u32[]{:S(2)}, u32[]{:S(2)}) collective-permute-start(bf16[2,48,512]{2,1,0:T(8,128)(2,1)S(1)} %get-tuple-element.33), channel_id=1, source_target_pairs={{0,6},{1,15},{2,4},{3,13},{4,2},{5,11},{6,0},{7,9},{8,14},{9,7},{1... | collective-permute-start | bytes 294920 | tf_op jit(solution)/shard_map/ppermute | solution.py:468
  10.4 4.9 %shard_map.129 = (bf16[34,512,256]{2,1,0:T(8,128)(2,1)S(1)}, bf16[640,2048]{1,0:T(8,128)(2,1)S(1)}, bf16[2048,512]{1,0:T(8,128)(2,1)S(1)}, bf16[8,96,1024]{2,1,0:T(8,128)(2,1)S(1)}, f32[8,128]{1,0:T(8,128)S(1)}) custom-call(f32[2,61,256]{2,1,0:T(8,128)S(1)} %get-tuple-element.27.refs_0_, f32[8,128]{1,0:T(8,128)S(1)} %get-tuple-element.29.refs_1_, s32[8]{0:T(128)} %refs_2_.1, ...), custom_call_target="tpu_custom_call" | custom-call | flops 4294967296 | bytes 16777216 | tf_op jit(solution)/shard_map/pallas_call | solution.py:476
  15.4 0.0 collective-permute-done.1.refs_2_
  15.4 0.0 collective-permute-done.2.refs_3_
  15.4 0.0 collective-permute-done.3.refs_4_
  15.4 0.4 %collective-permute-done.4.refs_5_ = bf16[2,48,512]{2,1,0:T(8,128)(2,1)S(1)} collective-permute-done((bf16[2,48,512]{2,1,0:T(8,128)(2,1)S(1)}, bf16[2,48,512]{2,1,0:T(8,128)(2,1)S(1)}, u32[]{:S(2)}, u32[]{:S(2)}) %collective-permute-start.4) | collective-permute-done | bytes 98336 | tf_op jit(solution)/shard_map/ppermute | solution.py:468
  15.7 0.0 collective-permute-start.5
  15.7 0.5 %collective-permute-start.6 = (bf16[2,48,512]{2,1,0:T(8,128)(2,1)S(1)}, bf16[2,48,512]{2,1,0:T(8,128)(2,1)S(1)}, u32[]{:S(2)}, u32[]{:S(2)}) collective-permute-start(bf16[2,48,512]{2,1,0:T(8,128)(2,1)S(1)} %collective-permute-done.3.refs_4_), channel_id=1, source_target_pairs={{0,1},{1,0},{2,3},{3,2},{4,5},{5,4},{6,7},{7,6},{8,9},{9,8},{10,11... | collective-permute-start | bytes 294920 | tf_op jit(solution)/shard_map/ppermute | solution.py:498
  16.3 0.0 collective-permute-start.7
  16.3 0.5 %collective-permute-start.8 = (bf16[48,512]{1,0:T(8,128)(2,1)S(1)}, bf16[48,512]{1,0:T(8,128)(2,1)S(1)}, u32[]{:S(2)}, u32[]{:S(2)}) collective-permute-start(bf16[48,512]{1,0:T(8,128)(2,1)S(1)} %collective-permute-done.1.refs_2_), channel_id=1, source_target_pairs={{0,1},{1,0},{2,3},{3,2},{4,5},{5,4},{6,7},{7,6},{8,9},{9,8},{10,11... | collective-permute-start | bytes 147464 | tf_op jit(solution)/shard_map/ppermute | solution.py:499
  16.8 1.2 %shard_map.130.refs_7_ = f32[5,48,256]{2,1,0:T(8,128)S(1)} custom-call(bf16[48,512]{1,0:T(8,128)(2,1)S(1)} %get-tuple-element.24.refs_0_, bf16[4,48,512]{2,1,0:T(8,128)(2,1)S(1)} %collective-permute-done.got_ref.refs_1_, bf16[48,512]{1,0:T(8,128)(2,1)S(1)} %collective-permute-done.1.refs_2_, bf16[2,48,512]{2,1,0:T(8,128)(2,1)S(1)} %collective-permute-done.2.refs_3_, ...), custom_call_target="tpu_custom_call" | custom-call | flops 213909504 | bytes 4456448 | tf_op jit(solution)/shard_map/pallas_call | solution.py:502
  17.9 0.0 collective-permute-done.8.refs_6_
  17.9 0.0 collective-permute-done.5.refs_3_
  18.0 0.0 collective-permute-done.6.refs_4_
  18.0 0.0 collective-permute-done.7.refs_5_
  18.0 0.0 copy-done
  18.0 0.0 copy-done.1
  18.0 4.4 %shard_map.131 = f32[1,32,1024]{2,1,0:T(8,128)} custom-call(bf16[48,512]{1,0:T(8,128)(2,1)S(1)} %get-tuple-element.24.refs_0_, bf16[4,48,512]{2,1,0:T(8,128)(2,1)S(1)} %collective-permute-done.got_ref.refs_1_, bf16[48,512]{1,0:T(8,128)(2,1)S(1)} %collective-permute-done.1.refs_2_, bf16[2,48,512]{2,1,0:T(8,128)(2,1)S(1)} %collective-permute-done.5.refs_3_, ...), custom_call_target="tpu_custom_call" | custom-call | flops 4294967296 | bytes 20971520 | tf_op jit(solution)/shard_map/pallas_call | solution.py:511
  (3 shorter events, 0.0 us)
Async XLA Ops:
  1.2 3.9 %collective-permute-start = (bf16[4,48,512]{2,1,0:T(8,128)(2,1)S(1)}, bf16[4,48,512]{2,1,0:T(8,128)(2,1)S(1)}, u32[]{:S(2)}, u32[]{:S(2)}) collective-permute-start(bf16[4,48,512]{2,1,0:T(8,128)(2,1)S(1)} %get-tuple-element.25), channel_id=1, source_target_pairs={{0,1},{1,0},{2,3},{3,2},{4,5},{5,4},{6,7},{7,6},{8,9},{9,8},{10,11... | collective-permute-start | bytes 589832 | tf_op jit(solution)/shard_map/ppermute | solution.py:459
  1.3 14.0 %collective-permute-start.1 = (bf16[48,512]{1,0:T(8,128)(2,1)S(1)}, bf16[48,512]{1,0:T(8,128)(2,1)S(1)}, u32[]{:S(2)}, u32[]{:S(2)}) collective-permute-start(bf16[48,512]{1,0:T(8,128)(2,1)S(1)} %get-tuple-element.26), channel_id=1, source_target_pairs={{0,8},{1,9},{2,10},{3,11},{4,12},{5,13},{6,14},{7,15},{8,0},{9,1},... | collective-permute-start | bytes 147464 | tf_op jit(solution)/shard_map/ppermute | solution.py:460
  5.1 10.2 %collective-permute-start.2 = (bf16[2,48,512]{2,1,0:T(8,128)(2,1)S(1)}, bf16[2,48,512]{2,1,0:T(8,128)(2,1)S(1)}, u32[]{:S(2)}, u32[]{:S(2)}) collective-permute-start(bf16[2,48,512]{2,1,0:T(8,128)(2,1)S(1)} %get-tuple-element.31), channel_id=1, source_target_pairs={{0,2},{1,11},{2,0},{3,9},{4,6},{5,15},{6,4},{7,13},{8,10},{9,3},{1... | collective-permute-start | bytes 294920 | tf_op jit(solution)/shard_map/ppermute | solution.py:468
  7.2 8.2 %collective-permute-start.3 = (bf16[2,48,512]{2,1,0:T(8,128)(2,1)S(1)}, bf16[2,48,512]{2,1,0:T(8,128)(2,1)S(1)}, u32[]{:S(2)}, u32[]{:S(2)}) collective-permute-start(bf16[2,48,512]{2,1,0:T(8,128)(2,1)S(1)} %get-tuple-element.32), channel_id=1, source_target_pairs={{0,4},{1,13},{2,6},{3,15},{4,0},{5,9},{6,2},{7,11},{8,12},{9,5},{1... | collective-permute-start | bytes 294920 | tf_op jit(solution)/shard_map/ppermute | solution.py:468
  9.5 6.2 %collective-permute-start.4 = (bf16[2,48,512]{2,1,0:T(8,128)(2,1)S(1)}, bf16[2,48,512]{2,1,0:T(8,128)(2,1)S(1)}, u32[]{:S(2)}, u32[]{:S(2)}) collective-permute-start(bf16[2,48,512]{2,1,0:T(8,128)(2,1)S(1)} %get-tuple-element.33), channel_id=1, source_target_pairs={{0,6},{1,15},{2,4},{3,13},{4,2},{5,11},{6,0},{7,9},{8,14},{9,7},{1... | collective-permute-start | bytes 294920 | tf_op jit(solution)/shard_map/ppermute | solution.py:468
  15.7 2.2 %collective-permute-start.5 = (bf16[2,48,512]{2,1,0:T(8,128)(2,1)S(1)}, bf16[2,48,512]{2,1,0:T(8,128)(2,1)S(1)}, u32[]{:S(2)}, u32[]{:S(2)}) collective-permute-start(bf16[2,48,512]{2,1,0:T(8,128)(2,1)S(1)} %collective-permute-done.2.refs_3_), channel_id=1, source_target_pairs={{0,1},{1,0},{2,3},{3,2},{4,5},{5,4},{6,7},{7,6},{8,9},{9,8},{10,11... | collective-permute-start | bytes 294920 | tf_op jit(solution)/shard_map/ppermute | solution.py:498
  15.7 2.2 %collective-permute-start.6 = (bf16[2,48,512]{2,1,0:T(8,128)(2,1)S(1)}, bf16[2,48,512]{2,1,0:T(8,128)(2,1)S(1)}, u32[]{:S(2)}, u32[]{:S(2)}) collective-permute-start(bf16[2,48,512]{2,1,0:T(8,128)(2,1)S(1)} %collective-permute-done.3.refs_4_), channel_id=1, source_target_pairs={{0,1},{1,0},{2,3},{3,2},{4,5},{5,4},{6,7},{7,6},{8,9},{9,8},{10,11... | collective-permute-start | bytes 294920 | tf_op jit(solution)/shard_map/ppermute | solution.py:498
  16.3 1.7 %collective-permute-start.7 = (bf16[2,48,512]{2,1,0:T(8,128)(2,1)S(1)}, bf16[2,48,512]{2,1,0:T(8,128)(2,1)S(1)}, u32[]{:S(2)}, u32[]{:S(2)}) collective-permute-start(bf16[2,48,512]{2,1,0:T(8,128)(2,1)S(1)} %collective-permute-done.4.refs_5_), channel_id=1, source_target_pairs={{0,1},{1,0},{2,3},{3,2},{4,5},{5,4},{6,7},{7,6},{8,9},{9,8},{10,11... | collective-permute-start | bytes 294920 | tf_op jit(solution)/shard_map/ppermute | solution.py:498
  16.3 1.7 %collective-permute-start.8 = (bf16[48,512]{1,0:T(8,128)(2,1)S(1)}, bf16[48,512]{1,0:T(8,128)(2,1)S(1)}, u32[]{:S(2)}, u32[]{:S(2)}) collective-permute-start(bf16[48,512]{1,0:T(8,128)(2,1)S(1)} %collective-permute-done.1.refs_2_), channel_id=1, source_target_pairs={{0,1},{1,0},{2,3},{3,2},{4,5},{5,4},{6,7},{7,6},{8,9},{9,8},{10,11... | collective-permute-start | bytes 147464 | tf_op jit(solution)/shard_map/ppermute | solution.py:499
  16.8 1.2 %copy-start = (bf16[96,96]{1,0:T(8,128)(2,1)S(1)}, bf16[96,96]{1,0:T(8,128)(2,1)}, u32[]{:S(2)}) copy-start(bf16[96,96]{1,0:T(8,128)(2,1)} %constant.22.clone.refs_11_) | copy-start | bytes 55300
  16.8 1.2 %copy-start.1 = (bf16[64,96]{1,0:T(8,128)(2,1)S(1)}, bf16[64,96]{1,0:T(8,128)(2,1)}, u32[]{:S(2)}) copy-start(bf16[64,96]{1,0:T(8,128)(2,1)} %constant.23.clone.refs_12_) | copy-start | bytes 36868

commit v10 on v9

--- a/solution.py
+++ b/solution.py
@@ -294,10 +294,15 @@
     return (chip ^ near_bit) * XT + mate
 
 
-def partial_sums(n_tile, pairs, upper, core, data_ref, w_ref):
+def partial_sums(n_tile, pairs, upper, core, data_ref, w_ref, late=None):
     base = 0
     for sources in pairs:
         total = jnp.zeros((LEN, LB), F32)
+        if late is not None:
+            inside = (late >= sources[0]) & (late <= sources[-1])
+            part = data_ref[jnp.where(inside, n_tile - 1 - late, n_tile)]
+            weight = w_ref[base + jnp.clip(late, sources[0], sources[-1]) - sources[0]]
+            total += jnp.dot(part, weight, preferred_element_type=F32)
         for j, src in enumerate(sources):
             if (src >= n_tile // 2) == upper:
                 part = data_ref[jnp.where(core == 0, src, n_tile - 1 - src)]
@@ -329,28 +334,18 @@
     absent = gather_pieces(near_bit, masks, True, data_ref, *refs[:3], held)
     data_ref[absent] = near_swap_ref[...]
     chip, core = place()
-
-    def volume(q):
-        block = jnp.where(core == 0, q, NQ - 1 - q)
-        return pl.ds(pl.multiple_of(block * LB, LB), LB)
-
+    data_ref[n_tile] = jnp.zeros(data_ref.shape[1:], BF)
     for upper in (False, True):
-
-        @pl.when((chip < near_bit) == upper)
-        def _():
-            for q, total in enumerate(partial_sums(n_tile, pairs, upper, core, data_ref, w_ref)):
-                vol_ref[:, volume(q)] = total + half_ref[q]
-
-    late = n_tile - 1 - absent
-    base = 0
-    for q, sources in enumerate(pairs):
-
-        @pl.when((core == 1) & (late >= sources[0]) & (late <= sources[-1]))
-        def _():
-            weight = w_ref[base + late - sources[0]]
-            vol_ref[:, volume(q)] += jnp.dot(data_ref[absent], weight, preferred_element_type=F32)
-
-        base += len(sources)
+        for col in range(XT):
+
+            @pl.when(((chip < near_bit) == upper) & (core == col))
+            def _():
+                late = n_tile - 1 - absent if col else None
+                sums = partial_sums(n_tile, pairs, upper, col, data_ref, w_ref, late)
+                for q, total in enumerate(sums):
+                    low = (NQ - 1 - q if col else q) * LB
+                    vol_ref[:, low : low + LB] = total + half_ref[q]
+
     near_half = vol_ref[:, :VH]
     far_half = jnp.concatenate(
         [vol_ref[:, 4 * LB :], vol_ref[:, 3 * LB : 4 * LB], vol_ref[:, VH : 3 * LB]], 1
@@ -498,7 +493,7 @@
         swapped = [lax.ppermute(a, "tile", mate) for a in arrived]
         near_swap = lax.ppermute(near_in, "tile", mate)
         held = (home, got, near_in)
-        pieces = pltpu.VMEM((n_tile, LEN, depth), BF)
+        pieces = pltpu.VMEM((n_tile + 1, LEN, depth), BF)
         half = pl.pallas_call(
             lambda *refs: half_kernel(near_bit, masks, pairs, n_tile, *refs),
             out_shape=shape(NQ, LEN, LB, dtype=F32),

time: 22.5 us -> 21.9 us (0.973)
  Pallas kernels: 11.7 us -> 11.1 us
    pallas_call x1, Pallas kernels: 4.36 us -> 3.78 us  [local(): pl.pallas_call(lambda *refs: score_kernel(near_bit, masks, pairs, n_tile,...]
  transfers between devices with their start and end apart: 9 -> 9, of which waited for: 1 -> 1; matrix products, arithmetic and copies ran while one was open for 0% -> 0% of each run, Pallas kernels for 27% -> 28%
where the time goes in v10:
time: 21.9 us; the launch traced here: 21.8 us
  Pallas kernels  11.1 us (51%)
  starting transfers between devices  10.2 us (47%)
  waiting for transfers between devices  0.37 us (2%)
    ppermute x3, starting transfers between devices, local(): lax.ppermute(p, 'tile', route(m))  5.28 us
    pallas_call x1, Pallas kernels, local(): pl.pallas_call(lambda *refs: prepare_kernel(n_det, n_tile, pairs, *refs),...  4.92 us
    pallas_call x1, Pallas kernels, local(): pl.pallas_call(lambda *refs: score_kernel(near_bit, masks, pairs, n_tile,...  3.78 us
    ppermute x1, starting transfers between devices, local(): near_in = lax.ppermute(near, 'tile', near_pairs)  3.77 us
    pallas_call x1, Pallas kernels, local(): pl.pallas_call(lambda *refs: pack_kernel(near_bit, masks, *refs), out_sha...  1.21 us
    pallas_call x1, Pallas kernels, local(): pl.pallas_call(lambda *refs: half_kernel(near_bit, masks, pairs, n_tile,...  1.16 us
    ppermute x3, starting transfers between devices, local(): swapped = [lax.ppermute(a, 'tile', mate) for a in arrived]  0.51 us
    ppermute x1, starting transfers between devices, local(): near_swap = lax.ppermute(near_in, 'tile', mate)  0.51 us
  transfers between devices with their start and end apart: 9, of which 1 were waited for; matrix products, arithmetic and copies ran while one was open for 0% of the time, Pallas kernels for 28%

profile of v10, /device:TPU:1, one launch (start us, length us, event | category | flops | bytes accessed | tf_op | source)
XLA Modules:
  0.0 21.8 jit_solution(8937129828226055394)
XLA Ops:
  0.0 1.2 %shard_map.127 = (f32[2,61,256]{2,1,0:T(8,128)S(1)}, bf16[48,512]{1,0:T(8,128)(2,1)S(1)}, bf16[48,512]{1,0:T(8,128)(2,1)S(1)}, bf16[4,48,512]{2,1,0:T(8,128)(2,1)S(1)}, bf16[3,48,512]{2,1,0:T(8,128)(2,1)S(1)}) custom-call(s32[2,61]{1,0:T(2,128)} %bitcast.4, f32[1,61]{1,0:T(1,128)} %bitcast.5, bf16[61,8,256]{2,1,0:T(8,128)(2,1)} %bitcast.3), custom_call_target="tpu_custom_call" | custom-call | tf_op jit(solution)/shard_map/pallas_call | solution.py:434
  1.2 0.1 collective-permute-start
  1.3 3.8 %collective-permute-start.1 = (bf16[48,512]{1,0:T(8,128)(2,1)S(1)}, bf16[48,512]{1,0:T(8,128)(2,1)S(1)}, u32[]{:S(2)}, u32[]{:S(2)}) collective-permute-start(bf16[48,512]{1,0:T(8,128)(2,1)S(1)} %get-tuple-element.26), channel_id=1, source_target_pairs={{0,8},{1,9},{2,10},{3,11},{4,12},{5,13},{6,14},{7,15},{8,0},{9,1},... | collective-permute-start | bytes 147464 | tf_op jit(solution)/shard_map/ppermute | solution.py:455
  5.1 0.0 collective-permute-done.got_ref.refs_1_
  5.1 2.1 %collective-permute-start.2 = (bf16[2,48,512]{2,1,0:T(8,128)(2,1)S(1)}, bf16[2,48,512]{2,1,0:T(8,128)(2,1)S(1)}, u32[]{:S(2)}, u32[]{:S(2)}) collective-permute-start(bf16[2,48,512]{2,1,0:T(8,128)(2,1)S(1)} %get-tuple-element.31), channel_id=1, source_target_pairs={{0,2},{1,11},{2,0},{3,9},{4,6},{5,15},{6,4},{7,13},{8,10},{9,3},{1... | collective-permute-start | bytes 294920 | tf_op jit(solution)/shard_map/ppermute | solution.py:463
  7.2 2.3 %collective-permute-start.3 = (bf16[2,48,512]{2,1,0:T(8,128)(2,1)S(1)}, bf16[2,48,512]{2,1,0:T(8,128)(2,1)S(1)}, u32[]{:S(2)}, u32[]{:S(2)}) collective-permute-start(bf16[2,48,512]{2,1,0:T(8,128)(2,1)S(1)} %get-tuple-element.32), channel_id=1, source_target_pairs={{0,4},{1,13},{2,6},{3,15},{4,0},{5,9},{6,2},{7,11},{8,12},{9,5},{1... | collective-permute-start | bytes 294920 | tf_op jit(solution)/shard_map/ppermute | solution.py:463
  9.5 0.9 %collective-permute-start.4 = (bf16[2,48,512]{2,1,0:T(8,128)(2,1)S(1)}, bf16[2,48,512]{2,1,0:T(8,128)(2,1)S(1)}, u32[]{:S(2)}, u32[]{:S(2)}) collective-permute-start(bf16[2,48,512]{2,1,0:T(8,128)(2,1)S(1)} %get-tuple-element.33), channel_id=1, source_target_pairs={{0,6},{1,15},{2,4},{3,13},{4,2},{5,11},{6,0},{7,9},{8,14},{9,7},{1... | collective-permute-start | bytes 294920 | tf_op jit(solution)/shard_map/ppermute | solution.py:463
  10.4 4.9 %shard_map.129 = (bf16[34,512,256]{2,1,0:T(8,128)(2,1)S(1)}, bf16[640,2048]{1,0:T(8,128)(2,1)S(1)}, bf16[2048,512]{1,0:T(8,128)(2,1)S(1)}, bf16[8,96,1024]{2,1,0:T(8,128)(2,1)S(1)}, f32[8,128]{1,0:T(8,128)S(1)}) custom-call(f32[2,61,256]{2,1,0:T(8,128)S(1)} %get-tuple-element.27.refs_0_, f32[8,128]{1,0:T(8,128)S(1)} %get-tuple-element.29.refs_1_, s32[8]{0:T(128)} %refs_2_.1, ...), custom_call_target="tpu_custom_call" | custom-call | flops 4294967296 | bytes 16777216 | tf_op jit(solution)/shard_map/pallas_call | solution.py:471
  15.4 0.0 collective-permute-done.1.refs_2_
  15.4 0.0 collective-permute-done.2.refs_3_
  15.4 0.0 collective-permute-done.3.refs_4_
  15.4 0.4 %collective-permute-done.4.refs_5_ = bf16[2,48,512]{2,1,0:T(8,128)(2,1)S(1)} collective-permute-done((bf16[2,48,512]{2,1,0:T(8,128)(2,1)S(1)}, bf16[2,48,512]{2,1,0:T(8,128)(2,1)S(1)}, u32[]{:S(2)}, u32[]{:S(2)}) %collective-permute-start.4) | collective-permute-done | bytes 98336 | tf_op jit(solution)/shard_map/ppermute | solution.py:463
  15.7 0.0 collective-permute-start.5
  15.7 0.5 %collective-permute-start.6 = (bf16[2,48,512]{2,1,0:T(8,128)(2,1)S(1)}, bf16[2,48,512]{2,1,0:T(8,128)(2,1)S(1)}, u32[]{:S(2)}, u32[]{:S(2)}) collective-permute-start(bf16[2,48,512]{2,1,0:T(8,128)(2,1)S(1)} %collective-permute-done.3.refs_4_), channel_id=1, source_target_pairs={{0,1},{1,0},{2,3},{3,2},{4,5},{5,4},{6,7},{7,6},{8,9},{9,8},{10,11... | collective-permute-start | bytes 294920 | tf_op jit(solution)/shard_map/ppermute | solution.py:493
  16.3 0.0 collective-permute-start.7
  16.3 0.5 %collective-permute-start.8 = (bf16[48,512]{1,0:T(8,128)(2,1)S(1)}, bf16[48,512]{1,0:T(8,128)(2,1)S(1)}, u32[]{:S(2)}, u32[]{:S(2)}) collective-permute-start(bf16[48,512]{1,0:T(8,128)(2,1)S(1)} %collective-permute-done.1.refs_2_), channel_id=1, source_target_pairs={{0,1},{1,0},{2,3},{3,2},{4,5},{5,4},{6,7},{7,6},{8,9},{9,8},{10,11... | collective-permute-start | bytes 147464 | tf_op jit(solution)/shard_map/ppermute | solution.py:494
  16.8 1.2 %shard_map.130.refs_7_ = f32[5,48,256]{2,1,0:T(8,128)S(1)} custom-call(bf16[48,512]{1,0:T(8,128)(2,1)S(1)} %get-tuple-element.24.refs_0_, bf16[4,48,512]{2,1,0:T(8,128)(2,1)S(1)} %collective-permute-done.got_ref.refs_1_, bf16[48,512]{1,0:T(8,128)(2,1)S(1)} %collective-permute-done.1.refs_2_, bf16[2,48,512]{2,1,0:T(8,128)(2,1)S(1)} %collective-permute-done.2.refs_3_, ...), custom_call_target="tpu_custom_call" | custom-call | flops 213909504 | bytes 4456448 | tf_op jit(solution)/shard_map/pallas_call | solution.py:497
  17.9 0.0 collective-permute-done.8.refs_6_
  17.9 0.0 collective-permute-done.5.refs_3_
  18.0 0.0 collective-permute-done.6.refs_4_
  18.0 0.0 collective-permute-done.7.refs_5_
  18.0 0.0 copy-done
  18.0 0.0 copy-done.1
  18.0 3.8 %shard_map.131 = f32[1,32,1024]{2,1,0:T(8,128)} custom-call(bf16[48,512]{1,0:T(8,128)(2,1)S(1)} %get-tuple-element.24.refs_0_, bf16[4,48,512]{2,1,0:T(8,128)(2,1)S(1)} %collective-permute-done.got_ref.refs_1_, bf16[48,512]{1,0:T(8,128)(2,1)S(1)} %collective-permute-done.1.refs_2_, bf16[2,48,512]{2,1,0:T(8,128)(2,1)S(1)} %collective-permute-done.5.refs_3_, ...), custom_call_target="tpu_custom_call" | custom-call | flops 4294967296 | bytes 20971520 | tf_op jit(solution)/shard_map/pallas_call | solution.py:506
  (3 shorter events, 0.0 us)
Async XLA Ops:
  1.2 3.9 %collective-permute-start = (bf16[4,48,512]{2,1,0:T(8,128)(2,1)S(1)}, bf16[4,48,512]{2,1,0:T(8,128)(2,1)S(1)}, u32[]{:S(2)}, u32[]{:S(2)}) collective-permute-start(bf16[4,48,512]{2,1,0:T(8,128)(2,1)S(1)} %get-tuple-element.25), channel_id=1, source_target_pairs={{0,1},{1,0},{2,3},{3,2},{4,5},{5,4},{6,7},{7,6},{8,9},{9,8},{10,11... | collective-permute-start | bytes 589832 | tf_op jit(solution)/shard_map/ppermute | solution.py:454
  1.3 14.0 %collective-permute-start.1 = (bf16[48,512]{1,0:T(8,128)(2,1)S(1)}, bf16[48,512]{1,0:T(8,128)(2,1)S(1)}, u32[]{:S(2)}, u32[]{:S(2)}) collective-permute-start(bf16[48,512]{1,0:T(8,128)(2,1)S(1)} %get-tuple-element.26), channel_id=1, source_target_pairs={{0,8},{1,9},{2,10},{3,11},{4,12},{5,13},{6,14},{7,15},{8,0},{9,1},... | collective-permute-start | bytes 147464 | tf_op jit(solution)/shard_map/ppermute | solution.py:455
  5.1 10.2 %collective-permute-start.2 = (bf16[2,48,512]{2,1,0:T(8,128)(2,1)S(1)}, bf16[2,48,512]{2,1,0:T(8,128)(2,1)S(1)}, u32[]{:S(2)}, u32[]{:S(2)}) collective-permute-start(bf16[2,48,512]{2,1,0:T(8,128)(2,1)S(1)} %get-tuple-element.31), channel_id=1, source_target_pairs={{0,2},{1,11},{2,0},{3,9},{4,6},{5,15},{6,4},{7,13},{8,10},{9,3},{1... | collective-permute-start | bytes 294920 | tf_op jit(solution)/shard_map/ppermute | solution.py:463
  7.2 8.2 %collective-permute-start.3 = (bf16[2,48,512]{2,1,0:T(8,128)(2,1)S(1)}, bf16[2,48,512]{2,1,0:T(8,128)(2,1)S(1)}, u32[]{:S(2)}, u32[]{:S(2)}) collective-permute-start(bf16[2,48,512]{2,1,0:T(8,128)(2,1)S(1)} %get-tuple-element.32), channel_id=1, source_target_pairs={{0,4},{1,13},{2,6},{3,15},{4,0},{5,9},{6,2},{7,11},{8,12},{9,5},{1... | collective-permute-start | bytes 294920 | tf_op jit(solution)/shard_map/ppermute | solution.py:463
  9.5 6.2 %collective-permute-start.4 = (bf16[2,48,512]{2,1,0:T(8,128)(2,1)S(1)}, bf16[2,48,512]{2,1,0:T(8,128)(2,1)S(1)}, u32[]{:S(2)}, u32[]{:S(2)}) collective-permute-start(bf16[2,48,512]{2,1,0:T(8,128)(2,1)S(1)} %get-tuple-element.33), channel_id=1, source_target_pairs={{0,6},{1,15},{2,4},{3,13},{4,2},{5,11},{6,0},{7,9},{8,14},{9,7},{1... | collective-permute-start | bytes 294920 | tf_op jit(solution)/shard_map/ppermute | solution.py:463
  15.7 2.2 %collective-permute-start.5 = (bf16[2,48,512]{2,1,0:T(8,128)(2,1)S(1)}, bf16[2,48,512]{2,1,0:T(8,128)(2,1)S(1)}, u32[]{:S(2)}, u32[]{:S(2)}) collective-permute-start(bf16[2,48,512]{2,1,0:T(8,128)(2,1)S(1)} %collective-permute-done.2.refs_3_), channel_id=1, source_target_pairs={{0,1},{1,0},{2,3},{3,2},{4,5},{5,4},{6,7},{7,6},{8,9},{9,8},{10,11... | collective-permute-start | bytes 294920 | tf_op jit(solution)/shard_map/ppermute | solution.py:493
  15.7 2.2 %collective-permute-start.6 = (bf16[2,48,512]{2,1,0:T(8,128)(2,1)S(1)}, bf16[2,48,512]{2,1,0:T(8,128)(2,1)S(1)}, u32[]{:S(2)}, u32[]{:S(2)}) collective-permute-start(bf16[2,48,512]{2,1,0:T(8,128)(2,1)S(1)} %collective-permute-done.3.refs_4_), channel_id=1, source_target_pairs={{0,1},{1,0},{2,3},{3,2},{4,5},{5,4},{6,7},{7,6},{8,9},{9,8},{10,11... | collective-permute-start | bytes 294920 | tf_op jit(solution)/shard_map/ppermute | solution.py:493
  16.3 1.7 %collective-permute-start.7 = (bf16[2,48,512]{2,1,0:T(8,128)(2,1)S(1)}, bf16[2,48,512]{2,1,0:T(8,128)(2,1)S(1)}, u32[]{:S(2)}, u32[]{:S(2)}) collective-permute-start(bf16[2,48,512]{2,1,0:T(8,128)(2,1)S(1)} %collective-permute-done.4.refs_5_), channel_id=1, source_target_pairs={{0,1},{1,0},{2,3},{3,2},{4,5},{5,4},{6,7},{7,6},{8,9},{9,8},{10,11... | collective-permute-start | bytes 294920 | tf_op jit(solution)/shard_map/ppermute | solution.py:493
  16.3 1.7 %collective-permute-start.8 = (bf16[48,512]{1,0:T(8,128)(2,1)S(1)}, bf16[48,512]{1,0:T(8,128)(2,1)S(1)}, u32[]{:S(2)}, u32[]{:S(2)}) collective-permute-start(bf16[48,512]{1,0:T(8,128)(2,1)S(1)} %collective-permute-done.1.refs_2_), channel_id=1, source_target_pairs={{0,1},{1,0},{2,3},{3,2},{4,5},{5,4},{6,7},{7,6},{8,9},{9,8},{10,11... | collective-permute-start | bytes 147464 | tf_op jit(solution)/shard_map/ppermute | solution.py:494
  16.8 1.2 %copy-start = (bf16[96,96]{1,0:T(8,128)(2,1)S(1)}, bf16[96,96]{1,0:T(8,128)(2,1)}, u32[]{:S(2)}) copy-start(bf16[96,96]{1,0:T(8,128)(2,1)} %constant.22.clone.refs_11_) | copy-start | bytes 55300
  16.8 1.2 %copy-start.1 = (bf16[64,96]{1,0:T(8,128)(2,1)S(1)}, bf16[64,96]{1,0:T(8,128)(2,1)}, u32[]{:S(2)}) copy-start(bf16[64,96]{1,0:T(8,128)(2,1)} %constant.23.clone.refs_12_) | copy-start | bytes 36868

commit v11 on v10

--- a/solution.py
+++ b/solution.py
@@ -280,17 +280,25 @@
     done_ref[...] = jnp.zeros_like(done_ref)
 
 
-def gather_pieces(near_bit, masks, from_mate, data_ref, home_ref, got_ref, near_ref, refs):
+def join_kernel(near_ref, *refs):
+    out_ref = refs[-1]
+    out_ref[0] = near_ref[...]
+    for j, ref in enumerate(refs[:-1]):
+        out_ref[1 + 2 * j] = ref[0]
+        out_ref[2 + 2 * j] = ref[1]
+
+
+def gather_pieces(near_bit, masks, from_mate, data_ref, home_ref, got_ref, near_ref, held_ref):
     chip, core = place()
     mate = 1 - core
     data_ref[chip * XT + core] = home_ref[...]
     data_ref[chip * XT + mate] = got_ref[0]
-    data_ref[(chip ^ near_bit) * XT + core] = near_ref[...]
+    data_ref[(chip ^ near_bit) * XT + core] = near_ref[0]
     taker, other = (mate, core) if from_mate else (core, mate)
-    for ref, mask in zip(refs, masks):
+    for j, mask in enumerate(masks):
         source = (chip ^ mask ^ (near_bit * taker)) * XT
-        data_ref[source + taker] = ref[0]
-        data_ref[source + other] = ref[1]
+        data_ref[source + taker] = held_ref[1 + 2 * j]
+        data_ref[source + other] = held_ref[2 + 2 * j]
     return (chip ^ near_bit) * XT + mate
 
 
@@ -312,9 +320,10 @@
 
 
 def half_kernel(near_bit, masks, pairs, n_tile, *refs):
-    w_ref, _, half_ref, data_ref = refs[3 + len(masks) :]
-    held = refs[3 : 3 + len(masks)]
-    absent = gather_pieces(near_bit, masks, False, data_ref, *refs[:3], held)
+    home_ref, got_ref, held_ref, w_ref, _, half_ref, data_ref = refs
+    absent = gather_pieces(
+        near_bit, masks, False, data_ref, home_ref, got_ref, held_ref, held_ref
+    )
     data_ref[absent] = jnp.zeros(data_ref.shape[1:], BF)
     chip, core = place()
     for upper in (False, True):
@@ -326,13 +335,11 @@
 
 
 def score_kernel(near_bit, masks, pairs, n_tile, *refs):
-    held, near_swap_ref = refs[3 : 3 + len(masks)], refs[3 + len(masks)]
-    half_ref, w_ref, tmpl_ref, plane_ref, line_ref, back_ref, inverse_ref = refs[
-        4 + len(masks) : 11 + len(masks)
-    ]
-    out_ref, data_ref, vol_ref, mid_ref = refs[11 + len(masks) :]
-    absent = gather_pieces(near_bit, masks, True, data_ref, *refs[:3], held)
-    data_ref[absent] = near_swap_ref[...]
+    home_ref, got_ref, held_ref, swap_ref = refs[:4]
+    half_ref, w_ref, tmpl_ref, plane_ref, line_ref, back_ref, inverse_ref = refs[4:11]
+    out_ref, data_ref, vol_ref, mid_ref = refs[11:]
+    absent = gather_pieces(near_bit, masks, True, data_ref, home_ref, got_ref, held_ref, swap_ref)
+    data_ref[absent] = swap_ref[0]
     chip, core = place()
     data_ref[n_tile] = jnp.zeros(data_ref.shape[1:], BF)
     for upper in (False, True):
@@ -417,6 +424,7 @@
     depth = (NTILT * n_det + 127) // 128 * 128
     near_bit = n_block // 2
     masks = [k for k in range(1, n_block) if not k & near_bit]
+    masks.sort(key=lambda k: k != near_bit // 2)
     n_op = len(masks)
     pairs = pair_list(n_det)
     n_pair = sum(len(p) for p in pairs)
@@ -490,23 +498,28 @@
             cost_estimate=cost(1 << 32, 16 << 20),
         )(turns, merged, *[pinned(c) for c in constants])
         near_in, done, *arrived = lax.optimization_barrier((near_in, done, *arrived))
-        swapped = [lax.ppermute(a, "tile", mate) for a in arrived]
-        near_swap = lax.ppermute(near_in, "tile", mate)
-        held = (home, got, near_in)
+        held = pl.pallas_call(
+            join_kernel,
+            out_shape=shape(1 + 2 * n_op, LEN, depth),
+            in_specs=[VMEM] * (1 + n_op),
+            out_specs=VMEM,
+            compiler_params=limit(4),
+        )(near_in, *arrived)
+        swapped = lax.ppermute(held, "tile", mate)
         pieces = pltpu.VMEM((n_tile + 1, LEN, depth), BF)
         half = pl.pallas_call(
             lambda *refs: half_kernel(near_bit, masks, pairs, n_tile, *refs),
             out_shape=shape(NQ, LEN, LB, dtype=F32),
-            in_specs=[VMEM] * (5 + n_op),
+            in_specs=[VMEM] * 5,
             out_specs=VMEM,
             scratch_shapes=[pieces],
             compiler_params=limit(12),
             cost_estimate=cost(n_pair * LEN * depth * LB, n_pair * depth * LB),
-        )(*held, *arrived, weights, done)
+        )(home, got, held, weights, done)
         return pl.pallas_call(
             lambda *refs: score_kernel(near_bit, masks, pairs, n_tile, *refs),
             out_shape=shape(1, EDGE, EDGE * Z, dtype=F32),
-            in_specs=[VMEM] * (11 + n_op),
+            in_specs=[VMEM] * 11,
             out_specs=VMEM,
             scratch_shapes=[
                 pieces,
@@ -516,9 +529,10 @@
             compiler_params=limit(28),
             cost_estimate=cost(4 << 30, 20 << 20),
         )(
-            *held,
-            *swapped,
-            near_swap,
+            home,
+            got,
+            held,
+            swapped,
             half,
             weights,
             spectra,

time: 21.9 us -> 21.1 us (0.963)
  starting transfers between devices: 10.2 us -> 8.38 us
  waiting for transfers between devices: 0.37 us -> 1.43 us
    ppermute x4 -> x1, starting transfers between devices: 1.02 us -> 0.07 us  [local(): swapped = lax.ppermute(held, 'tile', mate)]
    ppermute x3, starting transfers between devices: 5.28 us -> 4.41 us  [local(): lax.ppermute(p, 'tile', route(m))]
    ppermute x3, waiting for transfers between devices: 0.36 us -> 0.98 us  [local(): lax.ppermute(p, 'tile', route(m))]
    ppermute x4 -> x1, waiting for transfers between devices: 0.01 us -> 0.44 us  [local(): swapped = lax.ppermute(held, 'tile', mate)]
  transfers between devices with their start and end apart: 9 -> 6, of which waited for: 1 -> 2; matrix products, arithmetic and copies ran while one was open for 0% -> 0% of each run, Pallas kernels for 28% -> 29%
where the time goes in v11:
time: 21.1 us; the launch traced here: 21 us
  Pallas kernels  11.1 us (53%)
  starting transfers between devices  8.38 us (40%)
  waiting for transfers between devices  1.43 us (7%)
    pallas_call x1, Pallas kernels, local(): pl.pallas_call(lambda *refs: prepare_kernel(n_det, n_tile, pairs, *refs),...  4.92 us
    ppermute x3, starting transfers between devices, local(): lax.ppermute(p, 'tile', route(m))  4.41 us
    ppermute x1, starting transfers between devices, local(): near_in = lax.ppermute(near, 'tile', near_pairs)  3.77 us
    pallas_call x1, Pallas kernels, local(): pl.pallas_call(lambda *refs: score_kernel(near_bit, masks, pairs, n_tile,...  3.76 us
    pallas_call x1, Pallas kernels, local(): pl.pallas_call(lambda *refs: pack_kernel(near_bit, masks, *refs), out_sha...  1.21 us
    pallas_call x1, Pallas kernels, local(): pl.pallas_call(lambda *refs: half_kernel(near_bit, masks, pairs, n_tile,...  1.17 us
    ppermute x3, waiting for transfers between devices, local(): lax.ppermute(p, 'tile', route(m))  0.98 us
    ppermute x1, waiting for transfers between devices, local(): swapped = lax.ppermute(held, 'tile', mate)  0.44 us
  transfers between devices with their start and end apart: 6, of which 2 were waited for; matrix products, arithmetic and copies ran while one was open for 0% of the time, Pallas kernels for 29%

profile of v11, /device:TPU:1, one launch (start us, length us, event | category | flops | bytes accessed | tf_op | source)
XLA Modules:
  0.0 21.0 jit_solution(10234691144970633694)
XLA Ops:
  0.0 1.2 %shard_map.127 = (f32[2,61,256]{2,1,0:T(8,128)S(1)}, bf16[48,512]{1,0:T(8,128)(2,1)S(1)}, bf16[48,512]{1,0:T(8,128)(2,1)S(1)}, bf16[4,48,512]{2,1,0:T(8,128)(2,1)S(1)}, bf16[3,48,512]{2,1,0:T(8,128)(2,1)S(1)}) custom-call(s32[2,61]{1,0:T(2,128)} %bitcast.4, f32[1,61]{1,0:T(1,128)} %bitcast.5, bf16[61,8,256]{2,1,0:T(8,128)(2,1)} %bitcast.3), custom_call_target="tpu_custom_call" | custom-call | tf_op jit(solution)/shard_map/pallas_call | solution.py:442
  1.2 0.1 collective-permute-start
  1.3 3.8 %collective-permute-start.1 = (bf16[48,512]{1,0:T(8,128)(2,1)S(1)}, bf16[48,512]{1,0:T(8,128)(2,1)S(1)}, u32[]{:S(2)}, u32[]{:S(2)}) collective-permute-start(bf16[48,512]{1,0:T(8,128)(2,1)S(1)} %get-tuple-element.26), channel_id=1, source_target_pairs={{0,8},{1,9},{2,10},{3,11},{4,12},{5,13},{6,14},{7,15},{8,0},{9,1},... | collective-permute-start | bytes 147464 | tf_op jit(solution)/shard_map/ppermute | solution.py:463
  5.1 0.0 collective-permute-done.got_ref.refs_1_
  5.1 2.1 %collective-permute-start.2 = (bf16[2,48,512]{2,1,0:T(8,128)(2,1)S(1)}, bf16[2,48,512]{2,1,0:T(8,128)(2,1)S(1)}, u32[]{:S(2)}, u32[]{:S(2)}) collective-permute-start(bf16[2,48,512]{2,1,0:T(8,128)(2,1)S(1)} %get-tuple-element.31), channel_id=1, source_target_pairs={{0,4},{1,13},{2,6},{3,15},{4,0},{5,9},{6,2},{7,11},{8,12},{9,5},{1... | collective-permute-start | bytes 294920 | tf_op jit(solution)/shard_map/ppermute | solution.py:471
  7.3 1.4 %collective-permute-start.3 = (bf16[2,48,512]{2,1,0:T(8,128)(2,1)S(1)}, bf16[2,48,512]{2,1,0:T(8,128)(2,1)S(1)}, u32[]{:S(2)}, u32[]{:S(2)}) collective-permute-start(bf16[2,48,512]{2,1,0:T(8,128)(2,1)S(1)} %get-tuple-element.32), channel_id=1, source_target_pairs={{0,2},{1,11},{2,0},{3,9},{4,6},{5,15},{6,4},{7,13},{8,10},{9,3},{1... | collective-permute-start | bytes 294920 | tf_op jit(solution)/shard_map/ppermute | solution.py:471
  8.6 0.9 %collective-permute-start.4 = (bf16[2,48,512]{2,1,0:T(8,128)(2,1)S(1)}, bf16[2,48,512]{2,1,0:T(8,128)(2,1)S(1)}, u32[]{:S(2)}, u32[]{:S(2)}) collective-permute-start(bf16[2,48,512]{2,1,0:T(8,128)(2,1)S(1)} %get-tuple-element.33), channel_id=1, source_target_pairs={{0,6},{1,15},{2,4},{3,13},{4,2},{5,11},{6,0},{7,9},{8,14},{9,7},{1... | collective-permute-start | bytes 294920 | tf_op jit(solution)/shard_map/ppermute | solution.py:471
  9.6 4.9 %shard_map.129 = (bf16[34,512,256]{2,1,0:T(8,128)(2,1)S(1)}, bf16[640,2048]{1,0:T(8,128)(2,1)S(1)}, bf16[2048,512]{1,0:T(8,128)(2,1)S(1)}, bf16[8,96,1024]{2,1,0:T(8,128)(2,1)S(1)}, f32[8,128]{1,0:T(8,128)S(1)}) custom-call(f32[2,61,256]{2,1,0:T(8,128)S(1)} %get-tuple-element.27.refs_0_, f32[8,128]{1,0:T(8,128)S(1)} %get-tuple-element.29.refs_1_, s32[8]{0:T(128)} %refs_2_.1, ...), custom_call_target="tpu_custom_call" | custom-call | flops 4294967296 | bytes 16777216 | tf_op jit(solution)/shard_map/pallas_call | solution.py:479
  14.5 0.0 collective-permute-done.1.near_ref
  14.5 0.0 collective-permute-done.2.refs_0_
  14.5 0.0 collective-permute-done.3.refs_1_
  14.5 1.0 %collective-permute-done.4.refs_2_ = bf16[2,48,512]{2,1,0:T(8,128)(2,1)S(1)} collective-permute-done((bf16[2,48,512]{2,1,0:T(8,128)(2,1)S(1)}, bf16[2,48,512]{2,1,0:T(8,128)(2,1)S(1)}, u32[]{:S(2)}, u32[]{:S(2)}) %collective-permute-start.4) | collective-permute-done | bytes 98336 | tf_op jit(solution)/shard_map/ppermute | solution.py:471
  15.5 0.1 collective-permute-start.5
  15.6 0.0 copy-start
  15.6 0.0 copy-start.1
  15.6 1.2 %shard_map.131.refs_4_ = f32[5,48,256]{2,1,0:T(8,128)S(1)} custom-call(bf16[48,512]{1,0:T(8,128)(2,1)S(1)} %get-tuple-element.24.refs_0_, bf16[4,48,512]{2,1,0:T(8,128)(2,1)S(1)} %collective-permute-done.got_ref.refs_1_, bf16[7,48,512]{2,1,0:T(8,128)(2,1)S(1)} %shard_map.130.refs_2_, bf16[34,512,256]{2,1,0:T(8,128)(2,1)S(1)} %get-tuple-element.38.refs_3_.refs_5_, ...), custom_call_target="tpu_custom_call" | custom-call | flops 213909504 | bytes 4456448 | tf_op jit(solution)/shard_map/pallas_call | solution.py:510
  16.8 0.4 %collective-permute-done.5.refs_3_ = bf16[7,48,512]{2,1,0:T(8,128)(2,1)S(1)} collective-permute-done((bf16[7,48,512]{2,1,0:T(8,128)(2,1)S(1)}, bf16[7,48,512]{2,1,0:T(8,128)(2,1)S(1)}, u32[]{:S(2)}, u32[]{:S(2)}) %collective-permute-start.5) | collective-permute-done | bytes 344096 | tf_op jit(solution)/shard_map/ppermute | solution.py:508
  17.2 0.0 copy-done
  17.2 0.0 copy-done.1
  17.2 3.8 %shard_map.132 = f32[1,32,1024]{2,1,0:T(8,128)} custom-call(bf16[48,512]{1,0:T(8,128)(2,1)S(1)} %get-tuple-element.24.refs_0_, bf16[4,48,512]{2,1,0:T(8,128)(2,1)S(1)} %collective-permute-done.got_ref.refs_1_, bf16[7,48,512]{2,1,0:T(8,128)(2,1)S(1)} %shard_map.130.refs_2_, bf16[7,48,512]{2,1,0:T(8,128)(2,1)S(1)} %collective-permute-done.5.refs_3_, ...), custom_call_target="tpu_custom_call" | custom-call | flops 4294967296 | bytes 20971520 | tf_op jit(solution)/shard_map/pallas_call | solution.py:519
  (2 shorter events, 0.0 us)
Async XLA Ops:
  1.2 3.9 %collective-permute-start = (bf16[4,48,512]{2,1,0:T(8,128)(2,1)S(1)}, bf16[4,48,512]{2,1,0:T(8,128)(2,1)S(1)}, u32[]{:S(2)}, u32[]{:S(2)}) collective-permute-start(bf16[4,48,512]{2,1,0:T(8,128)(2,1)S(1)} %get-tuple-element.25), channel_id=1, source_target_pairs={{0,1},{1,0},{2,3},{3,2},{4,5},{5,4},{6,7},{7,6},{8,9},{9,8},{10,11... | collective-permute-start | bytes 589832 | tf_op jit(solution)/shard_map/ppermute | solution.py:462
  1.3 13.1 %collective-permute-start.1 = (bf16[48,512]{1,0:T(8,128)(2,1)S(1)}, bf16[48,512]{1,0:T(8,128)(2,1)S(1)}, u32[]{:S(2)}, u32[]{:S(2)}) collective-permute-start(bf16[48,512]{1,0:T(8,128)(2,1)S(1)} %get-tuple-element.26), channel_id=1, source_target_pairs={{0,8},{1,9},{2,10},{3,11},{4,12},{5,13},{6,14},{7,15},{8,0},{9,1},... | collective-permute-start | bytes 147464 | tf_op jit(solution)/shard_map/ppermute | solution.py:463
  5.1 9.4 %collective-permute-start.2 = (bf16[2,48,512]{2,1,0:T(8,128)(2,1)S(1)}, bf16[2,48,512]{2,1,0:T(8,128)(2,1)S(1)}, u32[]{:S(2)}, u32[]{:S(2)}) collective-permute-start(bf16[2,48,512]{2,1,0:T(8,128)(2,1)S(1)} %get-tuple-element.31), channel_id=1, source_target_pairs={{0,4},{1,13},{2,6},{3,15},{4,0},{5,9},{6,2},{7,11},{8,12},{9,5},{1... | collective-permute-start | bytes 294920 | tf_op jit(solution)/shard_map/ppermute | solution.py:471
  7.3 7.3 %collective-permute-start.3 = (bf16[2,48,512]{2,1,0:T(8,128)(2,1)S(1)}, bf16[2,48,512]{2,1,0:T(8,128)(2,1)S(1)}, u32[]{:S(2)}, u32[]{:S(2)}) collective-permute-start(bf16[2,48,512]{2,1,0:T(8,128)(2,1)S(1)} %get-tuple-element.32), channel_id=1, source_target_pairs={{0,2},{1,11},{2,0},{3,9},{4,6},{5,15},{6,4},{7,13},{8,10},{9,3},{1... | collective-permute-start | bytes 294920 | tf_op jit(solution)/shard_map/ppermute | solution.py:471
  8.6 6.8 %collective-permute-start.4 = (bf16[2,48,512]{2,1,0:T(8,128)(2,1)S(1)}, bf16[2,48,512]{2,1,0:T(8,128)(2,1)S(1)}, u32[]{:S(2)}, u32[]{:S(2)}) collective-permute-start(bf16[2,48,512]{2,1,0:T(8,128)(2,1)S(1)} %get-tuple-element.33), channel_id=1, source_target_pairs={{0,6},{1,15},{2,4},{3,13},{4,2},{5,11},{6,0},{7,9},{8,14},{9,7},{1... | collective-permute-start | bytes 294920 | tf_op jit(solution)/shard_map/ppermute | solution.py:471
  15.5 1.7 %collective-permute-start.5 = (bf16[7,48,512]{2,1,0:T(8,128)(2,1)S(1)}, bf16[7,48,512]{2,1,0:T(8,128)(2,1)S(1)}, u32[]{:S(2)}, u32[]{:S(2)}) collective-permute-start(bf16[7,48,512]{2,1,0:T(8,128)(2,1)S(1)} %shard_map.130.refs_2_), channel_id=1, source_target_pairs={{0,1},{1,0},{2,3},{3,2},{4,5},{5,4},{6,7},{7,6},{8,9},{9,8},{10,11... | collective-permute-start | bytes 1032200 | tf_op jit(solution)/shard_map/ppermute | solution.py:508
  15.6 1.6 %copy-start = (bf16[96,96]{1,0:T(8,128)(2,1)S(1)}, bf16[96,96]{1,0:T(8,128)(2,1)}, u32[]{:S(2)}) copy-start(bf16[96,96]{1,0:T(8,128)(2,1)} %constant.22.clone.refs_8_) | copy-start | bytes 55300
  15.6 1.6 %copy-start.1 = (bf16[64,96]{1,0:T(8,128)(2,1)S(1)}, bf16[64,96]{1,0:T(8,128)(2,1)}, u32[]{:S(2)}) copy-start(bf16[64,96]{1,0:T(8,128)(2,1)} %constant.23.clone.refs_9_) | copy-start | bytes 36868

commit v12 on v11

--- a/solution.py
+++ b/solution.py
@@ -247,14 +247,19 @@
     inverse_ref[FP + NF :] = jnp.zeros((FP - NF, OH), BF)
 
 
-def build_templates(col, rot_ref, bank_ref, plane_ref, line_ref, turn_ref, out_ref):
+def flat_templates(rot_ref, bank_ref, plane_ref, flat_ref):
     chosen = jnp.concatenate([bank_ref[rot_ref[r]] for r in range(NTPL)], 0)
     plane = jnp.concatenate([plane_ref[b * Z : b * Z + K] for b in range(K)], 0)
-    flat = jnp.dot(chosen, plane, preferred_element_type=F32).astype(BF)
+    flat_ref[...] = jnp.dot(chosen, plane, preferred_element_type=F32).astype(BF)
+
+
+def template_kernel(_, flat_ref, line_ref, turn_ref, out_ref, done_ref):
+    done_ref[...] = jnp.zeros_like(done_ref)
+    _, col = place()
     cos = jnp.where(col == 0, turn_ref[0, 0:1], turn_ref[0, 1:2])
     sin = jnp.where(col == 0, turn_ref[1, 0:1], turn_ref[1, 1:2])
     for r in range(NTPL):
-        part = flat[r * K : (r + 1) * K]
+        part = flat_ref[r * K : (r + 1) * K]
         stacked = jnp.concatenate([part[:, :FP], part[:, FP:]], 0)
         full = jnp.dot(line_ref[...], stacked, preferred_element_type=F32)
         real, imag = full[:LEN], -full[LEN:]
@@ -263,54 +268,48 @@
 
 
 def prepare_kernel(n_det, n_tile, pairs, turns_ref, _, *refs):
-    sources, outs, targets, (sem, whole_ref, part_ref) = refs[:8], refs[8:13], refs[13:21], refs[21:]
+    sources, outs, targets, (sem, whole_ref, part_ref) = refs[:6], refs[6:11], refs[11:17], refs[17:]
     fetch = [
         pltpu.make_async_copy(a, b, sem.at[i]) for i, (a, b) in enumerate(zip(sources, targets))
     ]
     for copy in fetch:
         copy.start()
-    w_ref, plane_ref, inverse_ref, tmpl_ref, done_ref = outs
+    w_ref, plane_ref, inverse_ref, flat_ref, done_ref = outs
     _, col = place()
     build_weights(n_det, n_tile, pairs, col, turns_ref, w_ref, whole_ref, part_ref)
     for copy in fetch:
         copy.wait()
-    rot_ref, bank_ref, fx_ref, fz_ref, ix_ref, iz_ref, line_ref, turn_ref = targets
+    rot_ref, bank_ref, fx_ref, fz_ref, ix_ref, iz_ref = targets
     build_planes(fx_ref, fz_ref, ix_ref, iz_ref, plane_ref, inverse_ref)
-    build_templates(col, rot_ref, bank_ref, plane_ref, line_ref, turn_ref, tmpl_ref)
+    flat_templates(rot_ref, bank_ref, plane_ref, flat_ref)
     done_ref[...] = jnp.zeros_like(done_ref)
 
 
-def join_kernel(near_ref, *refs):
+def join_kernel(*refs):
     out_ref = refs[-1]
-    out_ref[0] = near_ref[...]
     for j, ref in enumerate(refs[:-1]):
-        out_ref[1 + 2 * j] = ref[0]
-        out_ref[2 + 2 * j] = ref[1]
-
-
-def gather_pieces(near_bit, masks, from_mate, data_ref, home_ref, got_ref, near_ref, held_ref):
+        out_ref[2 * j] = ref[0]
+        out_ref[2 * j + 1] = ref[1]
+
+
+def gather_pieces(near_bit, masks, from_mate, data_ref, home_ref, got_ref, near_ref, near_swap_ref, held_ref):
     chip, core = place()
     mate = 1 - core
     data_ref[chip * XT + core] = home_ref[...]
     data_ref[chip * XT + mate] = got_ref[0]
-    data_ref[(chip ^ near_bit) * XT + core] = near_ref[0]
+    data_ref[(chip ^ near_bit) * XT + core] = near_ref[...]
+    data_ref[(chip ^ near_bit) * XT + mate] = near_swap_ref[...]
     taker, other = (mate, core) if from_mate else (core, mate)
     for j, mask in enumerate(masks):
         source = (chip ^ mask ^ (near_bit * taker)) * XT
-        data_ref[source + taker] = held_ref[1 + 2 * j]
-        data_ref[source + other] = held_ref[2 + 2 * j]
-    return (chip ^ near_bit) * XT + mate
-
-
-def partial_sums(n_tile, pairs, upper, core, data_ref, w_ref, late=None):
+        data_ref[source + taker] = held_ref[2 * j]
+        data_ref[source + other] = held_ref[2 * j + 1]
+
+
+def partial_sums(n_tile, pairs, upper, core, data_ref, w_ref):
     base = 0
     for sources in pairs:
         total = jnp.zeros((LEN, LB), F32)
-        if late is not None:
-            inside = (late >= sources[0]) & (late <= sources[-1])
-            part = data_ref[jnp.where(inside, n_tile - 1 - late, n_tile)]
-            weight = w_ref[base + jnp.clip(late, sources[0], sources[-1]) - sources[0]]
-            total += jnp.dot(part, weight, preferred_element_type=F32)
         for j, src in enumerate(sources):
             if (src >= n_tile // 2) == upper:
                 part = data_ref[jnp.where(core == 0, src, n_tile - 1 - src)]
@@ -320,11 +319,8 @@
 
 
 def half_kernel(near_bit, masks, pairs, n_tile, *refs):
-    home_ref, got_ref, held_ref, w_ref, _, half_ref, data_ref = refs
-    absent = gather_pieces(
-        near_bit, masks, False, data_ref, home_ref, got_ref, held_ref, held_ref
-    )
-    data_ref[absent] = jnp.zeros(data_ref.shape[1:], BF)
+    *pieces, w_ref, _, half_ref, data_ref = refs
+    gather_pieces(near_bit, masks, False, data_ref, *pieces)
     chip, core = place()
     for upper in (False, True):
 
@@ -335,21 +331,16 @@
 
 
 def score_kernel(near_bit, masks, pairs, n_tile, *refs):
-    home_ref, got_ref, held_ref, swap_ref = refs[:4]
-    half_ref, w_ref, tmpl_ref, plane_ref, line_ref, back_ref, inverse_ref = refs[4:11]
-    out_ref, data_ref, vol_ref, mid_ref = refs[11:]
-    absent = gather_pieces(near_bit, masks, True, data_ref, home_ref, got_ref, held_ref, swap_ref)
-    data_ref[absent] = swap_ref[0]
+    half_ref, w_ref, tmpl_ref, plane_ref, line_ref, back_ref, inverse_ref = refs[5:12]
+    out_ref, data_ref, vol_ref, mid_ref = refs[12:]
+    gather_pieces(near_bit, masks, True, data_ref, *refs[:5])
     chip, core = place()
-    data_ref[n_tile] = jnp.zeros(data_ref.shape[1:], BF)
     for upper in (False, True):
         for col in range(XT):
 
             @pl.when(((chip < near_bit) == upper) & (core == col))
             def _():
-                late = n_tile - 1 - absent if col else None
-                sums = partial_sums(n_tile, pairs, upper, col, data_ref, w_ref, late)
-                for q, total in enumerate(sums):
+                for q, total in enumerate(partial_sums(n_tile, pairs, upper, col, data_ref, w_ref)):
                     low = (NQ - 1 - q if col else q) * LB
                     vol_ref[:, low : low + LB] = total + half_ref[q]
 
@@ -473,53 +464,61 @@
             rot_index,
             template_bank,
             *[jnp.asarray(t, F32) for t in tables[:4]],
-            jnp.asarray(line_t),
-            jnp.asarray(tables[4], F32),
         )
-        weights, plane, inverse, spectra, done = pl.pallas_call(
+        weights, plane, inverse, flat, done = pl.pallas_call(
             lambda *refs: prepare_kernel(n_det, n_tile, pairs, *refs),
             out_shape=(
                 shape(n_pair, depth, LB),
                 shape(VH, 2 * FP),
                 shape(2 * FP, OH),
-                shape(NTPL, 2 * LEN, FP),
+                shape(NTPL * K, 2 * FP),
                 shape(8, 128, dtype=F32),
             ),
-            in_specs=[VMEM, VMEM] + [HBM] * 8,
+            in_specs=[VMEM, VMEM] + [HBM] * 6,
             out_specs=(VMEM,) * 5,
             scratch_shapes=[
                 pltpu.SMEM((NTPL,), jnp.int32),
                 *[pltpu.VMEM(c.shape, c.dtype) for c in constants[1:]],
-                pltpu.SemaphoreType.DMA((8,)),
+                pltpu.SemaphoreType.DMA((6,)),
                 pltpu.VMEM((depth, LB), BF),
                 pltpu.VMEM((depth, LB), BF),
             ],
             compiler_params=limit(24),
             cost_estimate=cost(1 << 32, 16 << 20),
         )(turns, merged, *[pinned(c) for c in constants])
-        near_in, done, *arrived = lax.optimization_barrier((near_in, done, *arrived))
+        near_in, done = lax.optimization_barrier((near_in, done))
+        near_swap = lax.ppermute(near_in, "tile", mate)
+        spectra, done = pl.pallas_call(
+            template_kernel,
+            out_shape=(shape(NTPL, 2 * LEN, FP), shape(8, 128, dtype=F32)),
+            in_specs=[VMEM] * 4,
+            out_specs=(VMEM,) * 2,
+            compiler_params=limit(8),
+            cost_estimate=cost(1 << 20, 1 << 14),
+        )(done, flat, jnp.asarray(line_t), jnp.asarray(tables[4], F32))
+        done, near_swap, *arrived = lax.optimization_barrier((done, near_swap, *arrived))
         held = pl.pallas_call(
             join_kernel,
-            out_shape=shape(1 + 2 * n_op, LEN, depth),
-            in_specs=[VMEM] * (1 + n_op),
+            out_shape=shape(2 * n_op, LEN, depth),
+            in_specs=[VMEM] * n_op,
             out_specs=VMEM,
             compiler_params=limit(4),
-        )(near_in, *arrived)
+        )(*arrived)
         swapped = lax.ppermute(held, "tile", mate)
-        pieces = pltpu.VMEM((n_tile + 1, LEN, depth), BF)
+        pieces = pltpu.VMEM((n_tile, LEN, depth), BF)
         half = pl.pallas_call(
             lambda *refs: half_kernel(near_bit, masks, pairs, n_tile, *refs),
             out_shape=shape(NQ, LEN, LB, dtype=F32),
-            in_specs=[VMEM] * 5,
+            in_specs=[VMEM] * 7,
             out_specs=VMEM,
             scratch_shapes=[pieces],
             compiler_params=limit(12),
             cost_estimate=cost(n_pair * LEN * depth * LB, n_pair * depth * LB),
-        )(home, got, held, weights, done)
+        )(home, got, near_in, near_swap, held, weights, done)
         return pl.pallas_call(
             lambda *refs: score_kernel(near_bit, masks, pairs, n_tile, *refs),
             out_shape=shape(1, EDGE, EDGE * Z, dtype=F32),
-            in_specs=[VMEM] * 11,
+            in_specs=[VMEM] * 12,
             out_specs=VMEM,
             scratch_shapes=[
                 pieces,
@@ -531,7 +530,8 @@
         )(
             home,
             got,
-            held,
+            near_in,
+            near_swap,
             swapped,
             half,
             weights,

time: 21.1 us -> 20.9 us (level)
  waiting for transfers between devices: 1.43 us -> 1.2 us
    ppermute x3, waiting for transfers between devices: 0.98 us -> 0.22 us  [local(): lax.ppermute(p, 'tile', route(m))]
    ppermute x0 -> x1, waiting for transfers between devices: none -> 0.6 us  [local(): near_swap = lax.ppermute(near_in, 'tile', mate)]
    pallas_call x1 -> x2, Pallas kernels: 0.02 us -> 0.61 us  [the longest x1 0.59 us: local(): pl.pallas_call(template_kernel, out_shape=(shape(NTPL, 2 * LEN, FP), shap...]
    pallas_call x1, Pallas kernels: 4.92 us -> 4.38 us  [local(): pl.pallas_call(lambda *refs: prepare_kernel(n_det, n_tile, pairs, *refs),...]
    pallas_call x1, Pallas kernels: 3.76 us -> 3.54 us  [local(): pl.pallas_call(lambda *refs: score_kernel(near_bit, masks, pairs, n_tile,...]
  transfers between devices with their start and end apart: 6 -> 7, of which waited for: 2 -> 3; matrix products, arithmetic and copies ran while one was open for 0% -> 0% of each run, Pallas kernels for 29% -> 30%
where the time goes in v12:
time: 20.9 us; the launch traced here: 20.7 us
  Pallas kernels  10.9 us (52%)
  starting transfers between devices  8.45 us (40%)
  waiting for transfers between devices  1.2 us (6%)
    ppermute x3, starting transfers between devices, local(): lax.ppermute(p, 'tile', route(m))  4.41 us
    pallas_call x1, Pallas kernels, local(): pl.pallas_call(lambda *refs: prepare_kernel(n_det, n_tile, pairs, *refs),...  4.38 us
    ppermute x1, starting transfers between devices, local(): near_in = lax.ppermute(near, 'tile', near_pairs)  3.77 us
    pallas_call x1, Pallas kernels, local(): pl.pallas_call(lambda *refs: score_kernel(near_bit, masks, pairs, n_tile,...  3.54 us
    pallas_call x1, Pallas kernels, local(): pl.pallas_call(lambda *refs: pack_kernel(near_bit, masks, *refs), out_sha...  1.21 us
    pallas_call x1, Pallas kernels, local(): pl.pallas_call(lambda *refs: half_kernel(near_bit, masks, pairs, n_tile,...  1.17 us
    ppermute x1, waiting for transfers between devices, local(): near_swap = lax.ppermute(near_in, 'tile', mate)  0.6 us
    pallas_call x1, Pallas kernels, local(): pl.pallas_call(template_kernel, out_shape=(shape(NTPL, 2 * LEN, FP), shap...  0.59 us
  transfers between devices with their start and end apart: 7, of which 3 were waited for; matrix products, arithmetic and copies ran while one was open for 0% of the time, Pallas kernels for 30%

profile of v12, /device:TPU:1, one launch (start us, length us, event | category | flops | bytes accessed | tf_op | source)
XLA Modules:
  0.0 20.7 jit_solution(15293516679421992973)
XLA Ops:
  0.0 1.2 %shard_map.127 = (f32[2,61,256]{2,1,0:T(8,128)S(1)}, bf16[48,512]{1,0:T(8,128)(2,1)S(1)}, bf16[48,512]{1,0:T(8,128)(2,1)S(1)}, bf16[4,48,512]{2,1,0:T(8,128)(2,1)S(1)}, bf16[3,48,512]{2,1,0:T(8,128)(2,1)S(1)}) custom-call(s32[2,61]{1,0:T(2,128)} %bitcast.4, f32[1,61]{1,0:T(1,128)} %bitcast.5, bf16[61,8,256]{2,1,0:T(8,128)(2,1)} %bitcast.3), custom_call_target="tpu_custom_call" | custom-call | tf_op jit(solution)/shard_map/pallas_call | solution.py:433
  1.2 0.1 collective-permute-start
  1.3 3.8 %collective-permute-start.1 = (bf16[48,512]{1,0:T(8,128)(2,1)S(1)}, bf16[48,512]{1,0:T(8,128)(2,1)S(1)}, u32[]{:S(2)}, u32[]{:S(2)}) collective-permute-start(bf16[48,512]{1,0:T(8,128)(2,1)S(1)} %get-tuple-element.30), channel_id=1, source_target_pairs={{0,8},{1,9},{2,10},{3,11},{4,12},{5,13},{6,14},{7,15},{8,0},{9,1},... | collective-permute-start | bytes 147464 | tf_op jit(solution)/shard_map/ppermute | solution.py:454
  5.1 0.0 collective-permute-done.got_ref.refs_1_
  5.1 2.1 %collective-permute-start.3 = (bf16[2,48,512]{2,1,0:T(8,128)(2,1)S(1)}, bf16[2,48,512]{2,1,0:T(8,128)(2,1)S(1)}, u32[]{:S(2)}, u32[]{:S(2)}) collective-permute-start(bf16[2,48,512]{2,1,0:T(8,128)(2,1)S(1)} %get-tuple-element.39), channel_id=1, source_target_pairs={{0,4},{1,13},{2,6},{3,15},{4,0},{5,9},{6,2},{7,11},{8,12},{9,5},{1... | collective-permute-start | bytes 294920 | tf_op jit(solution)/shard_map/ppermute | solution.py:462
  7.3 1.4 %collective-permute-start.4 = (bf16[2,48,512]{2,1,0:T(8,128)(2,1)S(1)}, bf16[2,48,512]{2,1,0:T(8,128)(2,1)S(1)}, u32[]{:S(2)}, u32[]{:S(2)}) collective-permute-start(bf16[2,48,512]{2,1,0:T(8,128)(2,1)S(1)} %get-tuple-element.40), channel_id=1, source_target_pairs={{0,2},{1,11},{2,0},{3,9},{4,6},{5,15},{6,4},{7,13},{8,10},{9,3},{1... | collective-permute-start | bytes 294920 | tf_op jit(solution)/shard_map/ppermute | solution.py:462
  8.6 0.9 %collective-permute-start.5 = (bf16[2,48,512]{2,1,0:T(8,128)(2,1)S(1)}, bf16[2,48,512]{2,1,0:T(8,128)(2,1)S(1)}, u32[]{:S(2)}, u32[]{:S(2)}) collective-permute-start(bf16[2,48,512]{2,1,0:T(8,128)(2,1)S(1)} %get-tuple-element.41), channel_id=1, source_target_pairs={{0,6},{1,15},{2,4},{3,13},{4,2},{5,11},{6,0},{7,9},{8,14},{9,7},{1... | collective-permute-start | bytes 294920 | tf_op jit(solution)/shard_map/ppermute | solution.py:462
  9.6 4.4 %shard_map.129 = (bf16[34,512,256]{2,1,0:T(8,128)(2,1)S(1)}, bf16[640,2048]{1,0:T(8,128)(2,1)S(1)}, bf16[2048,512]{1,0:T(8,128)(2,1)S(1)}, bf16[128,2048]{1,0:T(8,128)(2,1)S(1)}, f32[8,128]{1,0:T(8,128)S(1)}) custom-call(f32[2,61,256]{2,1,0:T(8,128)S(1)} %get-tuple-element.31.refs_0_, f32[8,128]{1,0:T(8,128)S(1)} %get-tuple-element.33.refs_1_, s32[8]{0:T(128)} %refs_2_.1, ...), custom_call_target="tpu_custom_call" | custom-call | flops 4294967296 | bytes 16777216 | tf_op jit(solution)/shard_map/pallas_call | solution.py:468
  14.0 0.0 collective-permute-done.1.refs_2_
  14.0 0.1 collective-permute-start.2
  14.0 0.0 copy-done.1
  14.1 0.0 copy-done.3
  14.1 0.6 %shard_map.130 = (bf16[8,96,1024]{2,1,0:T(8,128)(2,1)S(1)}, f32[8,128]{1,0:T(8,128)S(1)}) custom-call(f32[8,128]{1,0:T(8,128)S(1)} %get-tuple-element.36._, bf16[128,2048]{1,0:T(8,128)(2,1)S(1)} %get-tuple-element.37.flat_ref, bf16[96,32]{1,0:T(8,128)(2,1)S(1)} %copy-done.1, f32[2,2,1024]{2,1,0:T(2,128)S(1)} %copy-done.3), custom_call_target="tpu_custom_call" | custom-call | flops 1048576 | bytes 16384 | tf_op jit(solution)/shard_map/pallas_call | solution.py:491
  14.7 0.6 %collective-permute-done.2.refs_3_ = bf16[48,512]{1,0:T(8,128)(2,1)S(1)} collective-permute-done((bf16[48,512]{1,0:T(8,128)(2,1)S(1)}, bf16[48,512]{1,0:T(8,128)(2,1)S(1)}, u32[]{:S(2)}, u32[]{:S(2)}) %collective-permute-start.2) | collective-permute-done | bytes 49184 | tf_op jit(solution)/shard_map/ppermute | solution.py:490
  15.3 0.0 collective-permute-done.3.refs_0_
  15.3 0.0 collective-permute-done.4.refs_1_
  15.3 0.2 %collective-permute-done.5.refs_2_ = bf16[2,48,512]{2,1,0:T(8,128)(2,1)S(1)} collective-permute-done((bf16[2,48,512]{2,1,0:T(8,128)(2,1)S(1)}, bf16[2,48,512]{2,1,0:T(8,128)(2,1)S(1)}, u32[]{:S(2)}, u32[]{:S(2)}) %collective-permute-start.5) | collective-permute-done | bytes 98336 | tf_op jit(solution)/shard_map/ppermute | solution.py:462
  15.5 0.1 collective-permute-start.6
  15.6 0.0 copy-start
  15.6 0.0 copy-start.2
  15.6 1.2 %shard_map.132.refs_5_ = f32[5,48,256]{2,1,0:T(8,128)S(1)} custom-call(bf16[48,512]{1,0:T(8,128)(2,1)S(1)} %get-tuple-element.28.refs_0_, bf16[4,48,512]{2,1,0:T(8,128)(2,1)S(1)} %collective-permute-done.got_ref.refs_1_, bf16[48,512]{1,0:T(8,128)(2,1)S(1)} %collective-permute-done.1.refs_2_, bf16[48,512]{1,0:T(8,128)(2,1)S(1)} %collective-permute-done.2.refs_3_, ...), custom_call_target="tpu_custom_call" | custom-call | flops 213909504 | bytes 4456448 | tf_op jit(solution)/shard_map/pallas_call | solution.py:509
  16.8 0.4 %collective-permute-done.6.refs_4_ = bf16[6,48,512]{2,1,0:T(8,128)(2,1)S(1)} collective-permute-done((bf16[6,48,512]{2,1,0:T(8,128)(2,1)S(1)}, bf16[6,48,512]{2,1,0:T(8,128)(2,1)S(1)}, u32[]{:S(2)}, u32[]{:S(2)}) %collective-permute-start.6) | collective-permute-done | bytes 294944 | tf_op jit(solution)/shard_map/ppermute | solution.py:507
  17.2 0.0 copy-done
  17.2 3.5 %shard_map.133 = f32[1,32,1024]{2,1,0:T(8,128)} custom-call(bf16[48,512]{1,0:T(8,128)(2,1)S(1)} %get-tuple-element.28.refs_0_, bf16[4,48,512]{2,1,0:T(8,128)(2,1)S(1)} %collective-permute-done.got_ref.refs_1_, bf16[48,512]{1,0:T(8,128)(2,1)S(1)} %collective-permute-done.1.refs_2_, bf16[48,512]{1,0:T(8,128)(2,1)S(1)} %collective-permute-done.2.refs_3_, ...), custom_call_target="tpu_custom_call" | custom-call | flops 4294967296 | bytes 20971520 | tf_op jit(solution)/shard_map/pallas_call | solution.py:518
  (5 shorter events, 0.0 us)
Async XLA Ops:
  1.2 3.9 %collective-permute-start = (bf16[4,48,512]{2,1,0:T(8,128)(2,1)S(1)}, bf16[4,48,512]{2,1,0:T(8,128)(2,1)S(1)}, u32[]{:S(2)}, u32[]{:S(2)}) collective-permute-start(bf16[4,48,512]{2,1,0:T(8,128)(2,1)S(1)} %get-tuple-element.29), channel_id=1, source_target_pairs={{0,1},{1,0},{2,3},{3,2},{4,5},{5,4},{6,7},{7,6},{8,9},{9,8},{10,11... | collective-permute-start | bytes 589832 | tf_op jit(solution)/shard_map/ppermute | solution.py:453
  1.3 12.6 %collective-permute-start.1 = (bf16[48,512]{1,0:T(8,128)(2,1)S(1)}, bf16[48,512]{1,0:T(8,128)(2,1)S(1)}, u32[]{:S(2)}, u32[]{:S(2)}) collective-permute-start(bf16[48,512]{1,0:T(8,128)(2,1)S(1)} %get-tuple-element.30), channel_id=1, source_target_pairs={{0,8},{1,9},{2,10},{3,11},{4,12},{5,13},{6,14},{7,15},{8,0},{9,1},... | collective-permute-start | bytes 147464 | tf_op jit(solution)/shard_map/ppermute | solution.py:454
  5.1 10.1 %collective-permute-start.3 = (bf16[2,48,512]{2,1,0:T(8,128)(2,1)S(1)}, bf16[2,48,512]{2,1,0:T(8,128)(2,1)S(1)}, u32[]{:S(2)}, u32[]{:S(2)}) collective-permute-start(bf16[2,48,512]{2,1,0:T(8,128)(2,1)S(1)} %get-tuple-element.39), channel_id=1, source_target_pairs={{0,4},{1,13},{2,6},{3,15},{4,0},{5,9},{6,2},{7,11},{8,12},{9,5},{1... | collective-permute-start | bytes 294920 | tf_op jit(solution)/shard_map/ppermute | solution.py:462
  7.3 8.0 %collective-permute-start.4 = (bf16[2,48,512]{2,1,0:T(8,128)(2,1)S(1)}, bf16[2,48,512]{2,1,0:T(8,128)(2,1)S(1)}, u32[]{:S(2)}, u32[]{:S(2)}) collective-permute-start(bf16[2,48,512]{2,1,0:T(8,128)(2,1)S(1)} %get-tuple-element.40), channel_id=1, source_target_pairs={{0,2},{1,11},{2,0},{3,9},{4,6},{5,15},{6,4},{7,13},{8,10},{9,3},{1... | collective-permute-start | bytes 294920 | tf_op jit(solution)/shard_map/ppermute | solution.py:462
  8.6 6.8 %collective-permute-start.5 = (bf16[2,48,512]{2,1,0:T(8,128)(2,1)S(1)}, bf16[2,48,512]{2,1,0:T(8,128)(2,1)S(1)}, u32[]{:S(2)}, u32[]{:S(2)}) collective-permute-start(bf16[2,48,512]{2,1,0:T(8,128)(2,1)S(1)} %get-tuple-element.41), channel_id=1, source_target_pairs={{0,6},{1,15},{2,4},{3,13},{4,2},{5,11},{6,0},{7,9},{8,14},{9,7},{1... | collective-permute-start | bytes 294920 | tf_op jit(solution)/shard_map/ppermute | solution.py:462
  9.6 4.5 %copy-start.1 = (bf16[96,32]{1,0:T(8,128)(2,1)S(1)}, bf16[96,32]{1,0:T(8,128)(2,1)}, u32[]{:S(2)}) copy-start(bf16[96,32]{1,0:T(8,128)(2,1)} %constant.20.clone.line_ref) | copy-start | bytes 18436
  9.6 4.5 %copy-start.3 = (f32[2,2,1024]{2,1,0:T(2,128)S(1)}, f32[2,2,1024]{2,1,0:T(2,128)}, u32[]{:S(2)}) copy-start(f32[2,2,1024]{2,1,0:T(2,128)} %constant.21.clone.turn_ref) | copy-start | bytes 49156
  14.0 1.3 %collective-permute-start.2 = (bf16[48,512]{1,0:T(8,128)(2,1)S(1)}, bf16[48,512]{1,0:T(8,128)(2,1)S(1)}, u32[]{:S(2)}, u32[]{:S(2)}) collective-permute-start(bf16[48,512]{1,0:T(8,128)(2,1)S(1)} %collective-permute-done.1.refs_2_), channel_id=1, source_target_pairs={{0,1},{1,0},{2,3},{3,2},{4,5},{5,4},{6,7},{7,6},{8,9},{9,8},{10,11... | collective-permute-start | bytes 147464 | tf_op jit(solution)/shard_map/ppermute | solution.py:490
  15.5 1.6 %collective-permute-start.6 = (bf16[6,48,512]{2,1,0:T(8,128)(2,1)S(1)}, bf16[6,48,512]{2,1,0:T(8,128)(2,1)S(1)}, u32[]{:S(2)}, u32[]{:S(2)}) collective-permute-start(bf16[6,48,512]{2,1,0:T(8,128)(2,1)S(1)} %shard_map.131.refs_4_), channel_id=1, source_target_pairs={{0,1},{1,0},{2,3},{3,2},{4,5},{5,4},{6,7},{7,6},{8,9},{9,8},{10,11... | collective-permute-start | bytes 884744 | tf_op jit(solution)/shard_map/ppermute | solution.py:507
  15.6 1.6 %copy-start = (bf16[96,96]{1,0:T(8,128)(2,1)S(1)}, bf16[96,96]{1,0:T(8,128)(2,1)}, u32[]{:S(2)}) copy-start(bf16[96,96]{1,0:T(8,128)(2,1)} %constant.22.clone.refs_9_) | copy-start | bytes 55300
  15.6 1.6 %copy-start.2 = (bf16[64,96]{1,0:T(8,128)(2,1)S(1)}, bf16[64,96]{1,0:T(8,128)(2,1)}, u32[]{:S(2)}) copy-start(bf16[64,96]{1,0:T(8,128)(2,1)} %constant.23.clone.refs_10_) | copy-start | bytes 36868

commit v13 on v12

--- a/solution.py
+++ b/solution.py
@@ -219,7 +219,7 @@
         base += len(sources)
 
 
-def build_planes(fx_ref, fz_ref, ix_ref, iz_ref, plane_ref, inverse_ref):
+def build_plane(fx_ref, fz_ref, plane_ref):
     def forward(x, carry):
         cos_x, sin_x = fx_ref[0, pl.ds(x, 1)], fx_ref[1, pl.ds(x, 1)]
         cos_z, sin_z = fz_ref[0], fz_ref[1]
@@ -229,6 +229,9 @@
         return carry
 
     lax.fori_loop(0, XR // 2, forward, 0)
+
+
+def build_inverse(ix_ref, iz_ref, inverse_ref):
     odd = lax.broadcasted_iota(jnp.int32, (1, OH), 1) // EDGE % 2
     turn = 1.0 - 2.0 * odd.astype(F32)
 
@@ -253,7 +256,10 @@
     flat_ref[...] = jnp.dot(chosen, plane, preferred_element_type=F32).astype(BF)
 
 
-def template_kernel(_, flat_ref, line_ref, turn_ref, out_ref, done_ref):
+def template_kernel(
+    _, flat_ref, ix_ref, iz_ref, line_ref, turn_ref, out_ref, inverse_ref, done_ref
+):
+    build_inverse(ix_ref, iz_ref, inverse_ref)
     done_ref[...] = jnp.zeros_like(done_ref)
     _, col = place()
     cos = jnp.where(col == 0, turn_ref[0, 0:1], turn_ref[0, 1:2])
@@ -268,19 +274,19 @@
 
 
 def prepare_kernel(n_det, n_tile, pairs, turns_ref, _, *refs):
-    sources, outs, targets, (sem, whole_ref, part_ref) = refs[:6], refs[6:11], refs[11:17], refs[17:]
+    sources, outs, targets, (sem, whole_ref, part_ref) = refs[:4], refs[4:8], refs[8:12], refs[12:]
     fetch = [
         pltpu.make_async_copy(a, b, sem.at[i]) for i, (a, b) in enumerate(zip(sources, targets))
     ]
     for copy in fetch:
         copy.start()
-    w_ref, plane_ref, inverse_ref, flat_ref, done_ref = outs
+    w_ref, plane_ref, flat_ref, done_ref = outs
     _, col = place()
     build_weights(n_det, n_tile, pairs, col, turns_ref, w_ref, whole_ref, part_ref)
     for copy in fetch:
         copy.wait()
-    rot_ref, bank_ref, fx_ref, fz_ref, ix_ref, iz_ref = targets
-    build_planes(fx_ref, fz_ref, ix_ref, iz_ref, plane_ref, inverse_ref)
+    rot_ref, bank_ref, fx_ref, fz_ref = targets
+    build_plane(fx_ref, fz_ref, plane_ref)
     flat_templates(rot_ref, bank_ref, plane_ref, flat_ref)
     done_ref[...] = jnp.zeros_like(done_ref)
 
@@ -463,23 +469,22 @@
         constants = (
             rot_index,
             template_bank,
-            *[jnp.asarray(t, F32) for t in tables[:4]],
+            *[jnp.asarray(t, F32) for t in tables[:2]],
         )
-        weights, plane, inverse, flat, done = pl.pallas_call(
+        weights, plane, flat, done = pl.pallas_call(
             lambda *refs: prepare_kernel(n_det, n_tile, pairs, *refs),
             out_shape=(
                 shape(n_pair, depth, LB),
                 shape(VH, 2 * FP),
-                shape(2 * FP, OH),
                 shape(NTPL * K, 2 * FP),
                 shape(8, 128, dtype=F32),
             ),
-            in_specs=[VMEM, VMEM] + [HBM] * 6,
-            out_specs=(VMEM,) * 5,
+            in_specs=[VMEM, VMEM] + [HBM] * 4,
+            out_specs=(VMEM,) * 4,
             scratch_shapes=[
                 pltpu.SMEM((NTPL,), jnp.int32),
                 *[pltpu.VMEM(c.shape, c.dtype) for c in constants[1:]],
-                pltpu.SemaphoreType.DMA((6,)),
+                pltpu.SemaphoreType.DMA((4,)),
                 pltpu.VMEM((depth, LB), BF),
                 pltpu.VMEM((depth, LB), BF),
             ],
@@ -488,14 +493,25 @@
         )(turns, merged, *[pinned(c) for c in constants])
         near_in, done = lax.optimization_barrier((near_in, done))
         near_swap = lax.ppermute(near_in, "tile", mate)
-        spectra, done = pl.pallas_call(
+        spectra, inverse, done = pl.pallas_call(
             template_kernel,
-            out_shape=(shape(NTPL, 2 * LEN, FP), shape(8, 128, dtype=F32)),
-            in_specs=[VMEM] * 4,
-            out_specs=(VMEM,) * 2,
+            out_shape=(
+                shape(NTPL, 2 * LEN, FP),
+                shape(2 * FP, OH),
+                shape(8, 128, dtype=F32),
+            ),
+            in_specs=[VMEM] * 6,
+            out_specs=(VMEM,) * 3,
             compiler_params=limit(8),
             cost_estimate=cost(1 << 20, 1 << 14),
-        )(done, flat, jnp.asarray(line_t), jnp.asarray(tables[4], F32))
+        )(
+            done,
+            flat,
+            jnp.asarray(tables[2], F32),
+            jnp.asarray(tables[3], F32),
+            jnp.asarray(line_t),
+            jnp.asarray(tables[4], F32),
+        )
         done, near_swap, *arrived = lax.optimization_barrier((done, near_swap, *arrived))
         held = pl.pallas_call(
             join_kernel,

time: 20.9 us -> 20.9 us (level)
    ppermute x1, waiting for transfers between devices: 0.6 us -> 0.02 us  [local(): near_swap = lax.ppermute(near_in, 'tile', mate)]
    pallas_call x1, Pallas kernels: 4.38 us -> 3.8 us  [local(): pl.pallas_call(lambda *refs: prepare_kernel(n_det, n_tile, pairs, *refs),...]
    ppermute x3, waiting for transfers between devices: 0.22 us -> 0.79 us  [local(): lax.ppermute(p, 'tile', route(m))]
    pallas_call x1, Pallas kernels: 0.59 us -> 1.15 us  [local(): pl.pallas_call(template_kernel, out_shape=(shape(NTPL, 2 * LEN, FP), shap...]
  transfers between devices with their start and end apart: 7 -> 7, of which waited for: 3 -> 2; matrix products, arithmetic and copies ran while one was open for 0% -> 0% of each run, Pallas kernels for 30% -> 30%
where the time goes in v13:
time: 20.9 us; the launch traced here: 20.7 us
  Pallas kernels  10.9 us (52%)
  starting transfers between devices  8.45 us (40%)
  waiting for transfers between devices  1.18 us (6%)
    ppermute x3, starting transfers between devices, local(): lax.ppermute(p, 'tile', route(m))  4.41 us
    pallas_call x1, Pallas kernels, local(): pl.pallas_call(lambda *refs: prepare_kernel(n_det, n_tile, pairs, *refs),...  3.8 us
    ppermute x1, starting transfers between devices, local(): near_in = lax.ppermute(near, 'tile', near_pairs)  3.77 us
    pallas_call x1, Pallas kernels, local(): pl.pallas_call(lambda *refs: score_kernel(near_bit, masks, pairs, n_tile,...  3.55 us
    pallas_call x1, Pallas kernels, local(): pl.pallas_call(lambda *refs: pack_kernel(near_bit, masks, *refs), out_sha...  1.21 us
    pallas_call x1, Pallas kernels, local(): pl.pallas_call(lambda *refs: half_kernel(near_bit, masks, pairs, n_tile,...  1.17 us
    pallas_call x1, Pallas kernels, local(): pl.pallas_call(template_kernel, out_shape=(shape(NTPL, 2 * LEN, FP), shap...  1.15 us
    ppermute x3, waiting for transfers between devices, local(): lax.ppermute(p, 'tile', route(m))  0.79 us
  transfers between devices with their start and end apart: 7, of which 2 were waited for; matrix products, arithmetic and copies ran while one was open for 0% of the time, Pallas kernels for 30%

profile of v13, /device:TPU:1, one launch (start us, length us, event | category | flops | bytes accessed | tf_op | source)
XLA Modules:
  0.0 20.7 jit_solution(2404738133327014987)
XLA Ops:
  0.0 1.2 %shard_map.127 = (f32[2,61,256]{2,1,0:T(8,128)S(1)}, bf16[48,512]{1,0:T(8,128)(2,1)S(1)}, bf16[48,512]{1,0:T(8,128)(2,1)S(1)}, bf16[4,48,512]{2,1,0:T(8,128)(2,1)S(1)}, bf16[3,48,512]{2,1,0:T(8,128)(2,1)S(1)}) custom-call(s32[2,61]{1,0:T(2,128)} %bitcast.4, f32[1,61]{1,0:T(1,128)} %bitcast.5, bf16[61,8,256]{2,1,0:T(8,128)(2,1)} %bitcast.3), custom_call_target="tpu_custom_call" | custom-call | tf_op jit(solution)/shard_map/pallas_call | solution.py:439
  1.2 0.1 collective-permute-start
  1.3 3.8 %collective-permute-start.1 = (bf16[48,512]{1,0:T(8,128)(2,1)S(1)}, bf16[48,512]{1,0:T(8,128)(2,1)S(1)}, u32[]{:S(2)}, u32[]{:S(2)}) collective-permute-start(bf16[48,512]{1,0:T(8,128)(2,1)S(1)} %get-tuple-element.30), channel_id=1, source_target_pairs={{0,8},{1,9},{2,10},{3,11},{4,12},{5,13},{6,14},{7,15},{8,0},{9,1},... | collective-permute-start | bytes 147464 | tf_op jit(solution)/shard_map/ppermute | solution.py:460
  5.1 0.0 collective-permute-done.got_ref.refs_1_
  5.1 2.1 %collective-permute-start.3 = (bf16[2,48,512]{2,1,0:T(8,128)(2,1)S(1)}, bf16[2,48,512]{2,1,0:T(8,128)(2,1)S(1)}, u32[]{:S(2)}, u32[]{:S(2)}) collective-permute-start(bf16[2,48,512]{2,1,0:T(8,128)(2,1)S(1)} %get-tuple-element.39), channel_id=1, source_target_pairs={{0,4},{1,13},{2,6},{3,15},{4,0},{5,9},{6,2},{7,11},{8,12},{9,5},{1... | collective-permute-start | bytes 294920 | tf_op jit(solution)/shard_map/ppermute | solution.py:468
  7.3 1.4 %collective-permute-start.4 = (bf16[2,48,512]{2,1,0:T(8,128)(2,1)S(1)}, bf16[2,48,512]{2,1,0:T(8,128)(2,1)S(1)}, u32[]{:S(2)}, u32[]{:S(2)}) collective-permute-start(bf16[2,48,512]{2,1,0:T(8,128)(2,1)S(1)} %get-tuple-element.40), channel_id=1, source_target_pairs={{0,2},{1,11},{2,0},{3,9},{4,6},{5,15},{6,4},{7,13},{8,10},{9,3},{1... | collective-permute-start | bytes 294920 | tf_op jit(solution)/shard_map/ppermute | solution.py:468
  8.6 0.9 %collective-permute-start.5 = (bf16[2,48,512]{2,1,0:T(8,128)(2,1)S(1)}, bf16[2,48,512]{2,1,0:T(8,128)(2,1)S(1)}, u32[]{:S(2)}, u32[]{:S(2)}) collective-permute-start(bf16[2,48,512]{2,1,0:T(8,128)(2,1)S(1)} %get-tuple-element.41), channel_id=1, source_target_pairs={{0,6},{1,15},{2,4},{3,13},{4,2},{5,11},{6,0},{7,9},{8,14},{9,7},{1... | collective-permute-start | bytes 294920 | tf_op jit(solution)/shard_map/ppermute | solution.py:468
  9.6 3.8 %shard_map.129 = (bf16[34,512,256]{2,1,0:T(8,128)(2,1)S(1)}, bf16[640,2048]{1,0:T(8,128)(2,1)S(1)}, bf16[128,2048]{1,0:T(8,128)(2,1)S(1)}, f32[8,128]{1,0:T(8,128)S(1)}) custom-call(f32[2,61,256]{2,1,0:T(8,128)S(1)} %get-tuple-element.31.refs_0_, f32[8,128]{1,0:T(8,128)S(1)} %get-tuple-element.33.refs_1_, s32[8]{0:T(128)} %refs_2_.1, ...), custom_call_target="tpu_custom_call" | custom-call | flops 4294967296 | bytes 16777216 | tf_op jit(solution)/shard_map/pallas_call | solution.py:474
  13.4 0.0 collective-permute-done.1.refs_2_
  13.4 0.1 collective-permute-start.2
  13.5 0.0 copy-done
  13.5 0.0 copy-done.1
  13.5 1.2 %shard_map.130 = (bf16[8,96,1024]{2,1,0:T(8,128)(2,1)S(1)}, bf16[2048,512]{1,0:T(8,128)(2,1)S(1)}, f32[8,128]{1,0:T(8,128)S(1)}) custom-call(f32[8,128]{1,0:T(8,128)S(1)} %get-tuple-element.36._, bf16[128,2048]{1,0:T(8,128)(2,1)S(1)} %get-tuple-element.37.flat_ref, f32[2,24,512]{2,1,0:T(8,128)S(1)} %copy-done, f32[2,21,512]{2,1,0:T(8,128)S(1)} %copy-done.1, ...), custom_call_target="tpu_custom_call" | custom-call | flops 1048576 | bytes 16384 | tf_op jit(solution)/shard_map/pallas_call | solution.py:496
  14.7 0.0 collective-permute-done.2.refs_3_
  14.7 0.0 collective-permute-done.3.refs_0_
  14.7 0.0 collective-permute-done.4.refs_1_
  14.7 0.8 %collective-permute-done.5.refs_2_ = bf16[2,48,512]{2,1,0:T(8,128)(2,1)S(1)} collective-permute-done((bf16[2,48,512]{2,1,0:T(8,128)(2,1)S(1)}, bf16[2,48,512]{2,1,0:T(8,128)(2,1)S(1)}, u32[]{:S(2)}, u32[]{:S(2)}) %collective-permute-start.5) | collective-permute-done | bytes 98336 | tf_op jit(solution)/shard_map/ppermute | solution.py:468
  15.5 0.1 collective-permute-start.6
  15.6 0.0 copy-start.2
  15.6 0.0 copy-start.4
  15.6 1.2 %shard_map.132.refs_5_ = f32[5,48,256]{2,1,0:T(8,128)S(1)} custom-call(bf16[48,512]{1,0:T(8,128)(2,1)S(1)} %get-tuple-element.28.refs_0_, bf16[4,48,512]{2,1,0:T(8,128)(2,1)S(1)} %collective-permute-done.got_ref.refs_1_, bf16[48,512]{1,0:T(8,128)(2,1)S(1)} %collective-permute-done.1.refs_2_, bf16[48,512]{1,0:T(8,128)(2,1)S(1)} %collective-permute-done.2.refs_3_, ...), custom_call_target="tpu_custom_call" | custom-call | flops 213909504 | bytes 4456448 | tf_op jit(solution)/shard_map/pallas_call | solution.py:525
  16.8 0.4 %collective-permute-done.6.refs_4_ = bf16[6,48,512]{2,1,0:T(8,128)(2,1)S(1)} collective-permute-done((bf16[6,48,512]{2,1,0:T(8,128)(2,1)S(1)}, bf16[6,48,512]{2,1,0:T(8,128)(2,1)S(1)}, u32[]{:S(2)}, u32[]{:S(2)}) %collective-permute-start.6) | collective-permute-done | bytes 294944 | tf_op jit(solution)/shard_map/ppermute | solution.py:523
  17.2 0.0 copy-done.2
  17.2 3.5 %shard_map.133 = f32[1,32,1024]{2,1,0:T(8,128)} custom-call(bf16[48,512]{1,0:T(8,128)(2,1)S(1)} %get-tuple-element.28.refs_0_, bf16[4,48,512]{2,1,0:T(8,128)(2,1)S(1)} %collective-permute-done.got_ref.refs_1_, bf16[48,512]{1,0:T(8,128)(2,1)S(1)} %collective-permute-done.1.refs_2_, bf16[48,512]{1,0:T(8,128)(2,1)S(1)} %collective-permute-done.2.refs_3_, ...), custom_call_target="tpu_custom_call" | custom-call | flops 4294967296 | bytes 20971520 | tf_op jit(solution)/shard_map/pallas_call | solution.py:534
  (9 shorter events, 0.1 us)
Async XLA Ops:
  1.2 3.9 %collective-permute-start = (bf16[4,48,512]{2,1,0:T(8,128)(2,1)S(1)}, bf16[4,48,512]{2,1,0:T(8,128)(2,1)S(1)}, u32[]{:S(2)}, u32[]{:S(2)}) collective-permute-start(bf16[4,48,512]{2,1,0:T(8,128)(2,1)S(1)} %get-tuple-element.29), channel_id=1, source_target_pairs={{0,1},{1,0},{2,3},{3,2},{4,5},{5,4},{6,7},{7,6},{8,9},{9,8},{10,11... | collective-permute-start | bytes 589832 | tf_op jit(solution)/shard_map/ppermute | solution.py:459
  1.3 12.0 %collective-permute-start.1 = (bf16[48,512]{1,0:T(8,128)(2,1)S(1)}, bf16[48,512]{1,0:T(8,128)(2,1)S(1)}, u32[]{:S(2)}, u32[]{:S(2)}) collective-permute-start(bf16[48,512]{1,0:T(8,128)(2,1)S(1)} %get-tuple-element.30), channel_id=1, source_target_pairs={{0,8},{1,9},{2,10},{3,11},{4,12},{5,13},{6,14},{7,15},{8,0},{9,1},... | collective-permute-start | bytes 147464 | tf_op jit(solution)/shard_map/ppermute | solution.py:460
  5.1 9.6 %collective-permute-start.3 = (bf16[2,48,512]{2,1,0:T(8,128)(2,1)S(1)}, bf16[2,48,512]{2,1,0:T(8,128)(2,1)S(1)}, u32[]{:S(2)}, u32[]{:S(2)}) collective-permute-start(bf16[2,48,512]{2,1,0:T(8,128)(2,1)S(1)} %get-tuple-element.39), channel_id=1, source_target_pairs={{0,4},{1,13},{2,6},{3,15},{4,0},{5,9},{6,2},{7,11},{8,12},{9,5},{1... | collective-permute-start | bytes 294920 | tf_op jit(solution)/shard_map/ppermute | solution.py:468
  7.3 7.4 %collective-permute-start.4 = (bf16[2,48,512]{2,1,0:T(8,128)(2,1)S(1)}, bf16[2,48,512]{2,1,0:T(8,128)(2,1)S(1)}, u32[]{:S(2)}, u32[]{:S(2)}) collective-permute-start(bf16[2,48,512]{2,1,0:T(8,128)(2,1)S(1)} %get-tuple-element.40), channel_id=1, source_target_pairs={{0,2},{1,11},{2,0},{3,9},{4,6},{5,15},{6,4},{7,13},{8,10},{9,3},{1... | collective-permute-start | bytes 294920 | tf_op jit(solution)/shard_map/ppermute | solution.py:468
  8.6 6.8 %collective-permute-start.5 = (bf16[2,48,512]{2,1,0:T(8,128)(2,1)S(1)}, bf16[2,48,512]{2,1,0:T(8,128)(2,1)S(1)}, u32[]{:S(2)}, u32[]{:S(2)}) collective-permute-start(bf16[2,48,512]{2,1,0:T(8,128)(2,1)S(1)} %get-tuple-element.41), channel_id=1, source_target_pairs={{0,6},{1,15},{2,4},{3,13},{4,2},{5,11},{6,0},{7,9},{8,14},{9,7},{1... | collective-permute-start | bytes 294920 | tf_op jit(solution)/shard_map/ppermute | solution.py:468
  9.6 3.9 %copy-start = (f32[2,24,512]{2,1,0:T(8,128)S(1)}, f32[2,24,512]{2,1,0:T(8,128)}, u32[]{:S(2)}) copy-start(f32[2,24,512]{2,1,0:T(8,128)} %constant.18.clone.ix_ref) | copy-start | bytes 294916
  9.6 3.9 %copy-start.1 = (f32[2,21,512]{2,1,0:T(8,128)S(1)}, f32[2,21,512]{2,1,0:T(8,128)}, u32[]{:S(2)}) copy-start(f32[2,21,512]{2,1,0:T(8,128)} %constant.19.clone.iz_ref) | copy-start | bytes 258052
  9.6 3.9 %copy-start.3 = (bf16[96,32]{1,0:T(8,128)(2,1)S(1)}, bf16[96,32]{1,0:T(8,128)(2,1)}, u32[]{:S(2)}) copy-start(bf16[96,32]{1,0:T(8,128)(2,1)} %constant.20.clone.line_ref) | copy-start | bytes 18436
  9.6 3.9 %copy-start.5 = (f32[2,2,1024]{2,1,0:T(2,128)S(1)}, f32[2,2,1024]{2,1,0:T(2,128)}, u32[]{:S(2)}) copy-start(f32[2,2,1024]{2,1,0:T(2,128)} %constant.21.clone.turn_ref) | copy-start | bytes 49156
  13.4 1.3 %collective-permute-start.2 = (bf16[48,512]{1,0:T(8,128)(2,1)S(1)}, bf16[48,512]{1,0:T(8,128)(2,1)S(1)}, u32[]{:S(2)}, u32[]{:S(2)}) collective-permute-start(bf16[48,512]{1,0:T(8,128)(2,1)S(1)} %collective-permute-done.1.refs_2_), channel_id=1, source_target_pairs={{0,1},{1,0},{2,3},{3,2},{4,5},{5,4},{6,7},{7,6},{8,9},{9,8},{10,11... | collective-permute-start | bytes 147464 | tf_op jit(solution)/shard_map/ppermute | solution.py:495
  15.5 1.6 %collective-permute-start.6 = (bf16[6,48,512]{2,1,0:T(8,128)(2,1)S(1)}, bf16[6,48,512]{2,1,0:T(8,128)(2,1)S(1)}, u32[]{:S(2)}, u32[]{:S(2)}) collective-permute-start(bf16[6,48,512]{2,1,0:T(8,128)(2,1)S(1)} %shard_map.131.refs_4_), channel_id=1, source_target_pairs={{0,1},{1,0},{2,3},{3,2},{4,5},{5,4},{6,7},{7,6},{8,9},{9,8},{10,11... | collective-permute-start | bytes 884744 | tf_op jit(solution)/shard_map/ppermute | solution.py:523
  15.6 1.6 %copy-start.2 = (bf16[96,96]{1,0:T(8,128)(2,1)S(1)}, bf16[96,96]{1,0:T(8,128)(2,1)}, u32[]{:S(2)}) copy-start(bf16[96,96]{1,0:T(8,128)(2,1)} %constant.22.clone.refs_9_) | copy-start | bytes 55300
  15.6 1.6 %copy-start.4 = (bf16[64,96]{1,0:T(8,128)(2,1)S(1)}, bf16[64,96]{1,0:T(8,128)(2,1)}, u32[]{:S(2)}) copy-start(bf16[64,96]{1,0:T(8,128)(2,1)} %constant.23.clone.refs_10_) | copy-start | bytes 36868

commit v14 on v12

--- a/solution.py
+++ b/solution.py
@@ -215,7 +215,7 @@
             w_ref[base + j] = jnp.maximum(one - jnp.abs(off), jnp.zeros((), BF))
             return carry
 
-        lax.fori_loop(0, len(sources), build, 0)
+        lax.fori_loop(0, len(sources), build, 0, unroll=2)
         base += len(sources)
 
 

time: 20.9 us -> 20.9 us (level)
  transfers between devices with their start and end apart: 7 -> 7, of which waited for: 3 -> 3; matrix products, arithmetic and copies ran while one was open for 0% -> 0% of each run, Pallas kernels for 30% -> 29%
where the time goes in v14:
time: 20.9 us; the launch traced here: 20.7 us
  Pallas kernels  10.8 us (52%)
  starting transfers between devices  8.45 us (40%)
  waiting for transfers between devices  1.36 us (7%)
    ppermute x3, starting transfers between devices, local(): lax.ppermute(p, 'tile', route(m))  4.41 us
    pallas_call x1, Pallas kernels, local(): pl.pallas_call(lambda *refs: prepare_kernel(n_det, n_tile, pairs, *refs),...  4.21 us
    ppermute x1, starting transfers between devices, local(): near_in = lax.ppermute(near, 'tile', near_pairs)  3.77 us
    pallas_call x1, Pallas kernels, local(): pl.pallas_call(lambda *refs: score_kernel(near_bit, masks, pairs, n_tile,...  3.54 us
    pallas_call x1, Pallas kernels, local(): pl.pallas_call(lambda *refs: pack_kernel(near_bit, masks, *refs), out_sha...  1.21 us
    pallas_call x1, Pallas kernels, local(): pl.pallas_call(lambda *refs: half_kernel(near_bit, masks, pairs, n_tile,...  1.17 us
    ppermute x1, waiting for transfers between devices, local(): near_swap = lax.ppermute(near_in, 'tile', mate)  0.6 us
    pallas_call x1, Pallas kernels, local(): pl.pallas_call(template_kernel, out_shape=(shape(NTPL, 2 * LEN, FP), shap...  0.59 us
  transfers between devices with their start and end apart: 7, of which 3 were waited for; matrix products, arithmetic and copies ran while one was open for 0% of the time, Pallas kernels for 29%

profile of v14, /device:TPU:1, one launch (start us, length us, event | category | flops | bytes accessed | tf_op | source)
XLA Modules:
  0.0 20.7 jit_solution(3445860357898120355)
XLA Ops:
  0.0 1.2 %shard_map.127 = (f32[2,61,256]{2,1,0:T(8,128)S(1)}, bf16[48,512]{1,0:T(8,128)(2,1)S(1)}, bf16[48,512]{1,0:T(8,128)(2,1)S(1)}, bf16[4,48,512]{2,1,0:T(8,128)(2,1)S(1)}, bf16[3,48,512]{2,1,0:T(8,128)(2,1)S(1)}) custom-call(s32[2,61]{1,0:T(2,128)} %bitcast.4, f32[1,61]{1,0:T(1,128)} %bitcast.5, bf16[61,8,256]{2,1,0:T(8,128)(2,1)} %bitcast.3), custom_call_target="tpu_custom_call" | custom-call | tf_op jit(solution)/shard_map/pallas_call | solution.py:433
  1.2 0.1 collective-permute-start
  1.3 3.8 %collective-permute-start.1 = (bf16[48,512]{1,0:T(8,128)(2,1)S(1)}, bf16[48,512]{1,0:T(8,128)(2,1)S(1)}, u32[]{:S(2)}, u32[]{:S(2)}) collective-permute-start(bf16[48,512]{1,0:T(8,128)(2,1)S(1)} %get-tuple-element.30), channel_id=1, source_target_pairs={{0,8},{1,9},{2,10},{3,11},{4,12},{5,13},{6,14},{7,15},{8,0},{9,1},... | collective-permute-start | bytes 147464 | tf_op jit(solution)/shard_map/ppermute | solution.py:454
  5.1 0.0 collective-permute-done.got_ref.refs_1_
  5.1 2.1 %collective-permute-start.3 = (bf16[2,48,512]{2,1,0:T(8,128)(2,1)S(1)}, bf16[2,48,512]{2,1,0:T(8,128)(2,1)S(1)}, u32[]{:S(2)}, u32[]{:S(2)}) collective-permute-start(bf16[2,48,512]{2,1,0:T(8,128)(2,1)S(1)} %get-tuple-element.39), channel_id=1, source_target_pairs={{0,4},{1,13},{2,6},{3,15},{4,0},{5,9},{6,2},{7,11},{8,12},{9,5},{1... | collective-permute-start | bytes 294920 | tf_op jit(solution)/shard_map/ppermute | solution.py:462
  7.3 1.4 %collective-permute-start.4 = (bf16[2,48,512]{2,1,0:T(8,128)(2,1)S(1)}, bf16[2,48,512]{2,1,0:T(8,128)(2,1)S(1)}, u32[]{:S(2)}, u32[]{:S(2)}) collective-permute-start(bf16[2,48,512]{2,1,0:T(8,128)(2,1)S(1)} %get-tuple-element.40), channel_id=1, source_target_pairs={{0,2},{1,11},{2,0},{3,9},{4,6},{5,15},{6,4},{7,13},{8,10},{9,3},{1... | collective-permute-start | bytes 294920 | tf_op jit(solution)/shard_map/ppermute | solution.py:462
  8.6 0.9 %collective-permute-start.5 = (bf16[2,48,512]{2,1,0:T(8,128)(2,1)S(1)}, bf16[2,48,512]{2,1,0:T(8,128)(2,1)S(1)}, u32[]{:S(2)}, u32[]{:S(2)}) collective-permute-start(bf16[2,48,512]{2,1,0:T(8,128)(2,1)S(1)} %get-tuple-element.41), channel_id=1, source_target_pairs={{0,6},{1,15},{2,4},{3,13},{4,2},{5,11},{6,0},{7,9},{8,14},{9,7},{1... | collective-permute-start | bytes 294920 | tf_op jit(solution)/shard_map/ppermute | solution.py:462
  9.6 4.2 %shard_map.129 = (bf16[34,512,256]{2,1,0:T(8,128)(2,1)S(1)}, bf16[640,2048]{1,0:T(8,128)(2,1)S(1)}, bf16[2048,512]{1,0:T(8,128)(2,1)S(1)}, bf16[128,2048]{1,0:T(8,128)(2,1)S(1)}, f32[8,128]{1,0:T(8,128)S(1)}) custom-call(f32[2,61,256]{2,1,0:T(8,128)S(1)} %get-tuple-element.31.refs_0_, f32[8,128]{1,0:T(8,128)S(1)} %get-tuple-element.33.refs_1_, s32[8]{0:T(128)} %refs_2_.1, ...), custom_call_target="tpu_custom_call" | custom-call | flops 4294967296 | bytes 16777216 | tf_op jit(solution)/shard_map/pallas_call | solution.py:468
  13.8 0.0 collective-permute-done.1.refs_2_
  13.8 0.1 collective-permute-start.2
  13.9 0.0 copy-done.1
  13.9 0.0 copy-done.3
  13.9 0.6 %shard_map.130 = (bf16[8,96,1024]{2,1,0:T(8,128)(2,1)S(1)}, f32[8,128]{1,0:T(8,128)S(1)}) custom-call(f32[8,128]{1,0:T(8,128)S(1)} %get-tuple-element.36._, bf16[128,2048]{1,0:T(8,128)(2,1)S(1)} %get-tuple-element.37.flat_ref, bf16[96,32]{1,0:T(8,128)(2,1)S(1)} %copy-done.1, f32[2,2,1024]{2,1,0:T(2,128)S(1)} %copy-done.3), custom_call_target="tpu_custom_call" | custom-call | flops 1048576 | bytes 16384 | tf_op jit(solution)/shard_map/pallas_call | solution.py:491
  14.5 0.6 %collective-permute-done.2.refs_3_ = bf16[48,512]{1,0:T(8,128)(2,1)S(1)} collective-permute-done((bf16[48,512]{1,0:T(8,128)(2,1)S(1)}, bf16[48,512]{1,0:T(8,128)(2,1)S(1)}, u32[]{:S(2)}, u32[]{:S(2)}) %collective-permute-start.2) | collective-permute-done | bytes 49184 | tf_op jit(solution)/shard_map/ppermute | solution.py:490
  15.1 0.0 collective-permute-done.3.refs_0_
  15.1 0.0 collective-permute-done.4.refs_1_
  15.1 0.4 %collective-permute-done.5.refs_2_ = bf16[2,48,512]{2,1,0:T(8,128)(2,1)S(1)} collective-permute-done((bf16[2,48,512]{2,1,0:T(8,128)(2,1)S(1)}, bf16[2,48,512]{2,1,0:T(8,128)(2,1)S(1)}, u32[]{:S(2)}, u32[]{:S(2)}) %collective-permute-start.5) | collective-permute-done | bytes 98336 | tf_op jit(solution)/shard_map/ppermute | solution.py:462
  15.5 0.1 collective-permute-start.6
  15.6 0.0 copy-start
  15.6 0.0 copy-start.2
  15.6 1.2 %shard_map.132.refs_5_ = f32[5,48,256]{2,1,0:T(8,128)S(1)} custom-call(bf16[48,512]{1,0:T(8,128)(2,1)S(1)} %get-tuple-element.28.refs_0_, bf16[4,48,512]{2,1,0:T(8,128)(2,1)S(1)} %collective-permute-done.got_ref.refs_1_, bf16[48,512]{1,0:T(8,128)(2,1)S(1)} %collective-permute-done.1.refs_2_, bf16[48,512]{1,0:T(8,128)(2,1)S(1)} %collective-permute-done.2.refs_3_, ...), custom_call_target="tpu_custom_call" | custom-call | flops 213909504 | bytes 4456448 | tf_op jit(solution)/shard_map/pallas_call | solution.py:509
  16.8 0.4 %collective-permute-done.6.refs_4_ = bf16[6,48,512]{2,1,0:T(8,128)(2,1)S(1)} collective-permute-done((bf16[6,48,512]{2,1,0:T(8,128)(2,1)S(1)}, bf16[6,48,512]{2,1,0:T(8,128)(2,1)S(1)}, u32[]{:S(2)}, u32[]{:S(2)}) %collective-permute-start.6) | collective-permute-done | bytes 294944 | tf_op jit(solution)/shard_map/ppermute | solution.py:507
  17.2 0.0 copy-done
  17.2 3.5 %shard_map.133 = f32[1,32,1024]{2,1,0:T(8,128)} custom-call(bf16[48,512]{1,0:T(8,128)(2,1)S(1)} %get-tuple-element.28.refs_0_, bf16[4,48,512]{2,1,0:T(8,128)(2,1)S(1)} %collective-permute-done.got_ref.refs_1_, bf16[48,512]{1,0:T(8,128)(2,1)S(1)} %collective-permute-done.1.refs_2_, bf16[48,512]{1,0:T(8,128)(2,1)S(1)} %collective-permute-done.2.refs_3_, ...), custom_call_target="tpu_custom_call" | custom-call | flops 4294967296 | bytes 20971520 | tf_op jit(solution)/shard_map/pallas_call | solution.py:518
  (5 shorter events, 0.0 us)
Async XLA Ops:
  1.2 3.9 %collective-permute-start = (bf16[4,48,512]{2,1,0:T(8,128)(2,1)S(1)}, bf16[4,48,512]{2,1,0:T(8,128)(2,1)S(1)}, u32[]{:S(2)}, u32[]{:S(2)}) collective-permute-start(bf16[4,48,512]{2,1,0:T(8,128)(2,1)S(1)} %get-tuple-element.29), channel_id=1, source_target_pairs={{0,1},{1,0},{2,3},{3,2},{4,5},{5,4},{6,7},{7,6},{8,9},{9,8},{10,11... | collective-permute-start | bytes 589832 | tf_op jit(solution)/shard_map/ppermute | solution.py:453
  1.3 12.4 %collective-permute-start.1 = (bf16[48,512]{1,0:T(8,128)(2,1)S(1)}, bf16[48,512]{1,0:T(8,128)(2,1)S(1)}, u32[]{:S(2)}, u32[]{:S(2)}) collective-permute-start(bf16[48,512]{1,0:T(8,128)(2,1)S(1)} %get-tuple-element.30), channel_id=1, source_target_pairs={{0,8},{1,9},{2,10},{3,11},{4,12},{5,13},{6,14},{7,15},{8,0},{9,1},... | collective-permute-start | bytes 147464 | tf_op jit(solution)/shard_map/ppermute | solution.py:454
  5.1 10.0 %collective-permute-start.3 = (bf16[2,48,512]{2,1,0:T(8,128)(2,1)S(1)}, bf16[2,48,512]{2,1,0:T(8,128)(2,1)S(1)}, u32[]{:S(2)}, u32[]{:S(2)}) collective-permute-start(bf16[2,48,512]{2,1,0:T(8,128)(2,1)S(1)} %get-tuple-element.39), channel_id=1, source_target_pairs={{0,4},{1,13},{2,6},{3,15},{4,0},{5,9},{6,2},{7,11},{8,12},{9,5},{1... | collective-permute-start | bytes 294920 | tf_op jit(solution)/shard_map/ppermute | solution.py:462
  7.3 7.8 %collective-permute-start.4 = (bf16[2,48,512]{2,1,0:T(8,128)(2,1)S(1)}, bf16[2,48,512]{2,1,0:T(8,128)(2,1)S(1)}, u32[]{:S(2)}, u32[]{:S(2)}) collective-permute-start(bf16[2,48,512]{2,1,0:T(8,128)(2,1)S(1)} %get-tuple-element.40), channel_id=1, source_target_pairs={{0,2},{1,11},{2,0},{3,9},{4,6},{5,15},{6,4},{7,13},{8,10},{9,3},{1... | collective-permute-start | bytes 294920 | tf_op jit(solution)/shard_map/ppermute | solution.py:462
  8.6 6.8 %collective-permute-start.5 = (bf16[2,48,512]{2,1,0:T(8,128)(2,1)S(1)}, bf16[2,48,512]{2,1,0:T(8,128)(2,1)S(1)}, u32[]{:S(2)}, u32[]{:S(2)}) collective-permute-start(bf16[2,48,512]{2,1,0:T(8,128)(2,1)S(1)} %get-tuple-element.41), channel_id=1, source_target_pairs={{0,6},{1,15},{2,4},{3,13},{4,2},{5,11},{6,0},{7,9},{8,14},{9,7},{1... | collective-permute-start | bytes 294920 | tf_op jit(solution)/shard_map/ppermute | solution.py:462
  9.6 4.3 %copy-start.1 = (bf16[96,32]{1,0:T(8,128)(2,1)S(1)}, bf16[96,32]{1,0:T(8,128)(2,1)}, u32[]{:S(2)}) copy-start(bf16[96,32]{1,0:T(8,128)(2,1)} %constant.20.clone.line_ref) | copy-start | bytes 18436
  9.6 4.3 %copy-start.3 = (f32[2,2,1024]{2,1,0:T(2,128)S(1)}, f32[2,2,1024]{2,1,0:T(2,128)}, u32[]{:S(2)}) copy-start(f32[2,2,1024]{2,1,0:T(2,128)} %constant.21.clone.turn_ref) | copy-start | bytes 49156
  13.8 1.3 %collective-permute-start.2 = (bf16[48,512]{1,0:T(8,128)(2,1)S(1)}, bf16[48,512]{1,0:T(8,128)(2,1)S(1)}, u32[]{:S(2)}, u32[]{:S(2)}) collective-permute-start(bf16[48,512]{1,0:T(8,128)(2,1)S(1)} %collective-permute-done.1.refs_2_), channel_id=1, source_target_pairs={{0,1},{1,0},{2,3},{3,2},{4,5},{5,4},{6,7},{7,6},{8,9},{9,8},{10,11... | collective-permute-start | bytes 147464 | tf_op jit(solution)/shard_map/ppermute | solution.py:490
  15.5 1.6 %collective-permute-start.6 = (bf16[6,48,512]{2,1,0:T(8,128)(2,1)S(1)}, bf16[6,48,512]{2,1,0:T(8,128)(2,1)S(1)}, u32[]{:S(2)}, u32[]{:S(2)}) collective-permute-start(bf16[6,48,512]{2,1,0:T(8,128)(2,1)S(1)} %shard_map.131.refs_4_), channel_id=1, source_target_pairs={{0,1},{1,0},{2,3},{3,2},{4,5},{5,4},{6,7},{7,6},{8,9},{9,8},{10,11... | collective-permute-start | bytes 884744 | tf_op jit(solution)/shard_map/ppermute | solution.py:507
  15.6 1.6 %copy-start = (bf16[96,96]{1,0:T(8,128)(2,1)S(1)}, bf16[96,96]{1,0:T(8,128)(2,1)}, u32[]{:S(2)}) copy-start(bf16[96,96]{1,0:T(8,128)(2,1)} %constant.22.clone.refs_9_) | copy-start | bytes 55300
  15.6 1.6 %copy-start.2 = (bf16[64,96]{1,0:T(8,128)(2,1)S(1)}, bf16[64,96]{1,0:T(8,128)(2,1)}, u32[]{:S(2)}) copy-start(bf16[64,96]{1,0:T(8,128)(2,1)} %constant.23.clone.refs_10_) | copy-start | bytes 36868
